TPU v7x, 32 devices: a whole 2x2x4 slice. The times are simulated.
32 devices in a mesh: fsdp: 8 (over z, x), dp: 4 (over y, core).
Axes of the slice: x: 2, y: 2, z: 4, core: 2. Of those that a mesh axis runs over, the one named last changes fastest.
Arguments:
- inputs: bfloat16 [18464, 1024], P(('fsdp', 'dp')), may hold values from -6 to 6
- cotangent: bfloat16 [18464, 1024], P(('fsdp', 'dp')), may hold values from -6 to 6
- norm1_gain: float32 [1024], P('fsdp'), may hold values from 0.08 to 2.5
- norm1_bias: float32 [1024], P('fsdp'), may hold values from -1.2 to 1.2
- qkv_weight: float32 [1024, 3072], P('fsdp'), may hold values from -0.1875 to 0.1875
- qv_bias: float32 [2048], P('fsdp'), may hold values from -3 to 3
- out_weight: float32 [1024, 1024], P('fsdp'), may hold values from -3 to 3
- out_bias: float32 [1024], P('fsdp'), may hold values from -3 to 3
- norm2_gain: float32 [1024], P('fsdp'), may hold values from 0.08 to 2.5
- norm2_bias: float32 [1024], P('fsdp'), may hold values from -1.2 to 1.2
- in_weight: float32 [1024, 4096], P('fsdp'), may hold values from -0.1875 to 0.1875
- in_bias: float32 [4096], P('fsdp'), may hold values from -3 to 3
- down_weight: float32 [4096, 1024], P('fsdp'), may hold values from -0.09375 to 0.09375
- down_bias: float32 [1024], P('fsdp'), may hold values from -3 to 3
- qkv_rows: float32 [1024], P('fsdp'), may hold values from 0.34375 to 196.875
- qkv_cols: float32 [3072], replicated, may hold values from 0.9375 to 93.75
- out_rows: float32 [1024], P('fsdp'), may hold values from 0.003125 to 2.8125
- out_cols: float32 [1024], replicated, may hold values from 0.009375 to 0.9375
- in_rows: float32 [1024], P('fsdp'), may hold values from 0.05625 to 31.5625
- in_cols: float32 [4096], replicated, may hold values from 0.15625 to 15.625
- down_rows: float32 [4096], P('fsdp'), may hold values from 0.20833333 to 187.5
- down_cols: float32 [1024], replicated, may hold values from 0.625 to 62.5
- norm1_gain_moment: float32 [1024], P('fsdp'), may hold values from 0.104166667 to 281.25
- norm1_bias_moment: float32 [1024], P('fsdp'), may hold values from 0.104166667 to 281.25
- qv_bias_moment: float32 [2048], P('fsdp'), may hold values from 0.104166667 to 281.25
- out_bias_moment: float32 [1024], P('fsdp'), may hold values from 0.104166667 to 281.25
- norm2_gain_moment: float32 [1024], P('fsdp'), may hold values from 0.104166667 to 281.25
- norm2_bias_moment: float32 [1024], P('fsdp'), may hold values from 0.104166667 to 281.25
- in_bias_moment: float32 [4096], P('fsdp'), may hold values from 0.104166667 to 281.25
- down_bias_moment: float32 [1024], P('fsdp'), may hold values from 0.104166667 to 281.25
Outputs:
- output: bfloat16 [18464, 1024], P(('fsdp', 'dp'))
- input_grad: bfloat16 [18464, 1024], P(('fsdp', 'dp'))
- grad_norm1_gain: float32 [1024], P('fsdp')
- grad_norm1_bias: float32 [1024], P('fsdp')
- grad_qkv_weight: float32 [1024, 3072], P('fsdp')
- grad_qv_bias: float32 [2048], P('fsdp')
- grad_out_weight: float32 [1024, 1024], P('fsdp')
- grad_out_bias: float32 [1024], P('fsdp')
- grad_norm2_gain: float32 [1024], P('fsdp')
- grad_norm2_bias: float32 [1024], P('fsdp')
- grad_in_weight: float32 [1024, 4096], P('fsdp')
- grad_in_bias: float32 [4096], P('fsdp')
- grad_down_weight: float32 [4096, 1024], P('fsdp')
- grad_down_bias: float32 [1024], P('fsdp')
- new_qkv_rows: float32 [1024], P('fsdp')
- new_qkv_cols: float32 [3072], replicated
- new_out_rows: float32 [1024], P('fsdp')
- new_out_cols: float32 [1024], replicated
- new_in_rows: float32 [1024], P('fsdp')
- new_in_cols: float32 [4096], replicated
- new_down_rows: float32 [4096], P('fsdp')
- new_down_cols: float32 [1024], replicated
- new_norm1_gain_moment: float32 [1024], P('fsdp')
- new_norm1_bias_moment: float32 [1024], P('fsdp')
- new_qv_bias_moment: float32 [2048], P('fsdp')
- new_out_bias_moment: float32 [1024], P('fsdp')
- new_norm2_gain_moment: float32 [1024], P('fsdp')
- new_norm2_bias_moment: float32 [1024], P('fsdp')
- new_in_bias_moment: float32 [4096], P('fsdp')
- new_down_bias_moment: float32 [1024], P('fsdp')
- new_norm1_gain: float32 [1024], P('fsdp')
- new_norm1_bias: float32 [1024], P('fsdp')
- new_qkv_weight: float32 [1024, 3072], P('fsdp')
- new_qv_bias: float32 [2048], P('fsdp')
- new_out_weight: float32 [1024, 1024], P('fsdp')
- new_out_bias: float32 [1024], P('fsdp')
- new_norm2_gain: float32 [1024], P('fsdp')
- new_norm2_bias: float32 [1024], P('fsdp')
- new_in_weight: float32 [1024, 4096], P('fsdp')
- new_in_bias: float32 [4096], P('fsdp')
- new_down_weight: float32 [4096, 1024], P('fsdp')
- new_down_bias: float32 [1024], P('fsdp')
- clip_factors: float32 [12], replicated
All inputs are finite; a program needn't handle non-finite values.
Results may differ from a plain program's by a relative error of at most 0.01.
The roundings to bfloat16 on the way count: a program that leaves them out, or rounds other values in their place, can miss the bound.
Values may be sent and summed in bfloat16 or wider, within the bound.
No kernel may reach another device: no remote copies, remote signals or barrier semaphores. Data moves between devices by JAX's collectives and lax.ppermute only.
A program may use at most 256 MiB of HBM per device.

v0:
```python
import math

import jax
import jax.numpy as jnp
from jax import lax
from jax.sharding import PartitionSpec as P

HEAD_DIM = 64
SEQ = 577


ln_eps = 1e-06
clip_level = 0.05
step_rate = 4.0


def norm_rows(values):
    centre = values - jnp.mean(values, axis=-1, keepdims=True)
    spread = jnp.mean(centre * centre, axis=-1, keepdims=True)
    return centre * lax.rsqrt(spread + ln_eps)


def norm_affine(values, gain_full, bias_full):
    return norm_rows(values) * gain_full + bias_full


def gelu_exact(values):
    return jax.nn.gelu(values, approximate=False)


def plain_dot(left, right):
    return jnp.dot(left, right, preferred_element_type=jnp.float32)


def lead_dot(left, right):
    return lax.dot_general(
        left, right, (((0,), (0,)), ((), ())), preferred_element_type=jnp.float32
    )


def tail_dot(left, right):
    return lax.dot_general(
        left, right, (((1,), (1,)), ((), ())), preferred_element_type=jnp.float32
    )


def split_heads(rows):
    return rows.reshape(rows.shape[0], rows.shape[1] // HEAD_DIM, HEAD_DIM)


def attend(block):
    query_rows, key_rows, value_rows = block
    length, width = query_rows.shape
    scale = 1.0 / math.sqrt(HEAD_DIM)
    scores = (
        jnp.einsum(
            "qhd,khd->hqk",
            split_heads(query_rows),
            split_heads(key_rows),
            preferred_element_type=jnp.float32,
        )
        * scale
    )
    highest = jnp.max(scores, axis=-1, keepdims=True)
    exponent = jnp.exp(scores - highest)
    summed = jnp.sum(exponent, axis=-1, keepdims=True)
    probs = exponent / summed
    mixed = jnp.einsum(
        "hqk,khd->qhd",
        probs.astype(jnp.bfloat16),
        split_heads(value_rows),
        preferred_element_type=jnp.float32,
    )
    logsum = (highest + jnp.log(summed))[..., 0]
    return (mixed.reshape(length, width).astype(jnp.bfloat16), logsum)


def attend_back(block):
    query_rows, key_rows, value_rows, logsum, grad_rows = block
    length, width = query_rows.shape
    scale = 1.0 / math.sqrt(HEAD_DIM)
    query_h = split_heads(query_rows)
    key_h = split_heads(key_rows)
    value_h = split_heads(value_rows)
    grad_h = split_heads(grad_rows)
    scores = jnp.einsum("qhd,khd->hqk", query_h, key_h, preferred_element_type=jnp.float32) * scale
    probs = jnp.exp(scores - logsum[..., None])
    grad_probs = jnp.einsum("qhd,khd->hqk", grad_h, value_h, preferred_element_type=jnp.float32)
    grad_value = jnp.einsum(
        "hqk,qhd->khd", probs.astype(jnp.bfloat16), grad_h, preferred_element_type=jnp.float32
    )
    inner = jnp.sum(probs * grad_probs, axis=-1, keepdims=True)
    grad_scores = (probs * (grad_probs - inner)).astype(jnp.bfloat16) * jnp.asarray(
        scale, jnp.bfloat16
    )
    grad_query = jnp.einsum("hqk,khd->qhd", grad_scores, key_h, preferred_element_type=jnp.float32)
    grad_key = jnp.einsum("hqk,qhd->khd", grad_scores, query_h, preferred_element_type=jnp.float32)
    joined = jnp.concatenate(
        [
            grad_query.reshape(length, width),
            grad_key.reshape(length, width),
            grad_value.reshape(length, width),
        ],
        axis=1,
    )
    return joined.astype(jnp.bfloat16)


def on_device(
    inputs,
    cotangent,
    norm1_gain,
    norm1_bias,
    qkv_weight,
    qv_bias,
    out_weight,
    out_bias,
    norm2_gain,
    norm2_bias,
    in_weight,
    in_bias,
    down_weight,
    down_bias,
    qkv_rows,
    qkv_cols,
    out_rows,
    out_cols,
    in_rows,
    in_cols,
    down_rows,
    down_cols,
    norm1_gain_moment,
    norm1_bias_moment,
    qv_bias_moment,
    out_bias_moment,
    norm2_gain_moment,
    norm2_bias_moment,
    in_bias_moment,
    down_bias_moment,
):
    masters = [
        norm1_gain,
        norm1_bias,
        qkv_weight,
        qv_bias,
        out_weight,
        out_bias,
        norm2_gain,
        norm2_bias,
        in_weight,
        in_bias,
        down_weight,
        down_bias,
    ]
    halves = [member.astype(jnp.bfloat16) for member in masters]
    gathered = (
        lax.all_gather(halves[0], "fsdp", axis=0, tiled=True),
        lax.all_gather(halves[1], "fsdp", axis=0, tiled=True),
        lax.all_gather(halves[2], "fsdp", axis=0, tiled=True),
        lax.all_gather(halves[3], "fsdp", axis=0, tiled=True),
        lax.all_gather(halves[4], "fsdp", axis=0, tiled=True),
        lax.all_gather(halves[5], "fsdp", axis=0, tiled=True),
        lax.all_gather(halves[6], "fsdp", axis=0, tiled=True),
        lax.all_gather(halves[7], "fsdp", axis=0, tiled=True),
        lax.all_gather(halves[8], "fsdp", axis=0, tiled=True),
        lax.all_gather(halves[9], "fsdp", axis=0, tiled=True),
        lax.all_gather(halves[10], "fsdp", axis=0, tiled=True),
        lax.all_gather(halves[11], "fsdp", axis=0, tiled=True),
    )
    (
        gain_one,
        bias_one,
        weight_qkv,
        bias_qv,
        weight_out,
        bias_out,
        gain_two,
        bias_two,
        weight_in,
        bias_in,
        weight_down,
        bias_down,
    ) = gathered
    tokens, width = inputs.shape
    images = tokens // SEQ
    rows_in = inputs.astype(jnp.float32)
    normed_f, pull_one = jax.vjp(
        norm_affine, rows_in, gain_one.astype(jnp.float32), bias_one.astype(jnp.float32)
    )
    normed = normed_f.astype(jnp.bfloat16)
    qkv = plain_dot(normed, weight_qkv)
    bias_pair = bias_qv.astype(jnp.float32)
    query = (qkv[:, :width] + bias_pair[:width]).astype(jnp.bfloat16)
    keys = qkv[:, width : 2 * width].astype(jnp.bfloat16)
    values = (qkv[:, 2 * width :] + bias_pair[width:]).astype(jnp.bfloat16)
    query_img = query.reshape(images, SEQ, width)
    keys_img = keys.reshape(images, SEQ, width)
    values_img = values.reshape(images, SEQ, width)
    attended_img, logsum = lax.map(attend, (query_img, keys_img, values_img))
    attended = attended_img.reshape(tokens, width)
    middle = rows_in + plain_dot(attended, weight_out) + bias_out.astype(jnp.float32)
    normed_mid_f, pull_two = jax.vjp(
        norm_affine, middle, gain_two.astype(jnp.float32), bias_two.astype(jnp.float32)
    )
    normed_mid = normed_mid_f.astype(jnp.bfloat16)
    preact = plain_dot(normed_mid, weight_in) + bias_in.astype(jnp.float32)
    hidden_f, pull_gelu = jax.vjp(gelu_exact, preact)
    hidden = hidden_f.astype(jnp.bfloat16)
    final = middle + plain_dot(hidden, weight_down) + bias_down.astype(jnp.float32)
    output = final.astype(jnp.bfloat16)
    grad_out_rows = cotangent.astype(jnp.float32)
    term_down_weight = lead_dot(hidden, cotangent)
    term_down_bias = jnp.sum(grad_out_rows, axis=0)
    grad_hidden = tail_dot(cotangent, weight_down)
    (grad_preact,) = pull_gelu(grad_hidden)
    grad_preact_low = grad_preact.astype(jnp.bfloat16)
    term_in_weight = lead_dot(normed_mid, grad_preact_low)
    term_in_bias = jnp.sum(grad_preact_low.astype(jnp.float32), axis=0)
    grad_normed_mid = tail_dot(grad_preact_low, weight_in)
    grad_mid_norm, term_gain_two, term_bias_two = pull_two(grad_normed_mid)
    grad_mid = grad_out_rows + grad_mid_norm
    grad_mid_low = grad_mid.astype(jnp.bfloat16)
    term_out_weight = lead_dot(attended, grad_mid_low)
    term_out_bias = jnp.sum(grad_mid_low.astype(jnp.float32), axis=0)
    grad_attended = tail_dot(grad_mid_low, weight_out).astype(jnp.bfloat16)
    grad_qkv_img = lax.map(
        attend_back,
        (query_img, keys_img, values_img, logsum, grad_attended.reshape(images, SEQ, width)),
    )
    grad_qkv = grad_qkv_img.reshape(tokens, 3 * width)
    term_qkv_weight = lead_dot(normed, grad_qkv)
    column_sums = jnp.sum(grad_qkv.astype(jnp.float32), axis=0)
    term_qv_bias = jnp.concatenate([column_sums[:width], column_sums[2 * width :]])
    grad_normed = tail_dot(grad_qkv, weight_qkv)
    grad_in_norm, term_gain_one, term_bias_one = pull_one(grad_normed)
    input_grad = (grad_mid + grad_in_norm).astype(jnp.bfloat16)
    terms = [
        term_gain_one,
        term_bias_one,
        term_qkv_weight,
        term_qv_bias,
        term_out_weight,
        term_out_bias,
        term_gain_two,
        term_bias_two,
        term_in_weight,
        term_in_bias,
        term_down_weight,
        term_down_bias,
    ]
    pieces = (
        lax.psum_scatter(terms[0], ("fsdp", "dp"), scatter_dimension=0, tiled=True),
        lax.psum_scatter(terms[1], ("fsdp", "dp"), scatter_dimension=0, tiled=True),
        lax.psum_scatter(terms[2], ("fsdp", "dp"), scatter_dimension=0, tiled=True),
        lax.psum_scatter(terms[3], ("fsdp", "dp"), scatter_dimension=0, tiled=True),
        lax.psum_scatter(terms[4], ("fsdp", "dp"), scatter_dimension=0, tiled=True),
        lax.psum_scatter(terms[5], ("fsdp", "dp"), scatter_dimension=0, tiled=True),
        lax.psum_scatter(terms[6], ("fsdp", "dp"), scatter_dimension=0, tiled=True),
        lax.psum_scatter(terms[7], ("fsdp", "dp"), scatter_dimension=0, tiled=True),
        lax.psum_scatter(terms[8], ("fsdp", "dp"), scatter_dimension=0, tiled=True),
        lax.psum_scatter(terms[9], ("fsdp", "dp"), scatter_dimension=0, tiled=True),
        lax.psum_scatter(terms[10], ("fsdp", "dp"), scatter_dimension=0, tiled=True),
        lax.psum_scatter(terms[11], ("fsdp", "dp"), scatter_dimension=0, tiled=True),
    )
    shards = (
        lax.all_gather(pieces[0], "dp", axis=0, tiled=True),
        lax.all_gather(pieces[1], "dp", axis=0, tiled=True),
        lax.all_gather(pieces[2], "dp", axis=0, tiled=True),
        lax.all_gather(pieces[3], "dp", axis=0, tiled=True),
        lax.all_gather(pieces[4], "dp", axis=0, tiled=True),
        lax.all_gather(pieces[5], "dp", axis=0, tiled=True),
        lax.all_gather(pieces[6], "dp", axis=0, tiled=True),
        lax.all_gather(pieces[7], "dp", axis=0, tiled=True),
        lax.all_gather(pieces[8], "dp", axis=0, tiled=True),
        lax.all_gather(pieces[9], "dp", axis=0, tiled=True),
        lax.all_gather(pieces[10], "dp", axis=0, tiled=True),
        lax.all_gather(pieces[11], "dp", axis=0, tiled=True),
    )
    group_size = lax.axis_size("fsdp")
    images_all = images * group_size * lax.axis_size("dp")
    grads = [member / images_all for member in shards]
    row_states = [qkv_rows, out_rows, in_rows, down_rows]
    col_states = [qkv_cols, out_cols, in_cols, down_cols]
    moments = [
        norm1_gain_moment,
        norm1_bias_moment,
        qv_bias_moment,
        out_bias_moment,
        norm2_gain_moment,
        norm2_bias_moment,
        in_bias_moment,
        down_bias_moment,
    ]
    matrix_slots = {2: 0, 4: 1, 8: 2, 10: 3}
    vector_slots = {0: 0, 1: 1, 3: 2, 5: 3, 6: 4, 7: 5, 9: 6, 11: 7}
    prepared = []
    packs = []
    for number in range(12):
        weight = masters[number]
        squared = grads[number] * grads[number]
        if number in matrix_slots:
            position = matrix_slots[number]
            new_rows = 0.5 * row_states[position] + 0.5 * jnp.mean(squared, axis=1)
            prepared.append(new_rows)
            packs.append(
                jnp.concatenate(
                    [
                        jnp.sum(squared, axis=0),
                        jnp.stack([jnp.sum(new_rows), jnp.sum(weight * weight)]),
                    ]
                )
            )
        else:
            position = vector_slots[number]
            prepared.append(0.5 * moments[position] + 0.5 * squared)
            packs.append(jnp.sum(weight * weight).reshape(1))
    totals = [lax.psum(packed, "fsdp") for packed in packs]
    directions = []
    counts = []
    weight_sums = []
    direction_sums = []
    new_cols_all = [None] * 4
    for number in range(12):
        weight = masters[number]
        grad = grads[number]
        if number in matrix_slots:
            position = matrix_slots[number]
            rows_total = weight.shape[0] * group_size
            new_cols = 0.5 * col_states[position] + 0.5 * totals[number][:-2] / rows_total
            new_cols_all[position] = new_cols
            mean_rows = totals[number][-2] / rows_total
            estimate = prepared[number][:, None] * new_cols[None, :] / mean_rows
            direction = grad * lax.rsqrt(estimate)
            counts.append(rows_total * weight.shape[1])
            weight_sums.append(totals[number][-1])
        else:
            direction = grad * lax.rsqrt(prepared[number])
            counts.append(weight.shape[0] * group_size)
            weight_sums.append(totals[number][0])
        directions.append(direction)
        direction_sums.append(jnp.sum(direction * direction))
    direction_totals = [lax.psum(value_sum, "fsdp") for value_sum in direction_sums]
    new_params = []
    clips = []
    for number in range(12):
        weight = masters[number]
        clip_factor = jnp.maximum(
            1.0, jnp.sqrt(direction_totals[number] / counts[number]) / clip_level
        )
        rms_weight = jnp.sqrt(weight_sums[number] / counts[number])
        new_params.append(weight - step_rate * rms_weight * directions[number] / clip_factor)
        clips.append(clip_factor)
    clip_factors = jnp.stack(clips)
    new_rows_all = [prepared[2], prepared[4], prepared[8], prepared[10]]
    new_moments = [
        prepared[0],
        prepared[1],
        prepared[3],
        prepared[5],
        prepared[6],
        prepared[7],
        prepared[9],
        prepared[11],
    ]
    return (
        output,
        input_grad,
        grads[0],
        grads[1],
        grads[2],
        grads[3],
        grads[4],
        grads[5],
        grads[6],
        grads[7],
        grads[8],
        grads[9],
        grads[10],
        grads[11],
        new_rows_all[0],
        new_cols_all[0],
        new_rows_all[1],
        new_cols_all[1],
        new_rows_all[2],
        new_cols_all[2],
        new_rows_all[3],
        new_cols_all[3],
        new_moments[0],
        new_moments[1],
        new_moments[2],
        new_moments[3],
        new_moments[4],
        new_moments[5],
        new_moments[6],
        new_moments[7],
        new_params[0],
        new_params[1],
        new_params[2],
        new_params[3],
        new_params[4],
        new_params[5],
        new_params[6],
        new_params[7],
        new_params[8],
        new_params[9],
        new_params[10],
        new_params[11],
        clip_factors,
    )


def solution(mesh):
    in_specs = (
        P(("fsdp", "dp"), None),
        P(("fsdp", "dp"), None),
        P("fsdp"),
        P("fsdp"),
        P("fsdp", None),
        P("fsdp"),
        P("fsdp", None),
        P("fsdp"),
        P("fsdp"),
        P("fsdp"),
        P("fsdp", None),
        P("fsdp"),
        P("fsdp", None),
        P("fsdp"),
        P("fsdp"),
        P(),
        P("fsdp"),
        P(),
        P("fsdp"),
        P(),
        P("fsdp"),
        P(),
        P("fsdp"),
        P("fsdp"),
        P("fsdp"),
        P("fsdp"),
        P("fsdp"),
        P("fsdp"),
        P("fsdp"),
        P("fsdp"),
    )
    out_specs = (
        P(("fsdp", "dp"), None),
        P(("fsdp", "dp"), None),
        P("fsdp"),
        P("fsdp"),
        P("fsdp", None),
        P("fsdp"),
        P("fsdp", None),
        P("fsdp"),
        P("fsdp"),
        P("fsdp"),
        P("fsdp", None),
        P("fsdp"),
        P("fsdp", None),
        P("fsdp"),
        P("fsdp"),
        P(),
        P("fsdp"),
        P(),
        P("fsdp"),
        P(),
        P("fsdp"),
        P(),
        P("fsdp"),
        P("fsdp"),
        P("fsdp"),
        P("fsdp"),
        P("fsdp"),
        P("fsdp"),
        P("fsdp"),
        P("fsdp"),
        P("fsdp"),
        P("fsdp"),
        P("fsdp", None),
        P("fsdp"),
        P("fsdp", None),
        P("fsdp"),
        P("fsdp"),
        P("fsdp"),
        P("fsdp", None),
        P("fsdp"),
        P("fsdp", None),
        P("fsdp"),
        P(),
    )
    return jax.shard_map(
        on_device, mesh=mesh, in_specs=in_specs, out_specs=out_specs, check_vma=False
    )
```

profile of v0, /device:TPU:0, one launch (start us, length us, event | category | flops | bytes accessed | tf_op | source)
XLA Modules:
  0.0 1458.6 jit_solution(12676742999869469270)
XLA Ops:
  21.2 22.4 %all-gather.5 = bf16[8,1,128]{2,1,0:T(2,128)(2,1)S(1)} all-gather(bf16[1,1,128]{2,1,0:T(2,128)(2,1)S(1)} %get-tuple-element.209), channel_id=1, replica_groups=mesh['fsdp'=8,'dp'=4] {'fsdp'}, dimensions={0}, use_global_device_ids=true | all-gather | bytes 2304 | tf_op jit(solution)/shard_map/all_gather | solution.py:164
  44.2 16.4 %all-gather.4 = bf16[8,1,128]{2,1,0:T(2,128)(2,1)S(1)} all-gather(bf16[1,1,128]{2,1,0:T(2,128)(2,1)S(1)} %get-tuple-element.211), channel_id=1, replica_groups=mesh['fsdp'=8,'dp'=4] {'fsdp'}, dimensions={0}, use_global_device_ids=true | all-gather | bytes 2304 | tf_op jit(solution)/shard_map/all_gather | solution.py:163
  61.2 18.2 %all-gather.3 = bf16[8,1,128]{2,1,0:T(2,128)(2,1)S(1)} all-gather(bf16[1,1,128]{2,1,0:T(2,128)(2,1)S(1)} %get-tuple-element.213), channel_id=1, replica_groups=mesh['fsdp'=8,'dp'=4] {'fsdp'}, dimensions={0}, use_global_device_ids=true | all-gather | bytes 2304 | tf_op jit(solution)/shard_map/all_gather | solution.py:162
  80.0 16.5 %all-gather.1 = bf16[8,1,128]{2,1,0:T(2,128)(2,1)S(1)} all-gather(bf16[1,1,128]{2,1,0:T(2,128)(2,1)S(1)} %get-tuple-element.215), channel_id=1, replica_groups=mesh['fsdp'=8,'dp'=4] {'fsdp'}, dimensions={0}, use_global_device_ids=true | all-gather | bytes 2304 | tf_op jit(solution)/shard_map/all_gather | solution.py:158
  97.2 18.0 %all-gather = bf16[8,1,128]{2,1,0:T(2,128)(2,1)S(1)} all-gather(bf16[1,1,128]{2,1,0:T(2,128)(2,1)S(1)} %get-tuple-element.217), channel_id=1, replica_groups=mesh['fsdp'=8,'dp'=4] {'fsdp'}, dimensions={0}, use_global_device_ids=true | all-gather | bytes 2304 | tf_op jit(solution)/shard_map/all_gather | solution.py:157
  115.2 26.1 %all-gather.6 = bf16[8,1,512]{2,1,0:T(2,128)(2,1)S(1)} all-gather(bf16[1,1,512]{2,1,0:T(2,128)(2,1)S(1)} %reshape.379), channel_id=1, replica_groups=mesh['fsdp'=8,'dp'=4] {'fsdp'}, dimensions={0}, use_global_device_ids=true | all-gather | bytes 9216 | tf_op jit(solution)/shard_map/all_gather | solution.py:166
  141.3 16.6 %all-gather.2 = bf16[8,1,256]{2,1,0:T(2,128)(2,1)S(1)} all-gather(bf16[1,1,256]{2,1,0:T(2,128)(2,1)S(1)} %reshape.371), channel_id=1, replica_groups=mesh['fsdp'=8,'dp'=4] {'fsdp'}, dimensions={0}, use_global_device_ids=true | all-gather | bytes 4608 | tf_op jit(solution)/shard_map/all_gather | solution.py:160
  174.0 10.1 multiply_reduce_fusion.1
  184.1 10.6 fusion.2
  194.6 11.5 fusion.60
  211.1 78.8 %all-gather.21.cloned.1.call-done = bf16[1024,4096]{1,0:T(8,128)(2,1)} async-done(((bf16[128,4096]{1,0:T(8,128)(2,1)}), bf16[1024,4096]{1,0:T(8,128)(2,1)}) %all-gather.21.cloned.1.call-update) | async-done | bytes 8388624 | tf_op jit(solution)/shard_map/all_gather | solution.py:165
  289.9 11.5 fusion.85
  301.4 114.2 %all-gather.23.cloned.1.call-done = bf16[4096,1024]{1,0:T(8,128)(2,1)} async-done(((bf16[512,1024]{1,0:T(8,128)(2,1)}), bf16[4096,1024]{1,0:T(8,128)(2,1)}) %all-gather.23.cloned.1.call-update) | async-done | bytes 8388624 | tf_op jit(solution)/shard_map/all_gather | solution.py:167
  415.6 30.8 %convert_reduce_fusion = (f32[4096]{0:T(1024)S(1)}, bf16[577,4096]{1,0:T(8,128)(2,1)S(1)}, f32[577,4096]{1,0:T(8,128)}) fusion(f32[577,4096]{1,0:T(8,128)} %fusion.85, f32[4096]{0:T(1024)S(1)} %bitcast.135, bf16[577,1024]{1,0:T(8,128)(2,1)} %param.31, bf16[4096,1024]{1,0:T(8,128)(2,1)} %all-gather.23.cloned.1.call-done), kind=kOutput, calls=%fused_computation.22 | convolution fusion | flops 5017477120 | bytes 33236992 | tf_op jit(solution)/shard_map/dot_general | solution.py:42
  460.6 13.6 fusion.101
  474.2 13.4 fusion.57
  487.7 32.9 %fusion.47 = bf16[16,64,577]{2,1,0:T(8,128)(2,1)} fusion(bf16[577,16,64]{0,2,1:T(8,128)(2,1)} %bitcast.120, f32[16,577,577]{1,2,0:T(8,128)} %fusion.101, f32[16,577,577]{1,2,0:T(8,128)} %get-tuple-element.219, f32[16,577]{1,0:T(8,128)S(1)} %copy-done.23), kind=kOutput, calls=%fused_computation.85 | convolution fusion | flops 746361600 | bytes 45015232 | tf_op jit(solution)/shard_map/while/body/eval_jaxpr/hqk,khd->qhd/dot_general | solution.py:96
  520.6 33.0 %fusion.52 = bf16[16,64,577]{2,1,0:T(8,128)(2,1)} fusion(bf16[577,16,64]{0,2,1:T(8,128)(2,1)} %bitcast.118, f32[16,577,577]{1,2,0:T(8,128)} %fusion.101, f32[16,577,577]{1,2,0:T(8,128)} %get-tuple-element.219, f32[16,577]{1,0:T(8,128)S(1)} %copy-done.23), kind=kOutput, calls=%fused_computation.86 | convolution fusion | flops 746361600 | bytes 45015232 | tf_op jit(solution)/shard_map/while/body/eval_jaxpr/hqk,qhd->khd/dot_general | solution.py:97
  553.6 12.5 fusion.78
  566.8 13.0 fusion.84
  580.1 12.0 multiply_convert_fusion.1
  592.1 12.5 fusion.103
  610.3 109.9 %reduce-scatter.5.cloned.1.call-done = f32[32,3072]{1,0:T(8,128)} async-done(((f32[1024,3072]{1,0:T(8,128)}), f32[32,3072]{1,0:T(8,128)}) %reduce-scatter.5.cloned.1.call-update) | async-done | bytes 393232 | tf_op jit(solution)/shard_map/reduce_scatter | solution.py:254
  725.6 179.0 %reduce-scatter.9.cloned.1.call-done = f32[32,4096]{1,0:T(8,128)} async-done(((f32[1024,4096]{1,0:T(8,128)}), f32[32,4096]{1,0:T(8,128)}) %reduce-scatter.9.cloned.1.call-update) | async-done | bytes 524304 | tf_op jit(solution)/shard_map/reduce_scatter | solution.py:260
  918.4 47.9 %all-reduce.15 = (f32[1024]{0:T(1024)S(1)}, f32[1024]{0:T(1024)S(1)}, f32[2048]{0:T(1024)S(1)}, f32[1024]{0:T(1024)S(1)}, f32[1024]{0:T(1024)S(1)}, /*index=5*/f...) all-reduce(f32[1024]{0:T(1024)S(1)} %get-tuple-element.84, ...), channel_id=2, replica_groups=mesh['fsdp'=8,'dp'=4] {'fsdp','dp'}, use_global_device_ids=true, to_apply=%region_12.13.clone | all-reduce | flops 12288 | bytes 98304
  967.3 126.2 %reduce-scatter.11.cloned.1.call-done = f32[128,1024]{1,0:T(8,128)} async-done(((f32[4096,1024]{1,0:T(8,128)}), f32[128,1024]{1,0:T(8,128)}) %reduce-scatter.11.cloned.1.call-update) | async-done | bytes 524304 | tf_op jit(solution)/shard_map/reduce_scatter | solution.py:262
  1108.3 131.2 %reduce-scatter.7.cloned.1.call-done = f32[32,1024]{1,0:T(8,128)} async-done(((f32[1024,1024]{1,0:T(8,128)}), f32[32,1024]{1,0:T(8,128)}) %reduce-scatter.7.cloned.1.call-update) | async-done | bytes 131088 | tf_op jit(solution)/shard_map/reduce_scatter | solution.py:256
  1261.5 19.4 %all-gather.27.cloned.1.call-done = f32[128,4096]{1,0:T(8,128)} async-done(((f32[32,4096]{1,0:T(8,128)}), f32[128,4096]{1,0:T(8,128)}) %all-gather.27.cloned.1.call-update) | async-done | bytes 2097168 | tf_op jit(solution)/shard_map/all_gather | solution.py:274
  1284.7 20.4 %all-gather.29.cloned.1.call-done = f32[512,1024]{1,0:T(8,128)} async-done(((f32[128,1024]{1,0:T(8,128)}), f32[512,1024]{1,0:T(8,128)}) %all-gather.29.cloned.1.call-update) | async-done | bytes 2097168 | tf_op jit(solution)/shard_map/all_gather | solution.py:276
  1311.6 37.8 %all-reduce.17 = (f32[3074]{0:T(1024)S(1)}, f32[1026]{0:T(1024)S(1)}, f32[4098]{0:T(1024)S(1)}, f32[1026]{0:T(1024)S(1)}) all-reduce(f32[3074]{0:T(1024)S(1)} %concatenate.22, f32[1026]{0:T(1024)S(1)} %concatenate.23, f32[4098]{0:T(1024)S(1)} %concatenate.24, f32[1026]{0:T(1024)S(1)} %concatenate.25), channel_id=1, replica_groups=mesh['fsdp'=8,'dp'=4] {'fsdp'}, use_global_device_ids=true, to_apply=%region_35.36 | all-reduce | flops 9224 | bytes 73792 | tf_op jit(solution)/shard_map/psum | solution.py:317
  1364.0 33.0 %all-reduce.16 = (f32[]{:T(128)}, f32[1]{0:T(128)}, f32[]{:T(128)}, f32[1]{0:T(128)}, f32[]{:T(128)}, /*index=5*/f32[]{:T(128)}, f32[1]{0:T(128)}, f32[]{:T(128)...) all-reduce(f32[]{:T(128)} %get-tuple-element.230, ...), channel_id=1, replica_groups=mesh['fsdp'=8,'dp'=4] {'fsdp'}, use_global_device_ids=true, to_apply=%region_54.55 | all-reduce | flops 20 | bytes 160 | tf_op jit(solution)/shard_map/psum | solution.py:342
  1412.1 16.5 %all-gather.7 = bf16[8,1,128]{2,1,0:T(2,128)(2,1)S(1)} all-gather(bf16[1,1,128]{2,1,0:T(2,128)(2,1)S(1)} %get-tuple-element.207), channel_id=1, replica_groups=mesh['fsdp'=8,'dp'=4] {'fsdp'}, dimensions={0}, use_global_device_ids=true | all-gather | bytes 2304 | tf_op jit(solution)/shard_map/all_gather | solution.py:168
  (322 shorter events, 157.2 us)
Async XLA Ops:
  7.3 151.4 %all-gather.17.cloned.1.call-start = ((), (), s32[]{:S(2)}) async-start(), calls=%async_computation.4 | async-start | bytes 7077888 | tf_op jit(solution)/shard_map/all_gather | solution.py:159
  11.2 195.0 %all-gather.19.cloned.1.call-start = ((), (), s32[]{:S(2)}) async-start(), calls=%async_computation.5 | async-start | bytes 2359296 | tf_op jit(solution)/shard_map/all_gather | solution.py:161
  12.6 277.3 %all-gather.21.cloned.1.call-start = ((), (), s32[]{:S(2)}) async-start(), calls=%async_computation.6 | async-start | bytes 9437184 | tf_op jit(solution)/shard_map/all_gather | solution.py:165
  14.8 400.8 %all-gather.23.cloned.1.call-start = ((), (), s32[]{:S(2)}) async-start(), calls=%async_computation.7 | async-start | bytes 9437184 | tf_op jit(solution)/shard_map/all_gather | solution.py:167
  19.2 701.0 %reduce-scatter.5.cloned.1.call-start = ((), (), s32[]{:S(2)}) async-start(), calls=%async_computation.8 | async-start | bytes 12976128 | tf_op jit(solution)/shard_map/reduce_scatter | solution.py:254
  43.6 246.3 %copy-start.21 = (f32[8,1,128]{2,1,0:T(1,128)}, f32[8,1,128]{2,1,0:T(1,128)S(1)}, u32[]{:S(2)}) copy-start(f32[8,1,128]{2,1,0:T(1,128)S(1)} %convert_element_type.176) | copy-start | bytes 12292
  566.2 338.5 %reduce-scatter.9.cloned.1.call-start = ((), (), s32[]{:S(2)}) async-start(), calls=%async_computation.11 | async-start | bytes 17301504 | tf_op jit(solution)/shard_map/reduce_scatter | solution.py:260
  579.8 513.8 %reduce-scatter.11.cloned.1.call-start = ((), (), s32[]{:S(2)}) async-start(), calls=%async_computation.13 | async-start | bytes 17301504 | tf_op jit(solution)/shard_map/reduce_scatter | solution.py:262
  604.6 634.9 %reduce-scatter.7.cloned.1.call-start = ((), (), s32[]{:S(2)}) async-start(), calls=%async_computation.10 | async-start | bytes 4325376 | tf_op jit(solution)/shard_map/reduce_scatter | solution.py:256
  610.2 646.5 %all-gather.25.cloned.1.call-start = ((), (), s32[]{:S(2)}) async-start(), calls=%async_computation.9 | async-start | bytes 1966080 | tf_op jit(solution)/shard_map/all_gather | solution.py:268
  720.2 560.6 %all-gather.27.cloned.1.call-start = ((), (), s32[]{:S(2)}) async-start(), calls=%async_computation.12 | async-start | bytes 2621440 | tf_op jit(solution)/shard_map/all_gather | solution.py:274
  904.7 400.4 %all-gather.29.cloned.1.call-start = ((), (), s32[]{:S(2)}) async-start(), calls=%async_computation.14 | async-start | bytes 2621440 | tf_op jit(solution)/shard_map/all_gather | solution.py:276
  916.2 189.7 %copy-start.71 = (f32[128]{0:T(128)S(1)}, f32[128]{0:T(128)}, u32[]{:S(2)}) copy-start(f32[128]{0:T(128)} %param.56) | copy-start | bytes 1540
  916.2 189.7 %copy-start.72 = (f32[128]{0:T(128)S(1)}, f32[128]{0:T(128)}, u32[]{:S(2)}) copy-start(f32[128]{0:T(128)} %param.55) | copy-start | bytes 1540
  916.2 190.3 %copy-start.73 = (f32[128]{0:T(128)S(1)}, f32[128]{0:T(128)}, u32[]{:S(2)}) copy-start(f32[128]{0:T(128)} %param.59) | copy-start | bytes 1540
  916.2 190.3 %copy-start.74 = (f32[128]{0:T(128)S(1)}, f32[128]{0:T(128)}, u32[]{:S(2)}) copy-start(f32[128]{0:T(128)} %param.57) | copy-start | bytes 1540
  916.2 191.5 %copy-start.56 = (f32[512]{0:T(512)S(1)}, f32[512]{0:T(512)}, u32[]{:S(2)}) copy-start(f32[512]{0:T(512)} %param.58) | copy-start | bytes 6148
  918.4 328.0 %copy-start.76 = (f32[128]{0:T(128)S(1)}, f32[128]{0:T(128)}, u32[]{:S(2)}) copy-start(f32[128]{0:T(128)} %param.46) | copy-start | bytes 1540
  1104.6 333.2 %copy-start.37 = (f32[4,1,128]{2,1,0:T(1,128)}, f32[4,1,128]{2,1,0:T(1,128)S(1)}, u32[]{:S(2)}) copy-start(f32[4,1,128]{2,1,0:T(1,128)S(1)} %broadcast_multiply_fusion.6) | copy-start | bytes 6148
  1105.2 335.8 %copy-start.50 = (f32[256]{0:T(256)}, f32[256]{0:T(256)S(1)}, u32[]{:S(2)}) copy-start(f32[256]{0:T(256)S(1)} %get-tuple-element.151) | copy-start | bytes 3076
  1105.2 335.8 %copy-start.51 = (f32[256]{0:T(256)}, f32[256]{0:T(256)S(1)}, u32[]{:S(2)}) copy-start(f32[256]{0:T(256)S(1)} %get-tuple-element.152) | copy-start | bytes 3076
  1105.8 332.5 %copy-start.60 = (f32[128]{0:T(128)}, f32[128]{0:T(128)S(1)}, u32[]{:S(2)}) copy-start(f32[128]{0:T(128)S(1)} %get-tuple-element.231) | copy-start | bytes 1540
  1105.8 332.5 %copy-start.61 = (f32[128]{0:T(128)}, f32[128]{0:T(128)S(1)}, u32[]{:S(2)}) copy-start(f32[128]{0:T(128)S(1)} %get-tuple-element.232) | copy-start | bytes 1540
  1105.8 333.0 %copy-start.58 = (f32[128]{0:T(128)}, f32[128]{0:T(128)S(1)}, u32[]{:S(2)}) copy-start(f32[128]{0:T(128)S(1)} %get-tuple-element.154) | copy-start | bytes 1540
  1105.8 333.0 %copy-start.59 = (f32[128]{0:T(128)}, f32[128]{0:T(128)S(1)}, u32[]{:S(2)}) copy-start(f32[128]{0:T(128)S(1)} %get-tuple-element.155) | copy-start | bytes 1540
  1106.5 332.9 %copy-start.64 = (f32[128]{0:T(128)}, f32[128]{0:T(128)S(1)}, u32[]{:S(2)}) copy-start(f32[128]{0:T(128)S(1)} %get-tuple-element.228) | copy-start | bytes 1540
  1106.5 332.9 %copy-start.65 = (f32[128]{0:T(128)}, f32[128]{0:T(128)S(1)}, u32[]{:S(2)}) copy-start(f32[128]{0:T(128)S(1)} %get-tuple-element.229) | copy-start | bytes 1540
  1106.5 333.4 %copy-start.62 = (f32[128]{0:T(128)}, f32[128]{0:T(128)S(1)}, u32[]{:S(2)}) copy-start(f32[128]{0:T(128)S(1)} %get-tuple-element.145) | copy-start | bytes 1540
  1106.5 333.4 %copy-start.63 = (f32[128]{0:T(128)}, f32[128]{0:T(128)S(1)}, u32[]{:S(2)}) copy-start(f32[128]{0:T(128)S(1)} %get-tuple-element.146) | copy-start | bytes 1540
  1107.7 303.1 %copy-start.54 = (f32[128]{0:T(128)}, f32[128]{0:T(128)S(1)}, u32[]{:S(2)}) copy-start(f32[128]{0:T(128)S(1)} %get-tuple-element.137) | copy-start | bytes 1540
  1107.7 303.1 %copy-start.55 = (f32[128]{0:T(128)}, f32[128]{0:T(128)S(1)}, u32[]{:S(2)}) copy-start(f32[128]{0:T(128)S(1)} %get-tuple-element.138) | copy-start | bytes 1540
  1108.3 329.4 %copy-start.42 = (f32[512]{0:T(512)}, f32[512]{0:T(512)S(1)}, u32[]{:S(2)}) copy-start(f32[512]{0:T(512)S(1)} %get-tuple-element.140) | copy-start | bytes 6148
  (71 other events, 3300.1 us)
Sparse Core Ops, SparseCore 0:
  11.3 101.9 all-gather.16
  116.0 47.6 all-gather.18
  166.4 123.4 all-gather.20
  292.4 123.1 all-gather.22
  566.3 153.8 reduce-scatter.4
  722.5 182.1 reduce-scatter.8
  907.1 186.4 reduce-scatter.10
  1096.0 143.4 reduce-scatter.6
  1241.1 15.5 all-gather.24
  1258.2 22.6 all-gather.26
  1282.5 22.5 all-gather.28
where the time goes:
time: 1460 us
  waiting for transfers between devices  788 us (54%)
  blocking collectives  287 us (20%)
  matrix products  237 us (16%)
  other arithmetic  86.3 us (6%)
  between operations  35.5 us (2%)
  local copies, waits for them, and re-layouts  23.8 us (2%)
    reduce_scatter x1, waiting for transfers between devices, on_device(): lax.psum_scatter(terms[8], ('fsdp', 'dp'), scatter_dimension=0, tiled=True)  179 us
    reduce_scatter x1, waiting for transfers between devices, on_device(): lax.psum_scatter(terms[4], ('fsdp', 'dp'), scatter_dimension=0, tiled=True)  131 us
    reduce_scatter x1, waiting for transfers between devices, on_device(): lax.psum_scatter(terms[10], ('fsdp', 'dp'), scatter_dimension=0, tiled=True)  126 us
    all_gather x1, waiting for transfers between devices, on_device(): lax.all_gather(halves[10], 'fsdp', axis=0, tiled=True)  114 us
    reduce_scatter x1, waiting for transfers between devices, on_device(): lax.psum_scatter(terms[2], ('fsdp', 'dp'), scatter_dimension=0, tiled=True)  110 us
    all_gather x1, waiting for transfers between devices, on_device(): lax.all_gather(halves[8], 'fsdp', axis=0, tiled=True)  78.8 us
    unnamed x2, blocking collectives  53.6 us
    dot_general x4, matrix products, tail_dot(): lax.dot_general(left, right, (((1,), (1,)), ((), ())), preferred_element_...  47.7 us
  transfers between devices with their start and end apart: 11, of which 9 were waited for; matrix products, arithmetic and copies ran while one was open for 10% of the time, Pallas kernels for 0%

commit v1 on v0

v1 whole, which is shorter than its diff:
```python
import math

import jax
import jax.numpy as jnp
from jax import lax
from jax.experimental import pallas as pl
from jax.experimental.pallas import tpu as pltpu
from jax.sharding import Mesh
from jax.sharding import PartitionSpec as P

HEAD_DIM = 64
SEQ = 577


ln_eps = 1e-06
clip_level = 0.05
step_rate = 4.0


def norm_rows(values):
    centre = values - jnp.mean(values, axis=-1, keepdims=True)
    spread = jnp.mean(centre * centre, axis=-1, keepdims=True)
    return centre * lax.rsqrt(spread + ln_eps)


def norm_affine(values, gain_full, bias_full):
    return norm_rows(values) * gain_full + bias_full


def gelu_exact(values):
    return jax.nn.gelu(values, approximate=False)


def plain_dot(left, right):
    return jnp.dot(left, right, preferred_element_type=jnp.float32)


def lead_dot(left, right):
    return lax.dot_general(
        left, right, (((0,), (0,)), ((), ())), preferred_element_type=jnp.float32
    )


def tail_dot(left, right):
    return lax.dot_general(
        left, right, (((1,), (1,)), ((), ())), preferred_element_type=jnp.float32
    )


def split_heads(rows):
    return rows.reshape(rows.shape[0], rows.shape[1] // HEAD_DIM, HEAD_DIM)


def attend(block):
    query_rows, key_rows, value_rows = block
    length, width = query_rows.shape
    scale = 1.0 / math.sqrt(HEAD_DIM)
    scores = (
        jnp.einsum(
            "qhd,khd->hqk",
            split_heads(query_rows),
            split_heads(key_rows),
            preferred_element_type=jnp.float32,
        )
        * scale
    )
    highest = jnp.max(scores, axis=-1, keepdims=True)
    exponent = jnp.exp(scores - highest)
    summed = jnp.sum(exponent, axis=-1, keepdims=True)
    probs = exponent / summed
    mixed = jnp.einsum(
        "hqk,khd->qhd",
        probs.astype(jnp.bfloat16),
        split_heads(value_rows),
        preferred_element_type=jnp.float32,
    )
    logsum = (highest + jnp.log(summed))[..., 0]
    return (mixed.reshape(length, width).astype(jnp.bfloat16), logsum)


def attend_back(block):
    query_rows, key_rows, value_rows, logsum, grad_rows = block
    length, width = query_rows.shape
    scale = 1.0 / math.sqrt(HEAD_DIM)
    query_h = split_heads(query_rows)
    key_h = split_heads(key_rows)
    value_h = split_heads(value_rows)
    grad_h = split_heads(grad_rows)
    scores = jnp.einsum("qhd,khd->hqk", query_h, key_h, preferred_element_type=jnp.float32) * scale
    probs = jnp.exp(scores - logsum[..., None])
    grad_probs = jnp.einsum("qhd,khd->hqk", grad_h, value_h, preferred_element_type=jnp.float32)
    grad_value = jnp.einsum(
        "hqk,qhd->khd", probs.astype(jnp.bfloat16), grad_h, preferred_element_type=jnp.float32
    )
    inner = jnp.sum(probs * grad_probs, axis=-1, keepdims=True)
    grad_scores = (probs * (grad_probs - inner)).astype(jnp.bfloat16) * jnp.asarray(
        scale, jnp.bfloat16
    )
    grad_query = jnp.einsum("hqk,khd->qhd", grad_scores, key_h, preferred_element_type=jnp.float32)
    grad_key = jnp.einsum("hqk,qhd->khd", grad_scores, query_h, preferred_element_type=jnp.float32)
    joined = jnp.concatenate(
        [
            grad_query.reshape(length, width),
            grad_key.reshape(length, width),
            grad_value.reshape(length, width),
        ],
        axis=1,
    )
    return joined.astype(jnp.bfloat16)


ALL_AXES = ("z", "x", "y", "c")


def swap(value, axis):
    return lax.ppermute(value, axis, [(0, 1), (1, 0)])


def shift(value, axis, step):
    size = lax.axis_size(axis)
    return lax.ppermute(value, axis, [(i, (i + step) % size) for i in range(size)])


def partner(value, axis, step):
    size = lax.axis_size(axis)
    return lax.ppermute(value, axis, [(i, i ^ step) for i in range(size)])


def sum_over(value, axes):
    for axis in axes:
        step = 1
        while step < lax.axis_size(axis):
            value = value + partner(value, axis, step)
            step *= 2
    return value


def gather_small(vector):
    value = vector[None, :]
    for axis in ("x", "z"):
        step = 1
        while step < lax.axis_size(axis):
            other = partner(value, axis, step)
            low = (lax.axis_index(axis) // step) % 2 == 0
            value = jnp.where(
                low,
                jnp.concatenate([value, other], axis=0),
                jnp.concatenate([other, value], axis=0),
            )
            step *= 2
    return value


def gather_pieces(shard):
    half_rows = shard.shape[0] // 2
    core = lax.axis_index("c")
    half = lax.dynamic_slice_in_dim(shard, core * half_rows, half_rows, 0)
    rest = lax.dynamic_slice_in_dim(shard, (1 - core) * half_rows, half_rows, 0)
    along = [half] + [shift(half, "z", k) for k in range(1, lax.axis_size("z"))]
    pieces = []
    for k, near in enumerate(along):
        across = swap(near, "x")
        pieces.append(
            [[near, rest if k == 0 else swap(near, "c")], [across, swap(across, "c")]]
        )
    return pieces


def assemble(pieces, widths):
    count = len(pieces)
    flat = [piece for by_x in pieces for by_core in by_x for piece in by_core]
    half_rows = flat[0].shape[0]
    rows = half_rows * len(flat)
    place = jnp.stack(
        [lax.axis_index("z"), lax.axis_index("x"), lax.axis_index("c")]
    ).astype(jnp.int32)

    def body(place_ref, *refs):
        ins = refs[: len(flat)]
        outs = refs[len(flat) : len(flat) + len(widths)]
        sem = refs[-1]
        copies = []
        for number, ref in enumerate(ins):
            k, dx, h = number // 4, (number // 2) % 2, number % 2
            z = lax.rem(place_ref[0] + (count - k), count)
            x = dx + (1 - 2 * dx) * place_ref[1]
            c = h + (1 - 2 * h) * place_ref[2]
            row = pl.multiple_of(((z * 2 + x) * 2 + c) * half_rows, half_rows)
            at = 0
            for slot, width in enumerate(widths):
                source = ref if len(widths) == 1 else ref.at[:, pl.ds(at, width)]
                copy = pltpu.make_async_copy(
                    source,
                    outs[slot].at[pl.ds(row, half_rows), :],
                    sem.at[number * len(widths) + slot],
                )
                copy.start()
                copies.append(copy)
                at += width
        for copy in copies:
            copy.wait()

    return pl.pallas_call(
        body,
        out_shape=[jax.ShapeDtypeStruct((rows, width), jnp.bfloat16) for width in widths],
        in_specs=[pl.BlockSpec(memory_space=pltpu.SMEM)]
        + [pl.BlockSpec(memory_space=pl.ANY)] * len(flat),
        out_specs=[pl.BlockSpec(memory_space=pl.ANY)] * len(widths),
        scratch_shapes=[pltpu.SemaphoreType.DMA((len(flat) * len(widths),))],
        name="assemble",
    )(place, *flat)


def scatter_sum(term):
    low = lambda value: value.astype(jnp.bfloat16)
    z_size = lax.axis_size("z")
    z, x, core = lax.axis_index("z"), lax.axis_index("x"), lax.axis_index("c")
    half = term.shape[0] // (z_size * 4)
    cut = term.reshape(z_size, 2, 2, half, term.shape[1])
    pick = lax.dynamic_index_in_dim
    got = swap(low(pick(cut, 1 - core, 2, False)), "c")
    kept = pick(cut, core, 2, False) + got
    got = swap(low(pick(kept, 1 - x, 1, False)), "x")
    kept = pick(kept, x, 1, False) + got
    total = pick(kept, z, 0, False)
    for k in range(1, z_size):
        total = total + shift(low(pick(kept, (z + k) % z_size, 0, False)), "z", k)
    if lax.axis_size("y") == 2:
        mine = low(total)
        total = mine.astype(jnp.float32) + swap(mine, "y").astype(jnp.float32)
    else:
        total = lax.psum(total, "y")
    other = swap(total, "c")
    return jnp.where(
        core == 0,
        jnp.concatenate([total, other], axis=0),
        jnp.concatenate([other, total], axis=0),
    )


def on_device(
    inputs,
    cotangent,
    norm1_gain,
    norm1_bias,
    qkv_weight,
    qv_bias,
    out_weight,
    out_bias,
    norm2_gain,
    norm2_bias,
    in_weight,
    in_bias,
    down_weight,
    down_bias,
    qkv_rows,
    qkv_cols,
    out_rows,
    out_cols,
    in_rows,
    in_cols,
    down_rows,
    down_cols,
    norm1_gain_moment,
    norm1_bias_moment,
    qv_bias_moment,
    out_bias_moment,
    norm2_gain_moment,
    norm2_bias_moment,
    in_bias_moment,
    down_bias_moment,
):
    masters = [
        norm1_gain,
        norm1_bias,
        qkv_weight,
        qv_bias,
        out_weight,
        out_bias,
        norm2_gain,
        norm2_bias,
        in_weight,
        in_bias,
        down_weight,
        down_bias,
    ]
    halves = [member.astype(jnp.bfloat16) for member in masters]
    vectors = [0, 1, 3, 5, 6, 7, 9, 11]
    sizes = [masters[number].shape[0] for number in vectors]
    small = gather_small(jnp.concatenate([halves[number] for number in vectors]))
    full = {}
    at = 0
    for number, size in zip(vectors, sizes):
        full[number] = small[:, at : at + size].reshape(-1)
        at += size
    gain_one, bias_one, bias_qv, bias_out = full[0], full[1], full[3], full[5]
    gain_two, bias_two, bias_in, bias_down = full[6], full[7], full[9], full[11]
    (weight_qkv,) = assemble(gather_pieces(halves[2]), [halves[2].shape[1]])
    weight_out, weight_in = assemble(
        gather_pieces(jnp.concatenate([halves[4], halves[8]], axis=1)),
        [halves[4].shape[1], halves[8].shape[1]],
    )
    (weight_down,) = assemble(gather_pieces(halves[10]), [halves[10].shape[1]])
    tokens, width = inputs.shape
    images = tokens // SEQ
    rows_in = inputs.astype(jnp.float32)
    normed_f, pull_one = jax.vjp(
        norm_affine, rows_in, gain_one.astype(jnp.float32), bias_one.astype(jnp.float32)
    )
    normed = normed_f.astype(jnp.bfloat16)
    qkv = plain_dot(normed, weight_qkv)
    bias_pair = bias_qv.astype(jnp.float32)
    query = (qkv[:, :width] + bias_pair[:width]).astype(jnp.bfloat16)
    keys = qkv[:, width : 2 * width].astype(jnp.bfloat16)
    values = (qkv[:, 2 * width :] + bias_pair[width:]).astype(jnp.bfloat16)
    query_img = query.reshape(images, SEQ, width)
    keys_img = keys.reshape(images, SEQ, width)
    values_img = values.reshape(images, SEQ, width)
    attended_img, logsum = lax.map(attend, (query_img, keys_img, values_img))
    attended = attended_img.reshape(tokens, width)
    middle = rows_in + plain_dot(attended, weight_out) + bias_out.astype(jnp.float32)
    normed_mid_f, pull_two = jax.vjp(
        norm_affine, middle, gain_two.astype(jnp.float32), bias_two.astype(jnp.float32)
    )
    normed_mid = normed_mid_f.astype(jnp.bfloat16)
    preact = plain_dot(normed_mid, weight_in) + bias_in.astype(jnp.float32)
    hidden_f, pull_gelu = jax.vjp(gelu_exact, preact)
    hidden = hidden_f.astype(jnp.bfloat16)
    final = middle + plain_dot(hidden, weight_down) + bias_down.astype(jnp.float32)
    output = final.astype(jnp.bfloat16)
    grad_out_rows = cotangent.astype(jnp.float32)
    term_down_weight = lead_dot(hidden, cotangent)
    term_down_bias = jnp.sum(grad_out_rows, axis=0)
    grad_hidden = tail_dot(cotangent, weight_down)
    (grad_preact,) = pull_gelu(grad_hidden)
    grad_preact_low = grad_preact.astype(jnp.bfloat16)
    term_in_weight = lead_dot(normed_mid, grad_preact_low)
    term_in_bias = jnp.sum(grad_preact_low.astype(jnp.float32), axis=0)
    grad_normed_mid = tail_dot(grad_preact_low, weight_in)
    grad_mid_norm, term_gain_two, term_bias_two = pull_two(grad_normed_mid)
    grad_mid = grad_out_rows + grad_mid_norm
    grad_mid_low = grad_mid.astype(jnp.bfloat16)
    term_out_weight = lead_dot(attended, grad_mid_low)
    term_out_bias = jnp.sum(grad_mid_low.astype(jnp.float32), axis=0)
    grad_attended = tail_dot(grad_mid_low, weight_out).astype(jnp.bfloat16)
    grad_qkv_img = lax.map(
        attend_back,
        (query_img, keys_img, values_img, logsum, grad_attended.reshape(images, SEQ, width)),
    )
    grad_qkv = grad_qkv_img.reshape(tokens, 3 * width)
    term_qkv_weight = lead_dot(normed, grad_qkv)
    column_sums = jnp.sum(grad_qkv.astype(jnp.float32), axis=0)
    term_qv_bias = jnp.concatenate([column_sums[:width], column_sums[2 * width :]])
    grad_normed = tail_dot(grad_qkv, weight_qkv)
    grad_in_norm, term_gain_one, term_bias_one = pull_one(grad_normed)
    input_grad = (grad_mid + grad_in_norm).astype(jnp.bfloat16)
    group_size = lax.axis_size("z") * lax.axis_size("x")
    images_all = images * group_size * lax.axis_size("y") * lax.axis_size("c")
    grads = [None] * 12
    for number, term in (
        (10, term_down_weight),
        (8, term_in_weight),
        (4, term_out_weight),
        (2, term_qkv_weight),
    ):
        grads[number] = scatter_sum(term) / images_all
    vector_terms = {
        0: term_gain_one,
        1: term_bias_one,
        3: term_qv_bias,
        5: term_out_bias,
        6: term_gain_two,
        7: term_bias_two,
        9: term_in_bias,
        11: term_down_bias,
    }
    summed = sum_over(
        jnp.concatenate(
            [vector_terms[number].reshape(group_size, -1) for number in vectors], axis=1
        ),
        ("c", "x", "z", "y"),
    )
    here = lax.axis_index("z") * lax.axis_size("x") + lax.axis_index("x")
    mine = lax.dynamic_index_in_dim(summed, here, 0, False) / images_all
    at = 0
    for number, size in zip(vectors, sizes):
        grads[number] = mine[at : at + size]
        at += size
    row_states = [qkv_rows, out_rows, in_rows, down_rows]
    col_states = [qkv_cols, out_cols, in_cols, down_cols]
    moments = [
        norm1_gain_moment,
        norm1_bias_moment,
        qv_bias_moment,
        out_bias_moment,
        norm2_gain_moment,
        norm2_bias_moment,
        in_bias_moment,
        down_bias_moment,
    ]
    matrix_slots = {2: 0, 4: 1, 8: 2, 10: 3}
    vector_slots = {0: 0, 1: 1, 3: 2, 5: 3, 6: 4, 7: 5, 9: 6, 11: 7}
    prepared = [None] * 12
    new_params = [None] * 12
    clips = [None] * 12
    new_cols_all = [None] * 4

    def finish(number, direction, direction_total, weight_total, count):
        clip_factor = jnp.maximum(1.0, jnp.sqrt(direction_total / count) / clip_level)
        rms_weight = jnp.sqrt(weight_total / count)
        clips[number] = clip_factor
        new_params[number] = masters[number] - step_rate * rms_weight * direction / clip_factor

    for number in (10, 8, 4, 2):
        position = matrix_slots[number]
        weight, grad = masters[number], grads[number]
        squared = grad * grad
        new_rows = 0.5 * row_states[position] + 0.5 * jnp.mean(squared, axis=1)
        prepared[number] = new_rows
        pack = jnp.concatenate(
            [
                jnp.sum(squared, axis=0),
                jnp.sum(squared / new_rows[:, None], axis=0),
                jnp.stack([jnp.sum(new_rows), jnp.sum(weight * weight)]),
            ]
        )
        total = sum_over(pack, ("x", "z"))
        rows_total, cols = weight.shape[0] * group_size, weight.shape[1]
        new_cols = 0.5 * col_states[position] + 0.5 * total[:cols] / rows_total
        new_cols_all[position] = new_cols
        mean_rows = total[-2] / rows_total
        direction = grad * lax.rsqrt(new_rows[:, None] * new_cols[None, :] / mean_rows)
        direction_total = mean_rows * jnp.sum(total[cols : 2 * cols] / new_cols)
        finish(number, direction, direction_total, total[-1], rows_total * cols)
    sums = []
    directions = {}
    for number in vectors:
        weight, grad = masters[number], grads[number]
        prepared[number] = 0.5 * moments[vector_slots[number]] + 0.5 * grad * grad
        directions[number] = grad * lax.rsqrt(prepared[number])
        sums.append(jnp.sum(weight * weight))
        sums.append(jnp.sum(directions[number] * directions[number]))
    total = sum_over(jnp.stack(sums), ("x", "z"))
    for slot, number in enumerate(vectors):
        finish(
            number,
            directions[number],
            total[2 * slot + 1],
            total[2 * slot],
            masters[number].shape[0] * group_size,
        )
    clip_factors = jnp.stack(clips)
    new_rows_all = [prepared[2], prepared[4], prepared[8], prepared[10]]
    new_moments = [
        prepared[0],
        prepared[1],
        prepared[3],
        prepared[5],
        prepared[6],
        prepared[7],
        prepared[9],
        prepared[11],
    ]
    return (
        output,
        input_grad,
        grads[0],
        grads[1],
        grads[2],
        grads[3],
        grads[4],
        grads[5],
        grads[6],
        grads[7],
        grads[8],
        grads[9],
        grads[10],
        grads[11],
        new_rows_all[0],
        new_cols_all[0],
        new_rows_all[1],
        new_cols_all[1],
        new_rows_all[2],
        new_cols_all[2],
        new_rows_all[3],
        new_cols_all[3],
        new_moments[0],
        new_moments[1],
        new_moments[2],
        new_moments[3],
        new_moments[4],
        new_moments[5],
        new_moments[6],
        new_moments[7],
        new_params[0],
        new_params[1],
        new_params[2],
        new_params[3],
        new_params[4],
        new_params[5],
        new_params[6],
        new_params[7],
        new_params[8],
        new_params[9],
        new_params[10],
        new_params[11],
        clip_factors,
    )


def solution(mesh):
    group = mesh.shape["fsdp"]
    split = Mesh(mesh.devices.reshape(group // 2, 2, mesh.shape["dp"] // 2, 2), ALL_AXES)
    in_specs = (
        P(("z", "x", "y", "c"), None),
        P(("z", "x", "y", "c"), None),
        P(("z", "x")),
        P(("z", "x")),
        P(("z", "x"), None),
        P(("z", "x")),
        P(("z", "x"), None),
        P(("z", "x")),
        P(("z", "x")),
        P(("z", "x")),
        P(("z", "x"), None),
        P(("z", "x")),
        P(("z", "x"), None),
        P(("z", "x")),
        P(("z", "x")),
        P(),
        P(("z", "x")),
        P(),
        P(("z", "x")),
        P(),
        P(("z", "x")),
        P(),
        P(("z", "x")),
        P(("z", "x")),
        P(("z", "x")),
        P(("z", "x")),
        P(("z", "x")),
        P(("z", "x")),
        P(("z", "x")),
        P(("z", "x")),
    )
    out_specs = (
        P(("z", "x", "y", "c"), None),
        P(("z", "x", "y", "c"), None),
        P(("z", "x")),
        P(("z", "x")),
        P(("z", "x"), None),
        P(("z", "x")),
        P(("z", "x"), None),
        P(("z", "x")),
        P(("z", "x")),
        P(("z", "x")),
        P(("z", "x"), None),
        P(("z", "x")),
        P(("z", "x"), None),
        P(("z", "x")),
        P(("z", "x")),
        P(),
        P(("z", "x")),
        P(),
        P(("z", "x")),
        P(),
        P(("z", "x")),
        P(),
        P(("z", "x")),
        P(("z", "x")),
        P(("z", "x")),
        P(("z", "x")),
        P(("z", "x")),
        P(("z", "x")),
        P(("z", "x")),
        P(("z", "x")),
        P(("z", "x")),
        P(("z", "x")),
        P(("z", "x"), None),
        P(("z", "x")),
        P(("z", "x"), None),
        P(("z", "x")),
        P(("z", "x")),
        P(("z", "x")),
        P(("z", "x"), None),
        P(("z", "x")),
        P(("z", "x"), None),
        P(("z", "x")),
        P(),
    )
    return jax.shard_map(
        on_device, mesh=split, in_specs=in_specs, out_specs=out_specs, check_vma=False
    )
```

time: 1460 us -> 1680 us (1.15)
  Pallas kernels: 0 us -> 768 us
  waiting for transfers between devices: 788 us -> 392 us
  blocking collectives: 287 us -> 0 us
  starting transfers between devices: 1.07 us -> 76.4 us
  local copies, waits for them, and re-layouts: 23.8 us -> 72.7 us
  other arithmetic: 86.3 us -> 105 us
    pallas_call x0 -> x3, Pallas kernels: none -> 768 us  [assemble(): pl.pallas_call(body, out_shape=[jax.ShapeDtypeStruct((rows, width), jnp.b...]
    reduce_scatter x4 -> x0, waiting for transfers between devices: 546 us -> none  [the longest x1 179 us: on_device(): lax.psum_scatter(terms[8], ('fsdp', 'dp'), scatter_dimension=0, tiled=True)]
    ppermute x0 -> x93, waiting for transfers between devices: none -> 392 us  [the longest x49 145 us: swap(): return lax.ppermute(value, axis, [(0, 1), (1, 0)])]
    all_gather x7 -> x0, waiting for transfers between devices: 241 us -> none  [the longest x1 114 us: on_device(): lax.all_gather(halves[10], 'fsdp', axis=0, tiled=True)]
    all_gather x10 -> x0, blocking collectives: 162 us -> none  [the longest x1 26.1 us: on_device(): lax.all_gather(halves[9], 'fsdp', axis=0, tiled=True)]
    ppermute x0 -> x93, starting transfers between devices: none -> 76.4 us  [the longest x21 30.8 us: shift(): lax.ppermute(value, axis, [(i, (i + step) % size) for i in range(size)])]
    psum x2 -> x0, blocking collectives: 70.8 us -> none  [the longest x1 37.8 us: on_device(): totals = [lax.psum(packed, 'fsdp') for packed in packs]]
    unnamed x2 -> x0, blocking collectives: 53.6 us -> none
  transfers between devices with their start and end apart: 11 -> 93, of which waited for: 9 -> 41; matrix products, arithmetic and copies ran while one was open for 10% -> 9% of each run, Pallas kernels for 0% -> 12%
where the time goes in v1:
time: 1680 us; the launch traced here: 1670 us
  Pallas kernels  768 us (46%)
  waiting for transfers between devices  392 us (23%)
  matrix products  235 us (14%)
  other arithmetic  105 us (6%)
  starting transfers between devices  76.4 us (5%)
  local copies, waits for them, and re-layouts  72.7 us (4%)
  between operations  22 us (1%)
    pallas_call x3, Pallas kernels, assemble(): pl.pallas_call(body, out_shape=[jax.ShapeDtypeStruct((rows, width), jnp.b...  768 us
    ppermute x49, waiting for transfers between devices, swap(): return lax.ppermute(value, axis, [(0, 1), (1, 0)])  145 us
    ppermute x21, waiting for transfers between devices, shift(): lax.ppermute(value, axis, [(i, (i + step) % size) for i in range(size)])  136 us
    ppermute x23, waiting for transfers between devices, partner(): return lax.ppermute(value, axis, [(i, i ^ step) for i in range(size)])  112 us
    dot_general x4, matrix products, plain_dot(): return jnp.dot(left, right, preferred_element_type=jnp.float32)  50.6 us
    dot_general x4, matrix products, tail_dot(): lax.dot_general(left, right, (((1,), (1,)), ((), ())), preferred_element_...  39.6 us
  transfers between devices with their start and end apart: 93, of which 41 were waited for; matrix products, arithmetic and copies ran while one was open for 9% of the time, Pallas kernels for 12%

profile of v1, /device:TPU:0, one launch (start us, length us, event | category | flops | bytes accessed | tf_op | source)
XLA Modules:
  0.0 1670.7 jit_solution(10538626267108645963)
XLA Ops:
  29.2 25.8 %collective-permute-done.1 = bf16[2,1536]{1,0:T(2,128)(2,1)S(1)} collective-permute-done((bf16[2,1536]{1,0:T(2,128)(2,1)S(1)}, bf16[2,1536]{1,0:T(2,128)(2,1)S(1)}, u32[]{:S(2)}, u32[]{:S(2)}) %collective-permute-start.1) | collective-permute-done | bytes 6176 | tf_op jit(solution)/shard_map/ppermute | solution.py:126
  57.1 20.7 %collective-permute-done.2 = bf16[4,1536]{1,0:T(4,128)(2,1)S(1)} collective-permute-done((bf16[4,1536]{1,0:T(4,128)(2,1)S(1)}, bf16[4,1536]{1,0:T(4,128)(2,1)S(1)}, u32[]{:S(2)}, u32[]{:S(2)}) %collective-permute-start.2) | collective-permute-done | bytes 12320 | tf_op jit(solution)/shard_map/ppermute | solution.py:126
  119.2 192.5 %assemble.3 = bf16[1024,3072]{1,0:T(8,128)(2,1)} custom-call(s32[3]{0:T(128)} %pad_add_fusion.place_ref, bf16[64,3072]{1,0:T(8,128)(2,1)} %get-tuple-element.180.refs_0_, bf16[64,3072]{1,0:T(8,128)(2,1)} %get-tuple-element.179.refs_1_, bf16[64,3072]{1,0:T(8,128)(2,1)} %copy-done.48, bf16[64,3072]{1,0:T(8,128)(2,1)} %copy-done.55, ...), custom_call_target="tpu_custom_call" | custom-call | tf_op jit(solution)/shard_map/assemble/pallas_call | solution.py:203
  327.0 10.0 multiply_reduce_fusion.1
  338.1 10.5 fusion.2
  354.4 11.6 fusion.74
  367.9 319.7 %assemble.4 = (bf16[1024,1024]{1,0:T(8,128)(2,1)}, bf16[1024,4096]{1,0:T(8,128)(2,1)}) custom-call(s32[3]{0:T(128)} %pad_add_fusion.place_ref, bf16[64,5120]{1,0:T(8,128)(2,1)} %copy-done.27, bf16[64,5120]{1,0:T(8,128)(2,1)} %get-tuple-element.170.refs_1_, bf16[64,5120]{1,0:T(8,128)(2,1)} %collective-permute-done.17.refs_2_, bf16[64,5120]{1,0:T(8,128)(2,1)} %copy-done.39, ...), custom_call_target="tpu_custom_call" | custom-call | tf_op jit(solution)/shard_map/assemble/pallas_call | solution.py:203
  692.4 30.0 %multiply_convert_fusion.1 = (bf16[577,4096]{1,0:T(8,128)(2,1)}, f32[577,4096]{1,0:T(8,128)}, f32[577,4096]{1,0:T(8,128)}) fusion(f32[4096]{0:T(1024)S(1)} %bitcast.316, bf16[1024,4096]{1,0:T(8,128)(2,1)S(1)} %bitcast.322, f32[577,1024]{1,0:T(8,128)S(1)} %get-tuple-element.251, f32[1024]{0:T(1024)S(1)} %get-tuple-element.188, ...), kind=kOutput, calls=%fused_computation.32 | convolution fusion | flops 4999164928 | bytes 34415112 | tf_op jit(solution)/shard_map/dot_general | solution.py:35
  759.1 47.4 %collective-permute-done.72 = bf16[4,256,1024]{2,1,0:T(8,128)(2,1)} collective-permute-done((bf16[4,256,1024]{2,1,0:T(8,128)(2,1)}, bf16[4,256,1024]{2,1,0:T(8,128)(2,1)}, u32[]{:S(2)}, u32[]{:S(2)}) %collective-permute-start.72) | collective-permute-done | bytes 2097184 | tf_op jit(solution)/shard_map/ppermute | solution.py:116
  818.7 11.5 collective-permute-done.73
  830.2 10.6 collective-permute-done.75
  840.8 21.5 %collective-permute-done.74 = bf16[256,1024]{1,0:T(8,128)(2,1)} collective-permute-done((bf16[256,1024]{1,0:T(8,128)(2,1)S(1)}, bf16[256,1024]{1,0:T(8,128)(2,1)}, u32[]{:S(2)}, u32[]{:S(2)}) %collective-permute-start.74) | collective-permute-done | bytes 524320 | tf_op jit(solution)/shard_map/ppermute | solution.py:121
  865.9 12.3 collective-permute-done.76
  909.8 10.8 collective-permute-done.41.refs_12_
  921.3 30.1 %collective-permute-done.37.refs_8_ = bf16[256,1024]{1,0:T(8,128)(2,1)S(1)} collective-permute-done((bf16[256,1024]{1,0:T(8,128)(2,1)S(1)}, bf16[256,1024]{1,0:T(8,128)(2,1)S(1)}, u32[]{:S(2)}, u32[]{:S(2)}) %collective-permute-start.37) | collective-permute-done | bytes 524320 | tf_op jit(solution)/shard_map/ppermute | solution.py:121
  954.1 12.3 collective-permute-done.39.refs_10_
  975.2 256.2 %assemble.5 = bf16[4096,1024]{1,0:T(8,128)(2,1)} custom-call(s32[3]{0:T(128)} %pad_add_fusion.place_ref, bf16[256,1024]{1,0:T(8,128)(2,1)} %copy-done.29, bf16[256,1024]{1,0:T(8,128)(2,1)} %get-tuple-element.177.refs_1_, bf16[256,1024]{1,0:T(8,128)(2,1)} %collective-permute-done.31.refs_2_, bf16[256,1024]{1,0:T(8,128)(2,1)} %collective-permute-done.32.refs_3_, ...), custom_call_target="tpu_custom_call" | custom-call | tf_op jit(solution)/shard_map/assemble/pallas_call | solution.py:203
  1231.4 16.7 convert_reduce_fusion
  1248.1 10.2 multiply_reduce_fusion.2
  1266.8 13.5 fusion.184
  1280.4 13.4 fusion.71
  1293.8 32.9 %fusion.61 = bf16[16,64,577]{2,1,0:T(8,128)(2,1)} fusion(bf16[577,16,64]{0,2,1:T(8,128)(2,1)} %bitcast.299, f32[16,577,577]{1,2,0:T(8,128)} %fusion.184, f32[16,577,577]{1,2,0:T(8,128)} %get-tuple-element.249, f32[16,577]{1,0:T(8,128)S(1)} %copy-done.59), kind=kOutput, calls=%fused_computation.116 | convolution fusion | flops 746361600 | bytes 45015232 | tf_op jit(solution)/shard_map/while/body/eval_jaxpr/hqk,khd->qhd/dot_general | solution.py:99
  1326.7 33.3 %fusion.66 = bf16[16,64,577]{2,1,0:T(8,128)(2,1)} fusion(bf16[577,16,64]{0,2,1:T(8,128)(2,1)} %bitcast.297, f32[16,577,577]{1,2,0:T(8,128)} %fusion.184, f32[16,577,577]{1,2,0:T(8,128)} %get-tuple-element.249, f32[16,577]{1,0:T(8,128)S(1)} %copy-done.59), kind=kOutput, calls=%fused_computation.117 | convolution fusion | flops 746361600 | bytes 45015232 | tf_op jit(solution)/shard_map/while/body/eval_jaxpr/hqk,qhd->khd/dot_general | solution.py:100
  1360.0 10.2 fusion.153
  1381.6 13.3 fusion.151
  1424.3 10.4 stack.146
  1456.8 9.9 add_convert_fusion.1
  1489.2 26.7 %collective-permute-done.51 = bf16[4,64,3072]{2,1,0:T(8,128)(2,1)} collective-permute-done((bf16[4,64,3072]{2,1,0:T(8,128)(2,1)S(1)}, bf16[4,64,3072]{2,1,0:T(8,128)(2,1)}, u32[]{:S(2)}, u32[]{:S(2)}) %collective-permute-start.51) | collective-permute-done | bytes 1572896 | tf_op jit(solution)/shard_map/ppermute | solution.py:116
  1530.9 29.6 %collective-permute-done.81 = f32[2050]{0:T(1024)S(1)} collective-permute-done((f32[2050]{0:T(1024)S(1)}, f32[2050]{0:T(1024)S(1)}, u32[]{:S(2)}, u32[]{:S(2)}) %collective-permute-start.81) | collective-permute-done | bytes 8232 | tf_op jit(solution)/shard_map/ppermute | solution.py:126
  1572.9 9.9 collective-permute-done.66
  1582.9 9.6 collective-permute-done.68
  1592.4 22.6 %collective-permute-done.67 = bf16[64,4096]{1,0:T(8,128)(2,1)S(1)} collective-permute-done((bf16[64,4096]{1,0:T(8,128)(2,1)S(1)}, bf16[64,4096]{1,0:T(8,128)(2,1)S(1)}, u32[]{:S(2)}, u32[]{:S(2)}) %collective-permute-start.67) | collective-permute-done | bytes 524320 | tf_op jit(solution)/shard_map/ppermute | solution.py:121
  (600 shorter events, 352.9 us)
Async XLA Ops:
  4.7 74.0 %collective-permute-start.13 = (bf16[64,3072]{1,0:T(8,128)(2,1)}, bf16[64,3072]{1,0:T(8,128)(2,1)}, u32[]{:S(2)}, u32[]{:S(2)}) collective-permute-start(bf16[64,3072]{1,0:T(8,128)(2,1)} %get-tuple-element.180.refs_0_), channel_id=1, source_target_pairs={{0,24},{8,0},{16,8},{24,16},{1,25},{9,1},{17,9},{25,17},{2,26},{10... | collective-permute-start | bytes 1179656 | tf_op jit(solution)/shard_map/ppermute | solution.py:121
  9.8 71.1 %collective-permute-start.9 = (bf16[64,3072]{1,0:T(8,128)(2,1)}, bf16[64,3072]{1,0:T(8,128)(2,1)}, u32[]{:S(2)}, u32[]{:S(2)}) collective-permute-start(bf16[64,3072]{1,0:T(8,128)(2,1)} %get-tuple-element.180.refs_0_), channel_id=1, source_target_pairs={{0,16},{8,24},{16,0},{24,8},{1,17},{9,25},{17,1},{25,9},{2,18},{10... | collective-permute-start | bytes 1179656 | tf_op jit(solution)/shard_map/ppermute | solution.py:121
  14.0 78.4 %collective-permute-start.27 = (bf16[64,5120]{1,0:T(8,128)(2,1)S(1)}, bf16[64,5120]{1,0:T(8,128)(2,1)}, u32[]{:S(2)}, u32[]{:S(2)}) collective-permute-start(bf16[64,5120]{1,0:T(8,128)(2,1)S(1)} %get-tuple-element.171.refs_0_), channel_id=1, source_target_pairs={{0,24},{8,0},{16,8},{24,16},{1,25},{9,1},{17,9},{25,17},{2,26},{10... | collective-permute-start | bytes 1966088 | tf_op jit(solution)/shard_map/ppermute | solution.py:121
  14.5 78.0 %collective-permute-start.23 = (bf16[64,5120]{1,0:T(8,128)(2,1)S(1)}, bf16[64,5120]{1,0:T(8,128)(2,1)}, u32[]{:S(2)}, u32[]{:S(2)}) collective-permute-start(bf16[64,5120]{1,0:T(8,128)(2,1)S(1)} %get-tuple-element.171.refs_0_), channel_id=1, source_target_pairs={{0,16},{8,24},{16,0},{24,8},{1,17},{9,25},{17,1},{25,9},{2,18},{10... | collective-permute-start | bytes 1966088 | tf_op jit(solution)/shard_map/ppermute | solution.py:121
  27.1 27.9 %collective-permute-start.1 = (bf16[2,1536]{1,0:T(2,128)(2,1)S(1)}, bf16[2,1536]{1,0:T(2,128)(2,1)S(1)}, u32[]{:S(2)}, u32[]{:S(2)}) collective-permute-start(bf16[2,1536]{1,0:T(2,128)(2,1)S(1)} %broadcast_select_fusion), channel_id=1, source_target_pairs={{0,8},{8,0},{16,24},{24,16},{1,9},{9,1},{17,25},{25,17},{2,10},{10... | collective-permute-start | bytes 18440 | tf_op jit(solution)/shard_map/ppermute | solution.py:126
  55.1 22.7 %collective-permute-start.2 = (bf16[4,1536]{1,0:T(4,128)(2,1)S(1)}, bf16[4,1536]{1,0:T(4,128)(2,1)S(1)}, u32[]{:S(2)}, u32[]{:S(2)}) collective-permute-start(bf16[4,1536]{1,0:T(4,128)(2,1)S(1)} %maximum_select_fusion.5), channel_id=1, source_target_pairs={{0,16},{8,24},{16,0},{24,8},{1,17},{9,25},{17,1},{25,9},{2,18},{10... | collective-permute-start | bytes 36872 | tf_op jit(solution)/shard_map/ppermute | solution.py:126
  92.5 21.6 %collective-permute-start.7 = (bf16[64,3072]{1,0:T(8,128)(2,1)S(1)}, bf16[64,3072]{1,0:T(8,128)(2,1)S(1)}, u32[]{:S(2)}, u32[]{:S(2)}) collective-permute-start(bf16[64,3072]{1,0:T(8,128)(2,1)S(1)} %collective-permute-done.5.refs_4_), channel_id=1, source_target_pairs={{0,4},{4,0},{1,5},{5,1},{2,6},{6,2},{3,7},{7,3},{8,12},{12,8},{9,1... | collective-permute-start | bytes 1179656 | tf_op jit(solution)/shard_map/ppermute | solution.py:116
  114.8 222.2 %collective-permute-start.19 = (bf16[64,5120]{1,0:T(8,128)(2,1)S(1)}, bf16[64,5120]{1,0:T(8,128)(2,1)}, u32[]{:S(2)}, u32[]{:S(2)}) collective-permute-start(bf16[64,5120]{1,0:T(8,128)(2,1)S(1)} %get-tuple-element.171.refs_0_), channel_id=1, source_target_pairs={{0,8},{8,16},{16,24},{24,0},{1,9},{9,17},{17,25},{25,1},{2,10},{10... | collective-permute-start | bytes 1966088 | tf_op jit(solution)/shard_map/ppermute | solution.py:121
  115.3 221.9 %collective-permute-start.17 = (bf16[64,5120]{1,0:T(8,128)(2,1)S(1)}, bf16[64,5120]{1,0:T(8,128)(2,1)}, u32[]{:S(2)}, u32[]{:S(2)}) collective-permute-start(bf16[64,5120]{1,0:T(8,128)(2,1)S(1)} %get-tuple-element.171.refs_0_), channel_id=1, source_target_pairs={{0,4},{4,0},{1,5},{5,1},{2,6},{6,2},{3,7},{7,3},{8,12},{12,8},{9,1... | collective-permute-start | bytes 1966088 | tf_op jit(solution)/shard_map/ppermute | solution.py:116
  116.8 231.8 %collective-permute-start.29 = (bf16[64,5120]{1,0:T(8,128)(2,1)}, bf16[64,5120]{1,0:T(8,128)(2,1)}, u32[]{:S(2)}, u32[]{:S(2)}) collective-permute-start(bf16[64,5120]{1,0:T(8,128)(2,1)} %collective-permute-done.27.refs_12_), channel_id=1, source_target_pairs={{0,4},{4,0},{1,5},{5,1},{2,6},{6,2},{3,7},{7,3},{8,12},{12,8},{9,1... | collective-permute-start | bytes 1966088 | tf_op jit(solution)/shard_map/ppermute | solution.py:116
  117.4 231.3 %collective-permute-start.28 = (bf16[64,5120]{1,0:T(8,128)(2,1)}, bf16[64,5120]{1,0:T(8,128)(2,1)}, u32[]{:S(2)}, u32[]{:S(2)}) collective-permute-start(bf16[64,5120]{1,0:T(8,128)(2,1)} %collective-permute-done.27.refs_12_), channel_id=1, source_target_pairs={{0,1},{1,0},{2,3},{3,2},{4,5},{5,4},{6,7},{7,6},{8,9},{9,8},{10,11... | collective-permute-start | bytes 1966088 | tf_op jit(solution)/shard_map/ppermute | solution.py:116
  117.6 231.7 %collective-permute-start.25 = (bf16[64,5120]{1,0:T(8,128)(2,1)}, bf16[64,5120]{1,0:T(8,128)(2,1)}, u32[]{:S(2)}, u32[]{:S(2)}) collective-permute-start(bf16[64,5120]{1,0:T(8,128)(2,1)} %collective-permute-done.23.refs_8_), channel_id=1, source_target_pairs={{0,4},{4,0},{1,5},{5,1},{2,6},{6,2},{3,7},{7,3},{8,12},{12,8},{9,1... | collective-permute-start | bytes 1966088 | tf_op jit(solution)/shard_map/ppermute | solution.py:116
  758.4 48.1 %collective-permute-start.72 = (bf16[4,256,1024]{2,1,0:T(8,128)(2,1)}, bf16[4,256,1024]{2,1,0:T(8,128)(2,1)}, u32[]{:S(2)}, u32[]{:S(2)}) collective-permute-start(bf16[4,256,1024]{2,1,0:T(8,128)(2,1)} %fusion.58), channel_id=1, source_target_pairs={{0,4},{4,0},{1,5},{5,1},{2,6},{6,2},{3,7},{7,3},{8,12},{12,8},{9,1... | collective-permute-start | bytes 6291464 | tf_op jit(solution)/shard_map/ppermute | solution.py:116
  816.9 23.9 %collective-permute-start.75 = (bf16[256,1024]{1,0:T(8,128)(2,1)S(1)}, bf16[256,1024]{1,0:T(8,128)(2,1)}, u32[]{:S(2)}, u32[]{:S(2)}) collective-permute-start(bf16[256,1024]{1,0:T(8,128)(2,1)S(1)} %get-tuple-element.156), channel_id=1, source_target_pairs={{0,24},{8,0},{16,8},{24,16},{1,25},{9,1},{17,9},{25,17},{2,26},{10... | collective-permute-start | bytes 1572872 | tf_op jit(solution)/shard_map/ppermute | solution.py:121
  817.0 45.3 %collective-permute-start.74 = (bf16[256,1024]{1,0:T(8,128)(2,1)S(1)}, bf16[256,1024]{1,0:T(8,128)(2,1)}, u32[]{:S(2)}, u32[]{:S(2)}) collective-permute-start(bf16[256,1024]{1,0:T(8,128)(2,1)S(1)} %get-tuple-element.157), channel_id=1, source_target_pairs={{0,16},{8,24},{16,0},{24,8},{1,17},{9,25},{17,1},{25,9},{2,18},{10... | collective-permute-start | bytes 1572872 | tf_op jit(solution)/shard_map/ppermute | solution.py:121
  908.2 43.2 %collective-permute-start.37 = (bf16[256,1024]{1,0:T(8,128)(2,1)S(1)}, bf16[256,1024]{1,0:T(8,128)(2,1)S(1)}, u32[]{:S(2)}, u32[]{:S(2)}) collective-permute-start(bf16[256,1024]{1,0:T(8,128)(2,1)S(1)} %get-tuple-element.178.refs_0_), channel_id=1, source_target_pairs={{0,16},{8,24},{16,0},{24,8},{1,17},{9,25},{17,1},{25,9},{2,18},{10... | collective-permute-start | bytes 1572872 | tf_op jit(solution)/shard_map/ppermute | solution.py:121
  908.6 43.5 %collective-permute-start.33 = (bf16[256,1024]{1,0:T(8,128)(2,1)S(1)}, bf16[256,1024]{1,0:T(8,128)(2,1)}, u32[]{:S(2)}, u32[]{:S(2)}) collective-permute-start(bf16[256,1024]{1,0:T(8,128)(2,1)S(1)} %get-tuple-element.178.refs_0_), channel_id=1, source_target_pairs={{0,8},{8,16},{16,24},{24,0},{1,9},{9,17},{17,25},{25,1},{2,10},{10... | collective-permute-start | bytes 1572872 | tf_op jit(solution)/shard_map/ppermute | solution.py:121
  909.2 42.9 %collective-permute-start.31 = (bf16[256,1024]{1,0:T(8,128)(2,1)S(1)}, bf16[256,1024]{1,0:T(8,128)(2,1)}, u32[]{:S(2)}, u32[]{:S(2)}) collective-permute-start(bf16[256,1024]{1,0:T(8,128)(2,1)S(1)} %get-tuple-element.178.refs_0_), channel_id=1, source_target_pairs={{0,4},{4,0},{1,5},{5,1},{2,6},{6,2},{3,7},{7,3},{8,12},{12,8},{9,1... | collective-permute-start | bytes 1572872 | tf_op jit(solution)/shard_map/ppermute | solution.py:116
  920.6 32.9 %collective-permute-start.43 = (bf16[256,1024]{1,0:T(8,128)(2,1)S(1)}, bf16[256,1024]{1,0:T(8,128)(2,1)}, u32[]{:S(2)}, u32[]{:S(2)}) collective-permute-start(bf16[256,1024]{1,0:T(8,128)(2,1)S(1)} %collective-permute-done.41.refs_12_), channel_id=1, source_target_pairs={{0,4},{4,0},{1,5},{5,1},{2,6},{6,2},{3,7},{7,3},{8,12},{12,8},{9,1... | collective-permute-start | bytes 1572872 | tf_op jit(solution)/shard_map/ppermute | solution.py:116
  921.3 32.4 %collective-permute-start.42 = (bf16[256,1024]{1,0:T(8,128)(2,1)S(1)}, bf16[256,1024]{1,0:T(8,128)(2,1)S(1)}, u32[]{:S(2)}, u32[]{:S(2)}) collective-permute-start(bf16[256,1024]{1,0:T(8,128)(2,1)S(1)} %collective-permute-done.41.refs_12_), channel_id=1, source_target_pairs={{0,1},{1,0},{2,3},{3,2},{4,5},{5,4},{6,7},{7,6},{8,9},{9,8},{10,11... | collective-permute-start | bytes 1572872 | tf_op jit(solution)/shard_map/ppermute | solution.py:116
  1436.1 39.0 %collective-permute-start.50 = (bf16[4,2,64,3072]{3,2,0,1:T(8,128)(2,1)}, bf16[4,2,64,3072]{3,2,0,1:T(8,128)(2,1)}, u32[]{:S(2)}, u32[]{:S(2)}) collective-permute-start(bf16[4,2,64,3072]{3,2,0,1:T(8,128)(2,1)} %fusion.46), channel_id=1, source_target_pairs={{0,1},{1,0},{2,3},{3,2},{4,5},{5,4},{6,7},{7,6},{8,9},{9,8},{10,11... | collective-permute-start | bytes 9437192 | tf_op jit(solution)/shard_map/ppermute | solution.py:116
  1452.3 28.6 %collective-permute-start.64 = (bf16[4,2,64,4096]{3,2,0,1:T(8,128)(2,1)}, bf16[4,2,64,4096]{3,2,0,1:T(8,128)(2,1)}, u32[]{:S(2)}, u32[]{:S(2)}) collective-permute-start(bf16[4,2,64,4096]{3,2,0,1:T(8,128)(2,1)} %fusion.40), channel_id=1, source_target_pairs={{0,1},{1,0},{2,3},{3,2},{4,5},{5,4},{6,7},{7,6},{8,9},{9,8},{10,11... | collective-permute-start | bytes 12582920 | tf_op jit(solution)/shard_map/ppermute | solution.py:116
  1478.5 37.4 %collective-permute-start.51 = (bf16[4,64,3072]{2,1,0:T(8,128)(2,1)S(1)}, bf16[4,64,3072]{2,1,0:T(8,128)(2,1)}, u32[]{:S(2)}, u32[]{:S(2)}) collective-permute-start(bf16[4,64,3072]{2,1,0:T(8,128)(2,1)S(1)} %fusion.75), channel_id=1, source_target_pairs={{0,4},{4,0},{1,5},{5,1},{2,6},{6,2},{3,7},{7,3},{8,12},{12,8},{9,1... | collective-permute-start | bytes 4718600 | tf_op jit(solution)/shard_map/ppermute | solution.py:116
  1488.5 74.0 %collective-permute-start.65 = (bf16[4,64,4096]{2,1,0:T(8,128)(2,1)}, bf16[4,64,4096]{2,1,0:T(8,128)(2,1)}, u32[]{:S(2)}, u32[]{:S(2)}) collective-permute-start(bf16[4,64,4096]{2,1,0:T(8,128)(2,1)} %fusion.57), channel_id=1, source_target_pairs={{0,4},{4,0},{1,5},{5,1},{2,6},{6,2},{3,7},{7,3},{8,12},{12,8},{9,1... | collective-permute-start | bytes 6291464 | tf_op jit(solution)/shard_map/ppermute | solution.py:116
  1519.7 40.9 %collective-permute-start.52 = (bf16[64,3072]{1,0:T(8,128)(2,1)}, bf16[64,3072]{1,0:T(8,128)(2,1)S(1)}, u32[]{:S(2)}, u32[]{:S(2)}) collective-permute-start(bf16[64,3072]{1,0:T(8,128)(2,1)} %get-tuple-element.161), channel_id=1, source_target_pairs={{0,8},{8,16},{16,24},{24,0},{1,9},{9,17},{17,25},{25,1},{2,10},{10... | collective-permute-start | bytes 1179656 | tf_op jit(solution)/shard_map/ppermute | solution.py:121
  1519.7 40.9 %collective-permute-start.54 = (bf16[64,3072]{1,0:T(8,128)(2,1)}, bf16[64,3072]{1,0:T(8,128)(2,1)}, u32[]{:S(2)}, u32[]{:S(2)}) collective-permute-start(bf16[64,3072]{1,0:T(8,128)(2,1)} %get-tuple-element.162), channel_id=1, source_target_pairs={{0,24},{8,0},{16,8},{24,16},{1,25},{9,1},{17,9},{25,17},{2,26},{10... | collective-permute-start | bytes 1179656 | tf_op jit(solution)/shard_map/ppermute | solution.py:121
  1523.5 37.1 %collective-permute-start.53 = (bf16[64,3072]{1,0:T(8,128)(2,1)}, bf16[64,3072]{1,0:T(8,128)(2,1)}, u32[]{:S(2)}, u32[]{:S(2)}) collective-permute-start(bf16[64,3072]{1,0:T(8,128)(2,1)} %get-tuple-element.163), channel_id=1, source_target_pairs={{0,16},{8,24},{16,0},{24,8},{1,17},{9,25},{17,1},{25,9},{2,18},{10... | collective-permute-start | bytes 1179656 | tf_op jit(solution)/shard_map/ppermute | solution.py:121
  1526.2 34.4 %collective-permute-start.81 = (f32[2050]{0:T(1024)S(1)}, f32[2050]{0:T(1024)S(1)}, u32[]{:S(2)}, u32[]{:S(2)}) collective-permute-start(f32[2050]{0:T(1024)S(1)} %concatenate.92), channel_id=1, source_target_pairs={{0,4},{4,0},{1,5},{5,1},{2,6},{6,2},{3,7},{7,3},{8,12},{12,8},{9,1... | collective-permute-start | bytes 24608 | tf_op jit(solution)/shard_map/ppermute | solution.py:126
  1560.6 59.5 %collective-permute-start.82 = (f32[2050]{0:T(1024)S(1)}, f32[2050]{0:T(1024)S(1)}, u32[]{:S(2)}, u32[]{:S(2)}) collective-permute-start(f32[2050]{0:T(1024)S(1)} %add.493), channel_id=1, source_target_pairs={{0,8},{8,0},{16,24},{24,16},{1,9},{9,1},{17,25},{25,17},{2,10},{10... | collective-permute-start | bytes 24608 | tf_op jit(solution)/shard_map/ppermute | solution.py:126
  1568.2 24.2 %collective-permute-start.68 = (bf16[64,4096]{1,0:T(8,128)(2,1)S(1)}, bf16[64,4096]{1,0:T(8,128)(2,1)S(1)}, u32[]{:S(2)}, u32[]{:S(2)}) collective-permute-start(bf16[64,4096]{1,0:T(8,128)(2,1)S(1)} %get-tuple-element.159), channel_id=1, source_target_pairs={{0,24},{8,0},{16,8},{24,16},{1,25},{9,1},{17,9},{25,17},{2,26},{10... | collective-permute-start | bytes 1572872 | tf_op jit(solution)/shard_map/ppermute | solution.py:121
  1570.3 44.8 %collective-permute-start.67 = (bf16[64,4096]{1,0:T(8,128)(2,1)S(1)}, bf16[64,4096]{1,0:T(8,128)(2,1)S(1)}, u32[]{:S(2)}, u32[]{:S(2)}) collective-permute-start(bf16[64,4096]{1,0:T(8,128)(2,1)S(1)} %get-tuple-element.160), channel_id=1, source_target_pairs={{0,16},{8,24},{16,0},{24,8},{1,17},{9,25},{17,1},{25,9},{2,18},{10... | collective-permute-start | bytes 1572872 | tf_op jit(solution)/shard_map/ppermute | solution.py:121
  1572.9 51.9 %collective-permute-start.56 = (f32[64,3072]{1,0:T(8,128)S(1)}, f32[64,3072]{1,0:T(8,128)S(1)}, u32[]{:S(2)}, u32[]{:S(2)}) collective-permute-start(f32[64,3072]{1,0:T(8,128)S(1)} %convert_add_fusion.4), channel_id=1, source_target_pairs={{0,1},{1,0},{2,3},{3,2},{4,5},{5,4},{6,7},{7,6},{8,9},{9,8},{10,11... | collective-permute-start | bytes 2359304 | tf_op jit(solution)/shard_map/ppermute | solution.py:116
  (192 other events, 4793.9 us)

commit v2 on v1

v2 whole, which is shorter than its diff:
```python
import math

import jax
import jax.numpy as jnp
from jax import lax
from jax.experimental import pallas as pl
from jax.experimental.pallas import tpu as pltpu
from jax.sharding import Mesh
from jax.sharding import PartitionSpec as P

HEAD_DIM = 64
SEQ = 577
LANES = 128
SPAN = 256
CHUNKS = 2
VMEM_LIMIT = 60 * 1024 * 1024

ALL_AXES = ("z", "x", "y", "c")

ln_eps = 1e-06
clip_level = 0.05
step_rate = 4.0


def swap(value, axis):
    return lax.ppermute(value, axis, [(0, 1), (1, 0)])


def shift(value, axis, step):
    size = lax.axis_size(axis)
    return lax.ppermute(value, axis, [(i, (i + step) % size) for i in range(size)])


def partner(value, axis, step):
    size = lax.axis_size(axis)
    return lax.ppermute(value, axis, [(i, i ^ step) for i in range(size)])


def sum_over(value, axes):
    for axis in axes:
        step = 1
        while step < lax.axis_size(axis):
            value = value + partner(value, axis, step)
            step *= 2
    return value


def gather_small(vector):
    value = vector[None, :]
    for axis in ("x", "z"):
        step = 1
        while step < lax.axis_size(axis):
            other = partner(value, axis, step)
            low = (lax.axis_index(axis) // step) % 2 == 0
            value = jnp.where(
                low,
                jnp.concatenate([value, other], axis=0),
                jnp.concatenate([other, value], axis=0),
            )
            step *= 2
    return value


def gather_pieces(shard):
    along = [shard] + [shift(shard, "z", k) for k in range(1, lax.axis_size("z"))]
    pieces = []
    for near in along:
        pieces += [near, swap(near, "x")]
    return pieces


def scatter_sum(keep, send):
    got = swap(send, "x")
    kept = wide(keep) + wide(got)
    total = kept[0]
    for k in range(1, lax.axis_size("z")):
        total = total + wide(shift(low(kept[k]), "z", k))
    if lax.axis_size("y") == 2:
        mine = low(total)
        return wide(mine) + wide(swap(mine, "y"))
    return lax.psum(total, "y")


def row_pad(length):
    return -(-length // LANES) * LANES


def dot(left, right):
    return jnp.dot(left, right, preferred_element_type=jnp.float32)


def dot_tail(left, right):
    return lax.dot_general(
        left, right, (((1,), (1,)), ((), ())), preferred_element_type=jnp.float32
    )


def low(value):
    return value.astype(jnp.bfloat16)


def wide(value):
    return value.astype(jnp.float32)


def any_spec():
    return pl.BlockSpec(memory_space=pl.ANY)


def whole(shape):
    return pl.BlockSpec(shape, lambda *_: (0,) * len(shape))


def sds(shape, dtype):
    return jax.ShapeDtypeStruct(shape, dtype)


def call(body, place, ins, in_specs, outs, out_specs, scratch, name, grid=(1,)):
    return pl.pallas_call(
        body,
        out_shape=outs,
        grid_spec=pltpu.PrefetchScalarGridSpec(
            num_scalar_prefetch=1,
            grid=grid,
            in_specs=in_specs,
            out_specs=out_specs,
            scratch_shapes=scratch,
        ),
        compiler_params=pltpu.CompilerParams(
            vmem_limit_bytes=VMEM_LIMIT, dimension_semantics=("arbitrary",) * len(grid)
        ),
        name=name,
    )(place, *ins)


def shard_of(place_ref, number, z_size):
    k, dx = number // 2, number % 2
    z = lax.rem(place_ref[0] + (z_size - k), z_size)
    x = dx + (1 - 2 * dx) * place_ref[1]
    return z, x


def normalised(rows):
    centre = rows - jnp.mean(rows, axis=-1, keepdims=True)
    spread = jnp.mean(centre * centre, axis=-1, keepdims=True)
    return centre * lax.rsqrt(spread + ln_eps)


def project_qkv(place, rows, gain, bias, bias_q, bias_v, pieces):
    count = len(pieces)
    z_size = count // 2
    part, cols = pieces[0].shape
    width = part * count
    heads = cols // 3
    length = rows[0].shape[0]
    scale = 1.0 / math.sqrt(HEAD_DIM)

    def body(place_ref, own_ref, other_ref, gain_ref, bias_ref, bq_ref, bv_ref, *refs):
        ins, (normed_ref, q_ref, k_ref, v_ref, weight, sem) = refs[:count], refs[count:]
        copies = []
        for number, ref in enumerate(ins):
            z, x = shard_of(place_ref, number, z_size)
            row = pl.multiple_of((z * 2 + x) * part, part)
            copy = pltpu.make_async_copy(ref, weight.at[pl.ds(row, part), :], sem.at[number])
            copy.start()
            copies.append(copy)
        for image, ref in enumerate((own_ref, other_ref)):
            for at in range(0, length, LANES):
                block = wide(ref[at : at + LANES, :])
                normed_ref[image, at : at + LANES, :] = low(
                    normalised(block) * gain_ref[...] + bias_ref[...]
                )
        for copy in copies:
            copy.wait()
        for image in range(2):
            normed = normed_ref[image]
            query = low(dot(normed, weight[:, :heads]) + bq_ref[...])
            q_ref[image] = low(wide(query) * scale)
            k_ref[image] = low(dot(normed, weight[:, heads : 2 * heads]))
            v_ref[image] = low(dot(normed, weight[:, 2 * heads :]) + bv_ref[...])

    part_out = sds((2, length, heads), jnp.bfloat16)
    return call(
        body,
        place,
        (*rows, gain, bias, bias_q, bias_v, *pieces),
        [whole((length, width))] * 2
        + [whole((1, width))] * 2
        + [whole((1, heads))] * 2
        + [any_spec()] * count,
        [sds((2, length, width), jnp.bfloat16)] + [part_out] * 3,
        [whole((2, length, width))] + [whole((2, length, heads))] * 3,
        [pltpu.VMEM((width, cols), jnp.bfloat16), pltpu.SemaphoreType.DMA((count,))],
        "project_qkv",
    )


def attention(place, query, keys, values):
    _, length, heads = query.shape
    pairs = heads // LANES

    def body(place_ref, q_ref, k_ref, v_ref, out_ref, probs_ref):
        lane = lax.broadcasted_iota(jnp.int32, (length, LANES), 1)
        keys_block = k_ref[0]
        values_t = v_ref[0].T
        query_block = q_ref[0]
        mixed = []
        for head in range(2):
            inside = (lane >= head * HEAD_DIM) & (lane < (head + 1) * HEAD_DIM)
            query_head = jnp.where(inside, query_block, jnp.zeros_like(query_block))
            values_head = values_t[head * HEAD_DIM : (head + 1) * HEAD_DIM, :]
            parts = []
            for at in range(0, length, SPAN):
                span = min(SPAN, length - at)
                scores = dot_tail(keys_block, query_head[at : at + span, :])
                key_row = lax.broadcasted_iota(jnp.int32, scores.shape, 0)
                scores = jnp.where(key_row < SEQ, scores, -1e30)
                highest = jnp.max(scores, axis=0, keepdims=True)
                exponent = jnp.exp(scores - highest)
                summed = jnp.sum(exponent, axis=0, keepdims=True)
                probs = low(exponent * (1.0 / summed))
                probs_ref[0, 0, head, :, at : at + span] = probs
                parts.append(dot(values_head, probs))
            mixed.append(jnp.concatenate(parts, axis=1))
        out_ref[0] = low(jnp.concatenate(mixed, axis=0).T)

    block = pl.BlockSpec((1, length, LANES), lambda i, j, p: (i, 0, j))
    return call(
        body,
        place,
        (query, keys, values),
        [block] * 3,
        [
            sds((2, length, heads), jnp.bfloat16),
            sds((2, pairs, 2, length, length), jnp.bfloat16),
        ],
        [block, pl.BlockSpec((1, 1, 2, length, length), lambda i, j, p: (i, j, 0, 0, 0))],
        [],
        "attention",
        grid=(2, pairs),
    )


def attention_back(place, query, keys, values, probs, grad):
    _, length, heads = query.shape
    pairs = heads // LANES
    scale = 1.0 / math.sqrt(HEAD_DIM)

    def body(place_ref, q_ref, k_ref, v_ref, p_ref, g_ref, gq_ref, gk_ref, gv_ref):
        lane = lax.broadcasted_iota(jnp.int32, (length, LANES), 1)
        keys_t = k_ref[0].T
        values_block = v_ref[0]
        query_block = q_ref[0]
        grad_block = g_ref[0]
        grad_query = []
        grad_keys = []
        grad_values = []
        for head in range(2):
            inside = (lane >= head * HEAD_DIM) & (lane < (head + 1) * HEAD_DIM)
            grad_head = jnp.where(inside, grad_block, jnp.zeros_like(grad_block))
            keys_head = keys_t[head * HEAD_DIM : (head + 1) * HEAD_DIM, :]
            parts = []
            sum_keys = None
            sum_values = None
            for at in range(0, length, SPAN):
                span = min(SPAN, length - at)
                probs_low = p_ref[0, 0, head, :, at : at + span]
                probs_wide = wide(probs_low)
                grad_probs = dot_tail(values_block, grad_head[at : at + span, :])
                inner = jnp.sum(probs_wide * grad_probs, axis=0, keepdims=True)
                grad_scores = low(probs_wide * (grad_probs - inner))
                parts.append(dot(keys_head, grad_scores))
                to_keys = dot(grad_scores, query_block[at : at + span, :])
                to_values = dot(probs_low, grad_block[at : at + span, :])
                sum_keys = to_keys if sum_keys is None else sum_keys + to_keys
                sum_values = to_values if sum_values is None else sum_values + to_values
            grad_query.append(jnp.concatenate(parts, axis=1))
            grad_keys.append(sum_keys)
            grad_values.append(sum_values)
        first = lane < HEAD_DIM
        gq_ref[0] = low(jnp.concatenate(grad_query, axis=0).T * scale)
        gk_ref[0] = low(jnp.where(first, grad_keys[0], grad_keys[1]))
        gv_ref[0] = low(jnp.where(first, grad_values[0], grad_values[1]))

    block = pl.BlockSpec((1, length, LANES), lambda i, j, p: (i, 0, j))
    return call(
        body,
        place,
        (query, keys, values, probs, grad),
        [block] * 3
        + [pl.BlockSpec((1, 1, 2, length, length), lambda i, j, p: (i, j, 0, 0, 0)), block],
        [sds((2, length, heads), jnp.bfloat16)] * 3,
        [block] * 3,
        [],
        "attention_back",
        grid=(2, pairs),
    )


def project_out(place, mine, theirs, weight_mine, weight_theirs, rows, bias, gain, norm_bias):
    count, part, half = weight_mine.shape
    z_size = count // 2
    width = part * count
    _, length, heads = mine.shape

    def body(
        place_ref, mine_ref, theirs_ref, wm_ref, wt_ref, own_ref, other_ref, bias_ref, gain_ref,
        nb_ref, middle_ref, normed_ref, weight, total, sem,
    ):
        copies = []
        for number in range(count):
            z, x = shard_of(place_ref, number, z_size)
            row = pl.multiple_of((z * 2 + x) * part, part)
            for slot, ref in enumerate((wm_ref, wt_ref)):
                copy = pltpu.make_async_copy(
                    ref.at[number],
                    weight.at[slot, pl.ds(row, part), :],
                    sem.at[2 * number + slot],
                )
                copy.start()
                copies.append(copy)
        for copy in copies:
            copy.wait()
        core = place_ref[2]
        at_mine = pl.multiple_of(core * heads, heads)
        at_theirs = pl.multiple_of((1 - core) * heads, heads)
        for image, ref in enumerate((own_ref, other_ref)):
            for slot in range(2):
                branch = dot(mine_ref[image], weight[slot, pl.ds(at_mine, heads), :]) + dot(
                    theirs_ref[1 - image], weight[slot, pl.ds(at_theirs, heads), :]
                )
                total[slot] = branch
            for at in range(0, length, LANES):
                upto = at + LANES
                first, second = total[0, at:upto, :], total[1, at:upto, :]
                left = jnp.where(core == 0, first, second)
                right = jnp.where(core == 0, second, first)
                middle = (
                    wide(ref[at:upto, :])
                    + jnp.concatenate([left, right], axis=1)
                    + bias_ref[...]
                )
                if image == 0:
                    middle_ref[at:upto, :] = middle
                normed_ref[image, at:upto, :] = low(
                    normalised(middle) * gain_ref[...] + nb_ref[...]
                )

    return call(
        body,
        place,
        (mine, theirs, weight_mine, weight_theirs, *rows, bias, gain, norm_bias),
        [whole((2, length, heads))] * 2
        + [any_spec()] * 2
        + [whole((length, width))] * 2
        + [whole((1, width))] * 3,
        [sds((length, width), jnp.float32), sds((2, length, width), jnp.bfloat16)],
        [whole((length, width)), whole((2, length, width))],
        [
            pltpu.VMEM((2, width, half), jnp.bfloat16),
            pltpu.VMEM((2, length, half), jnp.float32),
            pltpu.SemaphoreType.DMA((2 * count,)),
        ],
        "project_out",
    )


def feed_forward(place, normed, cotangent, pieces, bias, running):
    count = len(pieces)
    z_size = count // 2
    blocks, part, wide_block = pieces[0].shape
    half_blocks = blocks // 2
    width = part * count
    _, length, _ = normed.shape
    first_call = running is None

    def body(place_ref, normed_ref, own_cot, other_cot, bias_ref, *refs):
        ins = refs[:count]
        refs = refs[count:]
        if not first_call:
            before, refs = refs[:4], refs[4:]
        out_own, out_other, gn_own, gn_other, bsum_ref, keep_ref, send_ref = refs[:7]
        w_in, w_down, normed_t, grads, sem, out_sem = refs[7:]
        step = pl.program_id(0)

        def copies():
            made = []
            for number, ref in enumerate(ins):
                z, x = shard_of(place_ref, number, z_size)
                row = pl.multiple_of((z * 2 + x) * part, part)
                row_in = pl.multiple_of(x * part, part)
                for b in range(half_blocks):
                    made.append(
                        pltpu.make_async_copy(
                            ref.at[b], w_in.at[b, pl.ds(row, part), :], sem.at[number * blocks + b]
                        )
                    )
                    made.append(
                        pltpu.make_async_copy(
                            ref.at[half_blocks + b],
                            w_down.at[z, pl.ds(row_in, part), pl.ds(b * wide_block, wide_block)],
                            sem.at[number * blocks + half_blocks + b],
                        )
                    )
            return made

        @pl.when(step == 0)
        def _():
            for copy in copies():
                copy.start()
            for image in range(2):
                normed_t[:, image * length : (image + 1) * length] = normed_ref[image].T
            for copy in copies():
                copy.wait()

        weight_in = w_in[step]
        weight_down = w_down[step]
        into = None
        down = None
        column_sum = None
        for image, cot_ref in enumerate((own_cot, other_cot)):
            preact = dot(normed_ref[image], weight_in) + bias_ref[0]
            phi = 0.5 * (1.0 + lax.erf(preact * math.sqrt(0.5)))
            density = jnp.exp(-0.5 * preact * preact) * (1.0 / math.sqrt(2.0 * math.pi))
            hidden = low(preact * phi)
            slope = phi + preact * density
            cot = cot_ref[...]
            grad = low(dot_tail(cot, weight_down) * slope)
            out_ref, gn_ref = ((out_own, gn_own), (out_other, gn_other))[image]
            to_out = dot(hidden, weight_down)
            to_normed = dot_tail(grad, weight_in)

            @pl.when(step == 0)
            def _():
                if first_call:
                    out_ref[...] = to_out
                    gn_ref[...] = to_normed
                else:
                    out_ref[...] = before[image][...] + to_out
                    gn_ref[...] = before[2 + image][...] + to_normed

            @pl.when(step > 0)
            def _():
                out_ref[...] += to_out
                gn_ref[...] += to_normed

            partial = jnp.sum(wide(grad), axis=0, keepdims=True)
            column_sum = partial if image == 0 else column_sum + partial
            to_in = dot(normed_t[:, image * length : (image + 1) * length], grad)
            into = to_in if image == 0 else into + to_in
            to_down = dot(hidden.T, cot)
            down = to_down if image == 0 else down + to_down
        bsum_ref[0] = column_sum
        for z in range(z_size):
            for x in range(2):
                k = lax.rem(z + z_size - place_ref[0], z_size)
                dx = x + (1 - 2 * x) * place_ref[1]
                at = (z * 2 + x) * part
                grads[dx, k, step] = low(into[at : at + part, :])
        for x in range(2):
            k = lax.rem(step + z_size - place_ref[0], z_size)
            dx = x + (1 - 2 * x) * place_ref[1]
            for b in range(half_blocks):
                grads[dx, k, half_blocks + b] = low(
                    down[x * part : (x + 1) * part, b * wide_block : (b + 1) * wide_block]
                )

        @pl.when(step == half_blocks - 1)
        def _():
            for slot, ref in enumerate((keep_ref, send_ref)):
                pltpu.make_async_copy(grads.at[slot], ref, out_sem.at[slot]).start()
            for slot, ref in enumerate((keep_ref, send_ref)):
                pltpu.make_async_copy(grads.at[slot], ref, out_sem.at[slot]).wait()

    total = sds((length, width), jnp.float32)
    piece_out = sds((z_size, blocks, part, wide_block), jnp.bfloat16)
    carried = () if first_call else tuple(running)
    return call(
        body,
        place,
        (normed, *cotangent, bias, *pieces, *carried),
        [whole((2, length, width))]
        + [whole((length, width))] * 2
        + [pl.BlockSpec((1, 1, wide_block), lambda b, p: (b, 0, 0))]
        + [any_spec()] * count
        + [whole((length, width))] * len(carried),
        [total] * 4 + [sds((half_blocks, 1, wide_block), jnp.float32)] + [piece_out] * 2,
        [whole((length, width))] * 4
        + [pl.BlockSpec((1, 1, wide_block), lambda b, p: (b, 0, 0))]
        + [any_spec()] * 2,
        [
            pltpu.VMEM((half_blocks, width, wide_block), jnp.bfloat16),
            pltpu.VMEM((half_blocks, wide_block, width), jnp.bfloat16),
            pltpu.VMEM((width, 2 * length), jnp.bfloat16),
            pltpu.VMEM((2, z_size, blocks, part, wide_block), jnp.bfloat16),
            pltpu.SemaphoreType.DMA((count * blocks,)),
            pltpu.SemaphoreType.DMA((2,)),
        ],
        "feed_forward",
        grid=(half_blocks,),
    )


def norm_back(place, rows, gain, grad_own, grad_other, passed, last):
    length, width = rows.shape
    sums = 2 if last else 3

    def body(place_ref, rows_ref, gain_ref, own_ref, other_ref, pass_ref, *refs):
        out_refs, sum_ref = refs[:-1], refs[-1]
        step = pl.program_id(0)
        values = wide(rows_ref[...])
        centre = values - jnp.mean(values, axis=-1, keepdims=True)
        spread = jnp.mean(centre * centre, axis=-1, keepdims=True)
        inverse = lax.rsqrt(spread + ln_eps)
        unit = centre * inverse
        grad = own_ref[...] + other_ref[...]
        scaled = grad * gain_ref[...]
        mean_one = jnp.mean(scaled, axis=-1, keepdims=True)
        mean_two = jnp.mean(scaled * unit, axis=-1, keepdims=True)
        result = wide(pass_ref[...]) + (scaled - mean_one - unit * mean_two) * inverse
        parts = [
            jnp.sum(grad * unit, axis=0, keepdims=True),
            jnp.sum(grad, axis=0, keepdims=True),
        ]
        if last:
            out_refs[0][...] = low(result)
        else:
            out_refs[0][...] = result
            rounded = low(result)
            out_refs[1][...] = rounded
            parts.append(jnp.sum(wide(rounded), axis=0, keepdims=True))
        joined = jnp.concatenate(parts, axis=0)

        @pl.when(step == 0)
        def _():
            sum_ref[...] = joined

        @pl.when(step > 0)
        def _():
            sum_ref[...] += joined

    block = pl.BlockSpec((LANES, width), lambda i, p: (i, 0))
    if last:
        outs = [sds((length, width), jnp.bfloat16)]
    else:
        outs = [sds((length, width), jnp.float32), sds((length, width), jnp.bfloat16)]
    return call(
        body,
        place,
        (rows, gain, grad_own, grad_other, passed),
        [block, whole((1, width)), block, block, block],
        outs + [sds((sums, width), jnp.float32)],
        [block] * len(outs) + [whole((sums, width))],
        [],
        "norm_back",
        grid=(length // LANES,),
    )


def out_back(place, grad_own, grad_other, mine, theirs, weight_mine, weight_theirs):
    count, part, half = weight_mine.shape
    z_size = count // 2
    width = part * count
    _, length, heads = mine.shape

    def body(
        place_ref, own_ref, other_ref, own_half, other_half, mine_ref, theirs_ref, wm_ref, wt_ref,
        ga_ref, keep_ref, send_ref, weight, turned, grads, sem, out_sem,
    ):
        copies = []
        for number in range(count):
            z, x = shard_of(place_ref, number, z_size)
            row = pl.multiple_of((z * 2 + x) * part, part)
            for slot, ref in enumerate((wm_ref, wt_ref)):
                copy = pltpu.make_async_copy(
                    ref.at[number],
                    weight.at[slot, pl.ds(row, part), :],
                    sem.at[2 * number + slot],
                )
                copy.start()
                copies.append(copy)
        core = place_ref[2]
        at_mine = pl.multiple_of(core * heads, heads)
        at_theirs = pl.multiple_of((1 - core) * heads, heads)
        for image in range(2):
            lanes = slice(image * length, (image + 1) * length)
            turned[pl.ds(at_mine, heads), lanes] = mine_ref[image].T
            turned[pl.ds(at_theirs, heads), lanes] = theirs_ref[1 - image].T
        term = dot(turned[:, :length], own_half[...]) + dot(turned[:, length:], other_half[...])
        for z in range(z_size):
            for x in range(2):
                k = lax.rem(z + z_size - place_ref[0], z_size)
                dx = x + (1 - 2 * x) * place_ref[1]
                at = (z * 2 + x) * part
                grads[dx, k] = low(term[at : at + part, :])
        for slot, ref in enumerate((keep_ref, send_ref)):
            pltpu.make_async_copy(grads.at[slot], ref, out_sem.at[slot]).start()
        for copy in copies:
            copy.wait()
        for image, ref in enumerate((own_ref, other_ref)):
            first, second = ref[:, :half], ref[:, half:]
            left = jnp.where(core == 0, first, second)
            right = jnp.where(core == 0, second, first)
            ga_ref[image] = low(
                dot_tail(left, weight[0, pl.ds(at_mine, heads), :])
                + dot_tail(right, weight[1, pl.ds(at_mine, heads), :])
            )
        for slot, ref in enumerate((keep_ref, send_ref)):
            pltpu.make_async_copy(grads.at[slot], ref, out_sem.at[slot]).wait()

    half_block = pl.BlockSpec((length, half), lambda i, p: (0, p[2]))
    piece_out = sds((z_size, part, half), jnp.bfloat16)
    return call(
        body,
        place,
        (
            grad_own,
            grad_other,
            grad_own,
            grad_other,
            mine,
            theirs,
            weight_mine,
            weight_theirs,
        ),
        [whole((length, width))] * 2
        + [half_block] * 2
        + [whole((2, length, heads))] * 2
        + [any_spec()] * 2,
        [sds((2, length, heads), jnp.bfloat16)] + [piece_out] * 2,
        [whole((2, length, heads))] + [any_spec()] * 2,
        [
            pltpu.VMEM((2, width, half), jnp.bfloat16),
            pltpu.VMEM((width, 2 * length), jnp.bfloat16),
            pltpu.VMEM((2, z_size, part, half), jnp.bfloat16),
            pltpu.SemaphoreType.DMA((2 * count,)),
            pltpu.SemaphoreType.DMA((2,)),
        ],
        "out_back",
    )


def qkv_term(place, normed, grad_q, grad_k, grad_v):
    _, length, width = normed.shape
    heads = grad_q.shape[-1]
    cols = 3 * heads

    def body(place_ref, normed_ref, gq_ref, gk_ref, gv_ref, sum_ref, keep_ref, send_ref, turned, grads, sem):
        z_size = grads.shape[1]
        part = grads.shape[2]
        for image in range(2):
            turned[:, image * length : (image + 1) * length] = normed_ref[image].T
        for slot, ref in enumerate((gq_ref, gk_ref, gv_ref)):
            term = dot(turned[:, :length], ref[0]) + dot(turned[:, length:], ref[1])
            for z in range(z_size):
                for x in range(2):
                    k = lax.rem(z + z_size - place_ref[0], z_size)
                    dx = x + (1 - 2 * x) * place_ref[1]
                    at = (z * 2 + x) * part
                    grads[dx, k, :, slot * heads : (slot + 1) * heads] = low(
                        term[at : at + part, :]
                    )
            sum_ref[slot : slot + 1, :] = jnp.sum(wide(ref[0]), axis=0, keepdims=True) + jnp.sum(
                wide(ref[1]), axis=0, keepdims=True
            )
        for slot, ref in enumerate((keep_ref, send_ref)):
            pltpu.make_async_copy(grads.at[slot], ref, sem.at[slot]).start()
        for slot, ref in enumerate((keep_ref, send_ref)):
            pltpu.make_async_copy(grads.at[slot], ref, sem.at[slot]).wait()

    z_size = lax.axis_size("z")
    part = width // (2 * z_size)
    piece_out = sds((z_size, part, cols), jnp.bfloat16)
    return call(
        body,
        place,
        (normed, grad_q, grad_k, grad_v),
        [whole((2, length, width))] + [whole((2, length, heads))] * 3,
        [sds((3, heads), jnp.float32)] + [piece_out] * 2,
        [whole((3, heads))] + [any_spec()] * 2,
        [
            pltpu.VMEM((width, 2 * length), jnp.bfloat16),
            pltpu.VMEM((2, z_size, part, cols), jnp.bfloat16),
            pltpu.SemaphoreType.DMA((2,)),
        ],
        "qkv_term",
    )


def qkv_back(place, grad_q, grad_k, grad_v, pieces):
    count = len(pieces)
    z_size = count // 2
    part, cols = pieces[0].shape
    width = part * count
    heads = cols // 3
    length = grad_q.shape[1]

    def body(place_ref, gq_ref, gk_ref, gv_ref, *refs):
        ins, (own_ref, other_ref, weight, sem) = refs[:count], refs[count:]
        copies = []
        for number, ref in enumerate(ins):
            z, x = shard_of(place_ref, number, z_size)
            row = pl.multiple_of((z * 2 + x) * part, part)
            copy = pltpu.make_async_copy(ref, weight.at[pl.ds(row, part), :], sem.at[number])
            copy.start()
            copies.append(copy)
        for copy in copies:
            copy.wait()
        for image, out_ref in enumerate((own_ref, other_ref)):
            out_ref[...] = (
                dot_tail(gq_ref[image], weight[:, :heads])
                + dot_tail(gk_ref[image], weight[:, heads : 2 * heads])
                + dot_tail(gv_ref[image], weight[:, 2 * heads :])
            )

    return call(
        body,
        place,
        (grad_q, grad_k, grad_v, *pieces),
        [whole((2, length, heads))] * 3 + [any_spec()] * count,
        [sds((length, width), jnp.float32)] * 2,
        [whole((length, width))] * 2,
        [pltpu.VMEM((width, cols), jnp.bfloat16), pltpu.SemaphoreType.DMA((count,))],
        "qkv_back",
    )


def on_device(
    inputs,
    cotangent,
    norm1_gain,
    norm1_bias,
    qkv_weight,
    qv_bias,
    out_weight,
    out_bias,
    norm2_gain,
    norm2_bias,
    in_weight,
    in_bias,
    down_weight,
    down_bias,
    qkv_rows,
    qkv_cols,
    out_rows,
    out_cols,
    in_rows,
    in_cols,
    down_rows,
    down_cols,
    norm1_gain_moment,
    norm1_bias_moment,
    qv_bias_moment,
    out_bias_moment,
    norm2_gain_moment,
    norm2_bias_moment,
    in_bias_moment,
    down_bias_moment,
):
    masters = [
        norm1_gain,
        norm1_bias,
        qkv_weight,
        qv_bias,
        out_weight,
        out_bias,
        norm2_gain,
        norm2_bias,
        in_weight,
        in_bias,
        down_weight,
        down_bias,
    ]
    core = lax.axis_index("c")
    place = jnp.stack([lax.axis_index("z"), lax.axis_index("x"), core]).astype(jnp.int32)
    group_size = lax.axis_size("z") * lax.axis_size("x")
    tokens, width = inputs.shape
    images_all = (tokens // SEQ) * group_size * lax.axis_size("y") * lax.axis_size("c")
    padding = ((0, row_pad(tokens) - tokens), (0, 0))
    rows_own = jnp.pad(inputs, padding)
    cot_own = jnp.pad(cotangent, padding)
    rows = (rows_own, swap(rows_own, "c"))
    cot = (cot_own, swap(cot_own, "c"))

    def half_cols(shard, groups):
        cut = shard.reshape(shard.shape[0], groups, 2, -1)
        return lax.dynamic_index_in_dim(cut, core, 2, False)

    def halves_of(pair):
        mine, theirs = pair
        return jnp.where(core == 0, mine, theirs), jnp.where(core == 0, theirs, mine)

    vectors = [0, 1, 3, 5, 6, 7, 9, 11]
    sizes = [masters[number].shape[0] for number in vectors]
    small = wide(gather_small(low(jnp.concatenate([masters[number] for number in vectors]))))
    full = {}
    at = 0
    for number, size in zip(vectors, sizes):
        full[number] = small[:, at : at + size].reshape(1, -1)
        at += size
    heads_bias = lax.dynamic_index_in_dim(
        full[3].reshape(2, 2, 1, width // 2), core, 1, False
    )

    rows_qkv = low(half_cols(qkv_weight, 3)).reshape(qkv_weight.shape[0], -1)
    pieces_qkv = gather_pieces(rows_qkv)
    pieces_out = gather_pieces(low(half_cols(out_weight, 1)).reshape(out_weight.shape[0], -1))
    weight_mine = jnp.stack(pieces_out)
    weight_theirs = swap(weight_mine, "c")

    part = in_weight.shape[0]
    per_shard = in_weight.shape[1] // group_size // 2 // CHUNKS
    hidden_chunk = per_shard * group_size
    wide_block = hidden_chunk // (group_size // 2)
    blocks = hidden_chunk // wide_block
    in_cut = low(
        lax.dynamic_index_in_dim(
            in_weight.reshape(part, group_size, 2, CHUNKS, per_shard), core, 2, False
        )
    )
    down_cut = low(
        lax.dynamic_index_in_dim(
            down_weight.reshape(2, CHUNKS, per_shard, width // wide_block, wide_block),
            core,
            0,
            False,
        )
    )
    bias_cut = lax.dynamic_index_in_dim(
        full[9].reshape(group_size, 2, CHUNKS, per_shard), core, 1, False
    )
    pieces_ff = []
    bias_ff = []
    for j in range(CHUNKS):
        from_in = in_cut[:, :, j].reshape(part, blocks, wide_block).transpose(1, 0, 2)
        from_down = down_cut[j].transpose(1, 0, 2)
        pieces_ff.append(gather_pieces(jnp.concatenate([from_in, from_down], axis=0)))
        bias_ff.append(bias_cut[:, j].reshape(blocks, 1, wide_block))

    normed, query, keys, values = project_qkv(
        place, rows, full[0], full[1], heads_bias[0], heads_bias[1], pieces_qkv
    )
    attended, probs = attention(place, query, keys, values)
    attended_theirs = swap(attended, "c")
    middle, normed_mid = project_out(
        place,
        attended,
        attended_theirs,
        weight_mine,
        weight_theirs,
        rows,
        full[5],
        full[6],
        full[7],
    )
    running = None
    hidden_sums = []
    grad_ff = []
    for j in range(CHUNKS):
        *running, sums, keep, send = feed_forward(
            place, normed_mid, cot, pieces_ff[j], bias_ff[j], running
        )
        hidden_sums.append(sums)
        grad_ff.append(scatter_sum(keep, send))
    out_share, out_given, normed_share, normed_given = running
    output = low(middle + out_share + swap(out_given, "c") + full[11])[:tokens]
    grad_mid, grad_mid_low, sums_mid = norm_back(
        place, middle, full[6], normed_share, swap(normed_given, "c"), cot_own, False
    )
    grad_mid_other = swap(grad_mid_low, "c")
    grad_attended, keep, send = out_back(
        place,
        grad_mid_low,
        grad_mid_other,
        attended,
        attended_theirs,
        weight_mine,
        weight_theirs,
    )
    grad_out_half = scatter_sum(keep, send)
    grad_q, grad_k, grad_v = attention_back(place, query, keys, values, probs, grad_attended)
    sums_qkv, keep, send = qkv_term(place, normed, grad_q, grad_k, grad_v)
    grad_qkv_half = scatter_sum(keep, send)
    share, given = qkv_back(place, grad_q, grad_k, grad_v, pieces_qkv)
    input_grad, sums_in = norm_back(
        place, rows_own, full[0], share, swap(given, "c"), grad_mid, True
    )
    input_grad = input_grad[:tokens]

    def both_cores(half):
        return halves_of((half, swap(half, "c")))

    grads = [None] * 12
    pair = both_cores(grad_qkv_half / images_all)
    grads[2] = jnp.stack(
        [half.reshape(part, 3, width // 2) for half in pair], axis=2
    ).reshape(qkv_weight.shape)
    pair = both_cores(grad_out_half / images_all)
    grads[4] = jnp.concatenate(pair, axis=1)
    pairs = [both_cores(half / images_all) for half in grad_ff]
    both = jnp.stack([jnp.stack(pair) for pair in pairs])
    by_in = both[:, :, :blocks].reshape(CHUNKS, 2, blocks, part, -1, per_shard)
    grads[8] = by_in.transpose(3, 2, 4, 1, 0, 5).reshape(in_weight.shape)
    grads[10] = both[:, :, blocks:].transpose(1, 0, 3, 2, 4).reshape(down_weight.shape)

    def by_core(cols, axis):
        empty = jnp.zeros_like(cols)
        return jnp.stack(
            [jnp.where(core == 0, cols, empty), jnp.where(core == 0, empty, cols)], axis=axis
        )

    hidden_cols = jnp.stack(hidden_sums).reshape(CHUNKS, group_size, per_shard)
    term_in_bias = by_core(hidden_cols.transpose(1, 0, 2), 1).reshape(-1)
    term_qv_bias = by_core(sums_qkv[::2], 1).reshape(-1)
    term_down_bias = jnp.sum(wide(cotangent), axis=0)
    vector_terms = {
        0: sums_in[0],
        1: sums_in[1],
        3: term_qv_bias,
        5: sums_mid[2],
        6: sums_mid[0],
        7: sums_mid[1],
        9: term_in_bias,
        11: term_down_bias,
    }
    here = lax.axis_index("z") * lax.axis_size("x") + lax.axis_index("x")
    for group in ((5, 6, 7, 9, 11), (0, 1, 3)):
        summed = sum_over(
            jnp.concatenate(
                [vector_terms[number].reshape(group_size, -1) for number in group], axis=1
            ),
            ("c", "x", "z", "y"),
        )
        mine = lax.dynamic_index_in_dim(summed, here, 0, False) / images_all
        at = 0
        for number in group:
            size = masters[number].shape[0]
            grads[number] = mine[at : at + size]
            at += size
    row_states = [qkv_rows, out_rows, in_rows, down_rows]
    col_states = [qkv_cols, out_cols, in_cols, down_cols]
    moments = [
        norm1_gain_moment,
        norm1_bias_moment,
        qv_bias_moment,
        out_bias_moment,
        norm2_gain_moment,
        norm2_bias_moment,
        in_bias_moment,
        down_bias_moment,
    ]
    matrix_slots = {2: 0, 4: 1, 8: 2, 10: 3}
    vector_slots = {0: 0, 1: 1, 3: 2, 5: 3, 6: 4, 7: 5, 9: 6, 11: 7}
    prepared = [None] * 12
    new_params = [None] * 12
    clips = [None] * 12
    new_cols_all = [None] * 4

    def finish(number, direction, direction_total, weight_total, count):
        clip_factor = jnp.maximum(1.0, jnp.sqrt(direction_total / count) / clip_level)
        rms_weight = jnp.sqrt(weight_total / count)
        clips[number] = clip_factor
        new_params[number] = masters[number] - step_rate * rms_weight * direction / clip_factor

    for number in (10, 8, 4, 2):
        position = matrix_slots[number]
        weight, grad = masters[number], grads[number]
        squared = grad * grad
        new_rows = 0.5 * row_states[position] + 0.5 * jnp.mean(squared, axis=1)
        prepared[number] = new_rows
        pack = jnp.concatenate(
            [
                jnp.sum(squared, axis=0),
                jnp.sum(squared / new_rows[:, None], axis=0),
                jnp.stack([jnp.sum(new_rows), jnp.sum(weight * weight)]),
            ]
        )
        total = sum_over(pack, ("x", "z"))
        rows_total, cols = weight.shape[0] * group_size, weight.shape[1]
        new_cols = 0.5 * col_states[position] + 0.5 * total[:cols] / rows_total
        new_cols_all[position] = new_cols
        mean_rows = total[-2] / rows_total
        direction = grad * lax.rsqrt(new_rows[:, None] * new_cols[None, :] / mean_rows)
        direction_total = mean_rows * jnp.sum(total[cols : 2 * cols] / new_cols)
        finish(number, direction, direction_total, total[-1], rows_total * cols)
    sums = []
    directions = {}
    for number in vectors:
        weight, grad = masters[number], grads[number]
        prepared[number] = 0.5 * moments[vector_slots[number]] + 0.5 * grad * grad
        directions[number] = grad * lax.rsqrt(prepared[number])
        sums.append(jnp.sum(weight * weight))
        sums.append(jnp.sum(directions[number] * directions[number]))
    total = sum_over(jnp.stack(sums), ("x", "z"))
    for slot, number in enumerate(vectors):
        finish(
            number,
            directions[number],
            total[2 * slot + 1],
            total[2 * slot],
            masters[number].shape[0] * group_size,
        )
    clip_factors = jnp.stack(clips)
    new_rows_all = [prepared[2], prepared[4], prepared[8], prepared[10]]
    new_moments = [
        prepared[0],
        prepared[1],
        prepared[3],
        prepared[5],
        prepared[6],
        prepared[7],
        prepared[9],
        prepared[11],
    ]
    return (
        output,
        input_grad,
        grads[0],
        grads[1],
        grads[2],
        grads[3],
        grads[4],
        grads[5],
        grads[6],
        grads[7],
        grads[8],
        grads[9],
        grads[10],
        grads[11],
        new_rows_all[0],
        new_cols_all[0],
        new_rows_all[1],
        new_cols_all[1],
        new_rows_all[2],
        new_cols_all[2],
        new_rows_all[3],
        new_cols_all[3],
        new_moments[0],
        new_moments[1],
        new_moments[2],
        new_moments[3],
        new_moments[4],
        new_moments[5],
        new_moments[6],
        new_moments[7],
        new_params[0],
        new_params[1],
        new_params[2],
        new_params[3],
        new_params[4],
        new_params[5],
        new_params[6],
        new_params[7],
        new_params[8],
        new_params[9],
        new_params[10],
        new_params[11],
        clip_factors,
    )


def solution(mesh):
    group = mesh.shape["fsdp"]
    split = Mesh(mesh.devices.reshape(group // 2, 2, mesh.shape["dp"] // 2, 2), ALL_AXES)
    in_specs = (
        P(("z", "x", "y", "c"), None),
        P(("z", "x", "y", "c"), None),
        P(("z", "x")),
        P(("z", "x")),
        P(("z", "x"), None),
        P(("z", "x")),
        P(("z", "x"), None),
        P(("z", "x")),
        P(("z", "x")),
        P(("z", "x")),
        P(("z", "x"), None),
        P(("z", "x")),
        P(("z", "x"), None),
        P(("z", "x")),
        P(("z", "x")),
        P(),
        P(("z", "x")),
        P(),
        P(("z", "x")),
        P(),
        P(("z", "x")),
        P(),
        P(("z", "x")),
        P(("z", "x")),
        P(("z", "x")),
        P(("z", "x")),
        P(("z", "x")),
        P(("z", "x")),
        P(("z", "x")),
        P(("z", "x")),
    )
    out_specs = (
        P(("z", "x", "y", "c"), None),
        P(("z", "x", "y", "c"), None),
        P(("z", "x")),
        P(("z", "x")),
        P(("z", "x"), None),
        P(("z", "x")),
        P(("z", "x"), None),
        P(("z", "x")),
        P(("z", "x")),
        P(("z", "x")),
        P(("z", "x"), None),
        P(("z", "x")),
        P(("z", "x"), None),
        P(("z", "x")),
        P(("z", "x")),
        P(),
        P(("z", "x")),
        P(),
        P(("z", "x")),
        P(),
        P(("z", "x")),
        P(),
        P(("z", "x")),
        P(("z", "x")),
        P(("z", "x")),
        P(("z", "x")),
        P(("z", "x")),
        P(("z", "x")),
        P(("z", "x")),
        P(("z", "x")),
        P(("z", "x")),
        P(("z", "x")),
        P(("z", "x"), None),
        P(("z", "x")),
        P(("z", "x"), None),
        P(("z", "x")),
        P(("z", "x")),
        P(("z", "x")),
        P(("z", "x"), None),
        P(("z", "x")),
        P(("z", "x"), None),
        P(("z", "x")),
        P(),
    )
    return jax.shard_map(
        on_device, mesh=split, in_specs=in_specs, out_specs=out_specs, check_vma=False
    )
```

time: 1680 us -> 751 us (0.45)
  Pallas kernels: 768 us -> 207 us
  matrix products: 235 us -> 0 us
  waiting for transfers between devices: 392 us -> 273 us
  other arithmetic: 105 us -> 76.6 us
    pallas_call x3 -> x11, Pallas kernels: 768 us -> 207 us  [call(): pl.pallas_call(body, out_shape=outs, grid_spec=pltpu.PrefetchScalarGridSp...]
    dot_general x18 -> x0, matrix products: 235 us -> none  [the longest x4 50.6 us: plain_dot(): return jnp.dot(left, right, preferred_element_type=jnp.float32)]
    ppermute x23 -> x28, waiting for transfers between devices: 112 us -> 46 us  [partner(): return lax.ppermute(value, axis, [(i, i ^ step) for i in range(size)])]
    ppermute x21 -> x24, waiting for transfers between devices: 136 us -> 71.3 us  [shift(): lax.ppermute(value, axis, [(i, (i + step) % size) for i in range(size)])]
    add x13 -> x0, other arithmetic: 28.4 us -> none  [the longest x4 16.5 us: scatter_sum(): kept = pick(cut, core, 2, False) + got]
    reduce_sum x9 -> x1, other arithmetic: 23.7 us -> 0.21 us  [on_device(): term_down_bias = jnp.sum(wide(cotangent), axis=0)]
    convert_element_type x15 -> x7, local copies, waits for them, and re-layouts: 23.1 us -> 4.18 us  [low(): return value.astype(jnp.bfloat16)]
    ppermute x49 -> x36, waiting for transfers between devices: 145 us -> 156 us  [swap(): return lax.ppermute(value, axis, [(0, 1), (1, 0)])]
  transfers between devices with their start and end apart: 93 -> 88, of which waited for: 41 -> 36; matrix products, arithmetic and copies ran while one was open for 9% -> 16% of each run, Pallas kernels for 12% -> 28%
where the time goes in v2:
time: 751 us; the launch traced here: 745 us
  waiting for transfers between devices  273 us (36%)
  Pallas kernels  207 us (28%)
  starting transfers between devices  92.8 us (12%)
  other arithmetic  76.6 us (10%)
  local copies, waits for them, and re-layouts  73.8 us (10%)
  between operations  21.7 us (3%)
    pallas_call x11, Pallas kernels, call(): pl.pallas_call(body, out_shape=outs, grid_spec=pltpu.PrefetchScalarGridSp...  207 us
    ppermute x36, waiting for transfers between devices, swap(): return lax.ppermute(value, axis, [(0, 1), (1, 0)])  156 us
    ppermute x24, waiting for transfers between devices, shift(): lax.ppermute(value, axis, [(i, (i + step) % size) for i in range(size)])  71.3 us
    ppermute x28, waiting for transfers between devices, partner(): return lax.ppermute(value, axis, [(i, i ^ step) for i in range(size)])  46 us
    ppermute x24, starting transfers between devices, shift(): lax.ppermute(value, axis, [(i, (i + step) % size) for i in range(size)])  32.9 us
    ppermute x36, starting transfers between devices, swap(): return lax.ppermute(value, axis, [(0, 1), (1, 0)])  30.7 us
    ppermute x28, starting transfers between devices, partner(): return lax.ppermute(value, axis, [(i, i ^ step) for i in range(size)])  29.2 us
    unnamed x234, local copies, waits for them, and re-layouts  26.2 us
  transfers between devices with their start and end apart: 88, of which 36 were waited for; matrix products, arithmetic and copies ran while one was open for 16% of the time, Pallas kernels for 28%

profile of v2, /device:TPU:0, one launch (start us, length us, event | category | flops | bytes accessed | tf_op | source)
XLA Modules:
  0.0 744.9 jit_solution(11941553340393587705)
XLA Ops:
  52.7 5.8 collective-permute-done.9.refs_6_
  60.9 14.9 %collective-permute-done.7.refs_4_ = bf16[128,1536]{1,0:T(8,128)(2,1)S(1)} collective-permute-done((bf16[128,1536]{1,0:T(8,128)(2,1)S(1)}, bf16[128,1536]{1,0:T(8,128)(2,1)S(1)}, u32[]{:S(2)}, u32[]{:S(2)}) %collective-permute-start.7) | collective-permute-done | bytes 393248 | tf_op jit(solution)/shard_map/ppermute | solution.py:31
  89.1 9.6 %project_qkv.1 = (bf16[2,640,1024]{2,1,0:T(8,128)(2,1)}, bf16[2,640,512]{2,1,0:T(8,128)(2,1)}, bf16[2,640,512]{2,1,0:T(8,128)(2,1)}, bf16[2,640,512]{2,1,0:T(8,128)(2,1)}) custom-call(s32[3]{0:T(128)} %pad_add_fusion.place_ref, bf16[640,1024]{1,0:T(8,128)(2,1)} %copy-done.1, bf16[640,1024]{1,0:T(8,128)(2,1)} %copy-done.17, f32[1,1024]{1,0:T(1,128)} %bitcast.297, ...), custom_call_target="tpu_custom_call" | custom-call | tf_op jit(solution)/shard_map/project_qkv/pallas_call | solution.py:119
  98.7 28.3 %attention.1 = (bf16[2,640,512]{2,1,0:T(8,128)(2,1)}, bf16[2,4,2,640,640]{4,3,2,1,0:T(8,128)(2,1)}) custom-call(s32[3]{0:T(128)} %pad_add_fusion.place_ref, bf16[2,640,512]{2,1,0:T(8,128)(2,1)} %get-tuple-element.81.q_ref, bf16[2,640,512]{2,1,0:T(8,128)(2,1)} %get-tuple-element.82.k_ref, bf16[2,640,512]{2,1,0:T(8,128)(2,1)} %get-tuple-element.83.v_ref), custom_call_target="tpu_custom_call" | custom-call | tf_op jit(solution)/shard_map/attention/pallas_call | solution.py:119
  132.1 11.3 %collective-permute-done.28.refs_1_ = bf16[8,128,256]{2,1,0:T(8,128)(2,1)S(1)} collective-permute-done((bf16[8,128,256]{2,1,0:T(8,128)(2,1)S(1)}, bf16[8,128,256]{2,1,0:T(8,128)(2,1)S(1)}, u32[]{:S(2)}, u32[]{:S(2)}) %collective-permute-start.28) | collective-permute-done | bytes 524320 | tf_op jit(solution)/shard_map/ppermute | solution.py:26
  143.9 10.7 %collective-permute-done.30.refs_3_ = bf16[8,128,256]{2,1,0:T(8,128)(2,1)S(1)} collective-permute-done((bf16[8,128,256]{2,1,0:T(8,128)(2,1)}, bf16[8,128,256]{2,1,0:T(8,128)(2,1)S(1)}, u32[]{:S(2)}, u32[]{:S(2)}) %collective-permute-start.30) | collective-permute-done | bytes 524320 | tf_op jit(solution)/shard_map/ppermute | solution.py:26
  156.5 9.4 %collective-permute-done.32.refs_5_ = bf16[8,128,256]{2,1,0:T(8,128)(2,1)} collective-permute-done((bf16[8,128,256]{2,1,0:T(8,128)(2,1)}, bf16[8,128,256]{2,1,0:T(8,128)(2,1)}, u32[]{:S(2)}, u32[]{:S(2)}) %collective-permute-start.32) | collective-permute-done | bytes 524320 | tf_op jit(solution)/shard_map/ppermute | solution.py:26
  171.3 10.9 %project_out.1 = (f32[640,1024]{1,0:T(8,128)}, bf16[2,640,1024]{2,1,0:T(8,128)(2,1)}) custom-call(s32[3]{0:T(128)} %pad_add_fusion.place_ref, bf16[2,640,512]{2,1,0:T(8,128)(2,1)} %get-tuple-element.84.mine_ref, bf16[2,640,512]{2,1,0:T(8,128)(2,1)} %collective-permute-done.11.theirs_ref, bf16[8,128,512]{2,1,0:T(8,128)(2,1)} %bitcast_dynamic-update-slice_fusion.wm_ref, ...), custom_call_target="tpu_custom_call" | custom-call | tf_op jit(solution)/shard_map/project_out/pallas_call | solution.py:119
  183.4 36.2 %feed_forward.2 = (f32[640,1024]{1,0:T(8,128)}, f32[640,1024]{1,0:T(8,128)}, f32[640,1024]{1,0:T(8,128)}, f32[640,1024]{1,0:T(8,128)}, f32[4,1,256]{2,1,0:T(1,12...) custom-call(s32[3]{0:T(128)} %pad_add_fusion.place_ref, ...), custom_call_target="tpu_custom_call" | custom-call | tf_op jit(solution)/shard_map/feed_forward/pallas_call | solution.py:119
  224.2 55.4 %collective-permute-done.21.refs_1_ = bf16[8,128,256]{2,1,0:T(8,128)(2,1)S(1)} collective-permute-done((bf16[8,128,256]{2,1,0:T(8,128)(2,1)S(1)}, bf16[8,128,256]{2,1,0:T(8,128)(2,1)S(1)}, u32[]{:S(2)}, u32[]{:S(2)}) %collective-permute-start.21) | collective-permute-done | bytes 524320 | tf_op jit(solution)/shard_map/ppermute | solution.py:26
  279.7 11.2 %collective-permute-done.23.refs_3_ = bf16[8,128,256]{2,1,0:T(8,128)(2,1)S(1)} collective-permute-done((bf16[8,128,256]{2,1,0:T(8,128)(2,1)S(1)}, bf16[8,128,256]{2,1,0:T(8,128)(2,1)S(1)}, u32[]{:S(2)}, u32[]{:S(2)}) %collective-permute-start.23) | collective-permute-done | bytes 524320 | tf_op jit(solution)/shard_map/ppermute | solution.py:26
  290.9 11.2 %collective-permute-done.25.refs_5_ = bf16[8,128,256]{2,1,0:T(8,128)(2,1)S(1)} collective-permute-done((bf16[8,128,256]{2,1,0:T(8,128)(2,1)}, bf16[8,128,256]{2,1,0:T(8,128)(2,1)S(1)}, u32[]{:S(2)}, u32[]{:S(2)}) %collective-permute-start.25) | collective-permute-done | bytes 524320 | tf_op jit(solution)/shard_map/ppermute | solution.py:26
  302.1 8.9 %collective-permute-done.27.refs_7_ = bf16[8,128,256]{2,1,0:T(8,128)(2,1)S(1)} collective-permute-done((bf16[8,128,256]{2,1,0:T(8,128)(2,1)}, bf16[8,128,256]{2,1,0:T(8,128)(2,1)S(1)}, u32[]{:S(2)}, u32[]{:S(2)}) %collective-permute-start.27) | collective-permute-done | bytes 524320 | tf_op jit(solution)/shard_map/ppermute | solution.py:26
  311.8 40.4 %feed_forward.3 = (f32[640,1024]{1,0:T(8,128)}, f32[640,1024]{1,0:T(8,128)}, f32[640,1024]{1,0:T(8,128)}, f32[640,1024]{1,0:T(8,128)}, f32[4,1,256]{2,1,0:T(1,12...) custom-call(s32[3]{0:T(128)} %pad_add_fusion.place_ref, ...), custom_call_target="tpu_custom_call" | custom-call | tf_op jit(solution)/shard_map/feed_forward/pallas_call | solution.py:119
  366.3 31.6 %collective-permute-done.67 = bf16[4,8,128,256]{3,2,1,0:T(8,128)(2,1)} collective-permute-done((bf16[4,8,128,256]{3,2,1,0:T(8,128)(2,1)}, bf16[4,8,128,256]{3,2,1,0:T(8,128)(2,1)}, u32[]{:S(2)}, u32[]{:S(2)}) %collective-permute-start.67) | collective-permute-done | bytes 2097184 | tf_op jit(solution)/shard_map/ppermute | solution.py:26
  399.4 4.5 fusion.47
  406.1 17.8 %collective-permute-done.64 = bf16[8,128,256]{2,1,0:T(8,128)(2,1)S(1)} collective-permute-done((bf16[8,128,256]{2,1,0:T(8,128)(2,1)S(1)}, bf16[8,128,256]{2,1,0:T(8,128)(2,1)S(1)}, u32[]{:S(2)}, u32[]{:S(2)}) %collective-permute-start.64) | collective-permute-done | bytes 524320 | tf_op jit(solution)/shard_map/ppermute | solution.py:31
  425.8 8.9 %norm_back.2 = (f32[640,1024]{1,0:T(8,128)}, bf16[640,1024]{1,0:T(8,128)(2,1)}, f32[3,1024]{1,0:T(4,128)}) custom-call(s32[3]{0:T(128)} %pad_add_fusion.place_ref, f32[640,1024]{1,0:T(8,128)} %get-tuple-element.85.rows_ref, f32[1,1024]{1,0:T(1,128)} %bitcast.292, f32[640,1024]{1,0:T(8,128)} %get-tuple-element.94.own_ref, ...), custom_call_target="tpu_custom_call" | custom-call | tf_op jit(solution)/shard_map/norm_back/pallas_call | solution.py:119
  435.7 11.7 %collective-permute-done.69 = bf16[8,128,256]{2,1,0:T(8,128)(2,1)} collective-permute-done((bf16[8,128,256]{2,1,0:T(8,128)(2,1)S(1)}, bf16[8,128,256]{2,1,0:T(8,128)(2,1)}, u32[]{:S(2)}, u32[]{:S(2)}) %collective-permute-start.69) | collective-permute-done | bytes 524320 | tf_op jit(solution)/shard_map/ppermute | solution.py:31
  447.4 10.2 %collective-permute-done.70 = bf16[8,128,256]{2,1,0:T(8,128)(2,1)} collective-permute-done((bf16[8,128,256]{2,1,0:T(8,128)(2,1)S(1)}, bf16[8,128,256]{2,1,0:T(8,128)(2,1)}, u32[]{:S(2)}, u32[]{:S(2)}) %collective-permute-start.70) | collective-permute-done | bytes 524320 | tf_op jit(solution)/shard_map/ppermute | solution.py:31
  470.4 4.5 collective-permute-done.59
  480.7 4.3 fusion.1
  488.0 10.8 %out_back.1 = (bf16[2,640,512]{2,1,0:T(8,128)(2,1)}, bf16[4,128,512]{2,1,0:T(8,128)(2,1)}, bf16[4,128,512]{2,1,0:T(8,128)(2,1)}) custom-call(s32[3]{0:T(128)} %pad_add_fusion.place_ref, bf16[640,1024]{1,0:T(8,128)(2,1)} %get-tuple-element.96.own_ref.own_half, bf16[640,1024]{1,0:T(8,128)(2,1)} %copy-done.16, ...), custom_call_target="tpu_custom_call" | custom-call | tf_op jit(solution)/shard_map/out_back/pallas_call | solution.py:119
  500.4 32.4 %attention_back.1 = (bf16[2,640,512]{2,1,0:T(8,128)(2,1)}, bf16[2,640,512]{2,1,0:T(8,128)(2,1)}, bf16[2,640,512]{2,1,0:T(8,128)(2,1)}) custom-call(s32[3]{0:T(128)} %pad_add_fusion.place_ref, bf16[2,640,512]{2,1,0:T(8,128)(2,1)} %get-tuple-element.81.q_ref, bf16[2,640,512]{2,1,0:T(8,128)(2,1)} %get-tuple-element.82.k_ref, ...), custom_call_target="tpu_custom_call" | custom-call | tf_op jit(solution)/shard_map/attention_back/pallas_call | solution.py:119
  532.7 11.1 %qkv_term.1 = (f32[3,512]{1,0:T(4,128)}, bf16[4,128,1536]{2,1,0:T(8,128)(2,1)}, bf16[4,128,1536]{2,1,0:T(8,128)(2,1)}) custom-call(s32[3]{0:T(128)} %pad_add_fusion.place_ref, bf16[2,640,1024]{2,1,0:T(8,128)(2,1)} %get-tuple-element.106.normed_ref, bf16[2,640,512]{2,1,0:T(8,128)(2,1)} %get-tuple-element.98.gq_ref, ...), custom_call_target="tpu_custom_call" | custom-call | tf_op jit(solution)/shard_map/qkv_term/pallas_call | solution.py:119
  545.2 10.5 %qkv_back.1 = (f32[640,1024]{1,0:T(8,128)}, f32[640,1024]{1,0:T(8,128)}) custom-call(s32[3]{0:T(128)} %pad_add_fusion.place_ref, bf16[2,640,512]{2,1,0:T(8,128)(2,1)} %get-tuple-element.98.gq_ref, bf16[2,640,512]{2,1,0:T(8,128)(2,1)} %get-tuple-element.99.gk_ref, bf16[2,640,512]{2,1,0:T(8,128)(2,1)} %get-tuple-element.100.gv_ref, ...), custom_call_target="tpu_custom_call" | custom-call | tf_op jit(solution)/shard_map/qkv_back/pallas_call | solution.py:119
  568.3 12.0 %collective-permute-done.82 = f32[2050]{0:T(1024)S(1)} collective-permute-done((f32[2050]{0:T(1024)S(1)}, f32[2050]{0:T(1024)S(1)}, u32[]{:S(2)}, u32[]{:S(2)}) %collective-permute-start.82) | collective-permute-done | bytes 8232 | tf_op jit(solution)/shard_map/ppermute | solution.py:36
  626.3 4.1 fusion.45
  639.9 7.9 %norm_back.3 = (bf16[640,1024]{1,0:T(8,128)(2,1)}, f32[2,1024]{1,0:T(2,128)}) custom-call(s32[3]{0:T(128)} %pad_add_fusion.place_ref, bf16[640,1024]{1,0:T(8,128)(2,1)} %copy-done.1, f32[1,1024]{1,0:T(1,128)} %bitcast.298, f32[640,1024]{1,0:T(8,128)} %get-tuple-element.101.own_ref, f32[640,1024]{1,0:T(8,128)} %collective-permute-done.38.other_ref, ...), custom_call_target="tpu_custom_call" | custom-call | tf_op jit(solution)/shard_map/norm_back/pallas_call | solution.py:119
  648.8 10.9 %collective-permute-done.46 = bf16[128,1536]{1,0:T(8,128)(2,1)S(1)} collective-permute-done((bf16[128,1536]{1,0:T(8,128)(2,1)}, bf16[128,1536]{1,0:T(8,128)(2,1)S(1)}, u32[]{:S(2)}, u32[]{:S(2)}) %collective-permute-start.46) | collective-permute-done | bytes 393248 | tf_op jit(solution)/shard_map/ppermute | solution.py:31
  668.4 7.1 collective-permute-start.41
  686.9 10.3 %stack.246 = f32[16]{0:T(128)S(1)} concatenate(f32[1]{0:T(128)} %bitcast.105, f32[1]{0:T(128)} %bitcast.106, f32[1]{0:T(128)} %bitcast.107, f32[1]{0:T(128)} %bitcast.108, f32[1]{0:T(128)} %bitcast.109, f32[1]{0:T(128)} %bitcast.110, f32[1]{0:T(128)} %bitcast.111, f32[1]{0:T(128)} %bitcast.112, f32[1]{0:T(128)} %bitcast.113, f32[1]{0:T(128)} %bitcast.114, f32[1]{0:T(128)} %bitcast.115, ...), dimensions={0} | concatenate | bytes 128 | tf_op jit(solution)/shard_map/stack | solution.py:994
  (549 shorter events, 248.3 us)
Async XLA Ops:
  2.7 36.1 %collective-permute-start.12 = (bf16[128,512]{1,0:T(8,128)(2,1)}, bf16[128,512]{1,0:T(8,128)(2,1)}, u32[]{:S(2)}, u32[]{:S(2)}) collective-permute-start(bf16[128,512]{1,0:T(8,128)(2,1)} %bitcast.260), channel_id=1, source_target_pairs={{0,4},{4,0},{1,5},{5,1},{2,6},{6,2},{3,7},{7,3},{8,12},{12,8},{9,1... | collective-permute-start | bytes 393224 | tf_op jit(solution)/shard_map/ppermute | solution.py:26
  5.7 33.9 %collective-permute-start.13 = (bf16[128,512]{1,0:T(8,128)(2,1)}, bf16[128,512]{1,0:T(8,128)(2,1)}, u32[]{:S(2)}, u32[]{:S(2)}) collective-permute-start(bf16[128,512]{1,0:T(8,128)(2,1)} %bitcast.260), channel_id=1, source_target_pairs={{0,8},{8,16},{16,24},{24,0},{1,9},{9,17},{17,25},{25,1},{2,10},{10... | collective-permute-start | bytes 393224 | tf_op jit(solution)/shard_map/ppermute | solution.py:31
  7.2 35.4 %collective-permute-start.15 = (bf16[128,512]{1,0:T(8,128)(2,1)}, bf16[128,512]{1,0:T(8,128)(2,1)}, u32[]{:S(2)}, u32[]{:S(2)}) collective-permute-start(bf16[128,512]{1,0:T(8,128)(2,1)} %bitcast.260), channel_id=1, source_target_pairs={{0,16},{8,24},{16,0},{24,8},{1,17},{9,25},{17,1},{25,9},{2,18},{10... | collective-permute-start | bytes 393224 | tf_op jit(solution)/shard_map/ppermute | solution.py:31
  9.8 34.1 %collective-permute-start.17 = (bf16[128,512]{1,0:T(8,128)(2,1)}, bf16[128,512]{1,0:T(8,128)(2,1)}, u32[]{:S(2)}, u32[]{:S(2)}) collective-permute-start(bf16[128,512]{1,0:T(8,128)(2,1)} %bitcast.260), channel_id=1, source_target_pairs={{0,24},{8,0},{16,8},{24,16},{1,25},{9,1},{17,9},{25,17},{2,26},{10... | collective-permute-start | bytes 393224 | tf_op jit(solution)/shard_map/ppermute | solution.py:31
  36.8 51.2 %collective-permute-start = (bf16[640,1024]{1,0:T(8,128)(2,1)S(1)}, bf16[640,1024]{1,0:T(8,128)(2,1)S(1)}, u32[]{:S(2)}, u32[]{:S(2)}) collective-permute-start(bf16[640,1024]{1,0:T(8,128)(2,1)S(1)} %pad.7.own_ref.rows_ref), channel_id=1, source_target_pairs={{0,1},{1,0},{2,3},{3,2},{4,5},{5,4},{6,7},{7,6},{8,9},{9,8},{10,11... | collective-permute-start | bytes 3932168 | tf_op jit(solution)/shard_map/ppermute | solution.py:26
  78.8 51.0 %collective-permute-start.29 = (bf16[8,128,256]{2,1,0:T(8,128)(2,1)S(1)}, bf16[8,128,256]{2,1,0:T(8,128)(2,1)}, u32[]{:S(2)}, u32[]{:S(2)}) collective-permute-start(bf16[8,128,256]{2,1,0:T(8,128)(2,1)S(1)} %copy-done.26), channel_id=1, source_target_pairs={{0,8},{8,16},{16,24},{24,0},{1,9},{9,17},{17,25},{25,1},{2,10},{10... | collective-permute-start | bytes 1572872 | tf_op jit(solution)/shard_map/ppermute | solution.py:31
  79.6 50.5 %collective-permute-start.31 = (bf16[8,128,256]{2,1,0:T(8,128)(2,1)S(1)}, bf16[8,128,256]{2,1,0:T(8,128)(2,1)}, u32[]{:S(2)}, u32[]{:S(2)}) collective-permute-start(bf16[8,128,256]{2,1,0:T(8,128)(2,1)S(1)} %copy-done.26), channel_id=1, source_target_pairs={{0,16},{8,24},{16,0},{24,8},{1,17},{9,25},{17,1},{25,9},{2,18},{10... | collective-permute-start | bytes 1572872 | tf_op jit(solution)/shard_map/ppermute | solution.py:31
  82.5 48.0 %collective-permute-start.33 = (bf16[8,128,256]{2,1,0:T(8,128)(2,1)S(1)}, bf16[8,128,256]{2,1,0:T(8,128)(2,1)}, u32[]{:S(2)}, u32[]{:S(2)}) collective-permute-start(bf16[8,128,256]{2,1,0:T(8,128)(2,1)S(1)} %copy-done.26), channel_id=1, source_target_pairs={{0,24},{8,0},{16,8},{24,16},{1,25},{9,1},{17,9},{25,17},{2,26},{10... | collective-permute-start | bytes 1572872 | tf_op jit(solution)/shard_map/ppermute | solution.py:31
  86.5 42.1 %collective-permute-start.18 = (bf16[128,512]{1,0:T(8,128)(2,1)}, bf16[128,512]{1,0:T(8,128)(2,1)S(1)}, u32[]{:S(2)}, u32[]{:S(2)}) collective-permute-start(bf16[128,512]{1,0:T(8,128)(2,1)} %collective-permute-done.17), channel_id=1, source_target_pairs={{0,4},{4,0},{1,5},{5,1},{2,6},{6,2},{3,7},{7,3},{8,12},{12,8},{9,1... | collective-permute-start | bytes 393224 | tf_op jit(solution)/shard_map/ppermute | solution.py:26
  127.0 42.2 %collective-permute-start.11 = (bf16[2,640,512]{2,1,0:T(8,128)(2,1)}, bf16[2,640,512]{2,1,0:T(8,128)(2,1)}, u32[]{:S(2)}, u32[]{:S(2)}) collective-permute-start(bf16[2,640,512]{2,1,0:T(8,128)(2,1)} %get-tuple-element.84.mine_ref), channel_id=1, source_target_pairs={{0,1},{1,0},{2,3},{3,2},{4,5},{5,4},{6,7},{7,6},{8,9},{9,8},{10,11... | collective-permute-start | bytes 3932168 | tf_op jit(solution)/shard_map/ppermute | solution.py:26
  129.8 38.3 %collective-permute-start.19 = (bf16[8,128,512]{2,1,0:T(8,128)(2,1)}, bf16[8,128,512]{2,1,0:T(8,128)(2,1)}, u32[]{:S(2)}, u32[]{:S(2)}) collective-permute-start(bf16[8,128,512]{2,1,0:T(8,128)(2,1)} %bitcast_dynamic-update-slice_fusion.wm_ref), channel_id=1, source_target_pairs={{0,1},{1,0},{2,3},{3,2},{4,5},{5,4},{6,7},{7,6},{8,9},{9,8},{10,11... | collective-permute-start | bytes 3145736 | tf_op jit(solution)/shard_map/ppermute | solution.py:26
  130.2 52.1 %collective-permute-start.20 = (bf16[640,1024]{1,0:T(8,128)(2,1)S(1)}, bf16[640,1024]{1,0:T(8,128)(2,1)S(1)}, u32[]{:S(2)}, u32[]{:S(2)}) collective-permute-start(bf16[640,1024]{1,0:T(8,128)(2,1)S(1)} %pad.8.own_cot.pass_ref), channel_id=1, source_target_pairs={{0,1},{1,0},{2,3},{3,2},{4,5},{5,4},{6,7},{7,6},{8,9},{9,8},{10,11... | collective-permute-start | bytes 3932168 | tf_op jit(solution)/shard_map/ppermute | solution.py:26
  165.9 55.7 %collective-permute-start.22 = (bf16[8,128,256]{2,1,0:T(8,128)(2,1)S(1)}, bf16[8,128,256]{2,1,0:T(8,128)(2,1)S(1)}, u32[]{:S(2)}, u32[]{:S(2)}) collective-permute-start(bf16[8,128,256]{2,1,0:T(8,128)(2,1)S(1)} %pad_maximum_fusion.2.refs_0_), channel_id=1, source_target_pairs={{0,8},{8,16},{16,24},{24,0},{1,9},{9,17},{17,25},{25,1},{2,10},{10... | collective-permute-start | bytes 1572872 | tf_op jit(solution)/shard_map/ppermute | solution.py:31
  168.1 54.1 %collective-permute-start.24 = (bf16[8,128,256]{2,1,0:T(8,128)(2,1)S(1)}, bf16[8,128,256]{2,1,0:T(8,128)(2,1)}, u32[]{:S(2)}, u32[]{:S(2)}) collective-permute-start(bf16[8,128,256]{2,1,0:T(8,128)(2,1)S(1)} %pad_maximum_fusion.2.refs_0_), channel_id=1, source_target_pairs={{0,16},{8,24},{16,0},{24,8},{1,17},{9,25},{17,1},{25,9},{2,18},{10... | collective-permute-start | bytes 1572872 | tf_op jit(solution)/shard_map/ppermute | solution.py:31
  169.2 54.5 %collective-permute-start.26 = (bf16[8,128,256]{2,1,0:T(8,128)(2,1)S(1)}, bf16[8,128,256]{2,1,0:T(8,128)(2,1)}, u32[]{:S(2)}, u32[]{:S(2)}) collective-permute-start(bf16[8,128,256]{2,1,0:T(8,128)(2,1)S(1)} %pad_maximum_fusion.2.refs_0_), channel_id=1, source_target_pairs={{0,24},{8,0},{16,8},{24,16},{1,25},{9,1},{17,9},{25,17},{2,26},{10... | collective-permute-start | bytes 1572872 | tf_op jit(solution)/shard_map/ppermute | solution.py:31
  219.6 141.7 %collective-permute-start.61 = (bf16[4,8,128,256]{3,2,1,0:T(8,128)(2,1)}, bf16[4,8,128,256]{3,2,1,0:T(8,128)(2,1)}, u32[]{:S(2)}, u32[]{:S(2)}) collective-permute-start(bf16[4,8,128,256]{3,2,1,0:T(8,128)(2,1)} %get-tuple-element.116), channel_id=1, source_target_pairs={{0,4},{4,0},{1,5},{5,1},{2,6},{6,2},{3,7},{7,3},{8,12},{12,8},{9,1... | collective-permute-start | bytes 6291464 | tf_op jit(solution)/shard_map/ppermute | solution.py:26
  220.2 59.5 %collective-permute-start.21 = (bf16[8,128,256]{2,1,0:T(8,128)(2,1)S(1)}, bf16[8,128,256]{2,1,0:T(8,128)(2,1)S(1)}, u32[]{:S(2)}, u32[]{:S(2)}) collective-permute-start(bf16[8,128,256]{2,1,0:T(8,128)(2,1)S(1)} %pad_maximum_fusion.2.refs_0_), channel_id=1, source_target_pairs={{0,4},{4,0},{1,5},{5,1},{2,6},{6,2},{3,7},{7,3},{8,12},{12,8},{9,1... | collective-permute-start | bytes 1572872 | tf_op jit(solution)/shard_map/ppermute | solution.py:26
  221.7 69.2 %collective-permute-start.23 = (bf16[8,128,256]{2,1,0:T(8,128)(2,1)S(1)}, bf16[8,128,256]{2,1,0:T(8,128)(2,1)S(1)}, u32[]{:S(2)}, u32[]{:S(2)}) collective-permute-start(bf16[8,128,256]{2,1,0:T(8,128)(2,1)S(1)} %collective-permute-done.22.refs_2_), channel_id=1, source_target_pairs={{0,4},{4,0},{1,5},{5,1},{2,6},{6,2},{3,7},{7,3},{8,12},{12,8},{9,1... | collective-permute-start | bytes 1572872 | tf_op jit(solution)/shard_map/ppermute | solution.py:26
  222.2 79.9 %collective-permute-start.25 = (bf16[8,128,256]{2,1,0:T(8,128)(2,1)}, bf16[8,128,256]{2,1,0:T(8,128)(2,1)S(1)}, u32[]{:S(2)}, u32[]{:S(2)}) collective-permute-start(bf16[8,128,256]{2,1,0:T(8,128)(2,1)} %collective-permute-done.24.refs_4_), channel_id=1, source_target_pairs={{0,4},{4,0},{1,5},{5,1},{2,6},{6,2},{3,7},{7,3},{8,12},{12,8},{9,1... | collective-permute-start | bytes 1572872 | tf_op jit(solution)/shard_map/ppermute | solution.py:26
  223.7 87.3 %collective-permute-start.27 = (bf16[8,128,256]{2,1,0:T(8,128)(2,1)}, bf16[8,128,256]{2,1,0:T(8,128)(2,1)S(1)}, u32[]{:S(2)}, u32[]{:S(2)}) collective-permute-start(bf16[8,128,256]{2,1,0:T(8,128)(2,1)} %collective-permute-done.26.refs_6_), channel_id=1, source_target_pairs={{0,4},{4,0},{1,5},{5,1},{2,6},{6,2},{3,7},{7,3},{8,12},{12,8},{9,1... | collective-permute-start | bytes 1572872 | tf_op jit(solution)/shard_map/ppermute | solution.py:26
  352.3 45.7 %collective-permute-start.67 = (bf16[4,8,128,256]{3,2,1,0:T(8,128)(2,1)}, bf16[4,8,128,256]{3,2,1,0:T(8,128)(2,1)}, u32[]{:S(2)}, u32[]{:S(2)}) collective-permute-start(bf16[4,8,128,256]{3,2,1,0:T(8,128)(2,1)} %get-tuple-element.118), channel_id=1, source_target_pairs={{0,4},{4,0},{1,5},{5,1},{2,6},{6,2},{3,7},{7,3},{8,12},{12,8},{9,1... | collective-permute-start | bytes 6291464 | tf_op jit(solution)/shard_map/ppermute | solution.py:26
  357.4 66.9 %collective-permute-start.36 = (f32[640,1024]{1,0:T(8,128)}, f32[640,1024]{1,0:T(8,128)}, u32[]{:S(2)}, u32[]{:S(2)}) collective-permute-start(f32[640,1024]{1,0:T(8,128)} %get-tuple-element.95), channel_id=1, source_target_pairs={{0,1},{1,0},{2,3},{3,2},{4,5},{5,4},{6,7},{7,6},{8,9},{9,8},{10,11... | collective-permute-start | bytes 7864328 | tf_op jit(solution)/shard_map/ppermute | solution.py:26
  360.8 119.9 %collective-permute-start.35 = (f32[640,1024]{1,0:T(8,128)}, f32[640,1024]{1,0:T(8,128)}, u32[]{:S(2)}, u32[]{:S(2)}) collective-permute-start(f32[640,1024]{1,0:T(8,128)} %get-tuple-element.92), channel_id=1, source_target_pairs={{0,1},{1,0},{2,3},{3,2},{4,5},{5,4},{6,7},{7,6},{8,9},{9,8},{10,11... | collective-permute-start | bytes 7864328 | tf_op jit(solution)/shard_map/ppermute | solution.py:26
  364.0 40.9 %collective-permute-start.62 = (bf16[8,128,256]{2,1,0:T(8,128)(2,1)S(1)}, bf16[8,128,256]{2,1,0:T(8,128)(2,1)S(1)}, u32[]{:S(2)}, u32[]{:S(2)}) collective-permute-start(bf16[8,128,256]{2,1,0:T(8,128)(2,1)S(1)} %get-tuple-element.311), channel_id=1, source_target_pairs={{0,8},{8,16},{16,24},{24,0},{1,9},{9,17},{17,25},{25,1},{2,10},{10... | collective-permute-start | bytes 1572872 | tf_op jit(solution)/shard_map/ppermute | solution.py:31
  364.5 40.9 %collective-permute-start.63 = (bf16[8,128,256]{2,1,0:T(8,128)(2,1)S(1)}, bf16[8,128,256]{2,1,0:T(8,128)(2,1)S(1)}, u32[]{:S(2)}, u32[]{:S(2)}) collective-permute-start(bf16[8,128,256]{2,1,0:T(8,128)(2,1)S(1)} %get-tuple-element.313), channel_id=1, source_target_pairs={{0,16},{8,24},{16,0},{24,8},{1,17},{9,25},{17,1},{25,9},{2,18},{10... | collective-permute-start | bytes 1572872 | tf_op jit(solution)/shard_map/ppermute | solution.py:31
  405.4 42.0 %collective-permute-start.69 = (bf16[8,128,256]{2,1,0:T(8,128)(2,1)S(1)}, bf16[8,128,256]{2,1,0:T(8,128)(2,1)}, u32[]{:S(2)}, u32[]{:S(2)}) collective-permute-start(bf16[8,128,256]{2,1,0:T(8,128)(2,1)S(1)} %get-tuple-element.308), channel_id=1, source_target_pairs={{0,16},{8,24},{16,0},{24,8},{1,17},{9,25},{17,1},{25,9},{2,18},{10... | collective-permute-start | bytes 1572872 | tf_op jit(solution)/shard_map/ppermute | solution.py:31
  423.9 33.8 %collective-permute-start.70 = (bf16[8,128,256]{2,1,0:T(8,128)(2,1)S(1)}, bf16[8,128,256]{2,1,0:T(8,128)(2,1)}, u32[]{:S(2)}, u32[]{:S(2)}) collective-permute-start(bf16[8,128,256]{2,1,0:T(8,128)(2,1)S(1)} %get-tuple-element.307), channel_id=1, source_target_pairs={{0,24},{8,0},{16,8},{24,16},{1,25},{9,1},{17,9},{25,17},{2,26},{10... | collective-permute-start | bytes 1572872 | tf_op jit(solution)/shard_map/ppermute | solution.py:31
  424.2 51.2 %collective-permute-start.65 = (bf16[8,128,256]{2,1,0:T(8,128)(2,1)S(1)}, bf16[8,128,256]{2,1,0:T(8,128)(2,1)}, u32[]{:S(2)}, u32[]{:S(2)}) collective-permute-start(bf16[8,128,256]{2,1,0:T(8,128)(2,1)S(1)} %fusion.11), channel_id=1, source_target_pairs={{0,2},{2,0},{1,3},{3,1},{4,6},{6,4},{5,7},{7,5},{8,10},{10,8},{9,1... | collective-permute-start | bytes 1572872 | tf_op jit(solution)/shard_map/ppermute | solution.py:26
  477.8 77.9 %collective-permute-start.66 = (f32[8,128,256]{2,1,0:T(8,128)}, f32[8,128,256]{2,1,0:T(8,128)}, u32[]{:S(2)}, u32[]{:S(2)}) collective-permute-start(f32[8,128,256]{2,1,0:T(8,128)} %add_multiply_fusion.1), channel_id=1, source_target_pairs={{0,1},{1,0},{2,3},{3,2},{4,5},{5,4},{6,7},{7,6},{8,9},{9,8},{10,11... | collective-permute-start | bytes 3145736 | tf_op jit(solution)/shard_map/ppermute | solution.py:26
  480.1 75.6 %collective-permute-start.72 = (f32[8,128,256]{2,1,0:T(8,128)}, f32[8,128,256]{2,1,0:T(8,128)}, u32[]{:S(2)}, u32[]{:S(2)}) collective-permute-start(f32[8,128,256]{2,1,0:T(8,128)} %add_multiply_fusion), channel_id=1, source_target_pairs={{0,1},{1,0},{2,3},{3,2},{4,5},{5,4},{6,7},{7,6},{8,9},{9,8},{10,11... | collective-permute-start | bytes 3145736 | tf_op jit(solution)/shard_map/ppermute | solution.py:26
  498.8 85.3 %collective-permute-start.50 = (bf16[4,128,512]{2,1,0:T(8,128)(2,1)}, bf16[4,128,512]{2,1,0:T(8,128)(2,1)S(1)}, u32[]{:S(2)}, u32[]{:S(2)}) collective-permute-start(bf16[4,128,512]{2,1,0:T(8,128)(2,1)} %get-tuple-element.111), channel_id=1, source_target_pairs={{0,4},{4,0},{1,5},{5,1},{2,6},{6,2},{3,7},{7,3},{8,12},{12,8},{9,1... | collective-permute-start | bytes 1572872 | tf_op jit(solution)/shard_map/ppermute | solution.py:26
  543.8 82.5 %collective-permute-start.44 = (bf16[4,128,1536]{2,1,0:T(8,128)(2,1)}, bf16[4,128,1536]{2,1,0:T(8,128)(2,1)}, u32[]{:S(2)}, u32[]{:S(2)}) collective-permute-start(bf16[4,128,1536]{2,1,0:T(8,128)(2,1)} %get-tuple-element.109), channel_id=1, source_target_pairs={{0,4},{4,0},{1,5},{5,1},{2,6},{6,2},{3,7},{7,3},{8,12},{12,8},{9,1... | collective-permute-start | bytes 4718600 | tf_op jit(solution)/shard_map/ppermute | solution.py:26
  (161 other events, 4763.8 us)

commit v3 on v2

v3 whole, which is shorter than its diff:
```python
import math

import jax
import jax.numpy as jnp
from jax import lax
from jax.experimental import pallas as pl
from jax.experimental.pallas import tpu as pltpu
from jax.sharding import Mesh
from jax.sharding import PartitionSpec as P

HEAD_DIM = 64
SEQ = 577
LANES = 128
TILE = 16
SPAN = 256
CHUNKS = 2
VMEM_LIMIT = 60 * 1024 * 1024

ALL_AXES = ("z", "x", "y", "c")

MATRICES = (2, 4, 8, 10)
VECTORS = (0, 1, 3, 5, 6, 7, 9, 11)

ln_eps = 1e-06
clip_level = 0.05
step_rate = 4.0


def swap(value, axis):
    return lax.ppermute(value, axis, [(0, 1), (1, 0)])


def shift(value, axis, step):
    size = lax.axis_size(axis)
    return lax.ppermute(value, axis, [(i, (i + step) % size) for i in range(size)])


def partner(value, axis, step):
    size = lax.axis_size(axis)
    return lax.ppermute(value, axis, [(i, i ^ step) for i in range(size)])


def swap_both(value):
    return lax.ppermute(value, ("y", "c"), [(i, 3 - i) for i in range(4)])


def sum_over(value, axes):
    for axis in axes:
        step = 1
        while step < lax.axis_size(axis):
            value = value + partner(value, axis, step)
            step *= 2
    return value


def gather_pieces(shard):
    along = [shard] + [shift(shard, "z", k) for k in range(1, lax.axis_size("z"))]
    pieces = []
    for near in along:
        pieces += [near, swap(near, "x")]
    return pieces


def scatter_sum(place, keep, send):
    size = lax.axis_size("z")
    held, *parts = fold_x(place, keep, swap(send, "x"))
    mine = fold_z(place, held, [shift(parts[k - 1], "z", k) for k in range(1, size)])
    if lax.axis_size("y") == 2:
        mine = low(mine)
        return [mine, swap(mine, "y")], [swap(mine, "c"), swap_both(mine)]
    total = lax.psum(mine, "y")
    return [total], [swap(total, "c")]


def row_pad(length):
    return -(-length // LANES) * LANES


def dot(left, right):
    return jnp.dot(left, right, preferred_element_type=jnp.float32)


def dot_tail(left, right):
    return lax.dot_general(
        left, right, (((1,), (1,)), ((), ())), preferred_element_type=jnp.float32
    )


def low(value):
    return value.astype(jnp.bfloat16)


def wide(value):
    return value.astype(jnp.float32)


def any_spec():
    return pl.BlockSpec(memory_space=pl.ANY)


def whole(shape):
    return pl.BlockSpec(shape, lambda *_: (0,) * len(shape))


def sds(shape, dtype):
    return jax.ShapeDtypeStruct(shape, dtype)


def call(body, place, ins, in_specs, outs, out_specs, scratch, name, grid=(1,), flops=0):
    moved = sum(math.prod(a.shape) * a.dtype.itemsize for a in [*ins, *outs])
    return pl.pallas_call(
        body,
        out_shape=outs,
        grid_spec=pltpu.PrefetchScalarGridSpec(
            num_scalar_prefetch=1,
            grid=grid,
            in_specs=in_specs,
            out_specs=out_specs,
            scratch_shapes=scratch,
        ),
        compiler_params=pltpu.CompilerParams(
            vmem_limit_bytes=VMEM_LIMIT, dimension_semantics=("arbitrary",) * len(grid)
        ),
        cost_estimate=pl.CostEstimate(flops=flops, bytes_accessed=moved, transcendentals=0),
        name=name,
    )(place, *ins)


def shard_of(place_ref, number, z_size):
    k, dx = number // 2, number % 2
    z = lax.rem(place_ref[0] + (z_size - k), z_size)
    x = dx + (1 - 2 * dx) * place_ref[1]
    return z, x


def normalised(rows):
    centre = rows - jnp.mean(rows, axis=-1, keepdims=True)
    spread = jnp.mean(centre * centre, axis=-1, keepdims=True)
    return centre * lax.rsqrt(spread + ln_eps)


def select(core, first, second):
    return jnp.where(core == 0, first, second)


def prepare_qkv(place, weight, vectors):
    part, cols = weight.shape
    half = cols // 6
    sizes = [vector.shape[-1] for vector in vectors]

    def body(place_ref, weight_ref, *refs):
        out_ref = refs[-1]
        core = place_ref[2]
        for slot in range(3):
            at = 2 * slot * half
            out_ref[:part, slot * half : (slot + 1) * half] = low(
                select(core, weight_ref[:, at : at + half], weight_ref[:, at + half : at + 2 * half])
            )
        at = 0
        for ref, size in zip(refs, sizes):
            out_ref[part:, at : at + size] = low(jnp.broadcast_to(ref[...], (TILE, size)))
            at += size

    shape = (part + TILE, cols // 2)
    return call(
        body,
        place,
        (weight, *vectors),
        [whole((part, cols))] + [whole((1, size)) for size in sizes],
        [sds(shape, jnp.bfloat16)],
        [whole(shape)],
        [],
        "prepare_qkv",
    )[0]


def prepare_rest(place, in_weight, down_weight, out_weight, inputs, cotangent):
    part, hidden = in_weight.shape
    width = down_weight.shape[1]
    per_core = down_weight.shape[0] // 2
    per_shard = per_core // CHUNKS
    shards = hidden // (2 * per_core)
    block = per_shard * 2
    blocks = shards // 2
    tokens = inputs.shape[0]
    length = row_pad(tokens)
    even = tokens // TILE * TILE

    def body(place_ref, in_ref, down_ref, out_w_ref, rows_ref, cot_ref, *refs):
        pieces, (rows_out, cot_out, sum_ref) = refs[:CHUNKS], refs[CHUNKS:]
        core = place_ref[2]
        for j in range(CHUNKS):
            for s in range(shards):
                at = s * 2 * per_core + j * per_shard
                pieces[j][s // 2, :, (s % 2) * per_shard : (s % 2 + 1) * per_shard] = low(
                    select(
                        core,
                        in_ref[:, at : at + per_shard],
                        in_ref[:, at + per_core : at + per_core + per_shard],
                    )
                )
            at = j * per_shard
            for b in range(width // block):
                cols = slice(b * block, (b + 1) * block)
                pieces[j][blocks + b] = low(
                    select(
                        core,
                        down_ref[at : at + per_shard, cols],
                        down_ref[at + per_core : at + per_core + per_shard, cols],
                    )
                )
        half = width // 2
        for b in range(half // block):
            at = b * block
            pieces[0][blocks + width // block + b] = low(
                select(
                    core,
                    out_w_ref[:, at : at + block],
                    out_w_ref[:, half + at : half + at + block],
                )
            )
        row = lax.broadcasted_iota(jnp.int32, (length - even, width), 0)
        for ref, to in ((rows_ref, rows_out), (cot_ref, cot_out)):
            to[:even, :] = ref[:even, :]
            last = jnp.zeros((length - even, width), jnp.float32)
            for extra in range(tokens - even):
                one = wide(ref[even + extra : even + extra + 1, :])
                last = jnp.where(row == extra, one, last)
            to[even:, :] = low(last)
        sum_ref[...] = jnp.sum(wide(cot_out[...]), axis=0, keepdims=True)

    extra = width // 2 // block
    counts = [blocks + width // block + (extra if j == 0 else 0) for j in range(CHUNKS)]
    outs = [sds((count, part, block), jnp.bfloat16) for count in counts]
    outs += [sds((length, width), jnp.bfloat16)] * 2 + [sds((1, width), jnp.float32)]
    ins = (in_weight, down_weight, out_weight, inputs, cotangent)
    return call(
        body,
        place,
        ins,
        [whole(a.shape) for a in ins],
        outs,
        [whole(a.shape) for a in outs],
        [],
        "prepare_rest",
    )


GAIN_ONE, BIAS_ONE, BIAS_OUT, GAIN_TWO, BIAS_TWO, BIAS_DOWN = range(6)


def project_qkv(place, rows, pieces, sizes):
    count = len(pieces)
    z_size = count // 2
    cols = pieces[0].shape[1]
    part = pieces[0].shape[0] - TILE
    width = part * count
    heads = cols // 3
    length = rows[0].shape[0]
    scale = 1.0 / math.sqrt(HEAD_DIM)
    starts = [sum(sizes[:number]) for number in range(len(sizes))]
    per_shard = sizes[6] // 2 // CHUNKS
    blocks = count // 2

    def body(place_ref, own_ref, other_ref, *refs):
        ins, refs = refs[:count], refs[count:]
        normed_ref, q_ref, k_ref, v_ref, vec_ref, hidden_bias_ref, weight, packed, sem = refs
        core = place_ref[2]
        copies = []
        for number, ref in enumerate(ins):
            z, x = shard_of(place_ref, number, z_size)
            row = pl.multiple_of((z * 2 + x) * part, part)
            for slot, copy in enumerate(
                (
                    pltpu.make_async_copy(
                        ref.at[pl.ds(0, part), :], weight.at[pl.ds(row, part), :], sem.at[2 * number]
                    ),
                    pltpu.make_async_copy(
                        ref.at[pl.ds(part, TILE), :], packed.at[z * 2 + x], sem.at[2 * number + 1]
                    ),
                )
            ):
                copy.start()
                copies.append(copy)
        for copy in copies:
            copy.wait()

        def vector(slot, shards=range(count)):
            at, size = starts[slot], sizes[slot]
            return jnp.concatenate(
                [wide(packed[s, 0:1, at : at + size]) for s in shards], axis=1
            )

        gain, bias = vector(0), vector(1)
        for row, value in (
            (GAIN_ONE, gain),
            (BIAS_ONE, bias),
            (BIAS_OUT, vector(3)),
            (GAIN_TWO, vector(4)),
            (BIAS_TWO, vector(5)),
            (BIAS_DOWN, vector(7)),
        ):
            vec_ref[row : row + 1, :] = value
        vec_ref[6:8, :] = jnp.zeros((2, width), jnp.float32)
        for j in range(CHUNKS):
            for b in range(blocks):
                for i in range(2):
                    at = starts[6] + j * per_shard
                    to = at + sizes[6] // 2
                    hidden_bias_ref[j, b, :, i * per_shard : (i + 1) * per_shard] = wide(
                        select(
                            core,
                            wide(packed[2 * b + i, 0:1, at : at + per_shard]),
                            wide(packed[2 * b + i, 0:1, to : to + per_shard]),
                        )
                    )
        bias_q = vector(2, range(blocks))
        bias_v = vector(2, range(blocks, count))
        bias_q = select(core, bias_q[:, :heads], bias_q[:, heads:])
        bias_v = select(core, bias_v[:, :heads], bias_v[:, heads:])
        for image, ref in enumerate((own_ref, other_ref)):
            for at in range(0, length, LANES):
                block = wide(ref[at : at + LANES, :])
                normed_ref[image, at : at + LANES, :] = low(normalised(block) * gain + bias)
            normed = normed_ref[image]
            query = low(dot(normed, weight[:, :heads]) + bias_q)
            q_ref[image] = low(wide(query) * scale)
            k_ref[image] = low(dot(normed, weight[:, heads : 2 * heads]))
            v_ref[image] = low(dot(normed, weight[:, 2 * heads :]) + bias_v)

    part_out = sds((2, length, heads), jnp.bfloat16)
    return call(
        body,
        place,
        (*rows, *pieces),
        [whole((length, width))] * 2 + [any_spec()] * count,
        [sds((2, length, width), jnp.bfloat16)]
        + [part_out] * 3
        + [
            sds((8, width), jnp.float32),
            sds((CHUNKS, blocks, 1, 2 * per_shard), jnp.float32),
        ],
        [whole((2, length, width))]
        + [whole((2, length, heads))] * 3
        + [whole((8, width)), whole((CHUNKS, blocks, 1, 2 * per_shard))],
        [
            pltpu.VMEM((width, cols), jnp.bfloat16),
            pltpu.VMEM((count, TILE, cols), jnp.bfloat16),
            pltpu.SemaphoreType.DMA((2 * count,)),
        ],
        "project_qkv",
        flops=4 * length * width * cols,
    )


def gather_out(place, pieces, first):
    count = len(pieces)
    z_size = count // 2
    total, part, block = pieces[0].shape
    width = part * count

    def body(place_ref, *refs):
        ins, out_ref, sem = refs[:count], refs[count], refs[count + 1]
        copies = []
        for number, ref in enumerate(ins):
            z, x = shard_of(place_ref, number, z_size)
            row = pl.multiple_of((z * 2 + x) * part, part)
            for b in range(total - first):
                copy = pltpu.make_async_copy(
                    ref.at[first + b],
                    out_ref.at[pl.ds(row, part), pl.ds(b * block, block)],
                    sem.at[number * (total - first) + b],
                )
                copy.start()
                copies.append(copy)
        for copy in copies:
            copy.wait()

    shape = (width, (total - first) * block)
    return call(
        body,
        place,
        tuple(pieces),
        [any_spec()] * count,
        [sds(shape, jnp.bfloat16)],
        [whole(shape)],
        [pltpu.SemaphoreType.DMA((count * (total - first),))],
        "gather_out",
    )[0]


def attention(place, query, keys, values):
    _, length, heads = query.shape
    pairs = heads // LANES

    def body(place_ref, q_ref, k_ref, v_ref, out_ref, probs_ref):
        lane = lax.broadcasted_iota(jnp.int32, (length, LANES), 1)
        keys_block = k_ref[0]
        values_t = v_ref[0].T
        query_block = q_ref[0]
        mixed = []
        for head in range(2):
            inside = (lane >= head * HEAD_DIM) & (lane < (head + 1) * HEAD_DIM)
            query_head = jnp.where(inside, query_block, jnp.zeros_like(query_block))
            values_head = values_t[head * HEAD_DIM : (head + 1) * HEAD_DIM, :]
            parts = []
            for at in range(0, length, SPAN):
                span = min(SPAN, length - at)
                scores = dot_tail(keys_block, query_head[at : at + span, :])
                key_row = lax.broadcasted_iota(jnp.int32, scores.shape, 0)
                scores = jnp.where(key_row < SEQ, scores, -1e30)
                highest = jnp.max(scores, axis=0, keepdims=True)
                exponent = jnp.exp(scores - highest)
                summed = jnp.sum(exponent, axis=0, keepdims=True)
                probs = low(exponent * (1.0 / summed))
                probs_ref[0, 0, head, :, at : at + span] = probs
                parts.append(dot(values_head, probs))
            mixed.append(jnp.concatenate(parts, axis=1))
        out_ref[0] = low(jnp.concatenate(mixed, axis=0).T)

    block = pl.BlockSpec((1, length, LANES), lambda i, j, p: (i, 0, j))
    return call(
        body,
        place,
        (query, keys, values),
        [block] * 3,
        [
            sds((2, length, heads), jnp.bfloat16),
            sds((2, pairs, 2, length, length), jnp.bfloat16),
        ],
        [block, pl.BlockSpec((1, 1, 2, length, length), lambda i, j, p: (i, j, 0, 0, 0))],
        [],
        "attention",
        grid=(2, pairs),
        flops=2 * pairs * 2 * 8 * length * length * LANES,
    )


def attention_back(place, query, keys, values, probs, grad):
    _, length, heads = query.shape
    pairs = heads // LANES
    scale = 1.0 / math.sqrt(HEAD_DIM)

    def body(place_ref, q_ref, k_ref, v_ref, p_ref, g_ref, gq_ref, gk_ref, gv_ref):
        lane = lax.broadcasted_iota(jnp.int32, (length, LANES), 1)
        keys_t = k_ref[0].T
        values_block = v_ref[0]
        query_block = q_ref[0]
        grad_block = g_ref[0]
        grad_query = []
        grad_keys = []
        grad_values = []
        for head in range(2):
            inside = (lane >= head * HEAD_DIM) & (lane < (head + 1) * HEAD_DIM)
            grad_head = jnp.where(inside, grad_block, jnp.zeros_like(grad_block))
            keys_head = keys_t[head * HEAD_DIM : (head + 1) * HEAD_DIM, :]
            parts = []
            sum_keys = None
            sum_values = None
            for at in range(0, length, SPAN):
                span = min(SPAN, length - at)
                probs_low = p_ref[0, 0, head, :, at : at + span]
                probs_wide = wide(probs_low)
                grad_probs = dot_tail(values_block, grad_head[at : at + span, :])
                inner = jnp.sum(probs_wide * grad_probs, axis=0, keepdims=True)
                grad_scores = low(probs_wide * (grad_probs - inner))
                parts.append(dot(keys_head, grad_scores))
                to_keys = dot(grad_scores, query_block[at : at + span, :])
                to_values = dot(probs_low, grad_block[at : at + span, :])
                sum_keys = to_keys if sum_keys is None else sum_keys + to_keys
                sum_values = to_values if sum_values is None else sum_values + to_values
            grad_query.append(jnp.concatenate(parts, axis=1))
            grad_keys.append(sum_keys)
            grad_values.append(sum_values)
        first = lane < HEAD_DIM
        gq_ref[0] = low(jnp.concatenate(grad_query, axis=0).T * scale)
        gk_ref[0] = low(jnp.where(first, grad_keys[0], grad_keys[1]))
        gv_ref[0] = low(jnp.where(first, grad_values[0], grad_values[1]))

    block = pl.BlockSpec((1, length, LANES), lambda i, j, p: (i, 0, j))
    return call(
        body,
        place,
        (query, keys, values, probs, grad),
        [block] * 3
        + [pl.BlockSpec((1, 1, 2, length, length), lambda i, j, p: (i, j, 0, 0, 0)), block],
        [sds((2, length, heads), jnp.bfloat16)] * 3,
        [block] * 3,
        [],
        "attention_back",
        grid=(2, pairs),
        flops=2 * pairs * 2 * 10 * length * length * LANES,
    )


def project_out(place, mine, theirs, weight_mine, weight_theirs, rows, vectors):
    width, half = weight_mine.shape
    _, length, heads = mine.shape

    def body(
        place_ref, mine_ref, theirs_ref, wm_ref, wt_ref, own_ref, other_ref, vec_ref, middle_ref,
        normed_ref, total,
    ):
        core = place_ref[2]
        at_mine = pl.multiple_of(core * heads, heads)
        at_theirs = pl.multiple_of((1 - core) * heads, heads)
        for image, ref in enumerate((own_ref, other_ref)):
            for slot, weight in enumerate((wm_ref, wt_ref)):
                total[slot] = dot(mine_ref[image], weight[pl.ds(at_mine, heads), :]) + dot(
                    theirs_ref[1 - image], weight[pl.ds(at_theirs, heads), :]
                )
            for at in range(0, length, LANES):
                upto = at + LANES
                first, second = total[0, at:upto, :], total[1, at:upto, :]
                left = select(core, first, second)
                right = select(core, second, first)
                middle = (
                    wide(ref[at:upto, :])
                    + jnp.concatenate([left, right], axis=1)
                    + vec_ref[BIAS_OUT : BIAS_OUT + 1, :]
                )
                if image == 0:
                    middle_ref[at:upto, :] = middle
                normed_ref[image, at:upto, :] = low(
                    normalised(middle) * vec_ref[GAIN_TWO : GAIN_TWO + 1, :]
                    + vec_ref[BIAS_TWO : BIAS_TWO + 1, :]
                )

    return call(
        body,
        place,
        (mine, theirs, weight_mine, weight_theirs, *rows, vectors),
        [whole((2, length, heads))] * 2
        + [whole((width, half))] * 2
        + [whole((length, width))] * 2
        + [whole(vectors.shape)],
        [sds((length, width), jnp.float32), sds((2, length, width), jnp.bfloat16)],
        [whole((length, width)), whole((2, length, width))],
        [pltpu.VMEM((2, length, half), jnp.float32)],
        "project_out",
        flops=8 * length * width * half,
    )


def feed_forward(place, normed, cotangent, pieces, bias, chunk, running):
    count = len(pieces)
    z_size = count // 2
    _, part, wide_block = pieces[0].shape
    half_blocks = bias.shape[1]
    width = part * count
    blocks = half_blocks + width // wide_block
    _, length, _ = normed.shape
    first_call = running is None

    def body(place_ref, normed_ref, own_cot, other_cot, bias_ref, *refs):
        ins = refs[:count]
        refs = refs[count:]
        if not first_call:
            before, refs = refs[:4], refs[4:]
        out_own, out_other, gn_own, gn_other, bsum_ref, keep_ref, send_ref = refs[:7]
        w_in, w_down, normed_t, grads, sem, out_sem = refs[7:]
        step = pl.program_id(0)

        def copies():
            made = []
            for number, ref in enumerate(ins):
                z, x = shard_of(place_ref, number, z_size)
                row = pl.multiple_of((z * 2 + x) * part, part)
                row_in = pl.multiple_of(x * part, part)
                for b in range(half_blocks):
                    made.append(
                        pltpu.make_async_copy(
                            ref.at[b], w_in.at[b, pl.ds(row, part), :], sem.at[number * blocks + b]
                        )
                    )
                    made.append(
                        pltpu.make_async_copy(
                            ref.at[half_blocks + b],
                            w_down.at[z, pl.ds(row_in, part), pl.ds(b * wide_block, wide_block)],
                            sem.at[number * blocks + half_blocks + b],
                        )
                    )
            return made

        @pl.when(step == 0)
        def _():
            for copy in copies():
                copy.start()
            for image in range(2):
                normed_t[:, image * length : (image + 1) * length] = normed_ref[image].T
            for copy in copies():
                copy.wait()

        weight_in = w_in[step]
        weight_down = w_down[step]
        into = None
        down = None
        column_sum = None
        for image, cot_ref in enumerate((own_cot, other_cot)):
            preact = dot(normed_ref[image], weight_in) + bias_ref[0, 0]
            phi = 0.5 * (1.0 + lax.erf(preact * math.sqrt(0.5)))
            density = jnp.exp(-0.5 * preact * preact) * (1.0 / math.sqrt(2.0 * math.pi))
            hidden = low(preact * phi)
            slope = phi + preact * density
            cot = cot_ref[...]
            grad = low(dot_tail(cot, weight_down) * slope)
            out_ref, gn_ref = ((out_own, gn_own), (out_other, gn_other))[image]
            to_out = dot(hidden, weight_down)
            to_normed = dot_tail(grad, weight_in)

            @pl.when(step == 0)
            def _():
                if first_call:
                    out_ref[...] = to_out
                    gn_ref[...] = to_normed
                else:
                    out_ref[...] = before[image][...] + to_out
                    gn_ref[...] = before[2 + image][...] + to_normed

            @pl.when(step > 0)
            def _():
                out_ref[...] += to_out
                gn_ref[...] += to_normed

            partial = jnp.sum(wide(grad), axis=0, keepdims=True)
            column_sum = partial if image == 0 else column_sum + partial
            to_in = dot(normed_t[:, image * length : (image + 1) * length], grad)
            into = to_in if image == 0 else into + to_in
            to_down = dot(hidden.T, cot)
            down = to_down if image == 0 else down + to_down
        bsum_ref[0] = column_sum
        for z in range(z_size):
            for x in range(2):
                k = lax.rem(z + z_size - place_ref[0], z_size)
                dx = x + (1 - 2 * x) * place_ref[1]
                at = (z * 2 + x) * part
                grads[dx, k, step] = low(into[at : at + part, :])
        for x in range(2):
            k = lax.rem(step + z_size - place_ref[0], z_size)
            dx = x + (1 - 2 * x) * place_ref[1]
            for b in range(half_blocks):
                grads[dx, k, half_blocks + b] = low(
                    down[x * part : (x + 1) * part, b * wide_block : (b + 1) * wide_block]
                )

        @pl.when(step == half_blocks - 1)
        def _():
            for slot, ref in enumerate((keep_ref, send_ref)):
                pltpu.make_async_copy(grads.at[slot], ref, out_sem.at[slot]).start()
            for slot, ref in enumerate((keep_ref, send_ref)):
                pltpu.make_async_copy(grads.at[slot], ref, out_sem.at[slot]).wait()

    total = sds((length, width), jnp.float32)
    piece_out = sds((z_size, blocks, part, wide_block), jnp.bfloat16)
    carried = () if first_call else tuple(running)
    return call(
        body,
        place,
        (normed, *cotangent, bias, *pieces, *carried),
        [whole((2, length, width))]
        + [whole((length, width))] * 2
        + [pl.BlockSpec((1, 1, 1, wide_block), lambda b, p: (chunk, b, 0, 0))]
        + [any_spec()] * count
        + [whole((length, width))] * len(carried),
        [total] * 4 + [sds((half_blocks, 1, wide_block), jnp.float32)] + [piece_out] * 2,
        [whole((length, width))] * 4
        + [pl.BlockSpec((1, 1, wide_block), lambda b, p: (b, 0, 0))]
        + [any_spec()] * 2,
        [
            pltpu.VMEM((half_blocks, width, wide_block), jnp.bfloat16),
            pltpu.VMEM((half_blocks, wide_block, width), jnp.bfloat16),
            pltpu.VMEM((width, 2 * length), jnp.bfloat16),
            pltpu.VMEM((2, z_size, blocks, part, wide_block), jnp.bfloat16),
            pltpu.SemaphoreType.DMA((count * blocks,)),
            pltpu.SemaphoreType.DMA((2,)),
        ],
        "feed_forward",
        grid=(half_blocks,),
        flops=24 * length * width * half_blocks * wide_block,
    )


def norm_back(place, rows, vectors, gain_row, grad_own, grad_other, passed, tokens, finish=None):
    length, width = rows.shape

    def body(place_ref, rows_ref, vec_ref, own_ref, other_ref, pass_ref, *refs):
        step = pl.program_id(0)
        values = wide(rows_ref[...])
        if finish is not None:
            first_ref, second_ref, *refs = refs
            refs[1][...] = low(
                values + first_ref[...] + second_ref[...] + vec_ref[BIAS_DOWN : BIAS_DOWN + 1, :]
            )
        sum_ref = refs[0]
        centre = values - jnp.mean(values, axis=-1, keepdims=True)
        spread = jnp.mean(centre * centre, axis=-1, keepdims=True)
        inverse = lax.rsqrt(spread + ln_eps)
        unit = centre * inverse
        grad = own_ref[...] + other_ref[...]
        scaled = grad * vec_ref[gain_row : gain_row + 1, :]
        mean_one = jnp.mean(scaled, axis=-1, keepdims=True)
        mean_two = jnp.mean(scaled * unit, axis=-1, keepdims=True)
        result = wide(pass_ref[...]) + (scaled - mean_one - unit * mean_two) * inverse
        rounded = low(result)
        parts = [
            jnp.sum(grad * unit, axis=0, keepdims=True),
            jnp.sum(grad, axis=0, keepdims=True),
            jnp.sum(wide(rounded), axis=0, keepdims=True),
            jnp.zeros((5, width), jnp.float32),
        ]
        if finish is None:
            refs[1][...] = rounded
        else:
            refs[2][...] = result
            refs[3][...] = rounded
        joined = jnp.concatenate(parts, axis=0)

        @pl.when(step == 0)
        def _():
            sum_ref[...] = joined

        @pl.when(step > 0)
        def _():
            sum_ref[...] += joined

    block = pl.BlockSpec((LANES, width), lambda i, p: (i, 0))
    outs = [sds((8, width), jnp.float32), sds((tokens, width), jnp.bfloat16)]
    if finish is not None:
        outs += [sds((length, width), jnp.float32), sds((length, width), jnp.bfloat16)]
    ins = (rows, vectors, grad_own, grad_other, passed, *(finish or ()))
    return call(
        body,
        place,
        ins,
        [block, whole(vectors.shape)] + [block] * (len(ins) - 2),
        outs,
        [whole((8, width))] + [block] * (len(outs) - 1),
        [],
        "norm_back",
        grid=(length // LANES,),
    )


def out_back(place, grad_own, grad_other, mine, theirs, weight_mine, weight_theirs):
    width, half = weight_mine.shape
    z_size = lax.axis_size("z")
    part = width // (2 * z_size)
    _, length, heads = mine.shape

    def body(
        place_ref, own_ref, other_ref, own_half, other_half, mine_ref, theirs_ref, wm_ref, wt_ref,
        ga_ref, keep_ref, send_ref, turned, grads, out_sem,
    ):
        core = place_ref[2]
        at_mine = pl.multiple_of(core * heads, heads)
        at_theirs = pl.multiple_of((1 - core) * heads, heads)
        for image in range(2):
            lanes = slice(image * length, (image + 1) * length)
            turned[pl.ds(at_mine, heads), lanes] = mine_ref[image].T
            turned[pl.ds(at_theirs, heads), lanes] = theirs_ref[1 - image].T
        term = dot(turned[:, :length], own_half[...]) + dot(turned[:, length:], other_half[...])
        for z in range(z_size):
            for x in range(2):
                k = lax.rem(z + z_size - place_ref[0], z_size)
                dx = x + (1 - 2 * x) * place_ref[1]
                at = (z * 2 + x) * part
                grads[dx, k] = low(term[at : at + part, :])
        for slot, ref in enumerate((keep_ref, send_ref)):
            pltpu.make_async_copy(grads.at[slot], ref, out_sem.at[slot]).start()
        for image, ref in enumerate((own_ref, other_ref)):
            first, second = ref[:, :half], ref[:, half:]
            left = select(core, first, second)
            right = select(core, second, first)
            ga_ref[image] = low(
                dot_tail(left, wm_ref[pl.ds(at_mine, heads), :])
                + dot_tail(right, wt_ref[pl.ds(at_mine, heads), :])
            )
        for slot, ref in enumerate((keep_ref, send_ref)):
            pltpu.make_async_copy(grads.at[slot], ref, out_sem.at[slot]).wait()

    half_block = pl.BlockSpec((length, half), lambda i, p: (0, p[2]))
    piece_out = sds((z_size, part, half), jnp.bfloat16)
    return call(
        body,
        place,
        (grad_own, grad_other, grad_own, grad_other, mine, theirs, weight_mine, weight_theirs),
        [whole((length, width))] * 2
        + [half_block] * 2
        + [whole((2, length, heads))] * 2
        + [whole((width, half))] * 2,
        [sds((2, length, heads), jnp.bfloat16)] + [piece_out] * 2,
        [whole((2, length, heads))] + [any_spec()] * 2,
        [
            pltpu.VMEM((width, 2 * length), jnp.bfloat16),
            pltpu.VMEM((2, z_size, part, half), jnp.bfloat16),
            pltpu.SemaphoreType.DMA((2,)),
        ],
        "out_back",
        flops=8 * length * width * half,
    )


def qkv_term(place, normed, grad_q, grad_k, grad_v):
    _, length, width = normed.shape
    heads = grad_q.shape[-1]
    cols = 3 * heads

    def body(place_ref, normed_ref, gq_ref, gk_ref, gv_ref, sum_ref, keep_ref, send_ref, turned, grads, sem):
        z_size = grads.shape[1]
        part = grads.shape[2]
        for image in range(2):
            turned[:, image * length : (image + 1) * length] = normed_ref[image].T
        for slot, ref in enumerate((gq_ref, gk_ref, gv_ref)):
            term = dot(turned[:, :length], ref[0]) + dot(turned[:, length:], ref[1])
            for z in range(z_size):
                for x in range(2):
                    k = lax.rem(z + z_size - place_ref[0], z_size)
                    dx = x + (1 - 2 * x) * place_ref[1]
                    at = (z * 2 + x) * part
                    grads[dx, k, :, slot * heads : (slot + 1) * heads] = low(
                        term[at : at + part, :]
                    )
            sum_ref[slot : slot + 1, :] = jnp.sum(wide(ref[0]), axis=0, keepdims=True) + jnp.sum(
                wide(ref[1]), axis=0, keepdims=True
            )
        for slot, ref in enumerate((keep_ref, send_ref)):
            pltpu.make_async_copy(grads.at[slot], ref, sem.at[slot]).start()
        for slot, ref in enumerate((keep_ref, send_ref)):
            pltpu.make_async_copy(grads.at[slot], ref, sem.at[slot]).wait()

    z_size = lax.axis_size("z")
    part = width // (2 * z_size)
    piece_out = sds((z_size, part, cols), jnp.bfloat16)
    return call(
        body,
        place,
        (normed, grad_q, grad_k, grad_v),
        [whole((2, length, width))] + [whole((2, length, heads))] * 3,
        [sds((3, heads), jnp.float32)] + [piece_out] * 2,
        [whole((3, heads))] + [any_spec()] * 2,
        [
            pltpu.VMEM((width, 2 * length), jnp.bfloat16),
            pltpu.VMEM((2, z_size, part, cols), jnp.bfloat16),
            pltpu.SemaphoreType.DMA((2,)),
        ],
        "qkv_term",
        flops=4 * length * width * cols,
    )


def qkv_back(place, grad_q, grad_k, grad_v, pieces):
    count = len(pieces)
    z_size = count // 2
    cols = pieces[0].shape[1]
    part = pieces[0].shape[0] - TILE
    width = part * count
    heads = cols // 3
    length = grad_q.shape[1]

    def body(place_ref, gq_ref, gk_ref, gv_ref, *refs):
        ins, (own_ref, other_ref, weight, sem) = refs[:count], refs[count:]
        copies = []
        for number, ref in enumerate(ins):
            z, x = shard_of(place_ref, number, z_size)
            row = pl.multiple_of((z * 2 + x) * part, part)
            copy = pltpu.make_async_copy(
                ref.at[pl.ds(0, part), :], weight.at[pl.ds(row, part), :], sem.at[number]
            )
            copy.start()
            copies.append(copy)
        for copy in copies:
            copy.wait()
        for image, out_ref in enumerate((own_ref, other_ref)):
            out_ref[...] = (
                dot_tail(gq_ref[image], weight[:, :heads])
                + dot_tail(gk_ref[image], weight[:, heads : 2 * heads])
                + dot_tail(gv_ref[image], weight[:, 2 * heads :])
            )

    return call(
        body,
        place,
        (grad_q, grad_k, grad_v, *pieces),
        [whole((2, length, heads))] * 3 + [any_spec()] * count,
        [sds((length, width), jnp.float32)] * 2,
        [whole((length, width))] * 2,
        [pltpu.VMEM((width, cols), jnp.bfloat16), pltpu.SemaphoreType.DMA((count,))],
        "qkv_back",
        flops=4 * length * width * cols,
    )


def fold_x(place, keep, got):
    size = keep.shape[0]

    def body(place_ref, keep_ref, got_ref, *outs):
        for k, out in enumerate(outs):
            total = wide(keep_ref[k]) + wide(got_ref[k])
            out[...] = total if k == 0 else low(total)

    rest = keep.shape[1:]
    outs = [sds(rest, jnp.float32)] + [sds(rest, jnp.bfloat16)] * (size - 1)
    return call(
        body,
        place,
        (keep, got),
        [whole(keep.shape)] * 2,
        outs,
        [whole(rest)] * size,
        [],
        "fold_x",
    )


def fold_z(place, held, got):
    final = jnp.bfloat16 if lax.axis_size("y") == 2 else jnp.float32

    def body(place_ref, held_ref, *refs):
        total = held_ref[...]
        for ref in refs[:-1]:
            total = total + wide(ref[...])
        refs[-1][...] = total.astype(final)

    return call(
        body,
        place,
        (held, *got),
        [whole(held.shape)] * (1 + len(got)),
        [sds(held.shape, final)],
        [whole(held.shape)],
        [],
        "fold_z",
    )[0]


def to_column(row):
    return jnp.concatenate(
        [
            jnp.broadcast_to(row[:, at : at + LANES], (LANES, LANES)).T[:, :1]
            for at in range(0, row.shape[1], LANES)
        ],
        axis=0,
    )


def to_row(column):
    return jnp.concatenate(
        [
            jnp.broadcast_to(column[at : at + LANES, :], (LANES, LANES)).T[:1, :]
            for at in range(0, column.shape[0], LANES)
        ],
        axis=1,
    )


def statistics(place, kinds, shares, weights, states, images, extra=None):
    flat = [a for chunks in shares for pair in chunks for side in pair for a in side]
    counts = [[[len(side) for side in pair] for pair in chunks] for chunks in shares]
    amount = len(kinds)
    vectors = 0 if extra is None else len(extra[1])

    def body(place_ref, *refs):
        core = place_ref[2]
        refs = list(refs)

        def take(n):
            taken = refs[:n]
            del refs[:n]
            return taken

        share_refs = take(len(flat))
        weight_refs, state_refs = take(amount), take(amount)
        if vectors:
            (terms_ref,) = take(1)
            param_refs, moment_refs = take(vectors), take(vectors)
        grad_refs, row_refs = take(amount), take(amount)
        (pack_ref,) = take(1)
        if vectors:
            vector_grads, new_moments = take(vectors), take(vectors)
        at_pack = 0
        for number, kind in enumerate(kinds):
            grad_ref, weight_ref = grad_refs[number], weight_refs[number]
            rows, cols = weights[number].shape
            for chunk, pair in enumerate(counts[number]):
                sides = []
                for n in pair:
                    sides.append(share_refs[:n])
                    del share_refs[:n]

                def halves(index):
                    mine, theirs = [
                        sum([wide(ref[index]) for ref in side[1:]], wide(side[0][index]))
                        * (1.0 / images)
                        for side in sides
                    ]
                    return select(core, mine, theirs), select(core, theirs, mine)

                shape = sides[0][0].shape
                if kind == "in":
                    blocks, _, block = cols // 2 // CHUNKS // shape[2], shape[1], shape[2]
                    per = block // 2
                    for b in range(blocks):
                        for c, half in enumerate(halves(b)):
                            for i in range(2):
                                at = ((2 * b + i) * 2 + c) * CHUNKS * per + chunk * per
                                grad_ref[:, at : at + per] = half[:, i * per : (i + 1) * per]
                elif kind == "down":
                    _, part, block = shape
                    first = shape[0] - cols // block
                    for b in range(cols // block):
                        for c, half in enumerate(halves(first + b)):
                            at = (c * CHUNKS + chunk) * part
                            grad_ref[at : at + part, b * block : (b + 1) * block] = half
                else:
                    groups = cols // (2 * SPLIT[kind])
                    for slot in range(SPLIT[kind]):
                        lanes = slice(slot * groups, (slot + 1) * groups)
                        for c, half in enumerate(halves((slice(None), lanes))):
                            at = (2 * slot + c) * groups
                            grad_ref[:, at : at + groups] = half
            squared = grad_ref[...] * grad_ref[...]
            new_rows = 0.5 * to_column(state_refs[number][...]) + 0.5 * jnp.mean(
                squared, axis=1, keepdims=True
            )
            row_refs[number][...] = to_row(new_rows)
            pack_ref[0:1, at_pack : at_pack + cols] = jnp.sum(squared, axis=0, keepdims=True)
            pack_ref[1:2, at_pack : at_pack + cols] = jnp.sum(
                squared * (1.0 / new_rows), axis=0, keepdims=True
            )
            at_pack += cols
            weight = weight_ref[...]
            pack_ref[0:1, at_pack : at_pack + LANES] = jnp.broadcast_to(
                jnp.sum(new_rows, axis=0, keepdims=True), (1, LANES)
            )
            pack_ref[1:2, at_pack : at_pack + LANES] = jnp.broadcast_to(
                jnp.sum(jnp.sum(weight * weight, axis=0, keepdims=True), axis=1, keepdims=True),
                (1, LANES),
            )
            at_pack += LANES
        at = 0
        if vectors:
            place_row = lax.broadcasted_iota(jnp.int32, extra[0].shape, 0)
            here = place_row == place_ref[0] * 2 + place_ref[1]
            mine = jnp.sum(
                jnp.where(here, terms_ref[...], 0.0), axis=0, keepdims=True
            )
        for number in range(vectors):
            size = extra[1][number].shape[1]
            grad = mine[:, at : at + size] * (1.0 / images)
            at += size
            param = param_refs[number][...]
            moment = 0.5 * moment_refs[number][...] + 0.5 * grad * grad
            direction = grad * lax.rsqrt(moment)
            vector_grads[number][...] = grad
            new_moments[number][...] = moment
            for row, value in enumerate((direction, param)):
                pack_ref[row : row + 1, at_pack : at_pack + LANES] = jnp.broadcast_to(
                    jnp.sum(value * value, axis=1, keepdims=True), (1, LANES)
                )
            at_pack += LANES

    lanes = sum(weight.shape[1] + LANES for weight in weights) + vectors * LANES
    ins = [*flat, *weights, *states]
    outs = [sds(weight.shape, jnp.float32) for weight in weights]
    outs += [sds(state.shape, jnp.float32) for state in states]
    outs.append(sds((2, lanes), jnp.float32))
    if vectors:
        terms, params, moments = extra
        ins += [terms, *params, *moments]
        outs += [sds(a.shape, jnp.float32) for a in (*params, *moments)]
    results = call(
        body,
        place,
        tuple(ins),
        [whole(a.shape) for a in ins],
        outs,
        [whole(a.shape) for a in outs],
        [],
        "statistics",
    )
    return (
        results[:amount],
        results[amount : 2 * amount],
        results[2 * amount],
        results[2 * amount + 1 : 2 * amount + 1 + vectors],
        results[2 * amount + 1 + vectors :],
    )


SPLIT = {"out": 1, "qkv": 3}


def update(place, grads, new_rows, weights, cols_states, pack, group, extra=None):
    amount = len(weights)
    vectors = 0 if extra is None else len(extra[0])

    def body(place_ref, *refs):
        refs = list(refs)

        def take(n):
            taken = refs[:n]
            del refs[:n]
            return taken

        grad_refs, row_refs, weight_refs, state_refs = [take(amount) for _ in range(4)]
        (pack_ref,) = take(1)
        if vectors:
            vector_grads, moment_refs, param_refs = [take(vectors) for _ in range(3)]
        new_refs, col_refs = take(amount), take(amount)
        (clip_ref,) = take(1)
        param_outs = take(vectors)
        at_pack = 0
        clip_ref[...] = jnp.zeros(clip_ref.shape, jnp.float32)
        for number in range(amount):
            rows, cols = weights[number].shape
            rows_total = rows * group
            count = rows_total * cols
            new_cols = (
                0.5 * state_refs[number][...]
                + 0.5 * pack_ref[0:1, at_pack : at_pack + cols] / rows_total
            )
            col_refs[number][...] = new_cols
            by_rows = pack_ref[1:2, at_pack : at_pack + cols]
            at_pack += cols
            mean_rows = pack_ref[0:1, at_pack : at_pack + 1] / rows_total
            weight_total = pack_ref[1:2, at_pack : at_pack + 1]
            at_pack += LANES
            total = mean_rows * jnp.sum(by_rows / new_cols, axis=1, keepdims=True)
            clip = jnp.maximum(1.0, jnp.sqrt(total / count) / clip_level)
            step = step_rate * jnp.sqrt(weight_total / count) / clip
            clip_ref[number : number + 1, :] = jnp.broadcast_to(clip, (1, LANES))
            estimate = to_column(row_refs[number][...]) * (new_cols / mean_rows)
            new_refs[number][...] = weight_refs[number][...] - step * (
                grad_refs[number][...] * lax.rsqrt(estimate)
            )
        for number in range(vectors):
            count = extra[2][number].shape[1] * group
            total = pack_ref[0:1, at_pack : at_pack + 1]
            weight_total = pack_ref[1:2, at_pack : at_pack + 1]
            at_pack += LANES
            clip = jnp.maximum(1.0, jnp.sqrt(total / count) / clip_level)
            step = step_rate * jnp.sqrt(weight_total / count) / clip
            slot = amount + number
            clip_ref[slot : slot + 1, :] = jnp.broadcast_to(clip, (1, LANES))
            direction = vector_grads[number][...] * lax.rsqrt(moment_refs[number][...])
            param_outs[number][...] = param_refs[number][...] - step * direction

    ins = [*grads, *new_rows, *weights, *cols_states, pack]
    outs = [sds(a.shape, jnp.float32) for a in (*weights, *cols_states)]
    outs.append(sds((TILE, LANES), jnp.float32))
    if vectors:
        ins += [*extra[0], *extra[1], *extra[2]]
        outs += [sds(a.shape, jnp.float32) for a in extra[2]]
    results = call(
        body,
        place,
        tuple(ins),
        [whole(a.shape) for a in ins],
        outs,
        [whole(a.shape) for a in outs],
        [],
        "update",
    )
    return (
        results[:amount],
        results[amount : 2 * amount],
        results[2 * amount],
        results[2 * amount + 1 :],
    )


def pack_terms(place, sums_mid, sums_in, sums_qkv, hidden_sums, down_sums, sizes):
    z_size = lax.axis_size("z")
    shards = 2 * z_size
    per_shard = sizes[6] // 2 // CHUNKS
    heads = sums_qkv.shape[1]

    def body(place_ref, mid_ref, in_ref, qkv_ref, *refs):
        hidden_refs, (down_ref, out_ref) = refs[:CHUNKS], refs[CHUNKS:]
        core = place_ref[2]

        def put(slot, row):
            at, size = sum(sizes[:slot]), sizes[slot]
            for s in range(shards):
                out_ref[s : s + 1, at : at + size] = row[:, s * size : (s + 1) * size]

        put(0, in_ref[0:1, :])
        put(1, in_ref[1:2, :])
        zero = jnp.zeros((1, heads), jnp.float32)
        halves = []
        for slot in (0, 2):
            row = qkv_ref[slot : slot + 1, :]
            halves += [select(core, row, zero), select(core, zero, row)]
        put(2, jnp.concatenate(halves, axis=1))
        put(3, mid_ref[2:3, :])
        put(4, mid_ref[0:1, :])
        put(5, mid_ref[1:2, :])
        put(7, down_ref[...])
        none = jnp.zeros((1, per_shard), jnp.float32)
        for s in range(shards):
            for j in range(CHUNKS):
                i = s % 2
                row = hidden_refs[j][s // 2, :, i * per_shard : (i + 1) * per_shard]
                for c in range(2):
                    at = sum(sizes[:6]) + (c * CHUNKS + j) * per_shard
                    here = select(core, row, none) if c == 0 else select(core, none, row)
                    out_ref[s : s + 1, at : at + per_shard] = here

    ins = (sums_mid, sums_in, sums_qkv, *hidden_sums, down_sums)
    shape = (shards, sum(sizes))
    return call(
        body,
        place,
        ins,
        [whole(a.shape) for a in ins],
        [sds(shape, jnp.float32)],
        [whole(shape)],
        [],
        "pack_terms",
    )[0]


def on_device(
    inputs,
    cotangent,
    norm1_gain,
    norm1_bias,
    qkv_weight,
    qv_bias,
    out_weight,
    out_bias,
    norm2_gain,
    norm2_bias,
    in_weight,
    in_bias,
    down_weight,
    down_bias,
    qkv_rows,
    qkv_cols,
    out_rows,
    out_cols,
    in_rows,
    in_cols,
    down_rows,
    down_cols,
    norm1_gain_moment,
    norm1_bias_moment,
    qv_bias_moment,
    out_bias_moment,
    norm2_gain_moment,
    norm2_bias_moment,
    in_bias_moment,
    down_bias_moment,
):
    masters = [
        norm1_gain,
        norm1_bias,
        qkv_weight,
        qv_bias,
        out_weight,
        out_bias,
        norm2_gain,
        norm2_bias,
        in_weight,
        in_bias,
        down_weight,
        down_bias,
    ]
    moments = [
        norm1_gain_moment,
        norm1_bias_moment,
        qv_bias_moment,
        out_bias_moment,
        norm2_gain_moment,
        norm2_bias_moment,
        in_bias_moment,
        down_bias_moment,
    ]
    place = jnp.stack(
        [lax.axis_index("z"), lax.axis_index("x"), lax.axis_index("c")]
    ).astype(jnp.int32)
    group = lax.axis_size("z") * lax.axis_size("x")
    tokens = inputs.shape[0]
    images = (tokens // SEQ) * group * lax.axis_size("y") * lax.axis_size("c")
    as_row = lambda vector: vector.reshape(1, -1)
    params = [as_row(masters[number]) for number in VECTORS]
    moments = [as_row(moment) for moment in moments]
    sizes = [param.shape[1] for param in params]

    pieces_qkv = gather_pieces(prepare_qkv(place, qkv_weight, params))
    *shards_ff, rows_own, cot_own, down_sums = prepare_rest(
        place, in_weight, down_weight, out_weight, inputs, cotangent
    )
    rows = (rows_own, swap(rows_own, "c"))
    cot = (cot_own, swap(cot_own, "c"))
    pieces_ff = [gather_pieces(shard) for shard in shards_ff]
    weight_mine = gather_out(place, pieces_ff[0], shards_ff[1].shape[0])
    weight_theirs = swap(weight_mine, "c")

    normed, query, keys, values, vectors, hidden_bias = project_qkv(
        place, rows, pieces_qkv, sizes
    )
    attended, probs = attention(place, query, keys, values)
    attended_theirs = swap(attended, "c")
    middle, normed_mid = project_out(
        place, attended, attended_theirs, weight_mine, weight_theirs, rows, vectors
    )
    running = None
    hidden_sums = []
    shares_ff = []
    for j in range(CHUNKS):
        *running, sums, keep, send = feed_forward(
            place, normed_mid, cot, pieces_ff[j], hidden_bias, j, running
        )
        hidden_sums.append(sums)
        shares_ff.append(scatter_sum(place, keep, send))
    out_share, out_given, normed_share, normed_given = running
    sums_mid, output, grad_mid, grad_mid_low = norm_back(
        place,
        middle,
        vectors,
        GAIN_TWO,
        normed_share,
        swap(normed_given, "c"),
        cot_own,
        tokens,
        (out_share, swap(out_given, "c")),
    )
    grad_attended, keep, send = out_back(
        place,
        grad_mid_low,
        swap(grad_mid_low, "c"),
        attended,
        attended_theirs,
        weight_mine,
        weight_theirs,
    )
    share_out = scatter_sum(place, keep, send)
    grad_q, grad_k, grad_v = attention_back(place, query, keys, values, probs, grad_attended)
    sums_qkv, keep, send = qkv_term(place, normed, grad_q, grad_k, grad_v)
    share_qkv = scatter_sum(place, keep, send)
    share, given = qkv_back(place, grad_q, grad_k, grad_v, pieces_qkv)
    sums_in, input_grad = norm_back(
        place, rows_own, vectors, GAIN_ONE, share, swap(given, "c"), grad_mid, tokens
    )
    terms = sum_over(
        pack_terms(place, sums_mid, sums_in, sums_qkv, hidden_sums, down_sums, sizes),
        ("c", "x", "z", "y"),
    )

    early = ("in", "down", "out")
    weights = [in_weight, down_weight, out_weight]
    states = [as_row(state) for state in (in_rows, down_rows, out_rows)]
    grads_early, rows_early, pack, _, _ = statistics(
        place, early, [shares_ff, shares_ff, [share_out]], weights, states, images
    )
    new_early, cols_early, clips_early, _ = update(
        place,
        grads_early,
        rows_early,
        weights,
        [as_row(state) for state in (in_cols, down_cols, out_cols)],
        sum_over(pack, ("x", "z")),
        group,
    )
    grads_late, rows_late, pack, vector_grads, new_moments = statistics(
        place,
        ("qkv",),
        [[share_qkv]],
        [qkv_weight],
        [as_row(qkv_rows)],
        images,
        (terms, params, moments),
    )
    new_late, cols_late, clips_late, new_vectors = update(
        place,
        grads_late,
        rows_late,
        [qkv_weight],
        [as_row(qkv_cols)],
        sum_over(pack, ("x", "z")),
        group,
        (vector_grads, new_moments, params),
    )

    flat = lambda value: value.reshape(-1)
    grads = [None] * 12
    new_params = [None] * 12
    for number, slot in ((8, 0), (10, 1), (4, 2)):
        grads[number], new_params[number] = grads_early[slot], new_early[slot]
    grads[2], new_params[2] = grads_late[0], new_late[0]
    for slot, number in enumerate(VECTORS):
        grads[number] = flat(vector_grads[slot])
        new_params[number] = flat(new_vectors[slot])
    late, first = clips_late[:, 0], clips_early[:, 0]
    clip_factors = jnp.stack(
        [
            late[1],
            late[2],
            late[0],
            late[3],
            first[2],
            late[4],
            late[5],
            late[6],
            first[0],
            late[7],
            first[1],
            late[8],
        ]
    )
    return (
        output,
        input_grad,
        *grads,
        flat(rows_late[0]),
        flat(cols_late[0]),
        flat(rows_early[2]),
        flat(cols_early[2]),
        flat(rows_early[0]),
        flat(cols_early[0]),
        flat(rows_early[1]),
        flat(cols_early[1]),
        *[flat(moment) for moment in new_moments],
        *new_params,
        clip_factors,
    )


def solution(mesh):
    group = mesh.shape["fsdp"]
    split = Mesh(mesh.devices.reshape(group // 2, 2, mesh.shape["dp"] // 2, 2), ALL_AXES)
    in_specs = (
        P(("z", "x", "y", "c"), None),
        P(("z", "x", "y", "c"), None),
        P(("z", "x")),
        P(("z", "x")),
        P(("z", "x"), None),
        P(("z", "x")),
        P(("z", "x"), None),
        P(("z", "x")),
        P(("z", "x")),
        P(("z", "x")),
        P(("z", "x"), None),
        P(("z", "x")),
        P(("z", "x"), None),
        P(("z", "x")),
        P(("z", "x")),
        P(),
        P(("z", "x")),
        P(),
        P(("z", "x")),
        P(),
        P(("z", "x")),
        P(),
        P(("z", "x")),
        P(("z", "x")),
        P(("z", "x")),
        P(("z", "x")),
        P(("z", "x")),
        P(("z", "x")),
        P(("z", "x")),
        P(("z", "x")),
    )
    out_specs = (
        P(("z", "x", "y", "c"), None),
        P(("z", "x", "y", "c"), None),
        P(("z", "x")),
        P(("z", "x")),
        P(("z", "x"), None),
        P(("z", "x")),
        P(("z", "x"), None),
        P(("z", "x")),
        P(("z", "x")),
        P(("z", "x")),
        P(("z", "x"), None),
        P(("z", "x")),
        P(("z", "x"), None),
        P(("z", "x")),
        P(("z", "x")),
        P(),
        P(("z", "x")),
        P(),
        P(("z", "x")),
        P(),
        P(("z", "x")),
        P(),
        P(("z", "x")),
        P(("z", "x")),
        P(("z", "x")),
        P(("z", "x")),
        P(("z", "x")),
        P(("z", "x")),
        P(("z", "x")),
        P(("z", "x")),
        P(("z", "x")),
        P(("z", "x")),
        P(("z", "x"), None),
        P(("z", "x")),
        P(("z", "x"), None),
        P(("z", "x")),
        P(("z", "x")),
        P(("z", "x")),
        P(("z", "x"), None),
        P(("z", "x")),
        P(("z", "x"), None),
        P(("z", "x")),
        P(),
    )
    return jax.shard_map(
        on_device, mesh=split, in_specs=in_specs, out_specs=out_specs, check_vma=False
    )
```

time: 751 us -> 630 us (0.84)
  other arithmetic: 76.6 us -> 5.05 us
  Pallas kernels: 207 us -> 273 us
  local copies, waits for them, and re-layouts: 73.8 us -> 16.5 us
  waiting for transfers between devices: 273 us -> 229 us
  between operations: 21.7 us -> 1.56 us
    ppermute x36 -> x32, waiting for transfers between devices: 156 us -> 58.9 us  [swap(): return lax.ppermute(value, axis, [(0, 1), (1, 0)])]
    ppermute x24 -> x21, waiting for transfers between devices: 71.3 us -> 140 us  [shift(): lax.ppermute(value, axis, [(i, (i + step) % size) for i in range(size)])]
    pallas_call x11 -> x27, Pallas kernels: 207 us -> 273 us  [call(): pl.pallas_call(body, out_shape=outs, grid_spec=pltpu.PrefetchScalarGridSp...]
    ppermute x28 -> x11, waiting for transfers between devices: 46 us -> 5.44 us  [partner(): return lax.ppermute(value, axis, [(i, i ^ step) for i in range(size)])]
    reduce_sum x33 -> x0, other arithmetic: 26 us -> none  [the longest x8 6.57 us: on_device(): sums.append(jnp.sum(weight * weight))]
    ppermute x0 -> x4, waiting for transfers between devices: none -> 24.5 us  [swap_both(): return lax.ppermute(value, ('y', 'c'), [(i, 3 - i) for i in range(4)])]
    ppermute x24 -> x21, starting transfers between devices: 32.9 us -> 56 us  [shift(): lax.ppermute(value, axis, [(i, (i + step) % size) for i in range(size)])]
    unnamed x234 -> x62, local copies, waits for them, and re-layouts: 26.2 us -> 5.66 us
  transfers between devices with their start and end apart: 88 -> 68, of which waited for: 36 -> 22; matrix products, arithmetic and copies ran while one was open for 16% -> 1% of each run, Pallas kernels for 28% -> 35%
where the time goes in v3:
time: 630 us; the launch traced here: 621 us
  Pallas kernels  273 us (43%)
  waiting for transfers between devices  229 us (36%)
  starting transfers between devices  95.9 us (15%)
  local copies, waits for them, and re-layouts  16.5 us (3%)
    pallas_call x27, Pallas kernels, call(): pl.pallas_call(body, out_shape=outs, grid_spec=pltpu.PrefetchScalarGridSp...  273 us
    ppermute x21, waiting for transfers between devices, shift(): lax.ppermute(value, axis, [(i, (i + step) % size) for i in range(size)])  140 us
    ppermute x32, waiting for transfers between devices, swap(): return lax.ppermute(value, axis, [(0, 1), (1, 0)])  58.9 us
    ppermute x21, starting transfers between devices, shift(): lax.ppermute(value, axis, [(i, (i + step) % size) for i in range(size)])  56 us
    ppermute x32, starting transfers between devices, swap(): return lax.ppermute(value, axis, [(0, 1), (1, 0)])  24.6 us
    ppermute x4, waiting for transfers between devices, swap_both(): return lax.ppermute(value, ('y', 'c'), [(i, 3 - i) for i in range(4)])  24.5 us
    ppermute x11, starting transfers between devices, partner(): return lax.ppermute(value, axis, [(i, i ^ step) for i in range(size)])  13.2 us
  transfers between devices with their start and end apart: 68, of which 22 were waited for; matrix products, arithmetic and copies ran while one was open for 1% of the time, Pallas kernels for 35%

profile of v3, /device:TPU:0, one launch (start us, length us, event | category | flops | bytes accessed | tf_op | source)
XLA Modules:
  0.0 621.4 jit_solution(3540696039581774296)
XLA Ops:
  4.3 5.0 collective-permute-start.6
  9.4 5.7 prepare_rest.1
  21.6 26.9 %collective-permute-done.4.refs_4_ = bf16[144,1536]{1,0:T(8,128)(2,1)S(1)} collective-permute-done((bf16[144,1536]{1,0:T(8,128)(2,1)}, bf16[144,1536]{1,0:T(8,128)(2,1)S(1)}, u32[]{:S(2)}, u32[]{:S(2)}) %collective-permute-start.4) | collective-permute-done | bytes 442400 | tf_op jit(solution)/shard_map/ppermute | solution.py:35
  50.1 27.1 %collective-permute-start.10 = (bf16[10,128,256]{2,1,0:T(8,128)(2,1)}, bf16[10,128,256]{2,1,0:T(8,128)(2,1)}, u32[]{:S(2)}, u32[]{:S(2)}) collective-permute-start(bf16[10,128,256]{2,1,0:T(8,128)(2,1)} %get-tuple-element.154.refs_0_), channel_id=1, source_target_pairs={{0,8},{8,16},{16,24},{24,0},{1,9},{9,17},{17,25},{25,1},{2,10},{10... | collective-permute-start | bytes 1966088 | tf_op jit(solution)/shard_map/ppermute | solution.py:35
  79.2 24.4 %collective-permute-done.12.refs_4_ = bf16[10,128,256]{2,1,0:T(8,128)(2,1)S(1)} collective-permute-done((bf16[10,128,256]{2,1,0:T(8,128)(2,1)}, bf16[10,128,256]{2,1,0:T(8,128)(2,1)S(1)}, u32[]{:S(2)}, u32[]{:S(2)}) %collective-permute-start.12) | collective-permute-done | bytes 655392 | tf_op jit(solution)/shard_map/ppermute | solution.py:35
  107.7 9.0 %collective-permute-done.3.refs_3_ = bf16[144,1536]{1,0:T(8,128)(2,1)S(1)} collective-permute-done((bf16[144,1536]{1,0:T(8,128)(2,1)S(1)}, bf16[144,1536]{1,0:T(8,128)(2,1)S(1)}, u32[]{:S(2)}, u32[]{:S(2)}) %collective-permute-start.3) | collective-permute-done | bytes 442400 | tf_op jit(solution)/shard_map/ppermute | solution.py:30
  119.3 11.0 %project_qkv.1 = (bf16[2,640,1024]{2,1,0:T(8,128)(2,1)}, bf16[2,640,512]{2,1,0:T(8,128)(2,1)}, bf16[2,640,512]{2,1,0:T(8,128)(2,1)}, bf16[2,640,512]{2,1,0:T(8,1...) custom-call(s32[3]{0:T(128)} %pad_add_fusion.place_ref, bf16[640,1024]{1,0:T(8,128)(2,1)} %get-tuple-element.149.own_ref.rows_ref, ...), custom_call_target="tpu_custom_call" | custom-call | flops 4026531840 | bytes 12754944 | tf_op jit(solution)/shard_map/project_qkv/pallas_call | solution.py:111
  130.3 28.3 %attention.1 = (bf16[2,640,512]{2,1,0:T(8,128)(2,1)}, bf16[2,4,2,640,640]{4,3,2,1,0:T(8,128)(2,1)}) custom-call(s32[3]{0:T(128)} %pad_add_fusion.place_ref, bf16[2,640,512]{2,1,0:T(8,128)(2,1)} %get-tuple-element.150.q_ref, bf16[2,640,512]{2,1,0:T(8,128)(2,1)} %get-tuple-element.151.k_ref, bf16[2,640,512]{2,1,0:T(8,128)(2,1)} %get-tuple-element.152.v_ref), custom_call_target="tpu_custom_call" | custom-call | flops 6710886400 | bytes 18350080 | tf_op jit(solution)/shard_map/attention/pallas_call | solution.py:111
  159.1 11.8 %collective-permute-done.11.refs_3_ = bf16[10,128,256]{2,1,0:T(8,128)(2,1)} collective-permute-done((bf16[10,128,256]{2,1,0:T(8,128)(2,1)}, bf16[10,128,256]{2,1,0:T(8,128)(2,1)}, u32[]{:S(2)}, u32[]{:S(2)}) %collective-permute-start.11) | collective-permute-done | bytes 655392 | tf_op jit(solution)/shard_map/ppermute | solution.py:30
  174.6 32.9 %collective-permute-done.21.refs_4_ = bf16[8,128,256]{2,1,0:T(8,128)(2,1)} collective-permute-done((bf16[8,128,256]{2,1,0:T(8,128)(2,1)}, bf16[8,128,256]{2,1,0:T(8,128)(2,1)}, u32[]{:S(2)}, u32[]{:S(2)}) %collective-permute-start.21) | collective-permute-done | bytes 524320 | tf_op jit(solution)/shard_map/ppermute | solution.py:35
  212.2 9.9 %project_out.1 = (f32[640,1024]{1,0:T(8,128)}, bf16[2,640,1024]{2,1,0:T(8,128)(2,1)}) custom-call(s32[3]{0:T(128)} %pad_add_fusion.place_ref, bf16[2,640,512]{2,1,0:T(8,128)(2,1)} %get-tuple-element.153.mine_ref, bf16[2,640,512]{2,1,0:T(8,128)(2,1)} %copy-done.5, bf16[1024,512]{1,0:T(8,128)(2,1)} %gather_out.1.wm_ref, bf16[1024,512]{1,0:T(8,128)(2,1)} %copy-done.7, ...), custom_call_target="tpu_custom_call" | custom-call | flops 2684354560 | bytes 12615680 | tf_op jit(solution)/shard_map/project_out/pallas_call | solution.py:111
  222.0 36.2 %feed_forward.2 = (f32[640,1024]{1,0:T(8,128)}, f32[640,1024]{1,0:T(8,128)}, f32[640,1024]{1,0:T(8,128)}, f32[640,1024]{1,0:T(8,128)}, f32[4,1,256]{2,1,0:T(1,12...) custom-call(s32[3]{0:T(128)} %pad_add_fusion.place_ref, ...), custom_call_target="tpu_custom_call" | custom-call | flops 16106127360 | bytes 25178112 | tf_op jit(solution)/shard_map/feed_forward/pallas_call | solution.py:111
  258.3 39.9 %feed_forward.3 = (f32[640,1024]{1,0:T(8,128)}, f32[640,1024]{1,0:T(8,128)}, f32[640,1024]{1,0:T(8,128)}, f32[640,1024]{1,0:T(8,128)}, f32[4,1,256]{2,1,0:T(1,12...) custom-call(s32[3]{0:T(128)} %pad_add_fusion.place_ref, ...), custom_call_target="tpu_custom_call" | custom-call | flops 16106127360 | bytes 34615296 | tf_op jit(solution)/shard_map/feed_forward/pallas_call | solution.py:111
  298.8 7.6 %collective-permute-done.25.other_ref = f32[640,1024]{1,0:T(8,128)S(1)} collective-permute-done((f32[640,1024]{1,0:T(8,128)}, f32[640,1024]{1,0:T(8,128)S(1)}, u32[]{:S(2)}, u32[]{:S(2)}) %collective-permute-start.25) | collective-permute-done | bytes 2621472 | tf_op jit(solution)/shard_map/ppermute | solution.py:30
  307.9 10.4 %norm_back.2 = (f32[8,1024]{1,0:T(8,128)}, bf16[577,1024]{1,0:T(8,128)(2,1)}, f32[640,1024]{1,0:T(8,128)}, bf16[640,1024]{1,0:T(8,128)(2,1)}) custom-call(s32[3]{0:T(128)} %pad_add_fusion.place_ref, f32[640,1024]{1,0:T(8,128)} %get-tuple-element.156.rows_ref, f32[8,1024]{1,0:T(8,128)} %get-tuple-element.155.vec_ref, f32[640,1024]{1,0:T(8,128)} %get-tuple-element.165.own_ref, ...), custom_call_target="tpu_custom_call" | custom-call | bytes 19597312 | tf_op jit(solution)/shard_map/norm_back/pallas_call | solution.py:111
  322.6 9.3 %out_back.1 = (bf16[2,640,512]{2,1,0:T(8,128)(2,1)}, bf16[4,128,512]{2,1,0:T(8,128)(2,1)}, bf16[4,128,512]{2,1,0:T(8,128)(2,1)}) custom-call(s32[3]{0:T(128)} %pad_add_fusion.place_ref, bf16[640,1024]{1,0:T(8,128)(2,1)} %get-tuple-element.171.own_ref.own_half, bf16[640,1024]{1,0:T(8,128)(2,1)} %copy-done, ...), custom_call_target="tpu_custom_call" | custom-call | flops 2684354560 | bytes 12320768 | tf_op jit(solution)/shard_map/out_back/pallas_call | solution.py:111
  332.0 32.5 %attention_back.1 = (bf16[2,640,512]{2,1,0:T(8,128)(2,1)}, bf16[2,640,512]{2,1,0:T(8,128)(2,1)}, bf16[2,640,512]{2,1,0:T(8,128)(2,1)}) custom-call(s32[3]{0:T(128)} %pad_add_fusion.place_ref, bf16[2,640,512]{2,1,0:T(8,128)(2,1)} %get-tuple-element.150.q_ref, bf16[2,640,512]{2,1,0:T(8,128)(2,1)} %get-tuple-element.151.k_ref, ...), custom_call_target="tpu_custom_call" | custom-call | flops 8388608000 | bytes 22282240 | tf_op jit(solution)/shard_map/attention_back/pallas_call | solution.py:111
  364.4 10.4 %qkv_back.1 = (f32[640,1024]{1,0:T(8,128)}, f32[640,1024]{1,0:T(8,128)}) custom-call(s32[3]{0:T(128)} %pad_add_fusion.place_ref, bf16[2,640,512]{2,1,0:T(8,128)(2,1)} %get-tuple-element.173.gq_ref, bf16[2,640,512]{2,1,0:T(8,128)(2,1)} %get-tuple-element.174.gk_ref, bf16[2,640,512]{2,1,0:T(8,128)(2,1)} %get-tuple-element.175.gv_ref, ...), custom_call_target="tpu_custom_call" | custom-call | flops 4026531840 | bytes 12713984 | tf_op jit(solution)/shard_map/qkv_back/pallas_call | solution.py:111
  375.2 4.6 fold_x.6
  379.7 11.0 %qkv_term.1 = (f32[3,512]{1,0:T(4,128)}, bf16[4,128,1536]{2,1,0:T(8,128)(2,1)}, bf16[4,128,1536]{2,1,0:T(8,128)(2,1)}) custom-call(s32[3]{0:T(128)} %pad_add_fusion.place_ref, bf16[2,640,1024]{2,1,0:T(8,128)(2,1)} %get-tuple-element.180.normed_ref, bf16[2,640,512]{2,1,0:T(8,128)(2,1)} %get-tuple-element.173.gq_ref, ...), custom_call_target="tpu_custom_call" | custom-call | flops 4026531840 | bytes 9705472 | tf_op jit(solution)/shard_map/qkv_term/pallas_call | solution.py:111
  391.8 20.4 %collective-permute-done.41.got_ref = bf16[4,8,128,256]{3,2,1,0:T(8,128)(2,1)} collective-permute-done((bf16[4,8,128,256]{3,2,1,0:T(8,128)(2,1)}, bf16[4,8,128,256]{3,2,1,0:T(8,128)(2,1)}, u32[]{:S(2)}, u32[]{:S(2)}) %collective-permute-start.41) | collective-permute-done | bytes 2097184 | tf_op jit(solution)/shard_map/ppermute | solution.py:30
  418.7 21.3 %collective-permute-done.51.refs_2_ = bf16[8,128,256]{2,1,0:T(8,128)(2,1)} collective-permute-done((bf16[8,128,256]{2,1,0:T(8,128)(2,1)}, bf16[8,128,256]{2,1,0:T(8,128)(2,1)}, u32[]{:S(2)}, u32[]{:S(2)}) %collective-permute-start.51) | collective-permute-done | bytes 524320 | tf_op jit(solution)/shard_map/ppermute | solution.py:35
  444.6 18.6 %collective-permute-done.43.refs_1_ = bf16[8,128,256]{2,1,0:T(8,128)(2,1)} collective-permute-done((bf16[8,128,256]{2,1,0:T(8,128)(2,1)}, bf16[8,128,256]{2,1,0:T(8,128)(2,1)}, u32[]{:S(2)}, u32[]{:S(2)}) %collective-permute-start.43) | collective-permute-done | bytes 524320 | tf_op jit(solution)/shard_map/ppermute | solution.py:35
  463.2 10.6 %collective-permute-done.44.refs_2_ = bf16[8,128,256]{2,1,0:T(8,128)(2,1)} collective-permute-done((bf16[8,128,256]{2,1,0:T(8,128)(2,1)}, bf16[8,128,256]{2,1,0:T(8,128)(2,1)}, u32[]{:S(2)}, u32[]{:S(2)}) %collective-permute-start.44) | collective-permute-done | bytes 524320 | tf_op jit(solution)/shard_map/ppermute | solution.py:35
  484.2 4.7 collective-permute-done.52.refs_5_.refs_13_
  489.8 8.4 %collective-permute-done.47.refs_3_.refs_11_ = bf16[8,128,256]{2,1,0:T(8,128)(2,1)} collective-permute-done((bf16[8,128,256]{2,1,0:T(8,128)(2,1)}, bf16[8,128,256]{2,1,0:T(8,128)(2,1)}, u32[]{:S(2)}, u32[]{:S(2)}) %collective-permute-start.47) | collective-permute-done | bytes 524320 | tf_op jit(solution)/shard_map/ppermute | solution.py:44
  502.2 7.6 %norm_back.3 = (f32[8,1024]{1,0:T(8,128)}, bf16[577,1024]{1,0:T(8,128)(2,1)}) custom-call(s32[3]{0:T(128)} %pad_add_fusion.place_ref, bf16[640,1024]{1,0:T(8,128)(2,1)} %get-tuple-element.149.own_ref.rows_ref, f32[8,1024]{1,0:T(8,128)} %get-tuple-element.155.vec_ref, f32[640,1024]{1,0:T(8,128)} %get-tuple-element.176.own_ref, f32[640,1024]{1,0:T(8,128)} %copy-done.2, ...), custom_call_target="tpu_custom_call" | custom-call | bytes 10422272 | tf_op jit(solution)/shard_map/norm_back/pallas_call | solution.py:111
  519.2 12.5 %collective-permute-start.58 = (bf16[128,512]{1,0:T(8,128)(2,1)}, bf16[128,512]{1,0:T(8,128)(2,1)S(1)}, u32[]{:S(2)}, u32[]{:S(2)}) collective-permute-start(bf16[128,512]{1,0:T(8,128)(2,1)} %get-tuple-element.214), channel_id=1, source_target_pairs={{0,24},{8,0},{16,8},{24,16},{1,25},{9,1},{17,9},{25,17},{2,26},{10... | collective-permute-start | bytes 393224 | tf_op jit(solution)/shard_map/ppermute | solution.py:35
  543.3 16.0 %collective-permute-done.61.refs_19_ = bf16[128,512]{1,0:T(8,128)(2,1)S(1)} collective-permute-done((bf16[128,512]{1,0:T(8,128)(2,1)}, bf16[128,512]{1,0:T(8,128)(2,1)S(1)}, u32[]{:S(2)}, u32[]{:S(2)}) %collective-permute-start.61) | collective-permute-done | bytes 131104 | tf_op jit(solution)/shard_map/ppermute | solution.py:44
  566.1 8.8 %statistics.3 = (f32[128,4096]{1,0:T(8,128)}, f32[512,1024]{1,0:T(8,128)}, f32[128,1024]{1,0:T(8,128)}, f32[1,128]{1,0:T(1,128)}, f32[1,512]{1,0:T(1,128)}, /*index=5*/f32[1,128]{1,0:T(1,128)}, f32[2,6528]{1,0:T(2,128)}) custom-call(s32[3]{0:T(128)} %pad_add_fusion.place_ref, bf16[8,128,256]{2,1,0:T(8,128)(2,1)} %fold_z.5.refs_0_.refs_8_, ...), custom_call_target="tpu_custom_call" | custom-call | bytes 18408448 | tf_op jit(solution)/shard_map/statistics/pallas_call | solution.py:111
  594.2 7.4 %update.3 = (f32[128,4096]{1,0:T(8,128)}, f32[512,1024]{1,0:T(8,128)}, f32[128,1024]{1,0:T(8,128)}, f32[1,4096]{1,0:T(1,128)}, f32[1,1024]{1,0:T(1,128)}, /*index=5*/f32[1,1024]{1,0:T(1,128)}, f32[16,128]{1,0:T(8,128)}) custom-call(s32[3]{0:T(128)} %pad_add_fusion.place_ref, f32[128,4096]{1,0:T(8,128)} %get-tuple-element.116.refs_0_, ...), custom_call_target="tpu_custom_call" | custom-call | bytes 14268416 | tf_op jit(solution)/shard_map/update/pallas_call | solution.py:111
  613.1 7.9 %stack.19 = f32[12]{0:T(128)} concatenate(f32[1]{0:T(128)} %bitcast.59, f32[1]{0:T(128)} %bitcast.60, f32[1]{0:T(128)} %bitcast.61, f32[1]{0:T(128)} %bitcast.62, f32[1]{0:T(128)} %bitcast.63, f32[1]{0:T(128)} %bitcast.64, f32[1]{0:T(128)} %bitcast.65, f32[1]{0:T(128)} %bitcast.66, f32[1]{0:T(128)} %bitcast.67, f32[1]{0:T(128)} %bitcast.68, f32[1]{0:T(128)} %bitcast.69, f32[1]{0:T(128)} %bitcast.70), dimensions={0} | concatenate | bytes 96 | tf_op jit(solution)/shard_map/stack | solution.py:1396
  (208 shorter events, 121.8 us)
Async XLA Ops:
  9.4 39.2 %collective-permute-start.4 = (bf16[144,1536]{1,0:T(8,128)(2,1)}, bf16[144,1536]{1,0:T(8,128)(2,1)S(1)}, u32[]{:S(2)}, u32[]{:S(2)}) collective-permute-start(bf16[144,1536]{1,0:T(8,128)(2,1)} %prepare_qkv.1.refs_0_), channel_id=1, source_target_pairs={{0,16},{8,24},{16,0},{24,8},{1,17},{9,25},{17,1},{25,9},{2,18},{10... | collective-permute-start | bytes 1327112 | tf_op jit(solution)/shard_map/ppermute | solution.py:35
  15.1 103.1 %collective-permute-start = (bf16[640,1024]{1,0:T(8,128)(2,1)}, bf16[640,1024]{1,0:T(8,128)(2,1)S(1)}, u32[]{:S(2)}, u32[]{:S(2)}) collective-permute-start(bf16[640,1024]{1,0:T(8,128)(2,1)} %get-tuple-element.149.own_ref.rows_ref), channel_id=1, source_target_pairs={{0,1},{1,0},{2,3},{3,2},{4,5},{5,4},{6,7},{7,6},{8,9},{9,8},{10,11... | collective-permute-start | bytes 3932168 | tf_op jit(solution)/shard_map/ppermute | solution.py:30
  15.1 34.9 %collective-permute-start.2 = (bf16[144,1536]{1,0:T(8,128)(2,1)S(1)}, bf16[144,1536]{1,0:T(8,128)(2,1)S(1)}, u32[]{:S(2)}, u32[]{:S(2)}) collective-permute-start(bf16[144,1536]{1,0:T(8,128)(2,1)S(1)} %copy-done.12), channel_id=1, source_target_pairs={{0,8},{8,16},{16,24},{24,0},{1,9},{9,17},{17,25},{25,1},{2,10},{10... | collective-permute-start | bytes 1327112 | tf_op jit(solution)/shard_map/ppermute | solution.py:35
  16.2 62.5 %collective-permute-start.14 = (bf16[10,128,256]{2,1,0:T(8,128)(2,1)}, bf16[10,128,256]{2,1,0:T(8,128)(2,1)S(1)}, u32[]{:S(2)}, u32[]{:S(2)}) collective-permute-start(bf16[10,128,256]{2,1,0:T(8,128)(2,1)} %get-tuple-element.154.refs_0_), channel_id=1, source_target_pairs={{0,24},{8,0},{16,8},{24,16},{1,25},{9,1},{17,9},{25,17},{2,26},{10... | collective-permute-start | bytes 1966088 | tf_op jit(solution)/shard_map/ppermute | solution.py:35
  20.3 83.3 %collective-permute-start.12 = (bf16[10,128,256]{2,1,0:T(8,128)(2,1)}, bf16[10,128,256]{2,1,0:T(8,128)(2,1)S(1)}, u32[]{:S(2)}, u32[]{:S(2)}) collective-permute-start(bf16[10,128,256]{2,1,0:T(8,128)(2,1)} %get-tuple-element.154.refs_0_), channel_id=1, source_target_pairs={{0,16},{8,24},{16,0},{24,8},{1,17},{9,25},{17,1},{25,9},{2,18},{10... | collective-permute-start | bytes 1966088 | tf_op jit(solution)/shard_map/ppermute | solution.py:35
  50.1 55.0 %collective-permute-start.10 = (bf16[10,128,256]{2,1,0:T(8,128)(2,1)}, bf16[10,128,256]{2,1,0:T(8,128)(2,1)}, u32[]{:S(2)}, u32[]{:S(2)}) collective-permute-start(bf16[10,128,256]{2,1,0:T(8,128)(2,1)} %get-tuple-element.154.refs_0_), channel_id=1, source_target_pairs={{0,8},{8,16},{16,24},{24,0},{1,9},{9,17},{17,25},{25,1},{2,10},{10... | collective-permute-start | bytes 1966088 | tf_op jit(solution)/shard_map/ppermute | solution.py:35
  105.1 53.5 %collective-permute-start.9 = (bf16[10,128,256]{2,1,0:T(8,128)(2,1)}, bf16[10,128,256]{2,1,0:T(8,128)(2,1)}, u32[]{:S(2)}, u32[]{:S(2)}) collective-permute-start(bf16[10,128,256]{2,1,0:T(8,128)(2,1)} %get-tuple-element.154.refs_0_), channel_id=1, source_target_pairs={{0,4},{4,0},{1,5},{5,1},{2,6},{6,2},{3,7},{7,3},{8,12},{12,8},{9,1... | collective-permute-start | bytes 1966088 | tf_op jit(solution)/shard_map/ppermute | solution.py:30
  105.6 53.5 %collective-permute-start.15 = (bf16[10,128,256]{2,1,0:T(8,128)(2,1)S(1)}, bf16[10,128,256]{2,1,0:T(8,128)(2,1)}, u32[]{:S(2)}, u32[]{:S(2)}) collective-permute-start(bf16[10,128,256]{2,1,0:T(8,128)(2,1)S(1)} %collective-permute-done.14.refs_6_), channel_id=1, source_target_pairs={{0,4},{4,0},{1,5},{5,1},{2,6},{6,2},{3,7},{7,3},{8,12},{12,8},{9,1... | collective-permute-start | bytes 1966088 | tf_op jit(solution)/shard_map/ppermute | solution.py:30
  107.1 52.0 %collective-permute-start.13 = (bf16[10,128,256]{2,1,0:T(8,128)(2,1)S(1)}, bf16[10,128,256]{2,1,0:T(8,128)(2,1)}, u32[]{:S(2)}, u32[]{:S(2)}) collective-permute-start(bf16[10,128,256]{2,1,0:T(8,128)(2,1)S(1)} %collective-permute-done.12.refs_4_), channel_id=1, source_target_pairs={{0,4},{4,0},{1,5},{5,1},{2,6},{6,2},{3,7},{7,3},{8,12},{12,8},{9,1... | collective-permute-start | bytes 1966088 | tf_op jit(solution)/shard_map/ppermute | solution.py:30
  116.7 54.2 %collective-permute-start.11 = (bf16[10,128,256]{2,1,0:T(8,128)(2,1)}, bf16[10,128,256]{2,1,0:T(8,128)(2,1)}, u32[]{:S(2)}, u32[]{:S(2)}) collective-permute-start(bf16[10,128,256]{2,1,0:T(8,128)(2,1)} %collective-permute-done.10.refs_2_), channel_id=1, source_target_pairs={{0,4},{4,0},{1,5},{5,1},{2,6},{6,2},{3,7},{7,3},{8,12},{12,8},{9,1... | collective-permute-start | bytes 1966088 | tf_op jit(solution)/shard_map/ppermute | solution.py:30
  158.6 52.5 %collective-permute-start.8 = (bf16[2,640,512]{2,1,0:T(8,128)(2,1)}, bf16[2,640,512]{2,1,0:T(8,128)(2,1)S(1)}, u32[]{:S(2)}, u32[]{:S(2)}) collective-permute-start(bf16[2,640,512]{2,1,0:T(8,128)(2,1)} %get-tuple-element.153.mine_ref), channel_id=1, source_target_pairs={{0,1},{1,0},{2,3},{3,2},{4,5},{5,4},{6,7},{7,6},{8,9},{9,8},{10,11... | collective-permute-start | bytes 3932168 | tf_op jit(solution)/shard_map/ppermute | solution.py:30
  158.6 63.4 %collective-permute-start.17 = (bf16[640,1024]{1,0:T(8,128)(2,1)S(1)}, bf16[640,1024]{1,0:T(8,128)(2,1)}, u32[]{:S(2)}, u32[]{:S(2)}) collective-permute-start(bf16[640,1024]{1,0:T(8,128)(2,1)S(1)} %copy-done.6), channel_id=1, source_target_pairs={{0,1},{1,0},{2,3},{3,2},{4,5},{5,4},{6,7},{7,6},{8,9},{9,8},{10,11... | collective-permute-start | bytes 3932168 | tf_op jit(solution)/shard_map/ppermute | solution.py:30
  173.9 35.7 %collective-permute-start.16 = (bf16[1024,512]{1,0:T(8,128)(2,1)}, bf16[1024,512]{1,0:T(8,128)(2,1)S(1)}, u32[]{:S(2)}, u32[]{:S(2)}) collective-permute-start(bf16[1024,512]{1,0:T(8,128)(2,1)} %gather_out.1.wm_ref), channel_id=1, source_target_pairs={{0,1},{1,0},{2,3},{3,2},{4,5},{5,4},{6,7},{7,6},{8,9},{9,8},{10,11... | collective-permute-start | bytes 3145736 | tf_op jit(solution)/shard_map/ppermute | solution.py:30
  174.1 35.0 %collective-permute-start.19 = (bf16[8,128,256]{2,1,0:T(8,128)(2,1)}, bf16[8,128,256]{2,1,0:T(8,128)(2,1)}, u32[]{:S(2)}, u32[]{:S(2)}) collective-permute-start(bf16[8,128,256]{2,1,0:T(8,128)(2,1)} %get-tuple-element.160.refs_0_), channel_id=1, source_target_pairs={{0,8},{8,16},{16,24},{24,0},{1,9},{9,17},{17,25},{25,1},{2,10},{10... | collective-permute-start | bytes 1572872 | tf_op jit(solution)/shard_map/ppermute | solution.py:35
  207.6 50.7 %collective-permute-start.18 = (bf16[8,128,256]{2,1,0:T(8,128)(2,1)}, bf16[8,128,256]{2,1,0:T(8,128)(2,1)}, u32[]{:S(2)}, u32[]{:S(2)}) collective-permute-start(bf16[8,128,256]{2,1,0:T(8,128)(2,1)} %get-tuple-element.160.refs_0_), channel_id=1, source_target_pairs={{0,4},{4,0},{1,5},{5,1},{2,6},{6,2},{3,7},{7,3},{8,12},{12,8},{9,1... | collective-permute-start | bytes 1572872 | tf_op jit(solution)/shard_map/ppermute | solution.py:30
  209.1 49.2 %collective-permute-start.24 = (bf16[8,128,256]{2,1,0:T(8,128)(2,1)}, bf16[8,128,256]{2,1,0:T(8,128)(2,1)}, u32[]{:S(2)}, u32[]{:S(2)}) collective-permute-start(bf16[8,128,256]{2,1,0:T(8,128)(2,1)} %collective-permute-done.23.refs_6_), channel_id=1, source_target_pairs={{0,4},{4,0},{1,5},{5,1},{2,6},{6,2},{3,7},{7,3},{8,12},{12,8},{9,1... | collective-permute-start | bytes 1572872 | tf_op jit(solution)/shard_map/ppermute | solution.py:30
  209.6 48.7 %collective-permute-start.22 = (bf16[8,128,256]{2,1,0:T(8,128)(2,1)}, bf16[8,128,256]{2,1,0:T(8,128)(2,1)}, u32[]{:S(2)}, u32[]{:S(2)}) collective-permute-start(bf16[8,128,256]{2,1,0:T(8,128)(2,1)} %collective-permute-done.21.refs_4_), channel_id=1, source_target_pairs={{0,4},{4,0},{1,5},{5,1},{2,6},{6,2},{3,7},{7,3},{8,12},{12,8},{9,1... | collective-permute-start | bytes 1572872 | tf_op jit(solution)/shard_map/ppermute | solution.py:30
  211.1 47.2 %collective-permute-start.20 = (bf16[8,128,256]{2,1,0:T(8,128)(2,1)}, bf16[8,128,256]{2,1,0:T(8,128)(2,1)}, u32[]{:S(2)}, u32[]{:S(2)}) collective-permute-start(bf16[8,128,256]{2,1,0:T(8,128)(2,1)} %collective-permute-done.19.refs_2_), channel_id=1, source_target_pairs={{0,4},{4,0},{1,5},{5,1},{2,6},{6,2},{3,7},{7,3},{8,12},{12,8},{9,1... | collective-permute-start | bytes 1572872 | tf_op jit(solution)/shard_map/ppermute | solution.py:30
  318.5 56.7 %collective-permute-start.48 = (bf16[4,8,128,256]{3,2,1,0:T(8,128)(2,1)}, bf16[4,8,128,256]{3,2,1,0:T(8,128)(2,1)}, u32[]{:S(2)}, u32[]{:S(2)}) collective-permute-start(bf16[4,8,128,256]{3,2,1,0:T(8,128)(2,1)} %get-tuple-element.204), channel_id=1, source_target_pairs={{0,4},{4,0},{1,5},{5,1},{2,6},{6,2},{3,7},{7,3},{8,12},{12,8},{9,1... | collective-permute-start | bytes 6291464 | tf_op jit(solution)/shard_map/ppermute | solution.py:30
  319.4 92.8 %collective-permute-start.41 = (bf16[4,8,128,256]{3,2,1,0:T(8,128)(2,1)}, bf16[4,8,128,256]{3,2,1,0:T(8,128)(2,1)}, u32[]{:S(2)}, u32[]{:S(2)}) collective-permute-start(bf16[4,8,128,256]{3,2,1,0:T(8,128)(2,1)} %get-tuple-element.198), channel_id=1, source_target_pairs={{0,4},{4,0},{1,5},{5,1},{2,6},{6,2},{3,7},{7,3},{8,12},{12,8},{9,1... | collective-permute-start | bytes 6291464 | tf_op jit(solution)/shard_map/ppermute | solution.py:30
  374.9 125.8 %collective-permute-start.28 = (f32[640,1024]{1,0:T(8,128)}, f32[640,1024]{1,0:T(8,128)S(1)}, u32[]{:S(2)}, u32[]{:S(2)}) collective-permute-start(f32[640,1024]{1,0:T(8,128)} %get-tuple-element.177), channel_id=1, source_target_pairs={{0,1},{1,0},{2,3},{3,2},{4,5},{5,4},{6,7},{7,6},{8,9},{9,8},{10,11... | collective-permute-start | bytes 7864328 | tf_op jit(solution)/shard_map/ppermute | solution.py:30
  379.7 37.0 %collective-permute-start.49 = (bf16[8,128,256]{2,1,0:T(8,128)(2,1)}, bf16[8,128,256]{2,1,0:T(8,128)(2,1)S(1)}, u32[]{:S(2)}, u32[]{:S(2)}) collective-permute-start(bf16[8,128,256]{2,1,0:T(8,128)(2,1)} %get-tuple-element.206), channel_id=1, source_target_pairs={{0,8},{8,16},{16,24},{24,0},{1,9},{9,17},{17,25},{25,1},{2,10},{10... | collective-permute-start | bytes 1572872 | tf_op jit(solution)/shard_map/ppermute | solution.py:35
  379.7 39.0 %collective-permute-start.50 = (bf16[8,128,256]{2,1,0:T(8,128)(2,1)}, bf16[8,128,256]{2,1,0:T(8,128)(2,1)S(1)}, u32[]{:S(2)}, u32[]{:S(2)}) collective-permute-start(bf16[8,128,256]{2,1,0:T(8,128)(2,1)} %get-tuple-element.207), channel_id=1, source_target_pairs={{0,16},{8,24},{16,0},{24,8},{1,17},{9,25},{17,1},{25,9},{2,18},{10... | collective-permute-start | bytes 1572872 | tf_op jit(solution)/shard_map/ppermute | solution.py:35
  390.8 88.6 %collective-permute-start.29 = (bf16[4,128,1536]{2,1,0:T(8,128)(2,1)}, bf16[4,128,1536]{2,1,0:T(8,128)(2,1)}, u32[]{:S(2)}, u32[]{:S(2)}) collective-permute-start(bf16[4,128,1536]{2,1,0:T(8,128)(2,1)} %get-tuple-element.182), channel_id=1, source_target_pairs={{0,4},{4,0},{1,5},{5,1},{2,6},{6,2},{3,7},{7,3},{8,12},{12,8},{9,1... | collective-permute-start | bytes 4718600 | tf_op jit(solution)/shard_map/ppermute | solution.py:30
  418.7 44.5 %collective-permute-start.43 = (bf16[8,128,256]{2,1,0:T(8,128)(2,1)}, bf16[8,128,256]{2,1,0:T(8,128)(2,1)}, u32[]{:S(2)}, u32[]{:S(2)}) collective-permute-start(bf16[8,128,256]{2,1,0:T(8,128)(2,1)} %get-tuple-element.201), channel_id=1, source_target_pairs={{0,16},{8,24},{16,0},{24,8},{1,17},{9,25},{17,1},{25,9},{2,18},{10... | collective-permute-start | bytes 1572872 | tf_op jit(solution)/shard_map/ppermute | solution.py:35
  440.0 33.7 %collective-permute-start.44 = (bf16[8,128,256]{2,1,0:T(8,128)(2,1)}, bf16[8,128,256]{2,1,0:T(8,128)(2,1)}, u32[]{:S(2)}, u32[]{:S(2)}) collective-permute-start(bf16[8,128,256]{2,1,0:T(8,128)(2,1)} %get-tuple-element.202), channel_id=1, source_target_pairs={{0,24},{8,0},{16,8},{24,16},{1,25},{9,1},{17,9},{25,17},{2,26},{10... | collective-permute-start | bytes 1572872 | tf_op jit(solution)/shard_map/ppermute | solution.py:35
  443.5 35.2 %collective-permute-start.54 = (bf16[8,128,256]{2,1,0:T(8,128)(2,1)}, bf16[8,128,256]{2,1,0:T(8,128)(2,1)S(1)}, u32[]{:S(2)}, u32[]{:S(2)}) collective-permute-start(bf16[8,128,256]{2,1,0:T(8,128)(2,1)} %fold_z.6.refs_4_.refs_12_), channel_id=1, source_target_pairs={{0,3},{1,2},{2,1},{3,0},{4,7},{5,6},{6,5},{7,4},{8,11},{9,10},{10,... | collective-permute-start | bytes 1572872 | tf_op jit(solution)/shard_map/ppermute | solution.py:44
  498.2 34.3 %collective-permute-start.32 = (bf16[128,1536]{1,0:T(8,128)(2,1)}, bf16[128,1536]{1,0:T(8,128)(2,1)}, u32[]{:S(2)}, u32[]{:S(2)}) collective-permute-start(bf16[128,1536]{1,0:T(8,128)(2,1)} %get-tuple-element.186), channel_id=1, source_target_pairs={{0,24},{8,0},{16,8},{24,16},{1,25},{9,1},{17,9},{25,17},{2,26},{10... | collective-permute-start | bytes 1179656 | tf_op jit(solution)/shard_map/ppermute | solution.py:35
  500.7 41.5 %collective-permute-start.45 = (bf16[8,128,256]{2,1,0:T(8,128)(2,1)S(1)}, bf16[8,128,256]{2,1,0:T(8,128)(2,1)}, u32[]{:S(2)}, u32[]{:S(2)}) collective-permute-start(bf16[8,128,256]{2,1,0:T(8,128)(2,1)S(1)} %copy-done.1), channel_id=1, source_target_pairs={{0,2},{2,0},{1,3},{3,1},{4,6},{6,4},{5,7},{7,5},{8,10},{10,8},{9,1... | collective-permute-start | bytes 1572872 | tf_op jit(solution)/shard_map/ppermute | solution.py:30
  536.6 44.9 %collective-permute-start.35 = (bf16[128,1536]{1,0:T(8,128)(2,1)}, bf16[128,1536]{1,0:T(8,128)(2,1)S(1)}, u32[]{:S(2)}, u32[]{:S(2)}) collective-permute-start(bf16[128,1536]{1,0:T(8,128)(2,1)} %fold_z.4.refs_0_), channel_id=1, source_target_pairs={{0,3},{1,2},{2,1},{3,0},{4,7},{5,6},{6,5},{7,4},{8,11},{9,10},{10,... | collective-permute-start | bytes 1179656 | tf_op jit(solution)/shard_map/ppermute | solution.py:44
  536.6 44.9 %collective-permute-start.34 = (bf16[128,1536]{1,0:T(8,128)(2,1)}, bf16[128,1536]{1,0:T(8,128)(2,1)S(1)}, u32[]{:S(2)}, u32[]{:S(2)}) collective-permute-start(bf16[128,1536]{1,0:T(8,128)(2,1)} %fold_z.4.refs_0_), channel_id=1, source_target_pairs={{0,1},{1,0},{2,3},{3,2},{4,5},{5,4},{6,7},{7,6},{8,9},{9,8},{10,11... | collective-permute-start | bytes 1179656 | tf_op jit(solution)/shard_map/ppermute | solution.py:30
  538.2 43.3 %collective-permute-start.33 = (bf16[128,1536]{1,0:T(8,128)(2,1)}, bf16[128,1536]{1,0:T(8,128)(2,1)S(1)}, u32[]{:S(2)}, u32[]{:S(2)}) collective-permute-start(bf16[128,1536]{1,0:T(8,128)(2,1)} %fold_z.4.refs_0_), channel_id=1, source_target_pairs={{0,2},{2,0},{1,3},{3,1},{4,6},{6,4},{5,7},{7,5},{8,10},{10,8},{9,1... | collective-permute-start | bytes 1179656 | tf_op jit(solution)/shard_map/ppermute | solution.py:30
  (67 other events, 1122.2 us)

commit v4 on v3

--- a/solution.py
+++ b/solution.py
@@ -53,22 +53,22 @@
     return value
 
 
-def gather_pieces(shard):
-    along = [shard] + [shift(shard, "z", k) for k in range(1, lax.axis_size("z"))]
-    pieces = []
-    for near in along:
-        pieces += [near, swap(near, "x")]
-    return pieces
-
-
-def scatter_sum(place, keep, send):
-    size = lax.axis_size("z")
-    held, *parts = fold_x(place, keep, swap(send, "x"))
-    mine = fold_z(place, held, [shift(parts[k - 1], "z", k) for k in range(1, size)])
+def gather_rows(shard, by_y):
+    near = lax.all_gather(shard, "z", axis=0, tiled=True)
+    near = near.reshape(lax.axis_size("z"), *shard.shape)
+    both = [near, swap(near, "x")]
+    if not by_y:
+        return [[one] for one in both]
+    return [[one, swap(one, "y")] for one in both]
+
+
+def scatter_sum(keep, send):
+    total = low(wide(keep) + wide(swap(send, "x")))
+    total = total.reshape(-1, total.shape[-1])
+    mine = lax.psum_scatter(total, "z", scatter_dimension=0, tiled=True)
     if lax.axis_size("y") == 2:
-        mine = low(mine)
         return [mine, swap(mine, "y")], [swap(mine, "c"), swap_both(mine)]
-    total = lax.psum(mine, "y")
+    total = lax.psum(wide(mine), "y")
     return [total], [swap(total, "c")]
 
 
@@ -126,11 +126,8 @@
     )(place, *ins)
 
 
-def shard_of(place_ref, number, z_size):
-    k, dx = number // 2, number % 2
-    z = lax.rem(place_ref[0] + (z_size - k), z_size)
-    x = dx + (1 - 2 * dx) * place_ref[1]
-    return z, x
+def shard_number(place_ref, z, dx):
+    return z * 2 + dx + (1 - 2 * dx) * place_ref[1]
 
 
 def normalised(rows):
@@ -145,11 +142,13 @@
 
 def prepare_qkv(place, weight, vectors):
     part, cols = weight.shape
+    width = cols // 2
     half = cols // 6
+    parts = 2
     sizes = [vector.shape[-1] for vector in vectors]
 
     def body(place_ref, weight_ref, *refs):
-        out_ref = refs[-1]
+        refs, (out_ref, *halves) = refs[: len(sizes)], (refs[-1], *refs[len(sizes) : -1])
         core = place_ref[2]
         for slot in range(3):
             at = 2 * slot * half
@@ -160,67 +159,69 @@
         for ref, size in zip(refs, sizes):
             out_ref[part:, at : at + size] = low(jnp.broadcast_to(ref[...], (TILE, size)))
             at += size
-
-    shape = (part + TILE, cols // 2)
+        for number, ref in enumerate(halves):
+            ref[...] = out_ref[:, number * width // parts : (number + 1) * width // parts]
+
+    shape = (part + TILE, width // parts)
     return call(
         body,
         place,
         (weight, *vectors),
         [whole((part, cols))] + [whole((1, size)) for size in sizes],
-        [sds(shape, jnp.bfloat16)],
-        [whole(shape)],
-        [],
+        [sds(shape, jnp.bfloat16)] * parts,
+        [whole(shape)] * parts,
+        [pltpu.VMEM((part + TILE, width), jnp.bfloat16)],
         "prepare_qkv",
-    )[0]
-
-
-def prepare_rest(place, in_weight, down_weight, out_weight, inputs, cotangent):
+    )
+
+
+def prepare_rest(place, in_weight, down_weight, out_weight, inputs, cotangent, by_y):
     part, hidden = in_weight.shape
     width = down_weight.shape[1]
     per_core = down_weight.shape[0] // 2
     per_shard = per_core // CHUNKS
     shards = hidden // (2 * per_core)
-    block = per_shard * 2
-    blocks = shards // 2
     tokens = inputs.shape[0]
     length = row_pad(tokens)
     even = tokens // TILE * TILE
+    cut = 2 if by_y else 1
+    rows_in, rows_down, rows_out = part // cut, per_shard // cut, part // cut // 2
 
     def body(place_ref, in_ref, down_ref, out_w_ref, rows_ref, cot_ref, *refs):
-        pieces, (rows_out, cot_out, sum_ref) = refs[:CHUNKS], refs[CHUNKS:]
-        core = place_ref[2]
+        pieces, (rows_out_ref, cot_out, sum_ref) = refs[:CHUNKS], refs[CHUNKS:]
+        core, y = place_ref[2], place_ref[3]
+
+        def pick(ref, row, count, step, col, cols, by_row):
+            def of_core(r):
+                if by_row:
+                    return select(
+                        core, ref[r : r + count, col : col + cols], ref[r + step : r + step + count, col : col + cols]
+                    )
+                return select(
+                    core, ref[r : r + count, col : col + cols], ref[r : r + count, col + step : col + step + cols]
+                )
+
+            if cut == 1:
+                return low(of_core(row))
+            return low(select(y, of_core(row), of_core(row + count)))
+
         for j in range(CHUNKS):
             for s in range(shards):
                 at = s * 2 * per_core + j * per_shard
-                pieces[j][s // 2, :, (s % 2) * per_shard : (s % 2 + 1) * per_shard] = low(
-                    select(
-                        core,
-                        in_ref[:, at : at + per_shard],
-                        in_ref[:, at + per_core : at + per_core + per_shard],
-                    )
+                pieces[j][:rows_in, s * per_shard : (s + 1) * per_shard] = pick(
+                    in_ref, 0, rows_in, per_core, at, per_shard, False
                 )
-            at = j * per_shard
-            for b in range(width // block):
-                cols = slice(b * block, (b + 1) * block)
-                pieces[j][blocks + b] = low(
-                    select(
-                        core,
-                        down_ref[at : at + per_shard, cols],
-                        down_ref[at + per_core : at + per_core + per_shard, cols],
-                    )
-                )
+            pieces[j][rows_in : rows_in + rows_down, :] = pick(
+                down_ref, j * per_shard, rows_down, per_core, 0, width, True
+            )
         half = width // 2
-        for b in range(half // block):
-            at = b * block
-            pieces[0][blocks + width // block + b] = low(
-                select(
-                    core,
-                    out_w_ref[:, at : at + block],
-                    out_w_ref[:, half + at : half + at + block],
-                )
-            )
+        branch = pick(out_w_ref, 0, 2 * rows_out, half, 0, half, False)
+        for side in range(2):
+            pieces[0][rows_in + rows_down :, side * half : (side + 1) * half] = branch[
+                side * rows_out : (side + 1) * rows_out, :
+            ]
         row = lax.broadcasted_iota(jnp.int32, (length - even, width), 0)
-        for ref, to in ((rows_ref, rows_out), (cot_ref, cot_out)):
+        for ref, to in ((rows_ref, rows_out_ref), (cot_ref, cot_out)):
             to[:even, :] = ref[:even, :]
             last = jnp.zeros((length - even, width), jnp.float32)
             for extra in range(tokens - even):
@@ -229,9 +230,8 @@
             to[even:, :] = low(last)
         sum_ref[...] = jnp.sum(wide(cot_out[...]), axis=0, keepdims=True)
 
-    extra = width // 2 // block
-    counts = [blocks + width // block + (extra if j == 0 else 0) for j in range(CHUNKS)]
-    outs = [sds((count, part, block), jnp.bfloat16) for count in counts]
+    counts = [rows_in + rows_down + (rows_out if j == 0 else 0) for j in range(CHUNKS)]
+    outs = [sds((count, width), jnp.bfloat16) for count in counts]
     outs += [sds((length, width), jnp.bfloat16)] * 2 + [sds((1, width), jnp.float32)]
     ins = (in_weight, down_weight, out_weight, inputs, cotangent)
     return call(
@@ -250,10 +250,11 @@
 
 
 def project_qkv(place, rows, pieces, sizes):
-    count = len(pieces)
-    z_size = count // 2
-    cols = pieces[0].shape[1]
-    part = pieces[0].shape[0] - TILE
+    flat = [one for piece in pieces for (one,) in piece]
+    z_size, part, cols_part = flat[0].shape
+    part -= TILE
+    count = 2 * z_size
+    cols = cols_part * len(pieces)
     width = part * count
     heads = cols // 3
     length = rows[0].shape[0]
@@ -263,25 +264,22 @@
     blocks = count // 2
 
     def body(place_ref, own_ref, other_ref, *refs):
-        ins, refs = refs[:count], refs[count:]
+        ins, refs = refs[: len(flat)], refs[len(flat) :]
         normed_ref, q_ref, k_ref, v_ref, vec_ref, hidden_bias_ref, weight, packed, sem = refs
         core = place_ref[2]
         copies = []
         for number, ref in enumerate(ins):
-            z, x = shard_of(place_ref, number, z_size)
-            row = pl.multiple_of((z * 2 + x) * part, part)
-            for slot, copy in enumerate(
-                (
-                    pltpu.make_async_copy(
-                        ref.at[pl.ds(0, part), :], weight.at[pl.ds(row, part), :], sem.at[2 * number]
-                    ),
-                    pltpu.make_async_copy(
-                        ref.at[pl.ds(part, TILE), :], packed.at[z * 2 + x], sem.at[2 * number + 1]
-                    ),
-                )
-            ):
-                copy.start()
-                copies.append(copy)
+            lanes = pl.ds(number // 2 * cols_part, cols_part)
+            for z in range(z_size):
+                s = shard_number(place_ref, z, number % 2)
+                row = pl.multiple_of(s * part, part)
+                for source, to in (
+                    (ref.at[z, pl.ds(0, part), :], weight.at[pl.ds(row, part), lanes]),
+                    (ref.at[z, pl.ds(part, TILE), :], packed.at[s, :, lanes]),
+                ):
+                    copy = pltpu.make_async_copy(source, to, sem.at[len(copies)])
+                    copy.start()
+                    copies.append(copy)
         for copy in copies:
             copy.wait()
 
@@ -332,8 +330,8 @@
     return call(
         body,
         place,
-        (*rows, *pieces),
-        [whole((length, width))] * 2 + [any_spec()] * count,
+        (*rows, *flat),
+        [whole((length, width))] * 2 + [any_spec()] * len(flat),
         [sds((2, length, width), jnp.bfloat16)]
         + [part_out] * 3
         + [
@@ -346,7 +344,7 @@
         [
             pltpu.VMEM((width, cols), jnp.bfloat16),
             pltpu.VMEM((count, TILE, cols), jnp.bfloat16),
-            pltpu.SemaphoreType.DMA((2 * count,)),
+            pltpu.SemaphoreType.DMA((2 * z_size * len(flat),)),
         ],
         "project_qkv",
         flops=4 * length * width * cols,
@@ -354,37 +352,40 @@
 
 
 def gather_out(place, pieces, first):
-    count = len(pieces)
-    z_size = count // 2
-    total, part, block = pieces[0].shape
-    width = part * count
+    cut = len(pieces[0])
+    z_size, total, width = pieces[0][0].shape
+    rows = total - first
+    half = width // 2
+    part = width // (2 * z_size)
 
     def body(place_ref, *refs):
-        ins, out_ref, sem = refs[:count], refs[count], refs[count + 1]
+        ins, out_ref, sem = refs[: 2 * cut], refs[2 * cut], refs[2 * cut + 1]
         copies = []
         for number, ref in enumerate(ins):
-            z, x = shard_of(place_ref, number, z_size)
-            row = pl.multiple_of((z * 2 + x) * part, part)
-            for b in range(total - first):
-                copy = pltpu.make_async_copy(
-                    ref.at[first + b],
-                    out_ref.at[pl.ds(row, part), pl.ds(b * block, block)],
-                    sem.at[number * (total - first) + b],
-                )
-                copy.start()
-                copies.append(copy)
+            dx, h = number // cut, number % cut
+            y = h + (1 - 2 * h) * place_ref[3] if cut == 2 else 0
+            for z in range(z_size):
+                for side in range(2):
+                    row = shard_number(place_ref, z, dx) * part + (2 * y + side) * rows
+                    copy = pltpu.make_async_copy(
+                        ref.at[z, pl.ds(first, rows), pl.ds(side * half, half)],
+                        out_ref.at[pl.ds(pl.multiple_of(row, rows), rows), :],
+                        sem.at[len(copies)],
+                    )
+                    copy.start()
+                    copies.append(copy)
         for copy in copies:
             copy.wait()
 
-    shape = (width, (total - first) * block)
+    shape = (width, half)
     return call(
         body,
         place,
-        tuple(pieces),
-        [any_spec()] * count,
+        tuple(one for side in pieces for one in side),
+        [any_spec()] * (2 * cut),
         [sds(shape, jnp.bfloat16)],
         [whole(shape)],
-        [pltpu.SemaphoreType.DMA((count * (total - first),))],
+        [pltpu.SemaphoreType.DMA((2 * cut * z_size * 2,))],
         "gather_out",
     )[0]
 
@@ -543,18 +544,19 @@
 
 
 def feed_forward(place, normed, cotangent, pieces, bias, chunk, running):
-    count = len(pieces)
-    z_size = count // 2
-    _, part, wide_block = pieces[0].shape
-    half_blocks = bias.shape[1]
-    width = part * count
-    blocks = half_blocks + width // wide_block
+    cut = len(pieces[0])
+    z_size, _, width = pieces[0][0].shape
+    blocks, block = bias.shape[1], bias.shape[3]
+    hidden_width = blocks * block
+    part = width // (2 * z_size)
+    per_shard = hidden_width // (2 * z_size)
+    rows_in, rows_down = part // cut, per_shard // cut
+    in_block = block // per_shard
     _, length, _ = normed.shape
     first_call = running is None
 
     def body(place_ref, normed_ref, own_cot, other_cot, bias_ref, *refs):
-        ins = refs[:count]
-        refs = refs[count:]
+        ins, refs = refs[: 2 * cut], refs[2 * cut :]
         if not first_call:
             before, refs = refs[:4], refs[4:]
         out_own, out_other, gn_own, gn_other, bsum_ref, keep_ref, send_ref = refs[:7]
@@ -564,22 +566,22 @@
         def copies():
             made = []
             for number, ref in enumerate(ins):
-                z, x = shard_of(place_ref, number, z_size)
-                row = pl.multiple_of((z * 2 + x) * part, part)
-                row_in = pl.multiple_of(x * part, part)
-                for b in range(half_blocks):
-                    made.append(
-                        pltpu.make_async_copy(
-                            ref.at[b], w_in.at[b, pl.ds(row, part), :], sem.at[number * blocks + b]
+                dx, h = number // cut, number % cut
+                y = h + (1 - 2 * h) * place_ref[3] if cut == 2 else 0
+                for z in range(z_size):
+                    s = shard_number(place_ref, z, dx)
+                    for weight, at, rows, of_shard in (
+                        (w_in, 0, rows_in, part),
+                        (w_down, rows_in, rows_down, per_shard),
+                    ):
+                        row = pl.multiple_of(s * of_shard + y * rows, rows)
+                        made.append(
+                            pltpu.make_async_copy(
+                                ref.at[z, pl.ds(at, rows), :],
+                                weight.at[pl.ds(row, rows), :],
+                                sem.at[len(made)],
+                            )
                         )
-                    )
-                    made.append(
-                        pltpu.make_async_copy(
-                            ref.at[half_blocks + b],
-                            w_down.at[z, pl.ds(row_in, part), pl.ds(b * wide_block, wide_block)],
-                            sem.at[number * blocks + half_blocks + b],
-                        )
-                    )
             return made
 
         @pl.when(step == 0)
@@ -591,8 +593,9 @@
             for copy in copies():
                 copy.wait()
 
-        weight_in = w_in[step]
-        weight_down = w_down[step]
+        at_block = pl.multiple_of(step * block, block)
+        weight_in = w_in[:, pl.ds(at_block, block)]
+        weight_down = w_down[pl.ds(at_block, block), :]
         into = None
         down = None
         column_sum = None
@@ -631,19 +634,16 @@
         bsum_ref[0] = column_sum
         for z in range(z_size):
             for x in range(2):
-                k = lax.rem(z + z_size - place_ref[0], z_size)
                 dx = x + (1 - 2 * x) * place_ref[1]
                 at = (z * 2 + x) * part
-                grads[dx, k, step] = low(into[at : at + part, :])
-        for x in range(2):
-            k = lax.rem(step + z_size - place_ref[0], z_size)
+                grads[dx, z, :part, pl.ds(at_block, block)] = low(into[at : at + part, :])
+        for i in range(in_block):
+            s = step * in_block + i
+            z, x = s // 2, lax.rem(s, 2)
             dx = x + (1 - 2 * x) * place_ref[1]
-            for b in range(half_blocks):
-                grads[dx, k, half_blocks + b] = low(
-                    down[x * part : (x + 1) * part, b * wide_block : (b + 1) * wide_block]
-                )
-
-        @pl.when(step == half_blocks - 1)
+            grads[dx, z, part:, :] = low(down[i * per_shard : (i + 1) * per_shard, :])
+
+        @pl.when(step == blocks - 1)
         def _():
             for slot, ref in enumerate((keep_ref, send_ref)):
                 pltpu.make_async_copy(grads.at[slot], ref, out_sem.at[slot]).start()
@@ -651,32 +651,32 @@
                 pltpu.make_async_copy(grads.at[slot], ref, out_sem.at[slot]).wait()
 
     total = sds((length, width), jnp.float32)
-    piece_out = sds((z_size, blocks, part, wide_block), jnp.bfloat16)
+    piece_out = sds((z_size, part + per_shard, width), jnp.bfloat16)
     carried = () if first_call else tuple(running)
     return call(
         body,
         place,
-        (normed, *cotangent, bias, *pieces, *carried),
+        (normed, *cotangent, bias, *[one for side in pieces for one in side], *carried),
         [whole((2, length, width))]
         + [whole((length, width))] * 2
-        + [pl.BlockSpec((1, 1, 1, wide_block), lambda b, p: (chunk, b, 0, 0))]
-        + [any_spec()] * count
+        + [pl.BlockSpec((1, 1, 1, block), lambda b, p: (chunk, b, 0, 0))]
+        + [any_spec()] * (2 * cut)
         + [whole((length, width))] * len(carried),
-        [total] * 4 + [sds((half_blocks, 1, wide_block), jnp.float32)] + [piece_out] * 2,
+        [total] * 4 + [sds((blocks, 1, block), jnp.float32)] + [piece_out] * 2,
         [whole((length, width))] * 4
-        + [pl.BlockSpec((1, 1, wide_block), lambda b, p: (b, 0, 0))]
+        + [pl.BlockSpec((1, 1, block), lambda b, p: (b, 0, 0))]
         + [any_spec()] * 2,
         [
-            pltpu.VMEM((half_blocks, width, wide_block), jnp.bfloat16),
-            pltpu.VMEM((half_blocks, wide_block, width), jnp.bfloat16),
+            pltpu.VMEM((width, hidden_width), jnp.bfloat16),
+            pltpu.VMEM((hidden_width, width), jnp.bfloat16),
             pltpu.VMEM((width, 2 * length), jnp.bfloat16),
-            pltpu.VMEM((2, z_size, blocks, part, wide_block), jnp.bfloat16),
-            pltpu.SemaphoreType.DMA((count * blocks,)),
+            pltpu.VMEM((2, z_size, part + per_shard, width), jnp.bfloat16),
+            pltpu.SemaphoreType.DMA((4 * cut * z_size,)),
             pltpu.SemaphoreType.DMA((2,)),
         ],
         "feed_forward",
-        grid=(half_blocks,),
-        flops=24 * length * width * half_blocks * wide_block,
+        grid=(blocks,),
+        flops=24 * length * width * hidden_width,
     )
 
 
@@ -761,10 +761,9 @@
         term = dot(turned[:, :length], own_half[...]) + dot(turned[:, length:], other_half[...])
         for z in range(z_size):
             for x in range(2):
-                k = lax.rem(z + z_size - place_ref[0], z_size)
                 dx = x + (1 - 2 * x) * place_ref[1]
                 at = (z * 2 + x) * part
-                grads[dx, k] = low(term[at : at + part, :])
+                grads[dx, z] = low(term[at : at + part, :])
         for slot, ref in enumerate((keep_ref, send_ref)):
             pltpu.make_async_copy(grads.at[slot], ref, out_sem.at[slot]).start()
         for image, ref in enumerate((own_ref, other_ref)):
@@ -814,10 +813,9 @@
             term = dot(turned[:, :length], ref[0]) + dot(turned[:, length:], ref[1])
             for z in range(z_size):
                 for x in range(2):
-                    k = lax.rem(z + z_size - place_ref[0], z_size)
                     dx = x + (1 - 2 * x) * place_ref[1]
                     at = (z * 2 + x) * part
-                    grads[dx, k, :, slot * heads : (slot + 1) * heads] = low(
+                    grads[dx, z, :, slot * heads : (slot + 1) * heads] = low(
                         term[at : at + part, :]
                     )
             sum_ref[slot : slot + 1, :] = jnp.sum(wide(ref[0]), axis=0, keepdims=True) + jnp.sum(
@@ -849,25 +847,28 @@
 
 
 def qkv_back(place, grad_q, grad_k, grad_v, pieces):
-    count = len(pieces)
-    z_size = count // 2
-    cols = pieces[0].shape[1]
-    part = pieces[0].shape[0] - TILE
-    width = part * count
+    flat = [one for piece in pieces for (one,) in piece]
+    z_size, part, cols_part = flat[0].shape
+    part -= TILE
+    cols = cols_part * len(pieces)
+    width = 2 * z_size * part
     heads = cols // 3
     length = grad_q.shape[1]
 
     def body(place_ref, gq_ref, gk_ref, gv_ref, *refs):
-        ins, (own_ref, other_ref, weight, sem) = refs[:count], refs[count:]
+        ins, (own_ref, other_ref, weight, sem) = refs[: len(flat)], refs[len(flat) :]
         copies = []
         for number, ref in enumerate(ins):
-            z, x = shard_of(place_ref, number, z_size)
-            row = pl.multiple_of((z * 2 + x) * part, part)
-            copy = pltpu.make_async_copy(
-                ref.at[pl.ds(0, part), :], weight.at[pl.ds(row, part), :], sem.at[number]
-            )
-            copy.start()
-            copies.append(copy)
+            lanes = pl.ds(number // 2 * cols_part, cols_part)
+            for z in range(z_size):
+                row = pl.multiple_of(shard_number(place_ref, z, number % 2) * part, part)
+                copy = pltpu.make_async_copy(
+                    ref.at[z, pl.ds(0, part), :],
+                    weight.at[pl.ds(row, part), lanes],
+                    sem.at[len(copies)],
+                )
+                copy.start()
+                copies.append(copy)
         for copy in copies:
             copy.wait()
         for image, out_ref in enumerate((own_ref, other_ref)):
@@ -880,57 +881,17 @@
     return call(
         body,
         place,
-        (grad_q, grad_k, grad_v, *pieces),
-        [whole((2, length, heads))] * 3 + [any_spec()] * count,
+        (grad_q, grad_k, grad_v, *flat),
+        [whole((2, length, heads))] * 3 + [any_spec()] * len(flat),
         [sds((length, width), jnp.float32)] * 2,
         [whole((length, width))] * 2,
-        [pltpu.VMEM((width, cols), jnp.bfloat16), pltpu.SemaphoreType.DMA((count,))],
+        [
+            pltpu.VMEM((width, cols), jnp.bfloat16),
+            pltpu.SemaphoreType.DMA((z_size * len(flat),)),
+        ],
         "qkv_back",
         flops=4 * length * width * cols,
     )
-
-
-def fold_x(place, keep, got):
-    size = keep.shape[0]
-
-    def body(place_ref, keep_ref, got_ref, *outs):
-        for k, out in enumerate(outs):
-            total = wide(keep_ref[k]) + wide(got_ref[k])
-            out[...] = total if k == 0 else low(total)
-
-    rest = keep.shape[1:]
-    outs = [sds(rest, jnp.float32)] + [sds(rest, jnp.bfloat16)] * (size - 1)
-    return call(
-        body,
-        place,
-        (keep, got),
-        [whole(keep.shape)] * 2,
-        outs,
-        [whole(rest)] * size,
-        [],
-        "fold_x",
-    )
-
-
-def fold_z(place, held, got):
-    final = jnp.bfloat16 if lax.axis_size("y") == 2 else jnp.float32
-
-    def body(place_ref, held_ref, *refs):
-        total = held_ref[...]
-        for ref in refs[:-1]:
-            total = total + wide(ref[...])
-        refs[-1][...] = total.astype(final)
-
-    return call(
-        body,
-        place,
-        (held, *got),
-        [whole(held.shape)] * (1 + len(got)),
-        [sds(held.shape, final)],
-        [whole(held.shape)],
-        [],
-        "fold_z",
-    )[0]
 
 
 def to_column(row):
@@ -953,9 +914,14 @@
     )
 
 
-def statistics(place, kinds, shares, weights, states, images, extra=None):
-    flat = [a for chunks in shares for pair in chunks for side in pair for a in side]
-    counts = [[[len(side) for side in pair] for pair in chunks] for chunks in shares]
+def statistics(place, kinds, shares, weights, states, images, group, extra=None):
+    flat = []
+    places = []
+    for chunks in shares:
+        if not any(chunks is done for done, _ in places):
+            places.append((chunks, len(flat)))
+            flat += [a for pair in chunks for side in pair for a in side]
+    starts = [next(at for done, at in places if done is chunks) for chunks in shares]
     amount = len(kinds)
     vectors = 0 if extra is None else len(extra[1])
 
@@ -981,11 +947,12 @@
         for number, kind in enumerate(kinds):
             grad_ref, weight_ref = grad_refs[number], weight_refs[number]
             rows, cols = weights[number].shape
-            for chunk, pair in enumerate(counts[number]):
+            at_share = starts[number]
+            for chunk, pair in enumerate(shares[number]):
                 sides = []
-                for n in pair:
-                    sides.append(share_refs[:n])
-                    del share_refs[:n]
+                for side in pair:
+                    sides.append(share_refs[at_share : at_share + len(side)])
+                    at_share += len(side)
 
                 def halves(index):
                     mine, theirs = [
@@ -995,22 +962,18 @@
                     ]
                     return select(core, mine, theirs), select(core, theirs, mine)
 
-                shape = sides[0][0].shape
                 if kind == "in":
-                    blocks, _, block = cols // 2 // CHUNKS // shape[2], shape[1], shape[2]
-                    per = block // 2
-                    for b in range(blocks):
-                        for c, half in enumerate(halves(b)):
-                            for i in range(2):
-                                at = ((2 * b + i) * 2 + c) * CHUNKS * per + chunk * per
-                                grad_ref[:, at : at + per] = half[:, i * per : (i + 1) * per]
+                    per = cols // (2 * CHUNKS * group)
+                    for c, half in enumerate(halves((slice(0, rows), slice(None)))):
+                        for s in range(group):
+                            at = ((s * 2 + c) * CHUNKS + chunk) * per
+                            grad_ref[:, at : at + per] = half[:, s * per : (s + 1) * per]
                 elif kind == "down":
-                    _, part, block = shape
-                    first = shape[0] - cols // block
-                    for b in range(cols // block):
-                        for c, half in enumerate(halves(first + b)):
-                            at = (c * CHUNKS + chunk) * part
-                            grad_ref[at : at + part, b * block : (b + 1) * block] = half
+                    per = rows // (2 * CHUNKS)
+                    first = sides[0][0].shape[0] - per
+                    for c, half in enumerate(halves((slice(first, first + per), slice(None)))):
+                        at = (c * CHUNKS + chunk) * per
+                        grad_ref[at : at + per, :] = half
                 else:
                     groups = cols // (2 * SPLIT[kind])
                     for slot in range(SPLIT[kind]):
@@ -1276,9 +1239,8 @@
         in_bias_moment,
         down_bias_moment,
     ]
-    place = jnp.stack(
-        [lax.axis_index("z"), lax.axis_index("x"), lax.axis_index("c")]
-    ).astype(jnp.int32)
+    place = jnp.stack([lax.axis_index(axis) for axis in ("z", "x", "c", "y")]).astype(jnp.int32)
+    by_y = lax.axis_size("y") == 2
     group = lax.axis_size("z") * lax.axis_size("x")
     tokens = inputs.shape[0]
     images = (tokens // SEQ) * group * lax.axis_size("y") * lax.axis_size("c")
@@ -1287,13 +1249,13 @@
     moments = [as_row(moment) for moment in moments]
     sizes = [param.shape[1] for param in params]
 
-    pieces_qkv = gather_pieces(prepare_qkv(place, qkv_weight, params))
+    pieces_qkv = [gather_rows(one, False) for one in prepare_qkv(place, qkv_weight, params)]
     *shards_ff, rows_own, cot_own, down_sums = prepare_rest(
-        place, in_weight, down_weight, out_weight, inputs, cotangent
+        place, in_weight, down_weight, out_weight, inputs, cotangent, by_y
     )
     rows = (rows_own, swap(rows_own, "c"))
     cot = (cot_own, swap(cot_own, "c"))
-    pieces_ff = [gather_pieces(shard) for shard in shards_ff]
+    pieces_ff = [gather_rows(shard, by_y) for shard in shards_ff]
     weight_mine = gather_out(place, pieces_ff[0], shards_ff[1].shape[0])
     weight_theirs = swap(weight_mine, "c")
 
@@ -1313,7 +1275,7 @@
             place, normed_mid, cot, pieces_ff[j], hidden_bias, j, running
         )
         hidden_sums.append(sums)
-        shares_ff.append(scatter_sum(place, keep, send))
+        shares_ff.append(scatter_sum(keep, send))
     out_share, out_given, normed_share, normed_given = running
     sums_mid, output, grad_mid, grad_mid_low = norm_back(
         place,
@@ -1335,10 +1297,10 @@
         weight_mine,
         weight_theirs,
     )
-    share_out = scatter_sum(place, keep, send)
+    share_out = scatter_sum(keep, send)
     grad_q, grad_k, grad_v = attention_back(place, query, keys, values, probs, grad_attended)
     sums_qkv, keep, send = qkv_term(place, normed, grad_q, grad_k, grad_v)
-    share_qkv = scatter_sum(place, keep, send)
+    share_qkv = scatter_sum(keep, send)
     share, given = qkv_back(place, grad_q, grad_k, grad_v, pieces_qkv)
     sums_in, input_grad = norm_back(
         place, rows_own, vectors, GAIN_ONE, share, swap(given, "c"), grad_mid, tokens
@@ -1352,7 +1314,7 @@
     weights = [in_weight, down_weight, out_weight]
     states = [as_row(state) for state in (in_rows, down_rows, out_rows)]
     grads_early, rows_early, pack, _, _ = statistics(
-        place, early, [shares_ff, shares_ff, [share_out]], weights, states, images
+        place, early, [shares_ff, shares_ff, [share_out]], weights, states, images, group
     )
     new_early, cols_early, clips_early, _ = update(
         place,
@@ -1370,6 +1332,7 @@
         [qkv_weight],
         [as_row(qkv_rows)],
         images,
+        group,
         (terms, params, moments),
     )
     new_late, cols_late, clips_late, new_vectors = update(

time: 630 us -> 621 us (0.986)
  starting transfers between devices: 95.9 us -> 44.8 us
  blocking collectives: 0 us -> 37.8 us
  Pallas kernels: 273 us -> 245 us
  between operations: 1.56 us -> 15 us
  other arithmetic: 5.05 us -> 18.2 us
    ppermute x21 -> x0, waiting for transfers between devices: 140 us -> none  [shift(): lax.ppermute(value, axis, [(i, (i + step) % size) for i in range(size)])]
    ppermute x32 -> x28, waiting for transfers between devices: 58.9 us -> 187 us  [swap(): return lax.ppermute(value, axis, [(0, 1), (1, 0)])]
    ppermute x21 -> x0, starting transfers between devices: 56 us -> none  [shift(): lax.ppermute(value, axis, [(i, (i + step) % size) for i in range(size)])]
    all_gather x0 -> x2, blocking collectives: none -> 37.8 us  [gather_rows(): near = lax.all_gather(shard, 'z', axis=0, tiled=True)]
    all_gather x0 -> x2, waiting for transfers between devices: none -> 32 us  [gather_rows(): near = lax.all_gather(shard, 'z', axis=0, tiled=True)]
    pallas_call x27 -> x19, Pallas kernels: 273 us -> 245 us  [call(): pl.pallas_call(body, out_shape=outs, grid_spec=pltpu.PrefetchScalarGridSp...]
    ppermute x4, waiting for transfers between devices: 24.5 us -> 2.4 us  [swap_both(): return lax.ppermute(value, ('y', 'c'), [(i, 3 - i) for i in range(4)])]
    convert_element_type x0 -> x4, other arithmetic: none -> 13.1 us  [low(): return value.astype(jnp.bfloat16)]
  transfers between devices with their start and end apart: 68 -> 49, of which waited for: 22 -> 18; matrix products, arithmetic and copies ran while one was open for 1% -> 3% of each run, Pallas kernels for 35% -> 32%
where the time goes in v4:
time: 621 us; the launch traced here: 611 us
  Pallas kernels  245 us (39%)
  waiting for transfers between devices  232 us (37%)
  starting transfers between devices  44.8 us (7%)
  blocking collectives  37.8 us (6%)
  other arithmetic  18.2 us (3%)
  local copies, waits for them, and re-layouts  18.1 us (3%)
  between operations  15 us (2%)
    pallas_call x19, Pallas kernels, call(): pl.pallas_call(body, out_shape=outs, grid_spec=pltpu.PrefetchScalarGridSp...  245 us
    ppermute x28, waiting for transfers between devices, swap(): return lax.ppermute(value, axis, [(0, 1), (1, 0)])  187 us
    all_gather x2, blocking collectives, gather_rows(): near = lax.all_gather(shard, 'z', axis=0, tiled=True)  37.8 us
    all_gather x2, waiting for transfers between devices, gather_rows(): near = lax.all_gather(shard, 'z', axis=0, tiled=True)  32 us
    ppermute x28, starting transfers between devices, swap(): return lax.ppermute(value, axis, [(0, 1), (1, 0)])  24.8 us
    ppermute x11, starting transfers between devices, partner(): return lax.ppermute(value, axis, [(i, i ^ step) for i in range(size)])  17.5 us
    convert_element_type x4, other arithmetic, low(): return value.astype(jnp.bfloat16)  13.1 us
  transfers between devices with their start and end apart: 49, of which 18 were waited for; matrix products, arithmetic and copies ran while one was open for 3% of the time, Pallas kernels for 32%

profile of v4, /device:TPU:0, one launch (start us, length us, event | category | flops | bytes accessed | tf_op | source)
XLA Modules:
  0.0 611.1 jit_solution(6351521804395468944)
XLA Ops:
  7.9 5.6 prepare_rest.1
  17.1 32.0 %all-gather.3.cloned.1.call-done = bf16[640,1024]{1,0:T(8,128)(2,1)} async-done(((bf16[160,1024]{1,0:T(8,128)(2,1)}), bf16[640,1024]{1,0:T(8,128)(2,1)}) %all-gather.3.cloned.1.call-update) | async-done | bytes 1310736 | tf_op jit(solution)/shard_map/all_gather | solution.py:57
  50.5 18.9 %all_gather.13 = bf16[576,768]{1,0:T(8,128)(2,1)S(1)} all-gather(bf16[144,768]{1,0:T(8,128)(2,1)} %get-tuple-element.137), channel_id=1, replica_groups=mesh['z'=4,'x'=2,'y'=2,'c'=2] {'z'}, dimensions={0}, use_global_device_ids=true | all-gather | bytes 1105920 | tf_op jit(solution)/shard_map/all_gather | solution.py:57
  70.1 18.8 %all_gather.12 = bf16[576,768]{1,0:T(8,128)(2,1)S(1)} all-gather(bf16[144,768]{1,0:T(8,128)(2,1)} %get-tuple-element.136), channel_id=1, replica_groups=mesh['z'=4,'x'=2,'y'=2,'c'=2] {'z'}, dimensions={0}, use_global_device_ids=true | all-gather | bytes 1105920 | tf_op jit(solution)/shard_map/all_gather | solution.py:57
  92.8 7.2 %collective-permute-done.2.refs_3_ = bf16[4,144,768]{2,1,0:T(8,128)(2,1)} collective-permute-done((bf16[4,144,768]{2,1,0:T(8,128)(2,1)S(1)}, bf16[4,144,768]{2,1,0:T(8,128)(2,1)}, u32[]{:S(2)}, u32[]{:S(2)}) %collective-permute-start.2) | collective-permute-done | bytes 884768 | tf_op jit(solution)/shard_map/ppermute | solution.py:30
  100.1 17.1 %collective-permute-done.1.refs_1_ = bf16[4,144,768]{2,1,0:T(8,128)(2,1)} collective-permute-done((bf16[4,144,768]{2,1,0:T(8,128)(2,1)S(1)}, bf16[4,144,768]{2,1,0:T(8,128)(2,1)}, u32[]{:S(2)}, u32[]{:S(2)}) %collective-permute-start.1) | collective-permute-done | bytes 884768 | tf_op jit(solution)/shard_map/ppermute | solution.py:30
  117.2 11.0 %project_qkv.1 = (bf16[2,640,1024]{2,1,0:T(8,128)(2,1)}, bf16[2,640,512]{2,1,0:T(8,128)(2,1)}, bf16[2,640,512]{2,1,0:T(8,128)(2,1)}, bf16[2,640,512]{2,1,0:T(8,1...) custom-call(s32[4]{0:T(128)} %pad_add_fusion.place_ref, bf16[640,1024]{1,0:T(8,128)(2,1)} %get-tuple-element.135.own_ref.rows_ref, ...), custom_call_target="tpu_custom_call" | custom-call | flops 4026531840 | bytes 12754944 | tf_op jit(solution)/shard_map/project_qkv/pallas_call | solution.py:111
  128.2 28.2 %attention.1 = (bf16[2,640,512]{2,1,0:T(8,128)(2,1)}, bf16[2,4,2,640,640]{4,3,2,1,0:T(8,128)(2,1)}) custom-call(s32[4]{0:T(128)} %pad_add_fusion.place_ref, bf16[2,640,512]{2,1,0:T(8,128)(2,1)} %get-tuple-element.138.q_ref, bf16[2,640,512]{2,1,0:T(8,128)(2,1)} %get-tuple-element.139.k_ref, bf16[2,640,512]{2,1,0:T(8,128)(2,1)} %get-tuple-element.140.v_ref), custom_call_target="tpu_custom_call" | custom-call | flops 6710886400 | bytes 18350080 | tf_op jit(solution)/shard_map/attention/pallas_call | solution.py:111
  158.3 3.1 gather_out.1.wm_ref
  163.0 19.3 %collective-permute-done.10.refs_2_ = bf16[4,128,1024]{2,1,0:T(8,128)(2,1)} collective-permute-done((bf16[4,128,1024]{2,1,0:T(8,128)(2,1)}, bf16[4,128,1024]{2,1,0:T(8,128)(2,1)}, u32[]{:S(2)}, u32[]{:S(2)}) %collective-permute-start.10) | collective-permute-done | bytes 1048608 | tf_op jit(solution)/shard_map/ppermute | solution.py:30
  185.2 9.9 %project_out.1 = (f32[640,1024]{1,0:T(8,128)}, bf16[2,640,1024]{2,1,0:T(8,128)(2,1)}) custom-call(s32[4]{0:T(128)} %pad_add_fusion.place_ref, bf16[2,640,512]{2,1,0:T(8,128)(2,1)} %get-tuple-element.141.mine_ref, bf16[2,640,512]{2,1,0:T(8,128)(2,1)} %copy-done.4, bf16[1024,512]{1,0:T(8,128)(2,1)} %gather_out.1.wm_ref, bf16[1024,512]{1,0:T(8,128)(2,1)} %copy-done.6, ...), custom_call_target="tpu_custom_call" | custom-call | flops 2684354560 | bytes 12615680 | tf_op jit(solution)/shard_map/project_out/pallas_call | solution.py:111
  195.0 36.5 %feed_forward.2 = (f32[640,1024]{1,0:T(8,128)}, f32[640,1024]{1,0:T(8,128)}, f32[640,1024]{1,0:T(8,128)}, f32[640,1024]{1,0:T(8,128)}, f32[4,1,256]{2,1,0:T(1,12...) custom-call(s32[4]{0:T(128)} %pad_add_fusion.place_ref, ...), custom_call_target="tpu_custom_call" | custom-call | flops 16106127360 | bytes 25178112 | tf_op jit(solution)/shard_map/feed_forward/pallas_call | solution.py:111
  231.6 39.6 %feed_forward.3 = (f32[640,1024]{1,0:T(8,128)}, f32[640,1024]{1,0:T(8,128)}, f32[640,1024]{1,0:T(8,128)}, f32[640,1024]{1,0:T(8,128)}, f32[4,1,256]{2,1,0:T(1,12...) custom-call(s32[4]{0:T(128)} %pad_add_fusion.place_ref, ...), custom_call_target="tpu_custom_call" | custom-call | flops 16106127360 | bytes 34615296 | tf_op jit(solution)/shard_map/feed_forward/pallas_call | solution.py:111
  273.2 44.7 %collective-permute-done.29 = bf16[4,256,1024]{2,1,0:T(8,128)(2,1)S(1)} collective-permute-done((bf16[4,256,1024]{2,1,0:T(8,128)(2,1)}, bf16[4,256,1024]{2,1,0:T(8,128)(2,1)S(1)}, u32[]{:S(2)}, u32[]{:S(2)}) %collective-permute-start.29) | collective-permute-done | bytes 2097184 | tf_op jit(solution)/shard_map/ppermute | solution.py:30
  317.9 3.9 add_convert_fusion
  323.3 10.4 %norm_back.2 = (f32[8,1024]{1,0:T(8,128)}, bf16[577,1024]{1,0:T(8,128)(2,1)}, f32[640,1024]{1,0:T(8,128)}, bf16[640,1024]{1,0:T(8,128)(2,1)}) custom-call(s32[4]{0:T(128)} %pad_add_fusion.place_ref, f32[640,1024]{1,0:T(8,128)} %get-tuple-element.144.rows_ref, f32[8,1024]{1,0:T(8,128)} %get-tuple-element.143.vec_ref, f32[640,1024]{1,0:T(8,128)} %get-tuple-element.153.own_ref, ...), custom_call_target="tpu_custom_call" | custom-call | bytes 19597312 | tf_op jit(solution)/shard_map/norm_back/pallas_call | solution.py:111
  338.0 9.1 %out_back.1 = (bf16[2,640,512]{2,1,0:T(8,128)(2,1)}, bf16[4,128,512]{2,1,0:T(8,128)(2,1)}, bf16[4,128,512]{2,1,0:T(8,128)(2,1)}) custom-call(s32[4]{0:T(128)} %pad_add_fusion.place_ref, bf16[640,1024]{1,0:T(8,128)(2,1)} %get-tuple-element.159.own_ref.own_half, bf16[640,1024]{1,0:T(8,128)(2,1)} %copy-done, ...), custom_call_target="tpu_custom_call" | custom-call | flops 2684354560 | bytes 12320768 | tf_op jit(solution)/shard_map/out_back/pallas_call | solution.py:111
  348.7 44.5 %collective-permute-done.33 = bf16[4,128,512]{2,1,0:T(8,128)(2,1)S(1)} collective-permute-done((bf16[4,128,512]{2,1,0:T(8,128)(2,1)}, bf16[4,128,512]{2,1,0:T(8,128)(2,1)S(1)}, u32[]{:S(2)}, u32[]{:S(2)}) %collective-permute-start.33) | collective-permute-done | bytes 524320 | tf_op jit(solution)/shard_map/ppermute | solution.py:30
  395.5 3.9 add_convert_fusion.1
  399.5 32.2 %attention_back.1 = (bf16[2,640,512]{2,1,0:T(8,128)(2,1)}, bf16[2,640,512]{2,1,0:T(8,128)(2,1)}, bf16[2,640,512]{2,1,0:T(8,128)(2,1)}) custom-call(s32[4]{0:T(128)} %pad_add_fusion.place_ref, bf16[2,640,512]{2,1,0:T(8,128)(2,1)} %get-tuple-element.138.q_ref, bf16[2,640,512]{2,1,0:T(8,128)(2,1)} %get-tuple-element.139.k_ref, ...), custom_call_target="tpu_custom_call" | custom-call | flops 8388608000 | bytes 22282240 | tf_op jit(solution)/shard_map/attention_back/pallas_call | solution.py:111
  431.7 11.1 %qkv_term.1 = (f32[3,512]{1,0:T(4,128)}, bf16[4,128,1536]{2,1,0:T(8,128)(2,1)}, bf16[4,128,1536]{2,1,0:T(8,128)(2,1)}) custom-call(s32[4]{0:T(128)} %pad_add_fusion.place_ref, bf16[2,640,1024]{2,1,0:T(8,128)(2,1)} %get-tuple-element.168.normed_ref, bf16[2,640,512]{2,1,0:T(8,128)(2,1)} %get-tuple-element.161.gq_ref, ...), custom_call_target="tpu_custom_call" | custom-call | flops 4026531840 | bytes 9705472 | tf_op jit(solution)/shard_map/qkv_term/pallas_call | solution.py:111
  444.3 10.6 %qkv_back.1 = (f32[640,1024]{1,0:T(8,128)}, f32[640,1024]{1,0:T(8,128)}) custom-call(s32[4]{0:T(128)} %pad_add_fusion.place_ref, bf16[2,640,512]{2,1,0:T(8,128)(2,1)} %get-tuple-element.161.gq_ref, bf16[2,640,512]{2,1,0:T(8,128)(2,1)} %get-tuple-element.162.gk_ref, bf16[2,640,512]{2,1,0:T(8,128)(2,1)} %get-tuple-element.163.gv_ref, ...), custom_call_target="tpu_custom_call" | custom-call | flops 4026531840 | bytes 12713984 | tf_op jit(solution)/shard_map/qkv_back/pallas_call | solution.py:111
  455.0 24.1 %collective-permute-done.16 = bf16[4,128,1536]{2,1,0:T(8,128)(2,1)} collective-permute-done((bf16[4,128,1536]{2,1,0:T(8,128)(2,1)}, bf16[4,128,1536]{2,1,0:T(8,128)(2,1)}, u32[]{:S(2)}, u32[]{:S(2)}) %collective-permute-start.16) | collective-permute-done | bytes 1572896 | tf_op jit(solution)/shard_map/ppermute | solution.py:30
  479.2 3.4 add_convert_fusion.2
  486.0 8.2 %norm_back.3 = (f32[8,1024]{1,0:T(8,128)}, bf16[577,1024]{1,0:T(8,128)(2,1)}) custom-call(s32[4]{0:T(128)} %pad_add_fusion.place_ref, bf16[640,1024]{1,0:T(8,128)(2,1)} %get-tuple-element.135.own_ref.rows_ref, f32[8,1024]{1,0:T(8,128)} %get-tuple-element.143.vec_ref, f32[640,1024]{1,0:T(8,128)} %get-tuple-element.164.own_ref, f32[640,1024]{1,0:T(8,128)} %copy-done.1, ...), custom_call_target="tpu_custom_call" | custom-call | bytes 10422272 | tf_op jit(solution)/shard_map/norm_back/pallas_call | solution.py:111
  507.3 19.5 %collective-permute-done.34.refs_9_ = bf16[128,512]{1,0:T(8,128)(2,1)S(1)} collective-permute-done((bf16[128,512]{1,0:T(8,128)(2,1)S(1)}, bf16[128,512]{1,0:T(8,128)(2,1)S(1)}, u32[]{:S(2)}, u32[]{:S(2)}) %collective-permute-start.34) | collective-permute-done | bytes 131104 | tf_op jit(solution)/shard_map/ppermute | solution.py:30
  537.0 8.9 %collective-permute-done.26.refs_1_ = bf16[256,1024]{1,0:T(8,128)(2,1)S(1)} collective-permute-done((bf16[256,1024]{1,0:T(8,128)(2,1)}, bf16[256,1024]{1,0:T(8,128)(2,1)S(1)}, u32[]{:S(2)}, u32[]{:S(2)}) %collective-permute-start.26) | collective-permute-done | bytes 524320 | tf_op jit(solution)/shard_map/ppermute | solution.py:30
  546.6 8.2 %statistics.3 = (f32[128,4096]{1,0:T(8,128)}, f32[512,1024]{1,0:T(8,128)}, f32[128,1024]{1,0:T(8,128)}, f32[1,128]{1,0:T(1,128)}, f32[1,512]{1,0:T(1,128)}, /*index=5*/f32[1,128]{1,0:T(1,128)}, f32[2,6528]{1,0:T(2,128)}) custom-call(s32[4]{0:T(128)} %pad_add_fusion.place_ref, bf16[256,1024]{1,0:T(8,128)(2,1)} %reduce-scatter.7.cloned.1.call-done.refs_0_, ...), custom_call_target="tpu_custom_call" | custom-call | bytes 14214144 | tf_op jit(solution)/shard_map/statistics/pallas_call | solution.py:111
  565.0 4.5 statistics.2
  577.0 7.4 %update.3 = (f32[128,4096]{1,0:T(8,128)}, f32[512,1024]{1,0:T(8,128)}, f32[128,1024]{1,0:T(8,128)}, f32[1,4096]{1,0:T(1,128)}, f32[1,1024]{1,0:T(1,128)}, /*index=5*/f32[1,1024]{1,0:T(1,128)}, f32[16,128]{1,0:T(8,128)}) custom-call(s32[4]{0:T(128)} %pad_add_fusion.place_ref, f32[128,4096]{1,0:T(8,128)} %get-tuple-element.102.refs_0_, ...), custom_call_target="tpu_custom_call" | custom-call | bytes 14268416 | tf_op jit(solution)/shard_map/update/pallas_call | solution.py:111
  589.9 4.4 update.2
  595.9 7.9 %stack.23 = f32[12]{0:T(128)} concatenate(f32[1]{0:T(128)} %bitcast.68, f32[1]{0:T(128)} %bitcast.69, f32[1]{0:T(128)} %bitcast.70, f32[1]{0:T(128)} %bitcast.71, f32[1]{0:T(128)} %bitcast.72, f32[1]{0:T(128)} %bitcast.73, f32[1]{0:T(128)} %bitcast.74, f32[1]{0:T(128)} %bitcast.75, f32[1]{0:T(128)} %bitcast.76, f32[1]{0:T(128)} %bitcast.77, f32[1]{0:T(128)} %bitcast.78, f32[1]{0:T(128)} %bitcast.79), dimensions={0} | concatenate | bytes 96 | tf_op jit(solution)/shard_map/stack | solution.py:1359
  (154 shorter events, 82.2 us)
Async XLA Ops:
  7.2 41.8 %all-gather.3.cloned.1.call-start = ((), (), s32[]{:S(2)}) async-start(), calls=%async_computation.4 | async-start | bytes 1638400 | tf_op jit(solution)/shard_map/all_gather | solution.py:57
  13.5 143.3 %all-gather.5.cloned.1.call-start = ((), (), s32[]{:S(2)}) async-start(), calls=%async_computation.5 | async-start | bytes 1310720 | tf_op jit(solution)/shard_map/all_gather | solution.py:57
  13.6 103.6 %collective-permute-start = (bf16[640,1024]{1,0:T(8,128)(2,1)}, bf16[640,1024]{1,0:T(8,128)(2,1)}, u32[]{:S(2)}, u32[]{:S(2)}) collective-permute-start(bf16[640,1024]{1,0:T(8,128)(2,1)} %get-tuple-element.135.own_ref.rows_ref), channel_id=1, source_target_pairs={{0,1},{1,0},{2,3},{3,2},{4,5},{5,4},{6,7},{7,6},{8,9},{9,8},{10,11... | collective-permute-start | bytes 3932168 | tf_op jit(solution)/shard_map/ppermute | solution.py:30
  49.1 43.2 %collective-permute-start.5 = (bf16[4,160,1024]{2,1,0:T(8,128)(2,1)}, bf16[4,160,1024]{2,1,0:T(8,128)(2,1)}, u32[]{:S(2)}, u32[]{:S(2)}) collective-permute-start(bf16[4,160,1024]{2,1,0:T(8,128)(2,1)} %bitcast.84), channel_id=1, source_target_pairs={{0,4},{4,0},{1,5},{5,1},{2,6},{6,2},{3,7},{7,3},{8,12},{12,8},{9,1... | collective-permute-start | bytes 3932168 | tf_op jit(solution)/shard_map/ppermute | solution.py:30
  69.5 30.6 %collective-permute-start.2 = (bf16[4,144,768]{2,1,0:T(8,128)(2,1)S(1)}, bf16[4,144,768]{2,1,0:T(8,128)(2,1)}, u32[]{:S(2)}, u32[]{:S(2)}) collective-permute-start(bf16[4,144,768]{2,1,0:T(8,128)(2,1)S(1)} %bitcast.88), channel_id=1, source_target_pairs={{0,4},{4,0},{1,5},{5,1},{2,6},{6,2},{3,7},{7,3},{8,12},{12,8},{9,1... | collective-permute-start | bytes 2654216 | tf_op jit(solution)/shard_map/ppermute | solution.py:30
  88.9 28.2 %collective-permute-start.1 = (bf16[4,144,768]{2,1,0:T(8,128)(2,1)S(1)}, bf16[4,144,768]{2,1,0:T(8,128)(2,1)}, u32[]{:S(2)}, u32[]{:S(2)}) collective-permute-start(bf16[4,144,768]{2,1,0:T(8,128)(2,1)S(1)} %bitcast.91), channel_id=1, source_target_pairs={{0,4},{4,0},{1,5},{5,1},{2,6},{6,2},{3,7},{7,3},{8,12},{12,8},{9,1... | collective-permute-start | bytes 2654216 | tf_op jit(solution)/shard_map/ppermute | solution.py:30
  90.7 392.0 %reduce-scatter.9.cloned.1.call-start = ((), (), s32[]{:S(2)}) async-start(), calls=%async_computation.8 | async-start | bytes 2621440 | tf_op jit(solution)/shard_map/reduce_scatter | solution.py:68
  90.7 67.6 %collective-permute-start.4 = (bf16[4,160,1024]{2,1,0:T(8,128)(2,1)S(1)}, bf16[4,160,1024]{2,1,0:T(8,128)(2,1)}, u32[]{:S(2)}, u32[]{:S(2)}) collective-permute-start(bf16[4,160,1024]{2,1,0:T(8,128)(2,1)S(1)} %bitcast.87), channel_id=1, source_target_pairs={{0,2},{2,0},{1,3},{3,1},{4,6},{6,4},{5,7},{7,5},{8,10},{10,8},{9,1... | collective-permute-start | bytes 3932168 | tf_op jit(solution)/shard_map/ppermute | solution.py:30
  92.3 66.0 %collective-permute-start.6 = (bf16[4,160,1024]{2,1,0:T(8,128)(2,1)}, bf16[4,160,1024]{2,1,0:T(8,128)(2,1)}, u32[]{:S(2)}, u32[]{:S(2)}) collective-permute-start(bf16[4,160,1024]{2,1,0:T(8,128)(2,1)} %collective-permute-done.5.refs_2_), channel_id=1, source_target_pairs={{0,2},{2,0},{1,3},{3,1},{4,6},{6,4},{5,7},{7,5},{8,10},{10,8},{9,1... | collective-permute-start | bytes 3932168 | tf_op jit(solution)/shard_map/ppermute | solution.py:30
  156.3 27.4 %collective-permute-start.3 = (bf16[2,640,512]{2,1,0:T(8,128)(2,1)}, bf16[2,640,512]{2,1,0:T(8,128)(2,1)S(1)}, u32[]{:S(2)}, u32[]{:S(2)}) collective-permute-start(bf16[2,640,512]{2,1,0:T(8,128)(2,1)} %get-tuple-element.141.mine_ref), channel_id=1, source_target_pairs={{0,1},{1,0},{2,3},{3,2},{4,5},{5,4},{6,7},{7,6},{8,9},{9,8},{10,11... | collective-permute-start | bytes 3932168 | tf_op jit(solution)/shard_map/ppermute | solution.py:30
  156.3 38.7 %collective-permute-start.8 = (bf16[640,1024]{1,0:T(8,128)(2,1)}, bf16[640,1024]{1,0:T(8,128)(2,1)}, u32[]{:S(2)}, u32[]{:S(2)}) collective-permute-start(bf16[640,1024]{1,0:T(8,128)(2,1)} %get-tuple-element.146.own_cot.pass_ref), channel_id=1, source_target_pairs={{0,1},{1,0},{2,3},{3,2},{4,5},{5,4},{6,7},{7,6},{8,9},{9,8},{10,11... | collective-permute-start | bytes 3932168 | tf_op jit(solution)/shard_map/ppermute | solution.py:30
  156.8 25.4 %collective-permute-start.10 = (bf16[4,128,1024]{2,1,0:T(8,128)(2,1)}, bf16[4,128,1024]{2,1,0:T(8,128)(2,1)}, u32[]{:S(2)}, u32[]{:S(2)}) collective-permute-start(bf16[4,128,1024]{2,1,0:T(8,128)(2,1)} %bitcast.154), channel_id=1, source_target_pairs={{0,4},{4,0},{1,5},{5,1},{2,6},{6,2},{3,7},{7,3},{8,12},{12,8},{9,1... | collective-permute-start | bytes 3145736 | tf_op jit(solution)/shard_map/ppermute | solution.py:30
  161.4 22.4 %collective-permute-start.7 = (bf16[1024,512]{1,0:T(8,128)(2,1)}, bf16[1024,512]{1,0:T(8,128)(2,1)S(1)}, u32[]{:S(2)}, u32[]{:S(2)}) collective-permute-start(bf16[1024,512]{1,0:T(8,128)(2,1)} %gather_out.1.wm_ref), channel_id=1, source_target_pairs={{0,1},{1,0},{2,3},{3,2},{4,5},{5,4},{6,7},{7,6},{8,9},{9,8},{10,11... | collective-permute-start | bytes 3145736 | tf_op jit(solution)/shard_map/ppermute | solution.py:30
  161.5 70.1 %collective-permute-start.9 = (bf16[4,128,1024]{2,1,0:T(8,128)(2,1)}, bf16[4,128,1024]{2,1,0:T(8,128)(2,1)}, u32[]{:S(2)}, u32[]{:S(2)}) collective-permute-start(bf16[4,128,1024]{2,1,0:T(8,128)(2,1)} %bitcast.155), channel_id=1, source_target_pairs={{0,2},{2,0},{1,3},{3,1},{4,6},{6,4},{5,7},{7,5},{8,10},{10,8},{9,1... | collective-permute-start | bytes 3145736 | tf_op jit(solution)/shard_map/ppermute | solution.py:30
  182.3 49.3 %collective-permute-start.11 = (bf16[4,128,1024]{2,1,0:T(8,128)(2,1)}, bf16[4,128,1024]{2,1,0:T(8,128)(2,1)}, u32[]{:S(2)}, u32[]{:S(2)}) collective-permute-start(bf16[4,128,1024]{2,1,0:T(8,128)(2,1)} %collective-permute-done.10.refs_2_), channel_id=1, source_target_pairs={{0,2},{2,0},{1,3},{3,1},{4,6},{6,4},{5,7},{7,5},{8,10},{10,8},{9,1... | collective-permute-start | bytes 3145736 | tf_op jit(solution)/shard_map/ppermute | solution.py:30
  271.1 46.8 %collective-permute-start.29 = (bf16[4,256,1024]{2,1,0:T(8,128)(2,1)}, bf16[4,256,1024]{2,1,0:T(8,128)(2,1)S(1)}, u32[]{:S(2)}, u32[]{:S(2)}) collective-permute-start(bf16[4,256,1024]{2,1,0:T(8,128)(2,1)} %get-tuple-element.184), channel_id=1, source_target_pairs={{0,4},{4,0},{1,5},{5,1},{2,6},{6,2},{3,7},{7,3},{8,12},{12,8},{9,1... | collective-permute-start | bytes 6291464 | tf_op jit(solution)/shard_map/ppermute | solution.py:30
  272.7 49.2 %collective-permute-start.12 = (f32[640,1024]{1,0:T(8,128)}, f32[640,1024]{1,0:T(8,128)S(1)}, u32[]{:S(2)}, u32[]{:S(2)}) collective-permute-start(f32[640,1024]{1,0:T(8,128)} %get-tuple-element.154), channel_id=1, source_target_pairs={{0,1},{1,0},{2,3},{3,2},{4,5},{5,4},{6,7},{7,6},{8,9},{9,8},{10,11... | collective-permute-start | bytes 7864328 | tf_op jit(solution)/shard_map/ppermute | solution.py:30
  272.7 49.2 %collective-permute-start.13 = (f32[640,1024]{1,0:T(8,128)}, f32[640,1024]{1,0:T(8,128)}, u32[]{:S(2)}, u32[]{:S(2)}) collective-permute-start(f32[640,1024]{1,0:T(8,128)} %get-tuple-element.156), channel_id=1, source_target_pairs={{0,1},{1,0},{2,3},{3,2},{4,5},{5,4},{6,7},{7,6},{8,9},{9,8},{10,11... | collective-permute-start | bytes 7864328 | tf_op jit(solution)/shard_map/ppermute | solution.py:30
  321.8 161.0 %reduce-scatter.11.cloned.1.call-start = ((), (), s32[]{:S(2)}) async-start(), calls=%async_computation.9 | async-start | bytes 655360 | tf_op jit(solution)/shard_map/reduce_scatter | solution.py:68
  333.8 61.8 %collective-permute-start.25 = (bf16[4,256,1024]{2,1,0:T(8,128)(2,1)}, bf16[4,256,1024]{2,1,0:T(8,128)(2,1)}, u32[]{:S(2)}, u32[]{:S(2)}) collective-permute-start(bf16[4,256,1024]{2,1,0:T(8,128)(2,1)} %get-tuple-element.182), channel_id=1, source_target_pairs={{0,4},{4,0},{1,5},{5,1},{2,6},{6,2},{3,7},{7,3},{8,12},{12,8},{9,1... | collective-permute-start | bytes 6291464 | tf_op jit(solution)/shard_map/ppermute | solution.py:30
  347.2 46.1 %collective-permute-start.33 = (bf16[4,128,512]{2,1,0:T(8,128)(2,1)}, bf16[4,128,512]{2,1,0:T(8,128)(2,1)S(1)}, u32[]{:S(2)}, u32[]{:S(2)}) collective-permute-start(bf16[4,128,512]{2,1,0:T(8,128)(2,1)} %get-tuple-element.186), channel_id=1, source_target_pairs={{0,4},{4,0},{1,5},{5,1},{2,6},{6,2},{3,7},{7,3},{8,12},{12,8},{9,1... | collective-permute-start | bytes 1572872 | tf_op jit(solution)/shard_map/ppermute | solution.py:30
  395.2 105.4 %reduce-scatter.7.cloned.1.call-start = ((), (), s32[]{:S(2)}) async-start(), calls=%async_computation.7 | async-start | bytes 2621440 | tf_op jit(solution)/shard_map/reduce_scatter | solution.py:68
  399.4 133.2 %reduce-scatter.5.cloned.1.call-start = ((), (), s32[]{:S(2)}) async-start(), calls=%async_computation.6 | async-start | bytes 1966080 | tf_op jit(solution)/shard_map/reduce_scatter | solution.py:68
  442.8 36.4 %collective-permute-start.16 = (bf16[4,128,1536]{2,1,0:T(8,128)(2,1)}, bf16[4,128,1536]{2,1,0:T(8,128)(2,1)}, u32[]{:S(2)}, u32[]{:S(2)}) collective-permute-start(bf16[4,128,1536]{2,1,0:T(8,128)(2,1)} %get-tuple-element.170), channel_id=1, source_target_pairs={{0,4},{4,0},{1,5},{5,1},{2,6},{6,2},{3,7},{7,3},{8,12},{12,8},{9,1... | collective-permute-start | bytes 4718600 | tf_op jit(solution)/shard_map/ppermute | solution.py:30
  455.0 29.5 %collective-permute-start.15 = (f32[640,1024]{1,0:T(8,128)}, f32[640,1024]{1,0:T(8,128)S(1)}, u32[]{:S(2)}, u32[]{:S(2)}) collective-permute-start(f32[640,1024]{1,0:T(8,128)} %get-tuple-element.165), channel_id=1, source_target_pairs={{0,1},{1,0},{2,3},{3,2},{4,5},{5,4},{6,7},{7,6},{8,9},{9,8},{10,11... | collective-permute-start | bytes 7864328 | tf_op jit(solution)/shard_map/ppermute | solution.py:30
  482.6 48.3 %collective-permute-start.32 = (bf16[256,1024]{1,0:T(8,128)(2,1)}, bf16[256,1024]{1,0:T(8,128)(2,1)}, u32[]{:S(2)}, u32[]{:S(2)}) collective-permute-start(bf16[256,1024]{1,0:T(8,128)(2,1)} %reduce-scatter.9.cloned.1.call-done.refs_4_), channel_id=1, source_target_pairs={{0,3},{1,2},{2,1},{3,0},{4,7},{5,6},{6,5},{7,4},{8,11},{9,10},{10,... | collective-permute-start | bytes 1572872 | tf_op jit(solution)/shard_map/ppermute | solution.py:44
  496.8 35.8 %collective-permute-start.31 = (bf16[256,1024]{1,0:T(8,128)(2,1)S(1)}, bf16[256,1024]{1,0:T(8,128)(2,1)S(1)}, u32[]{:S(2)}, u32[]{:S(2)}) collective-permute-start(bf16[256,1024]{1,0:T(8,128)(2,1)S(1)} %copy-done.9), channel_id=1, source_target_pairs={{0,1},{1,0},{2,3},{3,2},{4,5},{5,4},{6,7},{7,6},{8,9},{9,8},{10,11... | collective-permute-start | bytes 1572872 | tf_op jit(solution)/shard_map/ppermute | solution.py:30
  499.3 33.6 %collective-permute-start.30 = (bf16[256,1024]{1,0:T(8,128)(2,1)S(1)}, bf16[256,1024]{1,0:T(8,128)(2,1)S(1)}, u32[]{:S(2)}, u32[]{:S(2)}) collective-permute-start(bf16[256,1024]{1,0:T(8,128)(2,1)S(1)} %copy-done.9), channel_id=1, source_target_pairs={{0,2},{2,0},{1,3},{3,1},{4,6},{6,4},{5,7},{7,5},{8,10},{10,8},{9,1... | collective-permute-start | bytes 1572872 | tf_op jit(solution)/shard_map/ppermute | solution.py:30
  500.6 32.4 %collective-permute-start.28 = (bf16[256,1024]{1,0:T(8,128)(2,1)}, bf16[256,1024]{1,0:T(8,128)(2,1)S(1)}, u32[]{:S(2)}, u32[]{:S(2)}) collective-permute-start(bf16[256,1024]{1,0:T(8,128)(2,1)} %reduce-scatter.7.cloned.1.call-done.refs_0_), channel_id=1, source_target_pairs={{0,3},{1,2},{2,1},{3,0},{4,7},{5,6},{6,5},{7,4},{8,11},{9,10},{10,... | collective-permute-start | bytes 1572872 | tf_op jit(solution)/shard_map/ppermute | solution.py:44
  532.7 31.3 %collective-permute-start.19 = (bf16[128,1536]{1,0:T(8,128)(2,1)}, bf16[128,1536]{1,0:T(8,128)(2,1)S(1)}, u32[]{:S(2)}, u32[]{:S(2)}) collective-permute-start(bf16[128,1536]{1,0:T(8,128)(2,1)} %reduce-scatter.5.cloned.1.call-done.refs_0_), channel_id=1, source_target_pairs={{0,3},{1,2},{2,1},{3,0},{4,7},{5,6},{6,5},{7,4},{8,11},{9,10},{10,... | collective-permute-start | bytes 1179656 | tf_op jit(solution)/shard_map/ppermute | solution.py:44
  532.9 31.1 %collective-permute-start.18 = (bf16[128,1536]{1,0:T(8,128)(2,1)}, bf16[128,1536]{1,0:T(8,128)(2,1)S(1)}, u32[]{:S(2)}, u32[]{:S(2)}) collective-permute-start(bf16[128,1536]{1,0:T(8,128)(2,1)} %reduce-scatter.5.cloned.1.call-done.refs_0_), channel_id=1, source_target_pairs={{0,1},{1,0},{2,3},{3,2},{4,5},{5,4},{6,7},{7,6},{8,9},{9,8},{10,11... | collective-permute-start | bytes 1179656 | tf_op jit(solution)/shard_map/ppermute | solution.py:30
  533.1 30.9 %collective-permute-start.17 = (bf16[128,1536]{1,0:T(8,128)(2,1)}, bf16[128,1536]{1,0:T(8,128)(2,1)S(1)}, u32[]{:S(2)}, u32[]{:S(2)}) collective-permute-start(bf16[128,1536]{1,0:T(8,128)(2,1)} %reduce-scatter.5.cloned.1.call-done.refs_0_), channel_id=1, source_target_pairs={{0,2},{2,0},{1,3},{3,1},{4,6},{6,4},{5,7},{7,5},{8,10},{10,8},{9,1... | collective-permute-start | bytes 1179656 | tf_op jit(solution)/shard_map/ppermute | solution.py:30
  (38 other events, 419.8 us)
Sparse Core Ops, SparseCore 0:
  13.6 35.3 all-gather.2
  90.8 26.4 all-gather.4
  321.9 42.7 reduce-scatter.8
  395.4 20.7 reduce-scatter.10
  419.0 42.0 reduce-scatter.6
  482.7 34.2 reduce-scatter.4

commit v5 on v4

--- a/solution.py
+++ b/solution.py
@@ -14,6 +14,8 @@
 TILE = 16
 SPAN = 256
 CHUNKS = 2
+GROUPS = 2
+GIVEN = 2
 VMEM_LIMIT = 60 * 1024 * 1024
 
 ALL_AXES = ("z", "x", "y", "c")
@@ -40,12 +42,12 @@
     return lax.ppermute(value, axis, [(i, i ^ step) for i in range(size)])
 
 
-def swap_both(value):
-    return lax.ppermute(value, ("y", "c"), [(i, 3 - i) for i in range(4)])
-
-
 def sum_over(value, axes):
     for axis in axes:
+        if lax.axis_size(axis) == 4:
+            got = [shift(value, axis, step) for step in (1, 2, 3)]
+            value = (value + got[1]) + (got[0] + got[2])
+            continue
         step = 1
         while step < lax.axis_size(axis):
             value = value + partner(value, axis, step)
@@ -53,23 +55,38 @@
     return value
 
 
-def gather_rows(shard, by_y):
+def along_z(shard):
     near = lax.all_gather(shard, "z", axis=0, tiled=True)
-    near = near.reshape(lax.axis_size("z"), *shard.shape)
-    both = [near, swap(near, "x")]
-    if not by_y:
-        return [[one] for one in both]
-    return [[one, swap(one, "y")] for one in both]
-
-
-def scatter_sum(keep, send):
-    total = low(wide(keep) + wide(swap(send, "x")))
-    total = total.reshape(-1, total.shape[-1])
-    mine = lax.psum_scatter(total, "z", scatter_dimension=0, tiled=True)
+    return near.reshape(lax.axis_size("z"), *shard.shape)
+
+
+def by_x(near):
+    return [[near], [swap(near, "x")]]
+
+
+def by_y_too(pieces, by_y):
+    return [[one, swap(one, "y")] if by_y else [one] for (one,) in pieces]
+
+
+def after(values, token):
+    return lax.optimization_barrier((values, token))[0]
+
+
+def fold(keep, got):
+    total = low(wide(keep) + wide(got))
+    return total.reshape(-1, total.shape[-1])
+
+
+def scatter_z(total):
+    return lax.psum_scatter(total, "z", scatter_dimension=0, tiled=True)
+
+
+def finish_sum(mine):
     if lax.axis_size("y") == 2:
-        return [mine, swap(mine, "y")], [swap(mine, "c"), swap_both(mine)]
-    total = lax.psum(wide(mine), "y")
-    return [total], [swap(total, "c")]
+        own = [mine, swap(mine, "y")]
+    else:
+        own = [lax.psum(wide(mine), "y")]
+    return own, [swap(one, "c") for one in own]
 
 
 def row_pad(length):
@@ -106,8 +123,7 @@
     return jax.ShapeDtypeStruct(shape, dtype)
 
 
-def call(body, place, ins, in_specs, outs, out_specs, scratch, name, grid=(1,), flops=0):
-    moved = sum(math.prod(a.shape) * a.dtype.itemsize for a in [*ins, *outs])
+def call(body, place, ins, in_specs, outs, out_specs, scratch, name, grid=(1,)):
     return pl.pallas_call(
         body,
         out_shape=outs,
@@ -121,7 +137,6 @@
         compiler_params=pltpu.CompilerParams(
             vmem_limit_bytes=VMEM_LIMIT, dimension_semantics=("arbitrary",) * len(grid)
         ),
-        cost_estimate=pl.CostEstimate(flops=flops, bytes_accessed=moved, transcendentals=0),
         name=name,
     )(place, *ins)
 
@@ -140,58 +155,97 @@
     return jnp.where(core == 0, first, second)
 
 
-def prepare_qkv(place, weight, vectors):
+def prepare_qkv(place, weight, out_weight, vectors):
     part, cols = weight.shape
-    width = cols // 2
     half = cols // 6
-    parts = 2
+    heads = half // GROUPS
+    width = 3 * heads
     sizes = [vector.shape[-1] for vector in vectors]
-
-    def body(place_ref, weight_ref, *refs):
-        refs, (out_ref, *halves) = refs[: len(sizes)], (refs[-1], *refs[len(sizes) : -1])
+    tiles = -(-sum(sizes) // width)
+
+    out_half = out_weight.shape[1] // 2
+
+    def body(place_ref, weight_ref, out_ref, *refs):
+        refs, groups = refs[: len(sizes)], refs[len(sizes) :]
         core = place_ref[2]
-        for slot in range(3):
-            at = 2 * slot * half
-            out_ref[:part, slot * half : (slot + 1) * half] = low(
-                select(core, weight_ref[:, at : at + half], weight_ref[:, at + half : at + 2 * half])
-            )
+        for number, ref in enumerate(groups):
+            for slot in range(3):
+                at = 2 * slot * half + number * heads
+                ref[:part, slot * heads : (slot + 1) * heads] = low(
+                    select(
+                        core,
+                        weight_ref[:, at : at + heads],
+                        weight_ref[:, at + half : at + half + heads],
+                    )
+                )
+        groups[-1][:, width:] = low(select(core, out_ref[:, :out_half], out_ref[:, out_half:]))
         at = 0
         for ref, size in zip(refs, sizes):
-            out_ref[part:, at : at + size] = low(jnp.broadcast_to(ref[...], (TILE, size)))
+            done = 0
+            while done < size:
+                tile, lane = divmod(at + done, width)
+                count = min(size - done, width - lane)
+                row = part + tile * TILE
+                groups[0][row : row + TILE, lane : lane + count] = low(
+                    jnp.broadcast_to(ref[:, done : done + count], (TILE, count))
+                )
+                done += count
             at += size
-        for number, ref in enumerate(halves):
-            ref[...] = out_ref[:, number * width // parts : (number + 1) * width // parts]
-
-    shape = (part + TILE, width // parts)
+
+    shapes = [
+        (part + (tiles * TILE if g == 0 else 0), width + (out_half if g == GROUPS - 1 else 0))
+        for g in range(GROUPS)
+    ]
     return call(
         body,
         place,
-        (weight, *vectors),
-        [whole((part, cols))] + [whole((1, size)) for size in sizes],
-        [sds(shape, jnp.bfloat16)] * parts,
-        [whole(shape)] * parts,
-        [pltpu.VMEM((part + TILE, width), jnp.bfloat16)],
+        (weight, out_weight, *vectors),
+        [whole((part, cols)), whole(out_weight.shape)] + [whole((1, size)) for size in sizes],
+        [sds(shape, jnp.bfloat16) for shape in shapes],
+        [whole(shape) for shape in shapes],
+        [],
         "prepare_qkv",
     )
 
 
-def prepare_rest(place, in_weight, down_weight, out_weight, inputs, cotangent, by_y):
+def pad_rows(place, rows):
+    tokens, width = rows.shape
+    length = row_pad(tokens)
+    even = tokens // TILE * TILE
+
+    def body(place_ref, ref, to):
+        row = lax.broadcasted_iota(jnp.int32, (length - even, width), 0)
+        to[:even, :] = ref[:even, :]
+        last = jnp.zeros((length - even, width), jnp.float32)
+        for extra in range(tokens - even):
+            one = wide(ref[even + extra : even + extra + 1, :])
+            last = jnp.where(row == extra, one, last)
+        to[even:, :] = low(last)
+
+    shape = (length, width)
+    return call(
+        body,
+        place,
+        (rows,),
+        [whole(rows.shape)],
+        [sds(shape, jnp.bfloat16)],
+        [whole(shape)],
+        [],
+        "pad_rows",
+    )[0]
+
+
+def prepare_rest(place, in_weight, down_weight, cotangent, cuts):
     part, hidden = in_weight.shape
     width = down_weight.shape[1]
     per_core = down_weight.shape[0] // 2
     per_shard = per_core // CHUNKS
     shards = hidden // (2 * per_core)
-    tokens = inputs.shape[0]
-    length = row_pad(tokens)
-    even = tokens // TILE * TILE
-    cut = 2 if by_y else 1
-    rows_in, rows_down, rows_out = part // cut, per_shard // cut, part // cut // 2
-
-    def body(place_ref, in_ref, down_ref, out_w_ref, rows_ref, cot_ref, *refs):
-        pieces, (rows_out_ref, cot_out, sum_ref) = refs[:CHUNKS], refs[CHUNKS:]
+    def body(place_ref, in_ref, down_ref, cot_ref, *refs):
+        pieces, (sum_ref,) = refs[:CHUNKS], refs[CHUNKS:]
         core, y = place_ref[2], place_ref[3]
 
-        def pick(ref, row, count, step, col, cols, by_row):
+        def pick(ref, row, count, step, col, cols, by_row, cut):
             def of_core(r):
                 if by_row:
                     return select(
@@ -205,35 +259,21 @@
                 return low(of_core(row))
             return low(select(y, of_core(row), of_core(row + count)))
 
-        for j in range(CHUNKS):
+        for j, cut in enumerate(cuts):
+            rows_in, rows_down = part // cut, per_shard // cut
             for s in range(shards):
                 at = s * 2 * per_core + j * per_shard
                 pieces[j][:rows_in, s * per_shard : (s + 1) * per_shard] = pick(
-                    in_ref, 0, rows_in, per_core, at, per_shard, False
+                    in_ref, 0, rows_in, per_core, at, per_shard, False, cut
                 )
-            pieces[j][rows_in : rows_in + rows_down, :] = pick(
-                down_ref, j * per_shard, rows_down, per_core, 0, width, True
+            pieces[j][rows_in:, :] = pick(
+                down_ref, j * per_shard, rows_down, per_core, 0, width, True, cut
             )
-        half = width // 2
-        branch = pick(out_w_ref, 0, 2 * rows_out, half, 0, half, False)
-        for side in range(2):
-            pieces[0][rows_in + rows_down :, side * half : (side + 1) * half] = branch[
-                side * rows_out : (side + 1) * rows_out, :
-            ]
-        row = lax.broadcasted_iota(jnp.int32, (length - even, width), 0)
-        for ref, to in ((rows_ref, rows_out_ref), (cot_ref, cot_out)):
-            to[:even, :] = ref[:even, :]
-            last = jnp.zeros((length - even, width), jnp.float32)
-            for extra in range(tokens - even):
-                one = wide(ref[even + extra : even + extra + 1, :])
-                last = jnp.where(row == extra, one, last)
-            to[even:, :] = low(last)
-        sum_ref[...] = jnp.sum(wide(cot_out[...]), axis=0, keepdims=True)
-
-    counts = [rows_in + rows_down + (rows_out if j == 0 else 0) for j in range(CHUNKS)]
-    outs = [sds((count, width), jnp.bfloat16) for count in counts]
-    outs += [sds((length, width), jnp.bfloat16)] * 2 + [sds((1, width), jnp.float32)]
-    ins = (in_weight, down_weight, out_weight, inputs, cotangent)
+        sum_ref[...] = jnp.sum(wide(cot_ref[...]), axis=0, keepdims=True)
+
+    outs = [sds(((part + per_shard) // cut, width), jnp.bfloat16) for cut in cuts]
+    outs += [sds((1, width), jnp.float32)]
+    ins = (in_weight, down_weight, cotangent)
     return call(
         body,
         place,
@@ -246,50 +286,85 @@
     )
 
 
-GAIN_ONE, BIAS_ONE, BIAS_OUT, GAIN_TWO, BIAS_TWO, BIAS_DOWN = range(6)
-
-
-def project_qkv(place, rows, pieces, sizes):
-    flat = [one for piece in pieces for (one,) in piece]
-    z_size, part, cols_part = flat[0].shape
-    part -= TILE
+GAIN_ONE, BIAS_ONE, BIAS_OUT, GAIN_TWO, BIAS_TWO, BIAS_DOWN, BIAS_QV = range(7)
+
+
+def weight_copies(place_ref, ins, weight, part, sem):
+    made = []
+    for dx, ref in enumerate(ins):
+        for z in range(ref.shape[0]):
+            row = pl.multiple_of(shard_number(place_ref, z, dx) * part, part)
+            made.append(
+                pltpu.make_async_copy(
+                    ref.at[z, pl.ds(0, part), pl.ds(0, weight.shape[1])],
+                    weight.at[pl.ds(row, part), :],
+                    sem.at[len(made)],
+                )
+            )
+    return made
+
+
+def write_qkv(normed, weight, bias_q, bias_v, image, q_ref, k_ref, v_ref):
+    heads = weight.shape[1] // 3
+    query = low(dot(normed, weight[:, :heads]) + bias_q)
+    q_ref[image] = low(wide(query) * (1.0 / math.sqrt(HEAD_DIM)))
+    k_ref[image] = low(dot(normed, weight[:, heads : 2 * heads]))
+    v_ref[image] = low(dot(normed, weight[:, 2 * heads :]) + bias_v)
+
+
+def project_first(place, rows, pieces, sizes):
+    flat = [one for (one,) in pieces]
+    z_size, part, cols = flat[0].shape
+    length, width = rows[0].shape
     count = 2 * z_size
-    cols = cols_part * len(pieces)
-    width = part * count
+    tiles = (part - width // count) // TILE
+    part = width // count
     heads = cols // 3
-    length = rows[0].shape[0]
-    scale = 1.0 / math.sqrt(HEAD_DIM)
+    half = heads * GROUPS
     starts = [sum(sizes[:number]) for number in range(len(sizes))]
     per_shard = sizes[6] // 2 // CHUNKS
     blocks = count // 2
 
     def body(place_ref, own_ref, other_ref, *refs):
-        ins, refs = refs[: len(flat)], refs[len(flat) :]
+        ins, refs = refs[:2], refs[2:]
         normed_ref, q_ref, k_ref, v_ref, vec_ref, hidden_bias_ref, weight, packed, sem = refs
         core = place_ref[2]
         copies = []
-        for number, ref in enumerate(ins):
-            lanes = pl.ds(number // 2 * cols_part, cols_part)
+        for dx, ref in enumerate(ins):
             for z in range(z_size):
-                s = shard_number(place_ref, z, number % 2)
-                row = pl.multiple_of(s * part, part)
-                for source, to in (
-                    (ref.at[z, pl.ds(0, part), :], weight.at[pl.ds(row, part), lanes]),
-                    (ref.at[z, pl.ds(part, TILE), :], packed.at[s, :, lanes]),
-                ):
-                    copy = pltpu.make_async_copy(source, to, sem.at[len(copies)])
-                    copy.start()
-                    copies.append(copy)
+                copies.append(
+                    pltpu.make_async_copy(
+                        ref.at[z, pl.ds(part, tiles * TILE), :],
+                        packed.at[shard_number(place_ref, z, dx)],
+                        sem.at[count + len(copies)],
+                    )
+                )
+        copies += weight_copies(place_ref, ins, weight, part, sem)
+        for copy in copies:
+            copy.start()
         for copy in copies:
             copy.wait()
 
+        def lanes(s, at, size):
+            found = []
+            done = 0
+            while done < size:
+                tile, lane = divmod(at + done, cols)
+                take = min(size - done, cols - lane)
+                found.append(wide(packed[s, tile * TILE : tile * TILE + 1, lane : lane + take]))
+                done += take
+            return found
+
         def vector(slot, shards=range(count)):
-            at, size = starts[slot], sizes[slot]
             return jnp.concatenate(
-                [wide(packed[s, 0:1, at : at + size]) for s in shards], axis=1
+                [one for s in shards for one in lanes(s, starts[slot], sizes[slot])], axis=1
             )
 
         gain, bias = vector(0), vector(1)
+        bias_q = vector(2, range(blocks))
+        bias_v = vector(2, range(blocks, count))
+        bias_q = select(core, bias_q[:, :half], bias_q[:, half:])
+        bias_v = select(core, bias_v[:, :half], bias_v[:, half:])
         for row, value in (
             (GAIN_ONE, gain),
             (BIAS_ONE, bias),
@@ -297,41 +372,41 @@
             (GAIN_TWO, vector(4)),
             (BIAS_TWO, vector(5)),
             (BIAS_DOWN, vector(7)),
+            (BIAS_QV, jnp.concatenate([bias_q, bias_v], axis=1)),
         ):
             vec_ref[row : row + 1, :] = value
-        vec_ref[6:8, :] = jnp.zeros((2, width), jnp.float32)
+        vec_ref[7:8, :] = jnp.zeros((1, width), jnp.float32)
         for j in range(CHUNKS):
             for b in range(blocks):
                 for i in range(2):
                     at = starts[6] + j * per_shard
                     to = at + sizes[6] // 2
-                    hidden_bias_ref[j, b, :, i * per_shard : (i + 1) * per_shard] = wide(
-                        select(
-                            core,
-                            wide(packed[2 * b + i, 0:1, at : at + per_shard]),
-                            wide(packed[2 * b + i, 0:1, to : to + per_shard]),
-                        )
+                    hidden_bias_ref[j, b, :, i * per_shard : (i + 1) * per_shard] = select(
+                        core,
+                        jnp.concatenate(lanes(2 * b + i, at, per_shard), axis=1),
+                        jnp.concatenate(lanes(2 * b + i, to, per_shard), axis=1),
                     )
-        bias_q = vector(2, range(blocks))
-        bias_v = vector(2, range(blocks, count))
-        bias_q = select(core, bias_q[:, :heads], bias_q[:, heads:])
-        bias_v = select(core, bias_v[:, :heads], bias_v[:, heads:])
         for image, ref in enumerate((own_ref, other_ref)):
             for at in range(0, length, LANES):
                 block = wide(ref[at : at + LANES, :])
                 normed_ref[image, at : at + LANES, :] = low(normalised(block) * gain + bias)
-            normed = normed_ref[image]
-            query = low(dot(normed, weight[:, :heads]) + bias_q)
-            q_ref[image] = low(wide(query) * scale)
-            k_ref[image] = low(dot(normed, weight[:, heads : 2 * heads]))
-            v_ref[image] = low(dot(normed, weight[:, 2 * heads :]) + bias_v)
+            write_qkv(
+                normed_ref[image],
+                weight,
+                bias_q[:, :heads],
+                bias_v[:, :heads],
+                image,
+                q_ref,
+                k_ref,
+                v_ref,
+            )
 
     part_out = sds((2, length, heads), jnp.bfloat16)
     return call(
         body,
         place,
         (*rows, *flat),
-        [whole((length, width))] * 2 + [any_spec()] * len(flat),
+        [whole((length, width))] * 2 + [any_spec()] * 2,
         [sds((2, length, width), jnp.bfloat16)]
         + [part_out] * 3
         + [
@@ -343,49 +418,76 @@
         + [whole((8, width)), whole((CHUNKS, blocks, 1, 2 * per_shard))],
         [
             pltpu.VMEM((width, cols), jnp.bfloat16),
-            pltpu.VMEM((count, TILE, cols), jnp.bfloat16),
-            pltpu.SemaphoreType.DMA((2 * z_size * len(flat),)),
+            pltpu.VMEM((count, tiles * TILE, cols), jnp.bfloat16),
+            pltpu.SemaphoreType.DMA((2 * count,)),
         ],
-        "project_qkv",
-        flops=4 * length * width * cols,
-    )
-
-
-def gather_out(place, pieces, first):
-    cut = len(pieces[0])
-    z_size, total, width = pieces[0][0].shape
-    rows = total - first
+        "project_first",
+    )
+
+
+def project_next(place, normed, vectors, pieces, group):
+    flat = [one for (one,) in pieces]
+    z_size, part, _ = flat[0].shape
+    _, length, width = normed.shape
     half = width // 2
-    part = width // (2 * z_size)
-
-    def body(place_ref, *refs):
-        ins, out_ref, sem = refs[: 2 * cut], refs[2 * cut], refs[2 * cut + 1]
-        copies = []
-        for number, ref in enumerate(ins):
-            dx, h = number // cut, number % cut
-            y = h + (1 - 2 * h) * place_ref[3] if cut == 2 else 0
-            for z in range(z_size):
-                for side in range(2):
-                    row = shard_number(place_ref, z, dx) * part + (2 * y + side) * rows
-                    copy = pltpu.make_async_copy(
-                        ref.at[z, pl.ds(first, rows), pl.ds(side * half, half)],
-                        out_ref.at[pl.ds(pl.multiple_of(row, rows), rows), :],
-                        sem.at[len(copies)],
-                    )
-                    copy.start()
-                    copies.append(copy)
+    heads = half // GROUPS
+    cols = 3 * heads
+
+    def body(place_ref, normed_ref, vec_ref, *refs):
+        ins, (q_ref, k_ref, v_ref, weight, sem) = refs[:2], refs[2:]
+        copies = weight_copies(place_ref, ins, weight, part, sem)
+        for copy in copies:
+            copy.start()
         for copy in copies:
             copy.wait()
-
-    shape = (width, half)
+        at = group * heads
+        bias_q = vec_ref[BIAS_QV : BIAS_QV + 1, at : at + heads]
+        bias_v = vec_ref[BIAS_QV : BIAS_QV + 1, half + at : half + at + heads]
+        for image in range(2):
+            write_qkv(normed_ref[image], weight, bias_q, bias_v, image, q_ref, k_ref, v_ref)
+
     return call(
         body,
         place,
-        tuple(one for side in pieces for one in side),
-        [any_spec()] * (2 * cut),
+        (normed, vectors, *flat),
+        [whole(normed.shape), whole(vectors.shape)] + [any_spec()] * 2,
+        [sds((2, length, heads), jnp.bfloat16)] * 3,
+        [whole((2, length, heads))] * 3,
+        [pltpu.VMEM((width, cols), jnp.bfloat16), pltpu.SemaphoreType.DMA((2 * z_size,))],
+        "project_next",
+    )
+
+
+def gather_out(place, pieces, first):
+    flat = [one for (one,) in pieces]
+    z_size, part, total = flat[0].shape
+    half = total - first
+
+    def body(place_ref, *refs):
+        ins, out_ref, sem = refs[:2], refs[2], refs[3]
+        copies = []
+        for dx, ref in enumerate(ins):
+            for z in range(z_size):
+                row = pl.multiple_of(shard_number(place_ref, z, dx) * part, part)
+                copy = pltpu.make_async_copy(
+                    ref.at[z, :, pl.ds(first, half)],
+                    out_ref.at[pl.ds(row, part), :],
+                    sem.at[len(copies)],
+                )
+                copy.start()
+                copies.append(copy)
+        for copy in copies:
+            copy.wait()
+
+    shape = (2 * z_size * part, half)
+    return call(
+        body,
+        place,
+        tuple(flat),
+        [any_spec()] * 2,
         [sds(shape, jnp.bfloat16)],
         [whole(shape)],
-        [pltpu.SemaphoreType.DMA((2 * cut * z_size * 2,))],
+        [pltpu.SemaphoreType.DMA((2 * z_size,))],
         "gather_out",
     )[0]
 
@@ -433,7 +535,6 @@
         [],
         "attention",
         grid=(2, pairs),
-        flops=2 * pairs * 2 * 8 * length * length * LANES,
     )
 
 
@@ -490,26 +591,32 @@
         [],
         "attention_back",
         grid=(2, pairs),
-        flops=2 * pairs * 2 * 10 * length * length * LANES,
-    )
+    )
+
+
+def head_rows(core, heads, group):
+    mine = pl.multiple_of((core * GROUPS + group) * heads, heads)
+    return mine, pl.multiple_of(((1 - core) * GROUPS + group) * heads, heads)
 
 
 def project_out(place, mine, theirs, weight_mine, weight_theirs, rows, vectors):
     width, half = weight_mine.shape
-    _, length, heads = mine.shape
-
-    def body(
-        place_ref, mine_ref, theirs_ref, wm_ref, wt_ref, own_ref, other_ref, vec_ref, middle_ref,
-        normed_ref, total,
-    ):
+    _, length, heads = mine[0].shape
+
+    def body(place_ref, *refs):
+        mine_refs, theirs_refs, refs = refs[:GROUPS], refs[GROUPS : 2 * GROUPS], refs[2 * GROUPS :]
+        wm_ref, wt_ref, own_ref, other_ref, vec_ref, middle_ref, normed_ref, total = refs
         core = place_ref[2]
-        at_mine = pl.multiple_of(core * heads, heads)
-        at_theirs = pl.multiple_of((1 - core) * heads, heads)
         for image, ref in enumerate((own_ref, other_ref)):
             for slot, weight in enumerate((wm_ref, wt_ref)):
-                total[slot] = dot(mine_ref[image], weight[pl.ds(at_mine, heads), :]) + dot(
-                    theirs_ref[1 - image], weight[pl.ds(at_theirs, heads), :]
-                )
+                branch = None
+                for g in range(GROUPS):
+                    at_mine, at_theirs = head_rows(core, heads, g)
+                    add = dot(mine_refs[g][image], weight[pl.ds(at_mine, heads), :]) + dot(
+                        theirs_refs[g][1 - image], weight[pl.ds(at_theirs, heads), :]
+                    )
+                    branch = add if branch is None else branch + add
+                total[slot] = branch
             for at in range(0, length, LANES):
                 upto = at + LANES
                 first, second = total[0, at:upto, :], total[1, at:upto, :]
@@ -530,8 +637,8 @@
     return call(
         body,
         place,
-        (mine, theirs, weight_mine, weight_theirs, *rows, vectors),
-        [whole((2, length, heads))] * 2
+        (*mine, *theirs, weight_mine, weight_theirs, *rows, vectors),
+        [whole((2, length, heads))] * (2 * GROUPS)
         + [whole((width, half))] * 2
         + [whole((length, width))] * 2
         + [whole(vectors.shape)],
@@ -539,7 +646,6 @@
         [whole((length, width)), whole((2, length, width))],
         [pltpu.VMEM((2, length, half), jnp.float32)],
         "project_out",
-        flops=8 * length * width * half,
     )
 
 
@@ -554,13 +660,17 @@
     in_block = block // per_shard
     _, length, _ = normed.shape
     first_call = running is None
+    last_call = chunk == CHUNKS - 1
 
     def body(place_ref, normed_ref, own_cot, other_cot, bias_ref, *refs):
         ins, refs = refs[: 2 * cut], refs[2 * cut :]
         if not first_call:
             before, refs = refs[:4], refs[4:]
         out_own, out_other, gn_own, gn_other, bsum_ref, keep_ref, send_ref = refs[:7]
-        w_in, w_down, normed_t, grads, sem, out_sem = refs[7:]
+        w_in, w_down, normed_t, grads, sem, out_sem, *held = refs[7:]
+        given = (out_other, gn_other)
+        if last_call:
+            out_other, gn_other = held
         step = pl.program_id(0)
 
         def copies():
@@ -645,12 +755,15 @@
 
         @pl.when(step == blocks - 1)
         def _():
+            for total_ref, ref in zip(held, given):
+                ref[...] = low(total_ref[...])
             for slot, ref in enumerate((keep_ref, send_ref)):
                 pltpu.make_async_copy(grads.at[slot], ref, out_sem.at[slot]).start()
             for slot, ref in enumerate((keep_ref, send_ref)):
                 pltpu.make_async_copy(grads.at[slot], ref, out_sem.at[slot]).wait()
 
     total = sds((length, width), jnp.float32)
+    other = sds((length, width), jnp.bfloat16 if last_call else jnp.float32)
     piece_out = sds((z_size, part + per_shard, width), jnp.bfloat16)
     carried = () if first_call else tuple(running)
     return call(
@@ -662,7 +775,7 @@
         + [pl.BlockSpec((1, 1, 1, block), lambda b, p: (chunk, b, 0, 0))]
         + [any_spec()] * (2 * cut)
         + [whole((length, width))] * len(carried),
-        [total] * 4 + [sds((blocks, 1, block), jnp.float32)] + [piece_out] * 2,
+        [total, other, total, other] + [sds((blocks, 1, block), jnp.float32)] + [piece_out] * 2,
         [whole((length, width))] * 4
         + [pl.BlockSpec((1, 1, block), lambda b, p: (b, 0, 0))]
         + [any_spec()] * 2,
@@ -673,30 +786,31 @@
             pltpu.VMEM((2, z_size, part + per_shard, width), jnp.bfloat16),
             pltpu.SemaphoreType.DMA((4 * cut * z_size,)),
             pltpu.SemaphoreType.DMA((2,)),
-        ],
+        ]
+        + [pltpu.VMEM((length, width), jnp.float32)] * (2 if last_call else 0),
         "feed_forward",
         grid=(blocks,),
-        flops=24 * length * width * hidden_width,
-    )
-
-
-def norm_back(place, rows, vectors, gain_row, grad_own, grad_other, passed, tokens, finish=None):
+    )
+
+
+def norm_back(place, rows, vectors, gain_row, grad_own, others, passed, tokens, finish=()):
     length, width = rows.shape
 
-    def body(place_ref, rows_ref, vec_ref, own_ref, other_ref, pass_ref, *refs):
+    def body(place_ref, rows_ref, vec_ref, own_ref, pass_ref, *refs):
+        other_refs, refs = refs[: len(others)], refs[len(others) :]
         step = pl.program_id(0)
         values = wide(rows_ref[...])
-        if finish is not None:
+        if finish:
             first_ref, second_ref, *refs = refs
             refs[1][...] = low(
-                values + first_ref[...] + second_ref[...] + vec_ref[BIAS_DOWN : BIAS_DOWN + 1, :]
+                values + first_ref[...] + wide(second_ref[...]) + vec_ref[BIAS_DOWN : BIAS_DOWN + 1, :]
             )
         sum_ref = refs[0]
         centre = values - jnp.mean(values, axis=-1, keepdims=True)
         spread = jnp.mean(centre * centre, axis=-1, keepdims=True)
         inverse = lax.rsqrt(spread + ln_eps)
         unit = centre * inverse
-        grad = own_ref[...] + other_ref[...]
+        grad = own_ref[...] + jnp.concatenate([wide(ref[...]) for ref in other_refs], axis=1)
         scaled = grad * vec_ref[gain_row : gain_row + 1, :]
         mean_one = jnp.mean(scaled, axis=-1, keepdims=True)
         mean_two = jnp.mean(scaled * unit, axis=-1, keepdims=True)
@@ -708,7 +822,7 @@
             jnp.sum(wide(rounded), axis=0, keepdims=True),
             jnp.zeros((5, width), jnp.float32),
         ]
-        if finish is None:
+        if not finish:
             refs[1][...] = rounded
         else:
             refs[2][...] = result
@@ -725,14 +839,17 @@
 
     block = pl.BlockSpec((LANES, width), lambda i, p: (i, 0))
     outs = [sds((8, width), jnp.float32), sds((tokens, width), jnp.bfloat16)]
-    if finish is not None:
+    if finish:
         outs += [sds((length, width), jnp.float32), sds((length, width), jnp.bfloat16)]
-    ins = (rows, vectors, grad_own, grad_other, passed, *(finish or ()))
+    other_block = pl.BlockSpec((LANES, others[0].shape[1]), lambda i, p: (i, 0))
+    ins = (rows, vectors, grad_own, passed, *others, *finish)
     return call(
         body,
         place,
         ins,
-        [block, whole(vectors.shape)] + [block] * (len(ins) - 2),
+        [block, whole(vectors.shape), block, block]
+        + [other_block] * len(others)
+        + [block] * len(finish),
         outs,
         [whole((8, width))] + [block] * (len(outs) - 1),
         [],
@@ -745,19 +862,19 @@
     width, half = weight_mine.shape
     z_size = lax.axis_size("z")
     part = width // (2 * z_size)
-    _, length, heads = mine.shape
-
-    def body(
-        place_ref, own_ref, other_ref, own_half, other_half, mine_ref, theirs_ref, wm_ref, wt_ref,
-        ga_ref, keep_ref, send_ref, turned, grads, out_sem,
-    ):
+    _, length, heads = mine[0].shape
+
+    def body(place_ref, own_ref, other_ref, own_half, other_half, *refs):
+        mine_refs, theirs_refs, refs = refs[:GROUPS], refs[GROUPS : 2 * GROUPS], refs[2 * GROUPS :]
+        wm_ref, wt_ref, *refs = refs
+        ga_refs, (keep_ref, send_ref, turned, grads, out_sem) = refs[:GROUPS], refs[GROUPS:]
         core = place_ref[2]
-        at_mine = pl.multiple_of(core * heads, heads)
-        at_theirs = pl.multiple_of((1 - core) * heads, heads)
         for image in range(2):
             lanes = slice(image * length, (image + 1) * length)
-            turned[pl.ds(at_mine, heads), lanes] = mine_ref[image].T
-            turned[pl.ds(at_theirs, heads), lanes] = theirs_ref[1 - image].T
+            for g in range(GROUPS):
+                at_mine, at_theirs = head_rows(core, heads, g)
+                turned[pl.ds(at_mine, heads), lanes] = mine_refs[g][image].T
+                turned[pl.ds(at_theirs, heads), lanes] = theirs_refs[g][1 - image].T
         term = dot(turned[:, :length], own_half[...]) + dot(turned[:, length:], other_half[...])
         for z in range(z_size):
             for x in range(2):
@@ -770,10 +887,12 @@
             first, second = ref[:, :half], ref[:, half:]
             left = select(core, first, second)
             right = select(core, second, first)
-            ga_ref[image] = low(
-                dot_tail(left, wm_ref[pl.ds(at_mine, heads), :])
-                + dot_tail(right, wt_ref[pl.ds(at_mine, heads), :])
-            )
+            for g in range(GROUPS):
+                at_mine, _ = head_rows(core, heads, g)
+                ga_refs[g][image] = low(
+                    dot_tail(left, wm_ref[pl.ds(at_mine, heads), :])
+                    + dot_tail(right, wt_ref[pl.ds(at_mine, heads), :])
+                )
         for slot, ref in enumerate((keep_ref, send_ref)):
             pltpu.make_async_copy(grads.at[slot], ref, out_sem.at[slot]).wait()
 
@@ -782,20 +901,19 @@
     return call(
         body,
         place,
-        (grad_own, grad_other, grad_own, grad_other, mine, theirs, weight_mine, weight_theirs),
+        (grad_own, grad_other, grad_own, grad_other, *mine, *theirs, weight_mine, weight_theirs),
         [whole((length, width))] * 2
         + [half_block] * 2
-        + [whole((2, length, heads))] * 2
+        + [whole((2, length, heads))] * (2 * GROUPS)
         + [whole((width, half))] * 2,
-        [sds((2, length, heads), jnp.bfloat16)] + [piece_out] * 2,
-        [whole((2, length, heads))] + [any_spec()] * 2,
+        [sds((2, length, heads), jnp.bfloat16)] * GROUPS + [piece_out] * 2,
+        [whole((2, length, heads))] * GROUPS + [any_spec()] * 2,
         [
             pltpu.VMEM((width, 2 * length), jnp.bfloat16),
             pltpu.VMEM((2, z_size, part, half), jnp.bfloat16),
             pltpu.SemaphoreType.DMA((2,)),
         ],
         "out_back",
-        flops=8 * length * width * half,
     )
 
 
@@ -842,55 +960,57 @@
             pltpu.SemaphoreType.DMA((2,)),
         ],
         "qkv_term",
-        flops=4 * length * width * cols,
-    )
-
-
-def qkv_back(place, grad_q, grad_k, grad_v, pieces):
+    )
+
+
+def qkv_back(place, grads, pieces):
     flat = [one for piece in pieces for (one,) in piece]
-    z_size, part, cols_part = flat[0].shape
-    part -= TILE
-    cols = cols_part * len(pieces)
+    z_size, _, cols = flat[0].shape
+    heads = cols // 3
+    length = grads[0][0].shape[1]
+    part = flat[-1].shape[1]
     width = 2 * z_size * part
-    heads = cols // 3
-    length = grad_q.shape[1]
-
-    def body(place_ref, gq_ref, gk_ref, gv_ref, *refs):
-        ins, (own_ref, other_ref, weight, sem) = refs[: len(flat)], refs[len(flat) :]
+
+    def body(place_ref, *refs):
+        grad_refs, refs = refs[: 3 * GROUPS], refs[3 * GROUPS :]
+        ins, (own_ref, *other_refs, weight, sem) = refs[: len(flat)], refs[len(flat) :]
         copies = []
-        for number, ref in enumerate(ins):
-            lanes = pl.ds(number // 2 * cols_part, cols_part)
-            for z in range(z_size):
-                row = pl.multiple_of(shard_number(place_ref, z, number % 2) * part, part)
-                copy = pltpu.make_async_copy(
-                    ref.at[z, pl.ds(0, part), :],
-                    weight.at[pl.ds(row, part), lanes],
-                    sem.at[len(copies)],
-                )
-                copy.start()
-                copies.append(copy)
+        for g in range(GROUPS):
+            copies += weight_copies(
+                place_ref, ins[2 * g : 2 * g + 2], weight.at[g], part, sem.at[g]
+            )
+        for copy in copies:
+            copy.start()
         for copy in copies:
             copy.wait()
-        for image, out_ref in enumerate((own_ref, other_ref)):
-            out_ref[...] = (
-                dot_tail(gq_ref[image], weight[:, :heads])
-                + dot_tail(gk_ref[image], weight[:, heads : 2 * heads])
-                + dot_tail(gv_ref[image], weight[:, 2 * heads :])
-            )
+        for image in range(2):
+            total = None
+            for g in range(GROUPS):
+                for slot in range(3):
+                    add = dot_tail(
+                        grad_refs[3 * g + slot][image],
+                        weight[g, :, slot * heads : (slot + 1) * heads],
+                    )
+                    total = add if total is None else total + add
+            if image == 0:
+                own_ref[...] = total
+            else:
+                for number, ref in enumerate(other_refs):
+                    at = number * width // GIVEN
+                    ref[...] = low(total[:, at : at + width // GIVEN])
 
     return call(
         body,
         place,
-        (grad_q, grad_k, grad_v, *flat),
-        [whole((2, length, heads))] * 3 + [any_spec()] * len(flat),
-        [sds((length, width), jnp.float32)] * 2,
-        [whole((length, width))] * 2,
+        (*[one for grad in grads for one in grad], *flat),
+        [whole((2, length, heads))] * (3 * GROUPS) + [any_spec()] * len(flat),
+        [sds((length, width), jnp.float32)] + [sds((length, width // GIVEN), jnp.bfloat16)] * GIVEN,
+        [whole((length, width))] + [whole((length, width // GIVEN))] * GIVEN,
         [
-            pltpu.VMEM((width, cols), jnp.bfloat16),
-            pltpu.SemaphoreType.DMA((z_size * len(flat),)),
+            pltpu.VMEM((GROUPS, width, cols), jnp.bfloat16),
+            pltpu.SemaphoreType.DMA((GROUPS, 2 * z_size)),
         ],
         "qkv_back",
-        flops=4 * length * width * cols,
     )
 
 
@@ -914,14 +1034,8 @@
     )
 
 
-def statistics(place, kinds, shares, weights, states, images, group, extra=None):
-    flat = []
-    places = []
-    for chunks in shares:
-        if not any(chunks is done for done, _ in places):
-            places.append((chunks, len(flat)))
-            flat += [a for pair in chunks for side in pair for a in side]
-    starts = [next(at for done, at in places if done is chunks) for chunks in shares]
+def statistics(place, kinds, pairs, shares, weights, states, images, group, extra=None):
+    flat = [a for pair in pairs for side in pair for a in side]
     amount = len(kinds)
     vectors = 0 if extra is None else len(extra[1])
 
@@ -934,7 +1048,7 @@
             del refs[:n]
             return taken
 
-        share_refs = take(len(flat))
+        sides_of = [[take(len(side)) for side in pair] for pair in pairs]
         weight_refs, state_refs = take(amount), take(amount)
         if vectors:
             (terms_ref,) = take(1)
@@ -947,14 +1061,14 @@
         for number, kind in enumerate(kinds):
             grad_ref, weight_ref = grad_refs[number], weight_refs[number]
             rows, cols = weights[number].shape
-            at_share = starts[number]
-            for chunk, pair in enumerate(shares[number]):
-                sides = []
-                for side in pair:
-                    sides.append(share_refs[at_share : at_share + len(side)])
-                    at_share += len(side)
-
-                def halves(index):
+            for chunk, (number_of, row0, col0) in enumerate(shares[number]):
+                sides = sides_of[number_of]
+
+                def halves(row, row_count, col, col_count):
+                    index = (
+                        slice(row0 + row, row0 + row + row_count),
+                        slice(col0 + col, col0 + col + col_count),
+                    )
                     mine, theirs = [
                         sum([wide(ref[index]) for ref in side[1:]], wide(side[0][index]))
                         * (1.0 / images)
@@ -964,23 +1078,22 @@
 
                 if kind == "in":
                     per = cols // (2 * CHUNKS * group)
-                    for c, half in enumerate(halves((slice(0, rows), slice(None)))):
+                    for c, half in enumerate(halves(0, rows, 0, per * group)):
                         for s in range(group):
                             at = ((s * 2 + c) * CHUNKS + chunk) * per
                             grad_ref[:, at : at + per] = half[:, s * per : (s + 1) * per]
                 elif kind == "down":
                     per = rows // (2 * CHUNKS)
-                    first = sides[0][0].shape[0] - per
-                    for c, half in enumerate(halves((slice(first, first + per), slice(None)))):
+                    for c, half in enumerate(halves(0, per, 0, cols)):
                         at = (c * CHUNKS + chunk) * per
                         grad_ref[at : at + per, :] = half
                 else:
-                    groups = cols // (2 * SPLIT[kind])
+                    amount_of = len(shares[number])
+                    lanes_of = cols // (2 * SPLIT[kind] * amount_of)
                     for slot in range(SPLIT[kind]):
-                        lanes = slice(slot * groups, (slot + 1) * groups)
-                        for c, half in enumerate(halves((slice(None), lanes))):
-                            at = (2 * slot + c) * groups
-                            grad_ref[:, at : at + groups] = half
+                        for c, half in enumerate(halves(0, rows, slot * lanes_of, lanes_of)):
+                            at = ((2 * slot + c) * amount_of + chunk) * lanes_of
+                            grad_ref[:, at : at + lanes_of] = half
             squared = grad_ref[...] * grad_ref[...]
             new_rows = 0.5 * to_column(state_refs[number][...]) + 0.5 * jnp.mean(
                 squared, axis=1, keepdims=True
@@ -1050,10 +1163,11 @@
     )
 
 
+CLIP_ORDER = (8, 10, 4, 2)
 SPLIT = {"out": 1, "qkv": 3}
 
 
-def update(place, grads, new_rows, weights, cols_states, pack, group, extra=None):
+def update(place, grads, new_rows, weights, cols_states, pack, group, extra=None, clips=None):
     amount = len(weights)
     vectors = 0 if extra is None else len(extra[0])
 
@@ -1069,11 +1183,13 @@
         (pack_ref,) = take(1)
         if vectors:
             vector_grads, moment_refs, param_refs = [take(vectors) for _ in range(3)]
+            (clips_ref,) = take(1)
         new_refs, col_refs = take(amount), take(amount)
         (clip_ref,) = take(1)
         param_outs = take(vectors)
         at_pack = 0
-        clip_ref[...] = jnp.zeros(clip_ref.shape, jnp.float32)
+        if not vectors:
+            clip_ref[...] = jnp.zeros(clip_ref.shape, jnp.float32)
         for number in range(amount):
             rows, cols = weights[number].shape
             rows_total = rows * group
@@ -1091,7 +1207,12 @@
             total = mean_rows * jnp.sum(by_rows / new_cols, axis=1, keepdims=True)
             clip = jnp.maximum(1.0, jnp.sqrt(total / count) / clip_level)
             step = step_rate * jnp.sqrt(weight_total / count) / clip
-            clip_ref[number : number + 1, :] = jnp.broadcast_to(clip, (1, LANES))
+            if vectors:
+                if number == 0:
+                    found = [clips_ref[at : at + 1, :1] for at in range(len(MATRICES) - amount)]
+                found.append(clip)
+            else:
+                clip_ref[number : number + 1, :] = jnp.broadcast_to(clip, (1, LANES))
             estimate = to_column(row_refs[number][...]) * (new_cols / mean_rows)
             new_refs[number][...] = weight_refs[number][...] - step * (
                 grad_refs[number][...] * lax.rsqrt(estimate)
@@ -1103,16 +1224,21 @@
             at_pack += LANES
             clip = jnp.maximum(1.0, jnp.sqrt(total / count) / clip_level)
             step = step_rate * jnp.sqrt(weight_total / count) / clip
-            slot = amount + number
-            clip_ref[slot : slot + 1, :] = jnp.broadcast_to(clip, (1, LANES))
+            found.append(clip)
             direction = vector_grads[number][...] * lax.rsqrt(moment_refs[number][...])
             param_outs[number][...] = param_refs[number][...] - step * direction
+        if vectors:
+            lane = lax.broadcasted_iota(jnp.int32, (1, LANES), 1)
+            row = jnp.zeros((1, LANES), jnp.float32)
+            for value, number in zip(found, (*CLIP_ORDER, *VECTORS)):
+                row = jnp.where(lane == number, value, row)
+            clip_ref[...] = row[:, : len(found)]
 
     ins = [*grads, *new_rows, *weights, *cols_states, pack]
     outs = [sds(a.shape, jnp.float32) for a in (*weights, *cols_states)]
-    outs.append(sds((TILE, LANES), jnp.float32))
+    outs.append(sds((1, len(MATRICES) + vectors) if vectors else (8, LANES), jnp.float32))
     if vectors:
-        ins += [*extra[0], *extra[1], *extra[2]]
+        ins += [*extra[0], *extra[1], *extra[2], clips]
         outs += [sds(a.shape, jnp.float32) for a in extra[2]]
     results = call(
         body,
@@ -1136,9 +1262,10 @@
     z_size = lax.axis_size("z")
     shards = 2 * z_size
     per_shard = sizes[6] // 2 // CHUNKS
-    heads = sums_qkv.shape[1]
-
-    def body(place_ref, mid_ref, in_ref, qkv_ref, *refs):
+    heads = sums_qkv[0].shape[1]
+
+    def body(place_ref, mid_ref, in_ref, *refs):
+        qkv_refs, refs = refs[:GROUPS], refs[GROUPS:]
         hidden_refs, (down_ref, out_ref) = refs[:CHUNKS], refs[CHUNKS:]
         core = place_ref[2]
 
@@ -1149,10 +1276,10 @@
 
         put(0, in_ref[0:1, :])
         put(1, in_ref[1:2, :])
-        zero = jnp.zeros((1, heads), jnp.float32)
+        zero = jnp.zeros((1, heads * GROUPS), jnp.float32)
         halves = []
         for slot in (0, 2):
-            row = qkv_ref[slot : slot + 1, :]
+            row = jnp.concatenate([ref[slot : slot + 1, :] for ref in qkv_refs], axis=1)
             halves += [select(core, row, zero), select(core, zero, row)]
         put(2, jnp.concatenate(halves, axis=1))
         put(3, mid_ref[2:3, :])
@@ -1169,7 +1296,7 @@
                     here = select(core, row, none) if c == 0 else select(core, none, row)
                     out_ref[s : s + 1, at : at + per_shard] = here
 
-    ins = (sums_mid, sums_in, sums_qkv, *hidden_sums, down_sums)
+    ins = (sums_mid, sums_in, *sums_qkv, *hidden_sums, down_sums)
     shape = (shards, sum(sizes))
     return call(
         body,
@@ -1249,144 +1376,192 @@
     moments = [as_row(moment) for moment in moments]
     sizes = [param.shape[1] for param in params]
 
-    pieces_qkv = [gather_rows(one, False) for one in prepare_qkv(place, qkv_weight, params)]
-    *shards_ff, rows_own, cot_own, down_sums = prepare_rest(
-        place, in_weight, down_weight, out_weight, inputs, cotangent, by_y
-    )
+    shard_first, shard_next = prepare_qkv(place, qkv_weight, out_weight, params)
+    near = along_z(shard_first)
+    pieces_first = by_x(near)
+    near_next = along_z(after(shard_next, near))
+    rows_own = pad_rows(after(place, near), inputs)
     rows = (rows_own, swap(rows_own, "c"))
-    cot = (cot_own, swap(cot_own, "c"))
-    pieces_ff = [gather_rows(shard, by_y) for shard in shards_ff]
-    weight_mine = gather_out(place, pieces_ff[0], shards_ff[1].shape[0])
+    *shards_ff, down_sums = prepare_rest(
+        after(place, rows_own), in_weight, down_weight, cotangent, (2 if by_y else 1, 1)
+    )
+    cot_own = pad_rows(after(place, (down_sums, rows[1])), cotangent)
+    near_ff = [along_z(shards_ff[0])]
+
+    normed, *first, vectors, hidden_bias = project_first(
+        after(place, cot_own), rows, pieces_first, sizes
+    )
+    near_ff.append(along_z(after(shards_ff[1], normed)))
+    cot = (cot_own, swap(after(cot_own, normed), "c"))
+    qkv = [first]
+    near_next = after(near_next, normed)
+    pieces_next = by_x(near_next)
+    mixed, prob = attention(after(place, near_next), *first)
+    attended = [mixed]
+    probs = [prob]
+    theirs = [swap(mixed, "c")]
+    pieces_next = after(pieces_next, mixed)
+    weight_mine = gather_out(place, pieces_next, 3 * first[0].shape[-1])
     weight_theirs = swap(weight_mine, "c")
-
-    normed, query, keys, values, vectors, hidden_bias = project_qkv(
-        place, rows, pieces_qkv, sizes
-    )
-    attended, probs = attention(place, query, keys, values)
-    attended_theirs = swap(attended, "c")
+    near_ff[0] = after(near_ff[0], weight_mine)
+    across = swap(near_ff[0], "x")
+    near_too = swap(near_ff[0], "y") if by_y else None
+    qkv.append(
+        project_next(after(place, near_ff[0]), normed, vectors, pieces_next, 1)
+    )
+    mixed, prob = attention(place, *qkv[1])
+    attended.append(mixed)
+    probs.append(prob)
+    theirs.append(swap(mixed, "c"))
+    across = after(across, mixed)
+    if by_y:
+        pieces_ff = [[near_ff[0], near_too], [across, swap(across, "y")]]
+    else:
+        pieces_ff = [[near_ff[0]], [across]]
     middle, normed_mid = project_out(
-        place, attended, attended_theirs, weight_mine, weight_theirs, rows, vectors
-    )
-    running = None
-    hidden_sums = []
-    shares_ff = []
-    for j in range(CHUNKS):
-        *running, sums, keep, send = feed_forward(
-            place, normed_mid, cot, pieces_ff[j], hidden_bias, j, running
-        )
-        hidden_sums.append(sums)
-        shares_ff.append(scatter_sum(keep, send))
+        after(place, across), attended, theirs, weight_mine, weight_theirs, rows, vectors
+    )
+    near_ff[1] = after(near_ff[1], normed_mid)
+    pieces_next_ff = by_x(near_ff[1])
+    *running, sums, keep, send = feed_forward(
+        after(place, near_ff[1]), normed_mid, cot, pieces_ff, hidden_bias, 0, None
+    )
+    hidden_sums = [sums]
+    got = swap(send, "x")
+    *running, sums, keep_next, send_next = feed_forward(
+        place, normed_mid, cot, pieces_next_ff, hidden_bias, 1, running
+    )
+    hidden_sums.append(sums)
+    folded = [fold(*after((keep, got), sums))]
+    got_next = swap(send_next, "x")
+    scattered = [scatter_z(folded[0])]
     out_share, out_given, normed_share, normed_given = running
     sums_mid, output, grad_mid, grad_mid_low = norm_back(
-        place,
+        after(place, folded[0]),
         middle,
         vectors,
         GAIN_TWO,
         normed_share,
-        swap(normed_given, "c"),
+        [swap(normed_given, "c")],
         cot_own,
         tokens,
         (out_share, swap(out_given, "c")),
     )
-    grad_attended, keep, send = out_back(
+    *grad_attended, keep, send = out_back(
         place,
         grad_mid_low,
         swap(grad_mid_low, "c"),
         attended,
-        attended_theirs,
+        theirs,
         weight_mine,
         weight_theirs,
     )
-    share_out = scatter_sum(keep, send)
-    grad_q, grad_k, grad_v = attention_back(place, query, keys, values, probs, grad_attended)
-    sums_qkv, keep, send = qkv_term(place, normed, grad_q, grad_k, grad_v)
-    share_qkv = scatter_sum(keep, send)
-    share, given = qkv_back(place, grad_q, grad_k, grad_v, pieces_qkv)
+    got = swap(send, "x")
+    grad_qkv = [attention_back(place, *qkv[0], probs[0], grad_attended[0])]
+    sums_first, keep_first, send_first = qkv_term(place, normed, *grad_qkv[0])
+    got_first = swap(send_first, "x")
+    folded.append(fold(*after((keep_next, got_next), sums_first)))
+    scattered.append(scatter_z(folded[1]))
+    grad_qkv.append(
+        attention_back(after(place, folded[1]), *qkv[1], probs[1], grad_attended[1])
+    )
+    sums_next, keep_next, send_next = qkv_term(place, normed, *grad_qkv[1])
+    sums_qkv = [sums_first, sums_next]
+    got_next = swap(send_next, "x")
+    held = after(((keep, got), (keep_first, got_first)), sums_next)
+    folded.append(jnp.concatenate([fold(*one) for one in held], axis=1))
+    scattered.append(scatter_z(folded[2]))
+    share, *given = qkv_back(after(place, folded[2]), grad_qkv, [pieces_first, pieces_next])
+    pairs = [finish_sum(after(scattered[0], share))]
     sums_in, input_grad = norm_back(
-        place, rows_own, vectors, GAIN_ONE, share, swap(given, "c"), grad_mid, tokens
-    )
-    terms = sum_over(
-        pack_terms(place, sums_mid, sums_in, sums_qkv, hidden_sums, down_sums, sizes),
-        ("c", "x", "z", "y"),
-    )
-
-    early = ("in", "down", "out")
-    weights = [in_weight, down_weight, out_weight]
-    states = [as_row(state) for state in (in_rows, down_rows, out_rows)]
+        after(place, scattered[0]),
+        rows_own,
+        vectors,
+        GAIN_ONE,
+        share,
+        [swap(one, "c") for one in given],
+        grad_mid,
+        tokens,
+    )
+    packed = pack_terms(
+        after(place, scattered[1]), sums_mid, sums_in, sums_qkv, hidden_sums, down_sums, sizes
+    )
+    folded.append(fold(*after((keep_next, got_next), packed)))
+    scattered.append(scatter_z(folded[3]))
+    pairs += [finish_sum(one) for one in scattered[1:]]
+    terms = sum_over(packed, ("c", "z", "x", "y"))
+
+    weights = [in_weight, down_weight]
+    states = [as_row(state) for state in (in_rows, down_rows)]
+    part = in_weight.shape[0]
     grads_early, rows_early, pack, _, _ = statistics(
-        place, early, [shares_ff, shares_ff, [share_out]], weights, states, images, group
+        place,
+        ("in", "down"),
+        pairs[:CHUNKS],
+        [[(j, row, 0) for j in range(CHUNKS)] for row in (0, part)],
+        weights,
+        states,
+        images,
+        group,
     )
     new_early, cols_early, clips_early, _ = update(
         place,
         grads_early,
         rows_early,
         weights,
-        [as_row(state) for state in (in_cols, down_cols, out_cols)],
-        sum_over(pack, ("x", "z")),
+        [as_row(state) for state in (in_cols, down_cols)],
+        sum_over(pack, ("z", "x")),
         group,
     )
+    weights = [out_weight, qkv_weight]
     grads_late, rows_late, pack, vector_grads, new_moments = statistics(
-        place,
-        ("qkv",),
-        [[share_qkv]],
-        [qkv_weight],
-        [as_row(qkv_rows)],
+        after(place, clips_early),
+        ("out", "qkv"),
+        pairs[CHUNKS:],
+        [[(0, 0, 0)], [(0, 0, out_weight.shape[1] // 2), (1, 0, 0)]],
+        weights,
+        [as_row(state) for state in (out_rows, qkv_rows)],
         images,
         group,
         (terms, params, moments),
     )
-    new_late, cols_late, clips_late, new_vectors = update(
+    new_late, cols_late, clip_factors, new_vectors = update(
         place,
         grads_late,
         rows_late,
-        [qkv_weight],
-        [as_row(qkv_cols)],
-        sum_over(pack, ("x", "z")),
+        weights,
+        [as_row(state) for state in (out_cols, qkv_cols)],
+        sum_over(pack, ("z", "x")),
         group,
         (vector_grads, new_moments, params),
+        clips_early,
     )
 
     flat = lambda value: value.reshape(-1)
     grads = [None] * 12
     new_params = [None] * 12
-    for number, slot in ((8, 0), (10, 1), (4, 2)):
+    for number, slot in ((8, 0), (10, 1)):
         grads[number], new_params[number] = grads_early[slot], new_early[slot]
-    grads[2], new_params[2] = grads_late[0], new_late[0]
+    for number, slot in ((4, 0), (2, 1)):
+        grads[number], new_params[number] = grads_late[slot], new_late[slot]
     for slot, number in enumerate(VECTORS):
         grads[number] = flat(vector_grads[slot])
         new_params[number] = flat(new_vectors[slot])
-    late, first = clips_late[:, 0], clips_early[:, 0]
-    clip_factors = jnp.stack(
-        [
-            late[1],
-            late[2],
-            late[0],
-            late[3],
-            first[2],
-            late[4],
-            late[5],
-            late[6],
-            first[0],
-            late[7],
-            first[1],
-            late[8],
-        ]
-    )
     return (
         output,
         input_grad,
         *grads,
+        flat(rows_late[1]),
+        flat(cols_late[1]),
         flat(rows_late[0]),
         flat(cols_late[0]),
-        flat(rows_early[2]),
-        flat(cols_early[2]),
         flat(rows_early[0]),
         flat(cols_early[0]),
         flat(rows_early[1]),
         flat(cols_early[1]),
         *[flat(moment) for moment in new_moments],
         *new_params,
-        clip_factors,
+        flat(clip_factors),
     )
 
 

time: 621 us -> 483 us (0.78)
  waiting for transfers between devices: 232 us -> 120 us
  Pallas kernels: 245 us -> 263 us
  blocking collectives: 37.8 us -> 23.7 us
  starting transfers between devices: 44.8 us -> 31 us
  local copies, waits for them, and re-layouts: 18.1 us -> 9.84 us
    ppermute x28 -> x33, waiting for transfers between devices: 187 us -> 84.2 us  [swap(): return lax.ppermute(value, axis, [(0, 1), (1, 0)])]
    all_gather x2 -> x3, waiting for transfers between devices: 32 us -> 0.04 us  [along_z(): near = lax.all_gather(shard, 'z', axis=0, tiled=True)]
    pallas_call x19 -> x25, Pallas kernels: 245 us -> 263 us  [call(): pl.pallas_call(body, out_shape=outs, grid_spec=pltpu.PrefetchScalarGridSp...]
    reduce_scatter x4, waiting for transfers between devices: 0.05 us -> 16.3 us  [scatter_z(): return lax.psum_scatter(total, 'z', scatter_dimension=0, tiled=True)]
    all_gather x2 -> x1, blocking collectives: 37.8 us -> 23.7 us  [along_z(): near = lax.all_gather(shard, 'z', axis=0, tiled=True)]
    ppermute x11 -> x5, starting transfers between devices: 17.5 us -> 3.47 us  [partner(): return lax.ppermute(value, axis, [(i, i ^ step) for i in range(size)])]
    ppermute x28 -> x33, starting transfers between devices: 24.8 us -> 16.8 us  [swap(): return lax.ppermute(value, axis, [(0, 1), (1, 0)])]
    ppermute x4 -> x9, starting transfers between devices: 2 us -> 9.95 us  [shift(): lax.ppermute(value, axis, [(i, (i + step) % size) for i in range(size)])]
  transfers between devices with their start and end apart: 49 -> 54, of which waited for: 18 -> 23; matrix products, arithmetic and copies ran while one was open for 3% -> 2% of each run, Pallas kernels for 32% -> 52%
where the time goes in v5:
time: 483 us; the launch traced here: 478 us
  Pallas kernels  263 us (54%)
  waiting for transfers between devices  120 us (25%)
  starting transfers between devices  31 us (6%)
  blocking collectives  23.7 us (5%)
  other arithmetic  15.3 us (3%)
  between operations  14.9 us (3%)
  local copies, waits for them, and re-layouts  9.84 us (2%)
    pallas_call x25, Pallas kernels, call(): pl.pallas_call(body, out_shape=outs, grid_spec=pltpu.PrefetchScalarGridSp...  263 us
    ppermute x33, waiting for transfers between devices, swap(): return lax.ppermute(value, axis, [(0, 1), (1, 0)])  84.2 us
    all_gather x1, blocking collectives, along_z(): near = lax.all_gather(shard, 'z', axis=0, tiled=True)  23.7 us
    ppermute x33, starting transfers between devices, swap(): return lax.ppermute(value, axis, [(0, 1), (1, 0)])  16.8 us
    reduce_scatter x4, waiting for transfers between devices, scatter_z(): return lax.psum_scatter(total, 'z', scatter_dimension=0, tiled=True)  16.3 us
    ppermute x9, starting transfers between devices, shift(): lax.ppermute(value, axis, [(i, (i + step) % size) for i in range(size)])  9.95 us
    ppermute x9, waiting for transfers between devices, shift(): lax.ppermute(value, axis, [(i, (i + step) % size) for i in range(size)])  9.95 us
    unnamed x76, local copies, waits for them, and re-layouts  9.84 us
  transfers between devices with their start and end apart: 54, of which 23 were waited for; matrix products, arithmetic and copies ran while one was open for 2% of the time, Pallas kernels for 52%

profile of v5, /device:TPU:0, one launch (start us, length us, event | category | flops | bytes accessed | tf_op | source)
XLA Modules:
  0.0 478.2 jit_solution(14467194932135455249)
XLA Ops:
  7.9 3.2 prepare_qkv.1
  11.1 23.7 %all_gather.12 = bf16[640,768]{1,0:T(8,128)(2,1)S(1)} all-gather(bf16[160,768]{1,0:T(8,128)(2,1)} %get-tuple-element.180), channel_id=1, replica_groups=mesh['z'=4,'x'=2,'y'=2,'c'=2] {'z'}, dimensions={0}, use_global_device_ids=true | all-gather | bytes 1228800 | tf_op jit(solution)/shard_map/all_gather | solution.py:59
  38.0 4.3 prepare_rest.1
  47.0 19.6 %collective-permute-done.1.refs_1_.refs_7_ = bf16[4,160,768]{2,1,0:T(8,128)(2,1)S(1)} collective-permute-done((bf16[4,160,768]{2,1,0:T(8,128)(2,1)S(1)}, bf16[4,160,768]{2,1,0:T(8,128)(2,1)S(1)}, u32[]{:S(2)}, u32[]{:S(2)}) %collective-permute-start.1) | collective-permute-done | bytes 983072 | tf_op jit(solution)/shard_map/ppermute | solution.py:32
  67.6 8.8 %project_first.1 = (bf16[2,640,1024]{2,1,0:T(8,128)(2,1)}, bf16[2,640,256]{2,1,0:T(8,128)(2,1)}, bf16[2,640,256]{2,1,0:T(8,128)(2,1)}, bf16[2,640,256]{2,1,0:T(8...) custom-call(s32[4]{0:T(128)} %pad_add_fusion.place_ref, bf16[640,1024]{1,0:T(8,128)(2,1)} %pad_rows.2.own_ref.refs_6_.rows_ref, ...), custom_call_target="tpu_custom_call" | custom-call | tf_op jit(solution)/shard_map/project_first/pallas_call | solution.py:127
  78.5 15.5 %attention.2 = (bf16[2,640,256]{2,1,0:T(8,128)(2,1)}, bf16[2,2,2,640,640]{4,3,2,1,0:T(8,128)(2,1)}) custom-call(s32[4]{0:T(128)} %pad_add_fusion.place_ref, bf16[2,640,256]{2,1,0:T(8,128)(2,1)} %get-tuple-element.194.q_ref, bf16[2,640,256]{2,1,0:T(8,128)(2,1)} %get-tuple-element.195.k_ref, bf16[2,640,256]{2,1,0:T(8,128)(2,1)} %get-tuple-element.196.v_ref), custom_call_target="tpu_custom_call" | custom-call | tf_op jit(solution)/shard_map/attention/pallas_call | solution.py:127
  94.0 13.2 %collective-permute-done.2.refs_1_.refs_9_ = bf16[4,128,1280]{2,1,0:T(8,128)(2,1)S(1)} collective-permute-done((bf16[4,128,1280]{2,1,0:T(8,128)(2,1)}, bf16[4,128,1280]{2,1,0:T(8,128)(2,1)S(1)}, u32[]{:S(2)}, u32[]{:S(2)}) %collective-permute-start.2) | collective-permute-done | bytes 1310752 | tf_op jit(solution)/shard_map/ppermute | solution.py:32
  114.9 7.2 %project_next.1 = (bf16[2,640,256]{2,1,0:T(8,128)(2,1)}, bf16[2,640,256]{2,1,0:T(8,128)(2,1)}, bf16[2,640,256]{2,1,0:T(8,128)(2,1)}) custom-call(s32[4]{0:T(128)} %pad_add_fusion.place_ref, bf16[2,640,1024]{2,1,0:T(8,128)(2,1)} %get-tuple-element.187.normed_ref, f32[8,1024]{1,0:T(8,128)} %get-tuple-element.202.vec_ref.refs_8_, ...), custom_call_target="tpu_custom_call" | custom-call | tf_op jit(solution)/shard_map/project_next/pallas_call | solution.py:127
  122.1 15.4 %attention.3 = (bf16[2,640,256]{2,1,0:T(8,128)(2,1)}, bf16[2,2,2,640,640]{4,3,2,1,0:T(8,128)(2,1)}) custom-call(s32[4]{0:T(128)} %pad_add_fusion.place_ref, bf16[2,640,256]{2,1,0:T(8,128)(2,1)} %get-tuple-element.203.q_ref, bf16[2,640,256]{2,1,0:T(8,128)(2,1)} %get-tuple-element.204.k_ref, bf16[2,640,256]{2,1,0:T(8,128)(2,1)} %get-tuple-element.205.v_ref), custom_call_target="tpu_custom_call" | custom-call | tf_op jit(solution)/shard_map/attention/pallas_call | solution.py:127
  141.3 9.9 %project_out.1 = (f32[640,1024]{1,0:T(8,128)}, bf16[2,640,1024]{2,1,0:T(8,128)(2,1)}) custom-call(s32[4]{0:T(128)} %pad_add_fusion.place_ref, bf16[2,640,256]{2,1,0:T(8,128)(2,1)} %get-tuple-element.197.refs_0_, bf16[2,640,256]{2,1,0:T(8,128)(2,1)} %get-tuple-element.206.refs_1_, bf16[2,640,256]{2,1,0:T(8,128)(2,1)} %collective-permute-done.4.refs_2_, ...), custom_call_target="tpu_custom_call" | custom-call | tf_op jit(solution)/shard_map/project_out/pallas_call | solution.py:127
  151.8 11.7 %collective-permute-done.9.refs_3_ = bf16[4,128,1024]{2,1,0:T(8,128)(2,1)} collective-permute-done((bf16[4,128,1024]{2,1,0:T(8,128)(2,1)}, bf16[4,128,1024]{2,1,0:T(8,128)(2,1)}, u32[]{:S(2)}, u32[]{:S(2)}) %collective-permute-start.9) | collective-permute-done | bytes 1048608 | tf_op jit(solution)/shard_map/ppermute | solution.py:32
  163.5 36.2 %feed_forward.2 = (f32[640,1024]{1,0:T(8,128)}, f32[640,1024]{1,0:T(8,128)}, f32[640,1024]{1,0:T(8,128)}, f32[640,1024]{1,0:T(8,128)}, f32[4,1,256]{2,1,0:T(1,12...) custom-call(s32[4]{0:T(128)} %pad_add_fusion.place_ref, ...), custom_call_target="tpu_custom_call" | custom-call | tf_op jit(solution)/shard_map/feed_forward/pallas_call | solution.py:127
  200.2 38.7 %feed_forward.3 = (f32[640,1024]{1,0:T(8,128)}, bf16[640,1024]{1,0:T(8,128)(2,1)}, f32[640,1024]{1,0:T(8,128)}, bf16[640,1024]{1,0:T(8,128)(2,1)}, f32[4,1,256]{...) custom-call(s32[4]{0:T(128)} %pad_add_fusion.place_ref, ...), custom_call_target="tpu_custom_call" | custom-call | tf_op jit(solution)/shard_map/feed_forward/pallas_call | solution.py:127
  239.0 8.4 %collective-permute-done.10 = bf16[4,256,1024]{2,1,0:T(8,128)(2,1)} collective-permute-done((bf16[4,256,1024]{2,1,0:T(8,128)(2,1)}, bf16[4,256,1024]{2,1,0:T(8,128)(2,1)}, u32[]{:S(2)}, u32[]{:S(2)}) %collective-permute-start.10) | collective-permute-done | bytes 2097184 | tf_op jit(solution)/shard_map/ppermute | solution.py:32
  247.4 3.9 add_convert_fusion.1
  257.4 10.1 %norm_back.2 = (f32[8,1024]{1,0:T(8,128)}, bf16[577,1024]{1,0:T(8,128)(2,1)}, f32[640,1024]{1,0:T(8,128)}, bf16[640,1024]{1,0:T(8,128)(2,1)}) custom-call(s32[4]{0:T(128)} %pad_add_fusion.place_ref, f32[640,1024]{1,0:T(8,128)} %get-tuple-element.224.rows_ref, f32[8,1024]{1,0:T(8,128)} %get-tuple-element.202.vec_ref.refs_8_, ...), custom_call_target="tpu_custom_call" | custom-call | tf_op jit(solution)/shard_map/norm_back/pallas_call | solution.py:127
  271.8 9.2 %out_back.1 = (bf16[2,640,256]{2,1,0:T(8,128)(2,1)}, bf16[2,640,256]{2,1,0:T(8,128)(2,1)}, bf16[4,128,512]{2,1,0:T(8,128)(2,1)}, bf16[4,128,512]{2,1,0:T(8,128)(2,1)}) custom-call(s32[4]{0:T(128)} %pad_add_fusion.place_ref, bf16[640,1024]{1,0:T(8,128)(2,1)} %get-tuple-element.231.own_ref.own_half, bf16[640,1024]{1,0:T(8,128)(2,1)} %copy-done.3, ...), custom_call_target="tpu_custom_call" | custom-call | tf_op jit(solution)/shard_map/out_back/pallas_call | solution.py:127
  281.1 17.6 %attention_back.2 = (bf16[2,640,256]{2,1,0:T(8,128)(2,1)}, bf16[2,640,256]{2,1,0:T(8,128)(2,1)}, bf16[2,640,256]{2,1,0:T(8,128)(2,1)}) custom-call(s32[4]{0:T(128)} %pad_add_fusion.place_ref, bf16[2,640,256]{2,1,0:T(8,128)(2,1)} %get-tuple-element.194.q_ref, bf16[2,640,256]{2,1,0:T(8,128)(2,1)} %get-tuple-element.195.k_ref, ...), custom_call_target="tpu_custom_call" | custom-call | tf_op jit(solution)/shard_map/attention_back/pallas_call | solution.py:127
  298.7 7.6 %qkv_term.2 = (f32[3,256]{1,0:T(4,128)}, bf16[4,128,768]{2,1,0:T(8,128)(2,1)}, bf16[4,128,768]{2,1,0:T(8,128)(2,1)}) custom-call(s32[4]{0:T(128)} %pad_add_fusion.place_ref, bf16[2,640,1024]{2,1,0:T(8,128)(2,1)} %get-tuple-element.187.normed_ref, bf16[2,640,256]{2,1,0:T(8,128)(2,1)} %get-tuple-element.236.gq_ref.refs_0_, ...), custom_call_target="tpu_custom_call" | custom-call | tf_op jit(solution)/shard_map/qkv_term/pallas_call | solution.py:127
  306.3 3.9 add_convert_fusion
  313.3 18.1 %attention_back.3 = (bf16[2,640,256]{2,1,0:T(8,128)(2,1)}, bf16[2,640,256]{2,1,0:T(8,128)(2,1)}, bf16[2,640,256]{2,1,0:T(8,128)(2,1)}) custom-call(s32[4]{0:T(128)} %pad_add_fusion.place_ref, bf16[2,640,256]{2,1,0:T(8,128)(2,1)} %get-tuple-element.203.q_ref, bf16[2,640,256]{2,1,0:T(8,128)(2,1)} %get-tuple-element.204.k_ref, ...), custom_call_target="tpu_custom_call" | custom-call | tf_op jit(solution)/shard_map/attention_back/pallas_call | solution.py:127
  331.5 7.6 %qkv_term.3 = (f32[3,256]{1,0:T(4,128)}, bf16[4,128,768]{2,1,0:T(8,128)(2,1)}, bf16[4,128,768]{2,1,0:T(8,128)(2,1)}) custom-call(s32[4]{0:T(128)} %pad_add_fusion.place_ref, bf16[2,640,1024]{2,1,0:T(8,128)(2,1)} %get-tuple-element.187.normed_ref, bf16[2,640,256]{2,1,0:T(8,128)(2,1)} %get-tuple-element.249.gq_ref.refs_3_, ...), custom_call_target="tpu_custom_call" | custom-call | tf_op jit(solution)/shard_map/qkv_term/pallas_call | solution.py:127
  344.1 10.0 %qkv_back.1 = (f32[640,1024]{1,0:T(8,128)}, bf16[640,512]{1,0:T(8,128)(2,1)}, bf16[640,512]{1,0:T(8,128)(2,1)}) custom-call(s32[4]{0:T(128)} %pad_add_fusion.place_ref, bf16[2,640,256]{2,1,0:T(8,128)(2,1)} %get-tuple-element.236.gq_ref.refs_0_, bf16[2,640,256]{2,1,0:T(8,128)(2,1)} %get-tuple-element.237.gk_ref.refs_1_, ...), custom_call_target="tpu_custom_call" | custom-call | tf_op jit(solution)/shard_map/qkv_back/pallas_call | solution.py:127
  358.4 7.6 %norm_back.3 = (f32[8,1024]{1,0:T(8,128)}, bf16[577,1024]{1,0:T(8,128)(2,1)}) custom-call(s32[4]{0:T(128)} %pad_add_fusion.place_ref, bf16[640,1024]{1,0:T(8,128)(2,1)} %pad_rows.2.own_ref.refs_6_.rows_ref, f32[8,1024]{1,0:T(8,128)} %get-tuple-element.202.vec_ref.refs_8_, f32[640,1024]{1,0:T(8,128)} %get-tuple-element.258.own_ref, ...), custom_call_target="tpu_custom_call" | custom-call | tf_op jit(solution)/shard_map/norm_back/pallas_call | solution.py:127
  374.9 9.3 %collective-permute-done.20.refs_1_ = bf16[256,1024]{1,0:T(8,128)(2,1)S(1)} collective-permute-done((bf16[256,1024]{1,0:T(8,128)(2,1)S(1)}, bf16[256,1024]{1,0:T(8,128)(2,1)S(1)}, u32[]{:S(2)}, u32[]{:S(2)}) %collective-permute-start.20) | collective-permute-done | bytes 524320 | tf_op jit(solution)/shard_map/ppermute | solution.py:32
  387.1 7.6 %collective-permute-done.23.refs_5_ = bf16[256,1024]{1,0:T(8,128)(2,1)S(1)} collective-permute-done((bf16[256,1024]{1,0:T(8,128)(2,1)S(1)}, bf16[256,1024]{1,0:T(8,128)(2,1)S(1)}, u32[]{:S(2)}, u32[]{:S(2)}) %collective-permute-start.23) | collective-permute-done | bytes 524320 | tf_op jit(solution)/shard_map/ppermute | solution.py:32
  395.2 16.3 %reduce-scatter.11.cloned.1.call-done.refs_4_ = bf16[128,768]{1,0:T(8,128)(2,1)} async-done(((bf16[512,768]{1,0:T(8,128)(2,1)}), bf16[128,768]{1,0:T(8,128)(2,1)}) %reduce-scatter.11.cloned.1.call-update) | async-done | bytes 196624 | tf_op jit(solution)/shard_map/reduce_scatter | solution.py:81
  416.1 7.9 %statistics.2 = (f32[128,4096]{1,0:T(8,128)}, f32[512,1024]{1,0:T(8,128)}, f32[1,128]{1,0:T(1,128)}, f32[1,512]{1,0:T(1,128)}, f32[2,5376]{1,0:T(2,128)}) custom-call(s32[4]{0:T(128)} %pad_add_fusion.place_ref, bf16[256,1024]{1,0:T(8,128)(2,1)} %reduce-scatter.5.cloned.1.call-done.refs_0_, bf16[256,1024]{1,0:T(8,128)(2,1)} %copy-done.19, ...), custom_call_target="tpu_custom_call" | custom-call | tf_op jit(solution)/shard_map/statistics/pallas_call | solution.py:127
  440.4 7.0 %update.2 = (f32[128,4096]{1,0:T(8,128)}, f32[512,1024]{1,0:T(8,128)}, f32[1,4096]{1,0:T(1,128)}, f32[1,1024]{1,0:T(1,128)}, f32[8,128]{1,0:T(8,128)}) custom-call(s32[4]{0:T(128)} %pad_add_fusion.place_ref, f32[128,4096]{1,0:T(8,128)} %get-tuple-element.147.refs_0_, f32[512,1024]{1,0:T(8,128)} %get-tuple-element.149.refs_1_, ...), custom_call_target="tpu_custom_call" | custom-call | tf_op jit(solution)/shard_map/update/pallas_call | solution.py:127
  448.4 4.9 %statistics.3 = (f32[128,1024]{1,0:T(8,128)}, f32[128,3072]{1,0:T(8,128)}, f32[1,128]{1,0:T(1,128)}, f32[1,128]{1,0:T(1,128)}, f32[2,5376]{1,0:T(2,128)}, /*inde...) custom-call(s32[4]{0:T(128)} %pad_add_fusion.place_ref, ...), custom_call_target="tpu_custom_call" | custom-call | tf_op jit(solution)/shard_map/statistics/pallas_call | solution.py:127
  462.0 3.5 collective-permute-done.46
  466.1 5.0 %update.3 = (f32[128,1024]{1,0:T(8,128)}, f32[128,3072]{1,0:T(8,128)}, f32[1,1024]{1,0:T(1,128)}, f32[1,3072]{1,0:T(1,128)}, f32[1,12]{1,0:T(1,128)}, /*index=5*...) custom-call(s32[4]{0:T(128)} %pad_add_fusion.place_ref, ...), custom_call_target="tpu_custom_call" | custom-call | tf_op jit(solution)/shard_map/update/pallas_call | solution.py:127
  (200 shorter events, 90.5 us)
Async XLA Ops:
  7.2 69.2 %all-gather.8.cloned.1.call-start = ((), (), s32[]{:S(2)}) async-start(), calls=%async_computation.6 | async-start | bytes 1638400 | tf_op jit(solution)/shard_map/all_gather | solution.py:59
  34.8 76.5 %all-gather.6.cloned.1.call-start = ((), (), s32[]{:S(2)}) async-start(), calls=%async_computation.5 | async-start | bytes 1310720 | tf_op jit(solution)/shard_map/all_gather | solution.py:59
  42.3 108.9 %all-gather.4.cloned.1.call-start = ((), (), s32[]{:S(2)}) async-start(), calls=%async_computation.4 | async-start | bytes 2621440 | tf_op jit(solution)/shard_map/all_gather | solution.py:59
  42.3 24.3 %collective-permute-start.1 = (bf16[4,160,768]{2,1,0:T(8,128)(2,1)S(1)}, bf16[4,160,768]{2,1,0:T(8,128)(2,1)S(1)}, u32[]{:S(2)}, u32[]{:S(2)}) collective-permute-start(bf16[4,160,768]{2,1,0:T(8,128)(2,1)S(1)} %bitcast.74), channel_id=1, source_target_pairs={{0,4},{4,0},{1,5},{5,1},{2,6},{6,2},{3,7},{7,3},{8,12},{12,8},{9,1... | collective-permute-start | bytes 2949128 | tf_op jit(solution)/shard_map/ppermute | solution.py:32
  76.4 30.8 %collective-permute-start.2 = (bf16[4,128,1280]{2,1,0:T(8,128)(2,1)}, bf16[4,128,1280]{2,1,0:T(8,128)(2,1)S(1)}, u32[]{:S(2)}, u32[]{:S(2)}) collective-permute-start(bf16[4,128,1280]{2,1,0:T(8,128)(2,1)} %bitcast.70), channel_id=1, source_target_pairs={{0,4},{4,0},{1,5},{5,1},{2,6},{6,2},{3,7},{7,3},{8,12},{12,8},{9,1... | collective-permute-start | bytes 3932168 | tf_op jit(solution)/shard_map/ppermute | solution.py:32
  78.0 276.8 %reduce-scatter.5.cloned.1.call-start = ((), (), s32[]{:S(2)}) async-start(), calls=%async_computation.7 | async-start | bytes 2621440 | tf_op jit(solution)/shard_map/reduce_scatter | solution.py:81
  111.3 26.2 %collective-permute-start.3 = (bf16[4,128,1024]{2,1,0:T(8,128)(2,1)}, bf16[4,128,1024]{2,1,0:T(8,128)(2,1)}, u32[]{:S(2)}, u32[]{:S(2)}) collective-permute-start(bf16[4,128,1024]{2,1,0:T(8,128)(2,1)} %bitcast.84), channel_id=1, source_target_pairs={{0,4},{4,0},{1,5},{5,1},{2,6},{6,2},{3,7},{7,3},{8,12},{12,8},{9,1... | collective-permute-start | bytes 3145736 | tf_op jit(solution)/shard_map/ppermute | solution.py:32
  112.8 25.3 %collective-permute-start.4 = (bf16[2,640,256]{2,1,0:T(8,128)(2,1)S(1)}, bf16[2,640,256]{2,1,0:T(8,128)(2,1)}, u32[]{:S(2)}, u32[]{:S(2)}) collective-permute-start(bf16[2,640,256]{2,1,0:T(8,128)(2,1)S(1)} %copy-done.7), channel_id=1, source_target_pairs={{0,1},{1,0},{2,3},{3,2},{4,5},{5,4},{6,7},{7,6},{8,9},{9,8},{10,11... | collective-permute-start | bytes 1966088 | tf_op jit(solution)/shard_map/ppermute | solution.py:32
  112.8 38.9 %collective-permute-start.7 = (bf16[640,1024]{1,0:T(8,128)(2,1)S(1)}, bf16[640,1024]{1,0:T(8,128)(2,1)S(1)}, u32[]{:S(2)}, u32[]{:S(2)}) collective-permute-start(bf16[640,1024]{1,0:T(8,128)(2,1)S(1)} %copy-done), channel_id=1, source_target_pairs={{0,1},{1,0},{2,3},{3,2},{4,5},{5,4},{6,7},{7,6},{8,9},{9,8},{10,11... | collective-permute-start | bytes 3932168 | tf_op jit(solution)/shard_map/ppermute | solution.py:32
  113.4 38.4 %collective-permute-start.8 = (bf16[4,128,1024]{2,1,0:T(8,128)(2,1)}, bf16[4,128,1024]{2,1,0:T(8,128)(2,1)}, u32[]{:S(2)}, u32[]{:S(2)}) collective-permute-start(bf16[4,128,1024]{2,1,0:T(8,128)(2,1)} %bitcast.85), channel_id=1, source_target_pairs={{0,2},{2,0},{1,3},{3,1},{4,6},{6,4},{5,7},{7,5},{8,10},{10,8},{9,1... | collective-permute-start | bytes 3145736 | tf_op jit(solution)/shard_map/ppermute | solution.py:32
  114.9 25.5 %collective-permute-start.6 = (bf16[1024,512]{1,0:T(8,128)(2,1)}, bf16[1024,512]{1,0:T(8,128)(2,1)}, u32[]{:S(2)}, u32[]{:S(2)}) collective-permute-start(bf16[1024,512]{1,0:T(8,128)(2,1)} %gather_out.1.refs_4_), channel_id=1, source_target_pairs={{0,1},{1,0},{2,3},{3,2},{4,5},{5,4},{6,7},{7,6},{8,9},{9,8},{10,11... | collective-permute-start | bytes 3145736 | tf_op jit(solution)/shard_map/ppermute | solution.py:32
  137.5 26.0 %collective-permute-start.9 = (bf16[4,128,1024]{2,1,0:T(8,128)(2,1)}, bf16[4,128,1024]{2,1,0:T(8,128)(2,1)}, u32[]{:S(2)}, u32[]{:S(2)}) collective-permute-start(bf16[4,128,1024]{2,1,0:T(8,128)(2,1)} %collective-permute-done.3.refs_2_), channel_id=1, source_target_pairs={{0,2},{2,0},{1,3},{3,1},{4,6},{6,4},{5,7},{7,5},{8,10},{10,8},{9,1... | collective-permute-start | bytes 3145736 | tf_op jit(solution)/shard_map/ppermute | solution.py:32
  151.1 49.1 %collective-permute-start.11 = (bf16[4,256,1024]{2,1,0:T(8,128)(2,1)}, bf16[4,256,1024]{2,1,0:T(8,128)(2,1)}, u32[]{:S(2)}, u32[]{:S(2)}) collective-permute-start(bf16[4,256,1024]{2,1,0:T(8,128)(2,1)} %bitcast.82), channel_id=1, source_target_pairs={{0,4},{4,0},{1,5},{5,1},{2,6},{6,2},{3,7},{7,3},{8,12},{12,8},{9,1... | collective-permute-start | bytes 6291464 | tf_op jit(solution)/shard_map/ppermute | solution.py:32
  199.7 47.7 %collective-permute-start.10 = (bf16[4,256,1024]{2,1,0:T(8,128)(2,1)}, bf16[4,256,1024]{2,1,0:T(8,128)(2,1)}, u32[]{:S(2)}, u32[]{:S(2)}) collective-permute-start(bf16[4,256,1024]{2,1,0:T(8,128)(2,1)} %get-tuple-element.215), channel_id=1, source_target_pairs={{0,4},{4,0},{1,5},{5,1},{2,6},{6,2},{3,7},{7,3},{8,12},{12,8},{9,1... | collective-permute-start | bytes 6291464 | tf_op jit(solution)/shard_map/ppermute | solution.py:32
  251.3 114.7 %reduce-scatter.7.cloned.1.call-start = ((), (), s32[]{:S(2)}) async-start(), calls=%async_computation.8 | async-start | bytes 2621440 | tf_op jit(solution)/shard_map/reduce_scatter | solution.py:81
  252.6 53.7 %collective-permute-start.17 = (bf16[4,256,1024]{2,1,0:T(8,128)(2,1)}, bf16[4,256,1024]{2,1,0:T(8,128)(2,1)}, u32[]{:S(2)}, u32[]{:S(2)}) collective-permute-start(bf16[4,256,1024]{2,1,0:T(8,128)(2,1)} %get-tuple-element.242), channel_id=1, source_target_pairs={{0,4},{4,0},{1,5},{5,1},{2,6},{6,2},{3,7},{7,3},{8,12},{12,8},{9,1... | collective-permute-start | bytes 6291464 | tf_op jit(solution)/shard_map/ppermute | solution.py:32
  310.2 84.5 %reduce-scatter.9.cloned.1.call-start = ((), (), s32[]{:S(2)}) async-start(), calls=%async_computation.9 | async-start | bytes 1638400 | tf_op jit(solution)/shard_map/reduce_scatter | solution.py:81
  311.3 30.8 %collective-permute-start.16 = (bf16[4,128,768]{2,1,0:T(8,128)(2,1)S(1)}, bf16[4,128,768]{2,1,0:T(8,128)(2,1)S(1)}, u32[]{:S(2)}, u32[]{:S(2)}) collective-permute-start(bf16[4,128,768]{2,1,0:T(8,128)(2,1)S(1)} %copy-done.36), channel_id=1, source_target_pairs={{0,4},{4,0},{1,5},{5,1},{2,6},{6,2},{3,7},{7,3},{8,12},{12,8},{9,1... | collective-permute-start | bytes 2359304 | tf_op jit(solution)/shard_map/ppermute | solution.py:32
  311.7 30.4 %collective-permute-start.15 = (bf16[4,128,512]{2,1,0:T(8,128)(2,1)S(1)}, bf16[4,128,512]{2,1,0:T(8,128)(2,1)S(1)}, u32[]{:S(2)}, u32[]{:S(2)}) collective-permute-start(bf16[4,128,512]{2,1,0:T(8,128)(2,1)S(1)} %copy-done.37), channel_id=1, source_target_pairs={{0,4},{4,0},{1,5},{5,1},{2,6},{6,2},{3,7},{7,3},{8,12},{12,8},{9,1... | collective-permute-start | bytes 1572872 | tf_op jit(solution)/shard_map/ppermute | solution.py:32
  343.6 67.8 %reduce-scatter.11.cloned.1.call-start = ((), (), s32[]{:S(2)}) async-start(), calls=%async_computation.10 | async-start | bytes 983040 | tf_op jit(solution)/shard_map/reduce_scatter | solution.py:81
  343.7 24.6 %collective-permute-start.33 = (bf16[4,128,768]{2,1,0:T(8,128)(2,1)}, bf16[4,128,768]{2,1,0:T(8,128)(2,1)S(1)}, u32[]{:S(2)}, u32[]{:S(2)}) collective-permute-start(bf16[4,128,768]{2,1,0:T(8,128)(2,1)} %get-tuple-element.272), channel_id=1, source_target_pairs={{0,4},{4,0},{1,5},{5,1},{2,6},{6,2},{3,7},{7,3},{8,12},{12,8},{9,1... | collective-permute-start | bytes 2359304 | tf_op jit(solution)/shard_map/ppermute | solution.py:32
  369.4 14.8 %collective-permute-start.20 = (bf16[256,1024]{1,0:T(8,128)(2,1)S(1)}, bf16[256,1024]{1,0:T(8,128)(2,1)S(1)}, u32[]{:S(2)}, u32[]{:S(2)}) collective-permute-start(bf16[256,1024]{1,0:T(8,128)(2,1)S(1)} %copy-done.17), channel_id=1, source_target_pairs={{0,2},{2,0},{1,3},{3,1},{4,6},{6,4},{5,7},{7,5},{8,10},{10,8},{9,1... | collective-permute-start | bytes 1572872 | tf_op jit(solution)/shard_map/ppermute | solution.py:32
  369.9 24.8 %collective-permute-start.23 = (bf16[256,1024]{1,0:T(8,128)(2,1)S(1)}, bf16[256,1024]{1,0:T(8,128)(2,1)S(1)}, u32[]{:S(2)}, u32[]{:S(2)}) collective-permute-start(bf16[256,1024]{1,0:T(8,128)(2,1)S(1)} %copy-done.18), channel_id=1, source_target_pairs={{0,2},{2,0},{1,3},{3,1},{4,6},{6,4},{5,7},{7,5},{8,10},{10,8},{9,1... | collective-permute-start | bytes 1572872 | tf_op jit(solution)/shard_map/ppermute | solution.py:32
  384.2 29.5 %collective-permute-start.22 = (bf16[256,1024]{1,0:T(8,128)(2,1)S(1)}, bf16[256,1024]{1,0:T(8,128)(2,1)S(1)}, u32[]{:S(2)}, u32[]{:S(2)}) collective-permute-start(bf16[256,1024]{1,0:T(8,128)(2,1)S(1)} %collective-permute-done.20.refs_1_), channel_id=1, source_target_pairs={{0,1},{1,0},{2,3},{3,2},{4,5},{5,4},{6,7},{7,6},{8,9},{9,8},{10,11... | collective-permute-start | bytes 1572872 | tf_op jit(solution)/shard_map/ppermute | solution.py:32
  387.1 28.2 %collective-permute-start.24 = (bf16[256,1024]{1,0:T(8,128)(2,1)S(1)}, bf16[256,1024]{1,0:T(8,128)(2,1)S(1)}, u32[]{:S(2)}, u32[]{:S(2)}) collective-permute-start(bf16[256,1024]{1,0:T(8,128)(2,1)S(1)} %copy-done.18), channel_id=1, source_target_pairs={{0,1},{1,0},{2,3},{3,2},{4,5},{5,4},{6,7},{7,6},{8,9},{9,8},{10,11... | collective-permute-start | bytes 1572872 | tf_op jit(solution)/shard_map/ppermute | solution.py:32
  394.7 20.7 %collective-permute-start.25 = (bf16[256,1024]{1,0:T(8,128)(2,1)S(1)}, bf16[256,1024]{1,0:T(8,128)(2,1)}, u32[]{:S(2)}, u32[]{:S(2)}) collective-permute-start(bf16[256,1024]{1,0:T(8,128)(2,1)S(1)} %collective-permute-done.23.refs_5_), channel_id=1, source_target_pairs={{0,1},{1,0},{2,3},{3,2},{4,5},{5,4},{6,7},{7,6},{8,9},{9,8},{10,11... | collective-permute-start | bytes 1572872 | tf_op jit(solution)/shard_map/ppermute | solution.py:32
  394.7 32.1 %collective-permute-start.30 = (bf16[128,1280]{1,0:T(8,128)(2,1)}, bf16[128,1280]{1,0:T(8,128)(2,1)S(1)}, u32[]{:S(2)}, u32[]{:S(2)}) collective-permute-start(bf16[128,1280]{1,0:T(8,128)(2,1)} %reduce-scatter.9.cloned.1.call-done.refs_0_), channel_id=1, source_target_pairs={{0,2},{2,0},{1,3},{3,1},{4,6},{6,4},{5,7},{7,5},{8,10},{10,8},{9,1... | collective-permute-start | bytes 983048 | tf_op jit(solution)/shard_map/ppermute | solution.py:32
  411.4 20.8 %collective-permute-start.34 = (bf16[128,768]{1,0:T(8,128)(2,1)}, bf16[128,768]{1,0:T(8,128)(2,1)S(1)}, u32[]{:S(2)}, u32[]{:S(2)}) collective-permute-start(bf16[128,768]{1,0:T(8,128)(2,1)} %reduce-scatter.11.cloned.1.call-done.refs_4_), channel_id=1, source_target_pairs={{0,2},{2,0},{1,3},{3,1},{4,6},{6,4},{5,7},{7,5},{8,10},{10,8},{9,1... | collective-permute-start | bytes 589832 | tf_op jit(solution)/shard_map/ppermute | solution.py:32
  426.9 20.6 %collective-permute-start.31 = (bf16[128,1280]{1,0:T(8,128)(2,1)S(1)}, bf16[128,1280]{1,0:T(8,128)(2,1)S(1)}, u32[]{:S(2)}, u32[]{:S(2)}) collective-permute-start(bf16[128,1280]{1,0:T(8,128)(2,1)S(1)} %copy-done.25), channel_id=1, source_target_pairs={{0,1},{1,0},{2,3},{3,2},{4,5},{5,4},{6,7},{7,6},{8,9},{9,8},{10,11... | collective-permute-start | bytes 983048 | tf_op jit(solution)/shard_map/ppermute | solution.py:32
  428.7 18.8 %collective-permute-start.32 = (bf16[128,1280]{1,0:T(8,128)(2,1)S(1)}, bf16[128,1280]{1,0:T(8,128)(2,1)S(1)}, u32[]{:S(2)}, u32[]{:S(2)}) collective-permute-start(bf16[128,1280]{1,0:T(8,128)(2,1)S(1)} %collective-permute-done.30.refs_1_), channel_id=1, source_target_pairs={{0,1},{1,0},{2,3},{3,2},{4,5},{5,4},{6,7},{7,6},{8,9},{9,8},{10,11... | collective-permute-start | bytes 983048 | tf_op jit(solution)/shard_map/ppermute | solution.py:32
  432.2 15.2 %collective-permute-start.35 = (bf16[128,768]{1,0:T(8,128)(2,1)S(1)}, bf16[128,768]{1,0:T(8,128)(2,1)S(1)}, u32[]{:S(2)}, u32[]{:S(2)}) collective-permute-start(bf16[128,768]{1,0:T(8,128)(2,1)S(1)} %copy-done.29), channel_id=1, source_target_pairs={{0,1},{1,0},{2,3},{3,2},{4,5},{5,4},{6,7},{7,6},{8,9},{9,8},{10,11... | collective-permute-start | bytes 589832 | tf_op jit(solution)/shard_map/ppermute | solution.py:32
  432.3 15.2 %collective-permute-start.36 = (bf16[128,768]{1,0:T(8,128)(2,1)S(1)}, bf16[128,768]{1,0:T(8,128)(2,1)S(1)}, u32[]{:S(2)}, u32[]{:S(2)}) collective-permute-start(bf16[128,768]{1,0:T(8,128)(2,1)S(1)} %collective-permute-done.34.refs_5_), channel_id=1, source_target_pairs={{0,1},{1,0},{2,3},{3,2},{4,5},{5,4},{6,7},{7,6},{8,9},{9,8},{10,11... | collective-permute-start | bytes 589832 | tf_op jit(solution)/shard_map/ppermute | solution.py:32
  (60 other events, 479.8 us)
Sparse Core Ops, SparseCore 0:
  35.0 32.5 all-gather.7
  69.7 26.9 all-gather.5
  98.8 45.3 all-gather.3
  251.4 41.7 reduce-scatter.4
  310.3 41.7 reduce-scatter.6
  354.9 31.5 reduce-scatter.8
  389.3 22.0 reduce-scatter.10

commit v6 on v5

--- a/solution.py
+++ b/solution.py
@@ -12,11 +12,11 @@
 SEQ = 577
 LANES = 128
 TILE = 16
-SPAN = 256
 CHUNKS = 2
 GROUPS = 2
 GIVEN = 2
-VMEM_LIMIT = 60 * 1024 * 1024
+VMEM_LIMIT = 60
+VMEM_LIMITS = {"attention": 40, "attention_back": 40, "qkv_term": 40, "out_back": 40, "norm_back": 40}
 
 ALL_AXES = ("z", "x", "y", "c")
 
@@ -81,11 +81,13 @@
     return lax.psum_scatter(total, "z", scatter_dimension=0, tiled=True)
 
 
-def finish_sum(mine):
+def sum_y(mine):
     if lax.axis_size("y") == 2:
-        own = [mine, swap(mine, "y")]
-    else:
-        own = [lax.psum(wide(mine), "y")]
+        return [mine, swap(mine, "y")]
+    return [lax.psum(wide(mine), "y")]
+
+
+def with_core(own):
     return own, [swap(one, "c") for one in own]
 
 
@@ -135,7 +137,7 @@
             scratch_shapes=scratch,
         ),
         compiler_params=pltpu.CompilerParams(
-            vmem_limit_bytes=VMEM_LIMIT, dimension_semantics=("arbitrary",) * len(grid)
+            vmem_limit_bytes=VMEM_LIMITS.get(name, VMEM_LIMIT) * 1024 * 1024, dimension_semantics=("arbitrary",) * len(grid)
         ),
         name=name,
     )(place, *ins)
@@ -212,27 +214,36 @@
     tokens, width = rows.shape
     length = row_pad(tokens)
     even = tokens // TILE * TILE
-
-    def body(place_ref, ref, to):
+    cols = width // GIVEN
+
+    def body(place_ref, ref, to, *parts):
         row = lax.broadcasted_iota(jnp.int32, (length - even, width), 0)
-        to[:even, :] = ref[:even, :]
         last = jnp.zeros((length - even, width), jnp.float32)
         for extra in range(tokens - even):
             one = wide(ref[even + extra : even + extra + 1, :])
             last = jnp.where(row == extra, one, last)
+        to[:even, :] = ref[:even, :]
         to[even:, :] = low(last)
-
-    shape = (length, width)
-    return call(
+        for number, part in enumerate(parts):
+            lanes = slice(number * cols, (number + 1) * cols)
+            part[...] = to[:, lanes]
+
+    shapes = [(length, width)] + [(length, cols)] * GIVEN
+    whole_rows, *parts = call(
         body,
         place,
         (rows,),
         [whole(rows.shape)],
-        [sds(shape, jnp.bfloat16)],
-        [whole(shape)],
+        [sds(shape, jnp.bfloat16) for shape in shapes],
+        [whole(shape) for shape in shapes],
         [],
         "pad_rows",
-    )[0]
+    )
+    return whole_rows, parts
+
+
+def joined(refs, rows=slice(None)):
+    return jnp.concatenate([ref[rows, :] for ref in refs], axis=1)
 
 
 def prepare_rest(place, in_weight, down_weight, cotangent, cuts):
@@ -315,7 +326,8 @@
 def project_first(place, rows, pieces, sizes):
     flat = [one for (one,) in pieces]
     z_size, part, cols = flat[0].shape
-    length, width = rows[0].shape
+    rows_own, rows_other = rows
+    length, width = rows_own.shape
     count = 2 * z_size
     tiles = (part - width // count) // TILE
     part = width // count
@@ -325,7 +337,8 @@
     per_shard = sizes[6] // 2 // CHUNKS
     blocks = count // 2
 
-    def body(place_ref, own_ref, other_ref, *refs):
+    def body(place_ref, own_ref, *refs):
+        other_refs, refs = refs[:GIVEN], refs[GIVEN:]
         ins, refs = refs[:2], refs[2:]
         normed_ref, q_ref, k_ref, v_ref, vec_ref, hidden_bias_ref, weight, packed, sem = refs
         core = place_ref[2]
@@ -377,18 +390,17 @@
             vec_ref[row : row + 1, :] = value
         vec_ref[7:8, :] = jnp.zeros((1, width), jnp.float32)
         for j in range(CHUNKS):
-            for b in range(blocks):
-                for i in range(2):
-                    at = starts[6] + j * per_shard
-                    to = at + sizes[6] // 2
-                    hidden_bias_ref[j, b, :, i * per_shard : (i + 1) * per_shard] = select(
-                        core,
-                        jnp.concatenate(lanes(2 * b + i, at, per_shard), axis=1),
-                        jnp.concatenate(lanes(2 * b + i, to, per_shard), axis=1),
-                    )
-        for image, ref in enumerate((own_ref, other_ref)):
+            for s in range(count):
+                at = starts[6] + j * per_shard
+                to = at + sizes[6] // 2
+                hidden_bias_ref[j, :, s * per_shard : (s + 1) * per_shard] = select(
+                    core,
+                    jnp.concatenate(lanes(s, at, per_shard), axis=1),
+                    jnp.concatenate(lanes(s, to, per_shard), axis=1),
+                )
+        for image, part_refs in enumerate(((own_ref,), other_refs)):
             for at in range(0, length, LANES):
-                block = wide(ref[at : at + LANES, :])
+                block = wide(joined(part_refs, slice(at, at + LANES)))
                 normed_ref[image, at : at + LANES, :] = low(normalised(block) * gain + bias)
             write_qkv(
                 normed_ref[image],
@@ -405,17 +417,19 @@
     return call(
         body,
         place,
-        (*rows, *flat),
-        [whole((length, width))] * 2 + [any_spec()] * 2,
+        (rows_own, *rows_other, *flat),
+        [whole((length, width))]
+        + [whole((length, width // GIVEN))] * GIVEN
+        + [any_spec()] * 2,
         [sds((2, length, width), jnp.bfloat16)]
         + [part_out] * 3
         + [
             sds((8, width), jnp.float32),
-            sds((CHUNKS, blocks, 1, 2 * per_shard), jnp.float32),
+            sds((CHUNKS, 1, count * per_shard), jnp.float32),
         ],
         [whole((2, length, width))]
         + [whole((2, length, heads))] * 3
-        + [whole((8, width)), whole((CHUNKS, blocks, 1, 2 * per_shard))],
+        + [whole((8, width)), whole((CHUNKS, 1, count * per_shard))],
         [
             pltpu.VMEM((width, cols), jnp.bfloat16),
             pltpu.VMEM((count, tiles * TILE, cols), jnp.bfloat16),
@@ -501,24 +515,20 @@
         keys_block = k_ref[0]
         values_t = v_ref[0].T
         query_block = q_ref[0]
-        mixed = []
+        key_row = lax.broadcasted_iota(jnp.int32, (length, length), 0)
+        scores = []
         for head in range(2):
             inside = (lane >= head * HEAD_DIM) & (lane < (head + 1) * HEAD_DIM)
             query_head = jnp.where(inside, query_block, jnp.zeros_like(query_block))
-            values_head = values_t[head * HEAD_DIM : (head + 1) * HEAD_DIM, :]
-            parts = []
-            for at in range(0, length, SPAN):
-                span = min(SPAN, length - at)
-                scores = dot_tail(keys_block, query_head[at : at + span, :])
-                key_row = lax.broadcasted_iota(jnp.int32, scores.shape, 0)
-                scores = jnp.where(key_row < SEQ, scores, -1e30)
-                highest = jnp.max(scores, axis=0, keepdims=True)
-                exponent = jnp.exp(scores - highest)
-                summed = jnp.sum(exponent, axis=0, keepdims=True)
-                probs = low(exponent * (1.0 / summed))
-                probs_ref[0, 0, head, :, at : at + span] = probs
-                parts.append(dot(values_head, probs))
-            mixed.append(jnp.concatenate(parts, axis=1))
+            scores.append(jnp.where(key_row < SEQ, dot_tail(keys_block, query_head), -1e30))
+        mixed = []
+        for head in range(2):
+            highest = jnp.max(scores[head], axis=0, keepdims=True)
+            exponent = jnp.exp(scores[head] - highest)
+            summed = jnp.sum(exponent, axis=0, keepdims=True)
+            probs = low(exponent * (1.0 / summed))
+            probs_ref[0, 0, head] = probs
+            mixed.append(dot(values_t[head * HEAD_DIM : (head + 1) * HEAD_DIM, :], probs))
         out_ref[0] = low(jnp.concatenate(mixed, axis=0).T)
 
     block = pl.BlockSpec((1, length, LANES), lambda i, j, p: (i, 0, j))
@@ -555,25 +565,15 @@
         for head in range(2):
             inside = (lane >= head * HEAD_DIM) & (lane < (head + 1) * HEAD_DIM)
             grad_head = jnp.where(inside, grad_block, jnp.zeros_like(grad_block))
+            probs_low = p_ref[0, 0, head]
+            probs_wide = wide(probs_low)
+            grad_probs = dot_tail(values_block, grad_head)
+            inner = jnp.sum(probs_wide * grad_probs, axis=0, keepdims=True)
+            grad_scores = low(probs_wide * (grad_probs - inner))
             keys_head = keys_t[head * HEAD_DIM : (head + 1) * HEAD_DIM, :]
-            parts = []
-            sum_keys = None
-            sum_values = None
-            for at in range(0, length, SPAN):
-                span = min(SPAN, length - at)
-                probs_low = p_ref[0, 0, head, :, at : at + span]
-                probs_wide = wide(probs_low)
-                grad_probs = dot_tail(values_block, grad_head[at : at + span, :])
-                inner = jnp.sum(probs_wide * grad_probs, axis=0, keepdims=True)
-                grad_scores = low(probs_wide * (grad_probs - inner))
-                parts.append(dot(keys_head, grad_scores))
-                to_keys = dot(grad_scores, query_block[at : at + span, :])
-                to_values = dot(probs_low, grad_block[at : at + span, :])
-                sum_keys = to_keys if sum_keys is None else sum_keys + to_keys
-                sum_values = to_values if sum_values is None else sum_values + to_values
-            grad_query.append(jnp.concatenate(parts, axis=1))
-            grad_keys.append(sum_keys)
-            grad_values.append(sum_values)
+            grad_query.append(dot(keys_head, grad_scores))
+            grad_keys.append(dot(grad_scores, query_block))
+            grad_values.append(dot(probs_low, grad_block))
         first = lane < HEAD_DIM
         gq_ref[0] = low(jnp.concatenate(grad_query, axis=0).T * scale)
         gk_ref[0] = low(jnp.where(first, grad_keys[0], grad_keys[1]))
@@ -605,9 +605,9 @@
 
     def body(place_ref, *refs):
         mine_refs, theirs_refs, refs = refs[:GROUPS], refs[GROUPS : 2 * GROUPS], refs[2 * GROUPS :]
-        wm_ref, wt_ref, own_ref, other_ref, vec_ref, middle_ref, normed_ref, total = refs
+        wm_ref, wt_ref, own_ref, *other_refs, vec_ref, middle_ref, normed_ref, total = refs
         core = place_ref[2]
-        for image, ref in enumerate((own_ref, other_ref)):
+        for image, part_refs in enumerate(((own_ref,), other_refs)):
             for slot, weight in enumerate((wm_ref, wt_ref)):
                 branch = None
                 for g in range(GROUPS):
@@ -623,7 +623,7 @@
                 left = select(core, first, second)
                 right = select(core, second, first)
                 middle = (
-                    wide(ref[at:upto, :])
+                    wide(joined(part_refs, slice(at, upto)))
                     + jnp.concatenate([left, right], axis=1)
                     + vec_ref[BIAS_OUT : BIAS_OUT + 1, :]
                 )
@@ -637,10 +637,11 @@
     return call(
         body,
         place,
-        (*mine, *theirs, weight_mine, weight_theirs, *rows, vectors),
+        (*mine, *theirs, weight_mine, weight_theirs, rows[0], *rows[1], vectors),
         [whole((2, length, heads))] * (2 * GROUPS)
         + [whole((width, half))] * 2
-        + [whole((length, width))] * 2
+        + [whole((length, width))]
+        + [whole((length, width // GIVEN))] * GIVEN
         + [whole(vectors.shape)],
         [sds((length, width), jnp.float32), sds((2, length, width), jnp.bfloat16)],
         [whole((length, width)), whole((2, length, width))],
@@ -652,115 +653,83 @@
 def feed_forward(place, normed, cotangent, pieces, bias, chunk, running):
     cut = len(pieces[0])
     z_size, _, width = pieces[0][0].shape
-    blocks, block = bias.shape[1], bias.shape[3]
-    hidden_width = blocks * block
+    hidden_width = bias.shape[2]
     part = width // (2 * z_size)
     per_shard = hidden_width // (2 * z_size)
     rows_in, rows_down = part // cut, per_shard // cut
-    in_block = block // per_shard
     _, length, _ = normed.shape
     first_call = running is None
     last_call = chunk == CHUNKS - 1
 
-    def body(place_ref, normed_ref, own_cot, other_cot, bias_ref, *refs):
+    def body(place_ref, normed_ref, own_cot, *refs):
+        other_cots, (bias_ref, *refs) = refs[:GIVEN], refs[GIVEN:]
         ins, refs = refs[: 2 * cut], refs[2 * cut :]
         if not first_call:
             before, refs = refs[:4], refs[4:]
         out_own, out_other, gn_own, gn_other, bsum_ref, keep_ref, send_ref = refs[:7]
-        w_in, w_down, normed_t, grads, sem, out_sem, *held = refs[7:]
-        given = (out_other, gn_other)
-        if last_call:
-            out_other, gn_other = held
-        step = pl.program_id(0)
-
-        def copies():
-            made = []
+        w_in, w_down, normed_t, grads, sem, out_sem = refs[7:]
+        copies = []
+        for weight, at, rows, of_shard in (
+            (w_in, 0, rows_in, part),
+            (w_down, rows_in, rows_down, per_shard),
+        ):
             for number, ref in enumerate(ins):
                 dx, h = number // cut, number % cut
                 y = h + (1 - 2 * h) * place_ref[3] if cut == 2 else 0
                 for z in range(z_size):
                     s = shard_number(place_ref, z, dx)
-                    for weight, at, rows, of_shard in (
-                        (w_in, 0, rows_in, part),
-                        (w_down, rows_in, rows_down, per_shard),
-                    ):
-                        row = pl.multiple_of(s * of_shard + y * rows, rows)
-                        made.append(
-                            pltpu.make_async_copy(
-                                ref.at[z, pl.ds(at, rows), :],
-                                weight.at[pl.ds(row, rows), :],
-                                sem.at[len(made)],
-                            )
-                        )
-            return made
-
-        @pl.when(step == 0)
-        def _():
-            for copy in copies():
-                copy.start()
-            for image in range(2):
-                normed_t[:, image * length : (image + 1) * length] = normed_ref[image].T
-            for copy in copies():
-                copy.wait()
-
-        at_block = pl.multiple_of(step * block, block)
-        weight_in = w_in[:, pl.ds(at_block, block)]
-        weight_down = w_down[pl.ds(at_block, block), :]
+                    row = pl.multiple_of(s * of_shard + y * rows, rows)
+                    copy = pltpu.make_async_copy(
+                        ref.at[z, pl.ds(at, rows), :],
+                        weight.at[pl.ds(row, rows), :],
+                        sem.at[len(copies)],
+                    )
+                    copy.start()
+                    copies.append(copy)
+        for image in range(2):
+            normed_t[:, image * length : (image + 1) * length] = normed_ref[image].T
+        for copy in copies:
+            copy.wait()
         into = None
         down = None
         column_sum = None
-        for image, cot_ref in enumerate((own_cot, other_cot)):
-            preact = dot(normed_ref[image], weight_in) + bias_ref[0, 0]
+        for image, cot_refs in enumerate(((own_cot,), other_cots)):
+            preact = dot(normed_ref[image], w_in[...]) + bias_ref[0]
             phi = 0.5 * (1.0 + lax.erf(preact * math.sqrt(0.5)))
             density = jnp.exp(-0.5 * preact * preact) * (1.0 / math.sqrt(2.0 * math.pi))
             hidden = low(preact * phi)
             slope = phi + preact * density
-            cot = cot_ref[...]
-            grad = low(dot_tail(cot, weight_down) * slope)
+            cot = joined(cot_refs)
+            grad = low(dot_tail(cot, w_down[...]) * slope)
             out_ref, gn_ref = ((out_own, gn_own), (out_other, gn_other))[image]
-            to_out = dot(hidden, weight_down)
-            to_normed = dot_tail(grad, weight_in)
-
-            @pl.when(step == 0)
-            def _():
-                if first_call:
-                    out_ref[...] = to_out
-                    gn_ref[...] = to_normed
-                else:
-                    out_ref[...] = before[image][...] + to_out
-                    gn_ref[...] = before[2 + image][...] + to_normed
-
-            @pl.when(step > 0)
-            def _():
-                out_ref[...] += to_out
-                gn_ref[...] += to_normed
-
+            to_out = dot(hidden, w_down[...])
+            to_normed = dot_tail(grad, w_in[...])
+            if not first_call:
+                to_out = before[image][...] + to_out
+                to_normed = before[2 + image][...] + to_normed
+            out_ref[...] = to_out.astype(out_ref.dtype)
+            gn_ref[...] = to_normed.astype(gn_ref.dtype)
             partial = jnp.sum(wide(grad), axis=0, keepdims=True)
             column_sum = partial if image == 0 else column_sum + partial
             to_in = dot(normed_t[:, image * length : (image + 1) * length], grad)
             into = to_in if image == 0 else into + to_in
             to_down = dot(hidden.T, cot)
             down = to_down if image == 0 else down + to_down
-        bsum_ref[0] = column_sum
+        bsum_ref[...] = column_sum
         for z in range(z_size):
             for x in range(2):
                 dx = x + (1 - 2 * x) * place_ref[1]
-                at = (z * 2 + x) * part
-                grads[dx, z, :part, pl.ds(at_block, block)] = low(into[at : at + part, :])
-        for i in range(in_block):
-            s = step * in_block + i
-            z, x = s // 2, lax.rem(s, 2)
-            dx = x + (1 - 2 * x) * place_ref[1]
-            grads[dx, z, part:, :] = low(down[i * per_shard : (i + 1) * per_shard, :])
-
-        @pl.when(step == blocks - 1)
-        def _():
-            for total_ref, ref in zip(held, given):
-                ref[...] = low(total_ref[...])
-            for slot, ref in enumerate((keep_ref, send_ref)):
-                pltpu.make_async_copy(grads.at[slot], ref, out_sem.at[slot]).start()
-            for slot, ref in enumerate((keep_ref, send_ref)):
-                pltpu.make_async_copy(grads.at[slot], ref, out_sem.at[slot]).wait()
+                s = z * 2 + x
+                grads[dx, z, :part, :] = low(into[s * part : (s + 1) * part, :])
+                grads[dx, z, part:, :] = low(down[s * per_shard : (s + 1) * per_shard, :])
+        copies = [
+            pltpu.make_async_copy(grads.at[slot], ref, out_sem.at[slot])
+            for slot, ref in enumerate((keep_ref, send_ref))
+        ]
+        for copy in copies:
+            copy.start()
+        for copy in copies:
+            copy.wait()
 
     total = sds((length, width), jnp.float32)
     other = sds((length, width), jnp.bfloat16 if last_call else jnp.float32)
@@ -769,16 +738,14 @@
     return call(
         body,
         place,
-        (normed, *cotangent, bias, *[one for side in pieces for one in side], *carried),
-        [whole((2, length, width))]
-        + [whole((length, width))] * 2
-        + [pl.BlockSpec((1, 1, 1, block), lambda b, p: (chunk, b, 0, 0))]
+        (normed, cotangent[0], *cotangent[1], bias, *[one for side in pieces for one in side], *carried),
+        [whole((2, length, width)), whole((length, width))]
+        + [whole((length, width // GIVEN))] * GIVEN
+        + [pl.BlockSpec((1, 1, hidden_width), lambda i, p: (chunk, 0, 0))]
         + [any_spec()] * (2 * cut)
         + [whole((length, width))] * len(carried),
-        [total, other, total, other] + [sds((blocks, 1, block), jnp.float32)] + [piece_out] * 2,
-        [whole((length, width))] * 4
-        + [pl.BlockSpec((1, 1, block), lambda b, p: (b, 0, 0))]
-        + [any_spec()] * 2,
+        [total, other, total, other] + [sds((1, hidden_width), jnp.float32)] + [piece_out] * 2,
+        [whole((length, width))] * 4 + [whole((1, hidden_width))] + [any_spec()] * 2,
         [
             pltpu.VMEM((width, hidden_width), jnp.bfloat16),
             pltpu.VMEM((hidden_width, width), jnp.bfloat16),
@@ -786,10 +753,8 @@
             pltpu.VMEM((2, z_size, part + per_shard, width), jnp.bfloat16),
             pltpu.SemaphoreType.DMA((4 * cut * z_size,)),
             pltpu.SemaphoreType.DMA((2,)),
-        ]
-        + [pltpu.VMEM((length, width), jnp.float32)] * (2 if last_call else 0),
+        ],
         "feed_forward",
-        grid=(blocks,),
     )
 
 
@@ -1289,8 +1254,7 @@
         none = jnp.zeros((1, per_shard), jnp.float32)
         for s in range(shards):
             for j in range(CHUNKS):
-                i = s % 2
-                row = hidden_refs[j][s // 2, :, i * per_shard : (i + 1) * per_shard]
+                row = hidden_refs[j][:, s * per_shard : (s + 1) * per_shard]
                 for c in range(2):
                     at = sum(sizes[:6]) + (c * CHUNKS + j) * per_shard
                     here = select(core, row, none) if c == 0 else select(core, none, row)
@@ -1370,6 +1334,7 @@
     by_y = lax.axis_size("y") == 2
     group = lax.axis_size("z") * lax.axis_size("x")
     tokens = inputs.shape[0]
+    part = in_weight.shape[0]
     images = (tokens // SEQ) * group * lax.axis_size("y") * lax.axis_size("c")
     as_row = lambda vector: vector.reshape(1, -1)
     params = [as_row(masters[number]) for number in VECTORS]
@@ -1380,34 +1345,35 @@
     near = along_z(shard_first)
     pieces_first = by_x(near)
     near_next = along_z(after(shard_next, near))
-    rows_own = pad_rows(after(place, near), inputs)
-    rows = (rows_own, swap(rows_own, "c"))
+    rows_own, parts = pad_rows(after(place, near), inputs)
+    rows = (rows_own, [swap(one, "c") for one in parts])
     *shards_ff, down_sums = prepare_rest(
         after(place, rows_own), in_weight, down_weight, cotangent, (2 if by_y else 1, 1)
     )
-    cot_own = pad_rows(after(place, (down_sums, rows[1])), cotangent)
+    cot_own, parts = pad_rows(after(place, (down_sums, rows[1])), cotangent)
     near_ff = [along_z(shards_ff[0])]
 
     normed, *first, vectors, hidden_bias = project_first(
-        after(place, cot_own), rows, pieces_first, sizes
+        after(place, (cot_own, near_next)), rows, pieces_first, sizes
     )
     near_ff.append(along_z(after(shards_ff[1], normed)))
-    cot = (cot_own, swap(after(cot_own, normed), "c"))
+    cot = (cot_own, [swap(one, "c") for one in after(parts, normed)])
     qkv = [first]
-    near_next = after(near_next, normed)
     pieces_next = by_x(near_next)
-    mixed, prob = attention(after(place, near_next), *first)
+    mixed, prob = attention(place, *first)
     attended = [mixed]
     probs = [prob]
     theirs = [swap(mixed, "c")]
     pieces_next = after(pieces_next, mixed)
     weight_mine = gather_out(place, pieces_next, 3 * first[0].shape[-1])
     weight_theirs = swap(weight_mine, "c")
-    near_ff[0] = after(near_ff[0], weight_mine)
+    near_ff[0] = after(near_ff[0], pieces_next)
     across = swap(near_ff[0], "x")
     near_too = swap(near_ff[0], "y") if by_y else None
     qkv.append(
-        project_next(after(place, near_ff[0]), normed, vectors, pieces_next, 1)
+        project_next(
+            after(place, (near_ff[0], weight_mine)), normed, vectors, pieces_next, 1
+        )
     )
     mixed, prob = attention(place, *qkv[1])
     attended.append(mixed)
@@ -1419,7 +1385,7 @@
     else:
         pieces_ff = [[near_ff[0]], [across]]
     middle, normed_mid = project_out(
-        after(place, across), attended, theirs, weight_mine, weight_theirs, rows, vectors
+        after(place, (across, near_too)), attended, theirs, weight_mine, weight_theirs, rows, vectors
     )
     near_ff[1] = after(near_ff[1], normed_mid)
     pieces_next_ff = by_x(near_ff[1])
@@ -1462,19 +1428,26 @@
     got_first = swap(send_first, "x")
     folded.append(fold(*after((keep_next, got_next), sums_first)))
     scattered.append(scatter_z(folded[1]))
+    scattered[0] = after(scattered[0], folded[1])
+    own_ff = [sum_y(scattered[0])]
     grad_qkv.append(
-        attention_back(after(place, folded[1]), *qkv[1], probs[1], grad_attended[1])
-    )
-    sums_next, keep_next, send_next = qkv_term(place, normed, *grad_qkv[1])
+        attention_back(after(place, scattered[0]), *qkv[1], probs[1], grad_attended[1])
+    )
+    own_ff[0] = after(own_ff[0], grad_qkv[1][0])
+    sums_next, keep_next, send_next = qkv_term(
+        after(place, own_ff[0]), normed, *grad_qkv[1]
+    )
     sums_qkv = [sums_first, sums_next]
     got_next = swap(send_next, "x")
     held = after(((keep, got), (keep_first, got_first)), sums_next)
     folded.append(jnp.concatenate([fold(*one) for one in held], axis=1))
     scattered.append(scatter_z(folded[2]))
     share, *given = qkv_back(after(place, folded[2]), grad_qkv, [pieces_first, pieces_next])
-    pairs = [finish_sum(after(scattered[0], share))]
+    pairs = [with_core(own_ff[0])]
+    scattered[1] = after(scattered[1], share)
+    own_ff.append(sum_y(scattered[1]))
     sums_in, input_grad = norm_back(
-        after(place, scattered[0]),
+        after(place, scattered[1]),
         rows_own,
         vectors,
         GAIN_ONE,
@@ -1484,16 +1457,15 @@
         tokens,
     )
     packed = pack_terms(
-        after(place, scattered[1]), sums_mid, sums_in, sums_qkv, hidden_sums, down_sums, sizes
+        place, sums_mid, sums_in, sums_qkv, hidden_sums, down_sums, sizes
     )
     folded.append(fold(*after((keep_next, got_next), packed)))
     scattered.append(scatter_z(folded[3]))
-    pairs += [finish_sum(one) for one in scattered[1:]]
+    pairs.append(with_core(after(own_ff[1], folded[3])))
     terms = sum_over(packed, ("c", "z", "x", "y"))
 
     weights = [in_weight, down_weight]
     states = [as_row(state) for state in (in_rows, down_rows)]
-    part = in_weight.shape[0]
     grads_early, rows_early, pack, _, _ = statistics(
         place,
         ("in", "down"),
@@ -1504,8 +1476,10 @@
         images,
         group,
     )
+    scattered[2] = after(scattered[2], rows_early[0])
+    own_mid = sum_y(scattered[2])
     new_early, cols_early, clips_early, _ = update(
-        place,
+        after(place, (terms, scattered[2])),
         grads_early,
         rows_early,
         weights,
@@ -1513,6 +1487,8 @@
         sum_over(pack, ("z", "x")),
         group,
     )
+    pairs.append(with_core(after(own_mid, clips_early)))
+    pairs.append(with_core(sum_y(after(scattered[3], clips_early))))
     weights = [out_weight, qkv_weight]
     grads_late, rows_late, pack, vector_grads, new_moments = statistics(
         after(place, clips_early),

time: 483 us -> 453 us (0.938)
  Pallas kernels: 263 us -> 203 us
  local copies, waits for them, and re-layouts: 9.84 us -> 39.9 us
  waiting for transfers between devices: 120 us -> 109 us
  starting transfers between devices: 31 us -> 37.5 us
    pallas_call x25, Pallas kernels: 263 us -> 203 us  [call(): pl.pallas_call(body, out_shape=outs, grid_spec=pltpu.PrefetchScalarGridSp...]
    ppermute x33 -> x35, waiting for transfers between devices: 84.2 us -> 50.5 us  [swap(): return lax.ppermute(value, axis, [(0, 1), (1, 0)])]
    unnamed x76 -> x156, local copies, waits for them, and re-layouts: 9.84 us -> 39.9 us
    all_gather x3, waiting for transfers between devices: 0.04 us -> 27.7 us  [along_z(): near = lax.all_gather(shard, 'z', axis=0, tiled=True)]
    reduce_scatter x4, waiting for transfers between devices: 16.3 us -> 0.01 us  [scatter_z(): return lax.psum_scatter(total, 'z', scatter_dimension=0, tiled=True)]
    ppermute x9, waiting for transfers between devices: 9.95 us -> 24.3 us  [shift(): lax.ppermute(value, axis, [(i, (i + step) % size) for i in range(size)])]
    ppermute x33 -> x35, starting transfers between devices: 16.8 us -> 22.7 us  [swap(): return lax.ppermute(value, axis, [(0, 1), (1, 0)])]
  transfers between devices with their start and end apart: 54 -> 56, of which waited for: 23 -> 28; matrix products, arithmetic and copies ran while one was open for 2% -> 2% of each run, Pallas kernels for 52% -> 43%
where the time goes in v6:
time: 453 us; the launch traced here: 444 us
  Pallas kernels  203 us (45%)
  waiting for transfers between devices  109 us (24%)
  local copies, waits for them, and re-layouts  39.9 us (9%)
  starting transfers between devices  37.5 us (8%)
  blocking collectives  23.7 us (5%)
  other arithmetic  16.1 us (4%)
  between operations  15.4 us (3%)
    pallas_call x25, Pallas kernels, call(): pl.pallas_call(body, out_shape=outs, grid_spec=pltpu.PrefetchScalarGridSp...  203 us
    ppermute x35, waiting for transfers between devices, swap(): return lax.ppermute(value, axis, [(0, 1), (1, 0)])  50.5 us
    unnamed x156, local copies, waits for them, and re-layouts  39.9 us
    all_gather x3, waiting for transfers between devices, along_z(): near = lax.all_gather(shard, 'z', axis=0, tiled=True)  27.7 us
    ppermute x9, waiting for transfers between devices, shift(): lax.ppermute(value, axis, [(i, (i + step) % size) for i in range(size)])  24.3 us
    all_gather x1, blocking collectives, along_z(): near = lax.all_gather(shard, 'z', axis=0, tiled=True)  23.7 us
    ppermute x35, starting transfers between devices, swap(): return lax.ppermute(value, axis, [(0, 1), (1, 0)])  22.7 us
    ppermute x9, starting transfers between devices, shift(): lax.ppermute(value, axis, [(i, (i + step) % size) for i in range(size)])  10.1 us
  transfers between devices with their start and end apart: 56, of which 28 were waited for; matrix products, arithmetic and copies ran while one was open for 2% of the time, Pallas kernels for 43%

profile of v6, /device:TPU:0, one launch (start us, length us, event | category | flops | bytes accessed | tf_op | source)
XLA Modules:
  0.0 444.3 jit_solution(6461632771320806578)
XLA Ops:
  11.1 23.7 %all_gather.12 = bf16[640,768]{1,0:T(8,128)(2,1)S(1)} all-gather(bf16[160,768]{1,0:T(8,128)(2,1)} %get-tuple-element.195), channel_id=1, replica_groups=mesh['z'=4,'x'=2,'y'=2,'c'=2] {'z'}, dimensions={0}, use_global_device_ids=true | all-gather | bytes 1228800 | tf_op jit(solution)/shard_map/all_gather | solution.py:59
  34.9 3.5 pad_rows.2
  38.4 4.3 prepare_rest.1
  44.9 22.7 %all-gather.4.cloned.1.call-done = bf16[512,1280]{1,0:T(8,128)(2,1)} async-done(((bf16[128,1280]{1,0:T(8,128)(2,1)}), bf16[512,1280]{1,0:T(8,128)(2,1)}) %all-gather.4.cloned.1.call-update) | async-done | bytes 1310736 | tf_op jit(solution)/shard_map/all_gather | solution.py:59
  73.6 9.0 %project_first.1 = (bf16[2,640,1024]{2,1,0:T(8,128)(2,1)}, bf16[2,640,256]{2,1,0:T(8,128)(2,1)}, bf16[2,640,256]{2,1,0:T(8,128)(2,1)}, bf16[2,640,256]{2,1,0:T(8...) custom-call(s32[4]{0:T(128)} %pad_add_fusion.place_ref, ...), custom_call_target="tpu_custom_call" | custom-call | tf_op jit(solution)/shard_map/project_first/pallas_call | solution.py:129
  85.9 6.9 %attention.2 = (bf16[2,640,256]{2,1,0:T(8,128)(2,1)S(1)}, bf16[2,2,2,640,640]{4,3,2,1,0:T(8,128)(2,1)S(1)}) custom-call(s32[4]{0:T(128)S(1)} %copy-done.50, bf16[2,640,256]{2,1,0:T(8,128)(2,1)S(1)} %copy-done.22, bf16[2,640,256]{2,1,0:T(8,128)(2,1)S(1)} %copy-done.24, bf16[2,640,256]{2,1,0:T(8,128)(2,1)S(1)} %copy-done.26), custom_call_target="tpu_custom_call" | custom-call | tf_op jit(solution)/shard_map/attention/pallas_call | solution.py:129
  104.2 7.5 %project_next.1 = (bf16[2,640,256]{2,1,0:T(8,128)(2,1)}, bf16[2,640,256]{2,1,0:T(8,128)(2,1)}, bf16[2,640,256]{2,1,0:T(8,128)(2,1)}) custom-call(s32[4]{0:T(128)} %pad_add_fusion.place_ref, bf16[2,640,1024]{2,1,0:T(8,128)(2,1)} %get-tuple-element.208.normed_ref, f32[8,1024]{1,0:T(8,128)} %get-tuple-element.219.vec_ref.refs_9_, ...), custom_call_target="tpu_custom_call" | custom-call | tf_op jit(solution)/shard_map/project_next/pallas_call | solution.py:129
  115.0 7.0 %attention.3 = (bf16[2,640,256]{2,1,0:T(8,128)(2,1)S(1)}, bf16[2,2,2,640,640]{4,3,2,1,0:T(8,128)(2,1)S(1)}) custom-call(s32[4]{0:T(128)S(1)} %copy-done.51, bf16[2,640,256]{2,1,0:T(8,128)(2,1)S(1)} %copy-done.16, bf16[2,640,256]{2,1,0:T(8,128)(2,1)S(1)} %copy-done.18, bf16[2,640,256]{2,1,0:T(8,128)(2,1)S(1)} %copy-done.20), custom_call_target="tpu_custom_call" | custom-call | tf_op jit(solution)/shard_map/attention/pallas_call | solution.py:129
  129.4 9.9 %project_out.1 = (f32[640,1024]{1,0:T(8,128)}, bf16[2,640,1024]{2,1,0:T(8,128)(2,1)}) custom-call(s32[4]{0:T(128)} %pad_add_fusion.place_ref, bf16[2,640,256]{2,1,0:T(8,128)(2,1)} %copy-done.28, bf16[2,640,256]{2,1,0:T(8,128)(2,1)} %copy-done.32, bf16[2,640,256]{2,1,0:T(8,128)(2,1)} %copy-done.30, bf16[2,640,256]{2,1,0:T(8,128)(2,1)} %copy-done.34, ...), custom_call_target="tpu_custom_call" | custom-call | tf_op jit(solution)/shard_map/project_out/pallas_call | solution.py:129
  139.4 5.0 %all-gather.6.cloned.1.call-done = bf16[1024,1024]{1,0:T(8,128)(2,1)} async-done(((bf16[256,1024]{1,0:T(8,128)(2,1)}), bf16[1024,1024]{1,0:T(8,128)(2,1)}) %all-gather.6.cloned.1.call-update) | async-done | bytes 2097168 | tf_op jit(solution)/shard_map/all_gather | solution.py:59
  145.8 4.4 collective-permute-done.11.refs_6_
  150.2 29.8 %feed_forward.2 = (f32[640,1024]{1,0:T(8,128)}, f32[640,1024]{1,0:T(8,128)}, f32[640,1024]{1,0:T(8,128)}, f32[640,1024]{1,0:T(8,128)}, f32[1,1024]{1,0:T(1,128)}...) custom-call(s32[4]{0:T(128)} %pad_add_fusion.place_ref, ...), custom_call_target="tpu_custom_call" | custom-call | tf_op jit(solution)/shard_map/feed_forward/pallas_call | solution.py:129
  180.6 12.4 %collective-permute-done.13.refs_4_ = bf16[4,256,1024]{2,1,0:T(8,128)(2,1)S(1)} collective-permute-done((bf16[4,256,1024]{2,1,0:T(8,128)(2,1)}, bf16[4,256,1024]{2,1,0:T(8,128)(2,1)S(1)}, u32[]{:S(2)}, u32[]{:S(2)}) %collective-permute-start.13) | collective-permute-done | bytes 2097184 | tf_op jit(solution)/shard_map/ppermute | solution.py:32
  194.4 32.3 %feed_forward.3 = (f32[640,1024]{1,0:T(8,128)}, bf16[640,1024]{1,0:T(8,128)(2,1)}, f32[640,1024]{1,0:T(8,128)}, bf16[640,1024]{1,0:T(8,128)(2,1)}, f32[1,1024]{1...) custom-call(s32[4]{0:T(128)} %pad_add_fusion.place_ref, ...), custom_call_target="tpu_custom_call" | custom-call | tf_op jit(solution)/shard_map/feed_forward/pallas_call | solution.py:129
  226.6 10.3 %collective-permute-done.12 = bf16[4,256,1024]{2,1,0:T(8,128)(2,1)} collective-permute-done((bf16[4,256,1024]{2,1,0:T(8,128)(2,1)}, bf16[4,256,1024]{2,1,0:T(8,128)(2,1)}, u32[]{:S(2)}, u32[]{:S(2)}) %collective-permute-start.12) | collective-permute-done | bytes 2097184 | tf_op jit(solution)/shard_map/ppermute | solution.py:32
  236.9 4.0 add_convert_fusion.1
  249.6 6.8 %norm_back.2 = (f32[8,1024]{1,0:T(8,128)S(1)}, bf16[577,1024]{1,0:T(8,128)(2,1)}, f32[640,1024]{1,0:T(8,128)S(1)}, bf16[640,1024]{1,0:T(8,128)(2,1)S(1)}) custom-call(s32[4]{0:T(128)S(1)} %copy-done.52, f32[640,1024]{1,0:T(8,128)S(1)} %copy-done.39, f32[8,1024]{1,0:T(8,128)S(1)} %copy-done.47, f32[640,1024]{1,0:T(8,128)S(1)} %copy-done.40, ...), custom_call_target="tpu_custom_call" | custom-call | tf_op jit(solution)/shard_map/norm_back/pallas_call | solution.py:129
  260.9 4.7 %out_back.1 = (bf16[2,640,256]{2,1,0:T(8,128)(2,1)S(1)}, bf16[2,640,256]{2,1,0:T(8,128)(2,1)S(1)}, bf16[4,128,512]{2,1,0:T(8,128)(2,1)S(1)}, bf16[4,128,512]{2,1,0:T(8,128)(2,1)}) custom-call(s32[4]{0:T(128)S(1)} %copy-done.52, bf16[640,1024]{1,0:T(8,128)(2,1)S(1)} %get-tuple-element.253.own_ref.own_half, ...), custom_call_target="tpu_custom_call" | custom-call | tf_op jit(solution)/shard_map/out_back/pallas_call | solution.py:129
  269.5 10.8 %attention_back.2 = (bf16[2,640,256]{2,1,0:T(8,128)(2,1)S(1)}, bf16[2,640,256]{2,1,0:T(8,128)(2,1)S(1)}, bf16[2,640,256]{2,1,0:T(8,128)(2,1)S(1)}) custom-call(s32[4]{0:T(128)S(1)} %copy-done.52, bf16[2,640,256]{2,1,0:T(8,128)(2,1)S(1)} %copy-done.23, bf16[2,640,256]{2,1,0:T(8,128)(2,1)S(1)} %copy-done.25, bf16[2,640,256]{2,1,0:T(8,128)(2,1)S(1)} %copy-done.27, ...), custom_call_target="tpu_custom_call" | custom-call | tf_op jit(solution)/shard_map/attention_back/pallas_call | solution.py:129
  280.4 4.3 qkv_term.2
  284.8 4.6 %collective-permute-done.16 = bf16[4,256,1024]{2,1,0:T(8,128)(2,1)S(1)} collective-permute-done((bf16[4,256,1024]{2,1,0:T(8,128)(2,1)}, bf16[4,256,1024]{2,1,0:T(8,128)(2,1)S(1)}, u32[]{:S(2)}, u32[]{:S(2)}) %collective-permute-start.16) | collective-permute-done | bytes 2097184 | tf_op jit(solution)/shard_map/ppermute | solution.py:32
  303.0 11.0 %attention_back.3 = (bf16[2,640,256]{2,1,0:T(8,128)(2,1)S(1)}, bf16[2,640,256]{2,1,0:T(8,128)(2,1)S(1)}, bf16[2,640,256]{2,1,0:T(8,128)(2,1)S(1)}) custom-call(s32[4]{0:T(128)S(1)} %copy-done.52, bf16[2,640,256]{2,1,0:T(8,128)(2,1)S(1)} %copy-done.17, bf16[2,640,256]{2,1,0:T(8,128)(2,1)S(1)} %copy-done.19, bf16[2,640,256]{2,1,0:T(8,128)(2,1)S(1)} %copy-done.21, ...), custom_call_target="tpu_custom_call" | custom-call | tf_op jit(solution)/shard_map/attention_back/pallas_call | solution.py:129
  314.1 4.3 qkv_term.3
  326.3 10.0 %qkv_back.1 = (f32[640,1024]{1,0:T(8,128)}, bf16[640,512]{1,0:T(8,128)(2,1)}, bf16[640,512]{1,0:T(8,128)(2,1)}) custom-call(s32[4]{0:T(128)} %pad_add_fusion.place_ref, bf16[2,640,256]{2,1,0:T(8,128)(2,1)} %copy-done.10, bf16[2,640,256]{2,1,0:T(8,128)(2,1)} %copy-done.11, bf16[2,640,256]{2,1,0:T(8,128)(2,1)} %copy-done.12, bf16[2,640,256]{2,1,0:T(8,128)(2,1)} %copy-done.13, ...), custom_call_target="tpu_custom_call" | custom-call | tf_op jit(solution)/shard_map/qkv_back/pallas_call | solution.py:129
  343.2 4.2 norm_back.3
  362.3 7.8 %collective-permute-done.24 = f32[8,1536]{1,0:T(8,128)S(1)} collective-permute-done((f32[8,1536]{1,0:T(8,128)S(1)}, f32[8,1536]{1,0:T(8,128)S(1)}, u32[]{:S(2)}, u32[]{:S(2)}) %collective-permute-start.24) | collective-permute-done | bytes 49184 | tf_op jit(solution)/shard_map/ppermute | solution.py:37
  371.9 7.7 %statistics.2 = (f32[128,4096]{1,0:T(8,128)}, f32[512,1024]{1,0:T(8,128)}, f32[1,128]{1,0:T(1,128)}, f32[1,512]{1,0:T(1,128)}, f32[2,5376]{1,0:T(2,128)}) custom-call(s32[4]{0:T(128)} %pad_add_fusion.place_ref, bf16[256,1024]{1,0:T(8,128)(2,1)} %reduce-scatter.7.cloned.1.call-done.refs_0_, bf16[256,1024]{1,0:T(8,128)(2,1)} %collective-permute-done.20.refs_1_, ...), custom_call_target="tpu_custom_call" | custom-call | tf_op jit(solution)/shard_map/statistics/pallas_call | solution.py:129
  396.7 7.1 %update.2 = (f32[128,4096]{1,0:T(8,128)}, f32[512,1024]{1,0:T(8,128)}, f32[1,4096]{1,0:T(1,128)}, f32[1,1024]{1,0:T(1,128)}, f32[8,128]{1,0:T(8,128)}) custom-call(s32[4]{0:T(128)} %pad_add_fusion.place_ref, f32[128,4096]{1,0:T(8,128)} %get-tuple-element.162.refs_0_, f32[512,1024]{1,0:T(8,128)} %get-tuple-element.164.refs_1_, ...), custom_call_target="tpu_custom_call" | custom-call | tf_op jit(solution)/shard_map/update/pallas_call | solution.py:129
  405.9 3.7 collective-permute-done.42.refs_5_
  411.8 4.9 %statistics.3 = (f32[128,1024]{1,0:T(8,128)}, f32[128,3072]{1,0:T(8,128)}, f32[1,128]{1,0:T(1,128)}, f32[1,128]{1,0:T(1,128)}, f32[2,5376]{1,0:T(2,128)}, /*inde...) custom-call(s32[4]{0:T(128)} %pad_add_fusion.place_ref, ...), custom_call_target="tpu_custom_call" | custom-call | tf_op jit(solution)/shard_map/statistics/pallas_call | solution.py:129
  421.9 3.7 collective-permute-done.46
  432.0 5.0 %update.3 = (f32[128,1024]{1,0:T(8,128)}, f32[128,3072]{1,0:T(8,128)}, f32[1,1024]{1,0:T(1,128)}, f32[1,3072]{1,0:T(1,128)}, f32[1,12]{1,0:T(1,128)}, /*index=5*...) custom-call(s32[4]{0:T(128)} %pad_add_fusion.place_ref, ...), custom_call_target="tpu_custom_call" | custom-call | tf_op jit(solution)/shard_map/update/pallas_call | solution.py:129
  (284 shorter events, 135.5 us)
Async XLA Ops:
  7.2 60.4 %all-gather.4.cloned.1.call-start = ((), (), s32[]{:S(2)}) async-start(), calls=%async_computation.4 | async-start | bytes 1638400 | tf_op jit(solution)/shard_map/all_gather | solution.py:59
  34.9 62.8 %all-gather.8.cloned.1.call-start = ((), (), s32[]{:S(2)}) async-start(), calls=%async_computation.6 | async-start | bytes 1310720 | tf_op jit(solution)/shard_map/all_gather | solution.py:59
  42.8 101.5 %all-gather.6.cloned.1.call-start = ((), (), s32[]{:S(2)}) async-start(), calls=%async_computation.5 | async-start | bytes 2621440 | tf_op jit(solution)/shard_map/all_gather | solution.py:59
  42.8 29.7 %collective-permute-start.2 = (bf16[4,160,768]{2,1,0:T(8,128)(2,1)S(1)}, bf16[4,160,768]{2,1,0:T(8,128)(2,1)S(1)}, u32[]{:S(2)}, u32[]{:S(2)}) collective-permute-start(bf16[4,160,768]{2,1,0:T(8,128)(2,1)S(1)} %bitcast.74), channel_id=1, source_target_pairs={{0,4},{4,0},{1,5},{5,1},{2,6},{6,2},{3,7},{7,3},{8,12},{12,8},{9,1... | collective-permute-start | bytes 2949128 | tf_op jit(solution)/shard_map/ppermute | solution.py:32
  44.4 24.7 %collective-permute-start = (bf16[640,512]{1,0:T(8,128)(2,1)}, bf16[640,512]{1,0:T(8,128)(2,1)}, u32[]{:S(2)}, u32[]{:S(2)}) collective-permute-start(bf16[640,512]{1,0:T(8,128)(2,1)} %get-tuple-element.201), channel_id=1, source_target_pairs={{0,1},{1,0},{2,3},{3,2},{4,5},{5,4},{6,7},{7,6},{8,9},{9,8},{10,11... | collective-permute-start | bytes 1966088 | tf_op jit(solution)/shard_map/ppermute | solution.py:32
  44.4 24.7 %collective-permute-start.1 = (bf16[640,512]{1,0:T(8,128)(2,1)}, bf16[640,512]{1,0:T(8,128)(2,1)}, u32[]{:S(2)}, u32[]{:S(2)}) collective-permute-start(bf16[640,512]{1,0:T(8,128)(2,1)} %get-tuple-element.202), channel_id=1, source_target_pairs={{0,1},{1,0},{2,3},{3,2},{4,5},{5,4},{6,7},{7,6},{8,9},{9,8},{10,11... | collective-permute-start | bytes 1966088 | tf_op jit(solution)/shard_map/ppermute | solution.py:32
  67.6 30.1 %collective-permute-start.3 = (bf16[4,128,1280]{2,1,0:T(8,128)(2,1)}, bf16[4,128,1280]{2,1,0:T(8,128)(2,1)S(1)}, u32[]{:S(2)}, u32[]{:S(2)}) collective-permute-start(bf16[4,128,1280]{2,1,0:T(8,128)(2,1)} %bitcast.70), channel_id=1, source_target_pairs={{0,4},{4,0},{1,5},{5,1},{2,6},{6,2},{3,7},{7,3},{8,12},{12,8},{9,1... | collective-permute-start | bytes 3932168 | tf_op jit(solution)/shard_map/ppermute | solution.py:32
  82.5 210.8 %reduce-scatter.7.cloned.1.call-start = ((), (), s32[]{:S(2)}) async-start(), calls=%async_computation.8 | async-start | bytes 2621440 | tf_op jit(solution)/shard_map/reduce_scatter | solution.py:81
  97.7 27.1 %collective-permute-start.4 = (bf16[4,128,1024]{2,1,0:T(8,128)(2,1)}, bf16[4,128,1024]{2,1,0:T(8,128)(2,1)}, u32[]{:S(2)}, u32[]{:S(2)}) collective-permute-start(bf16[4,128,1024]{2,1,0:T(8,128)(2,1)} %bitcast.84), channel_id=1, source_target_pairs={{0,4},{4,0},{1,5},{5,1},{2,6},{6,2},{3,7},{7,3},{8,12},{12,8},{9,1... | collective-permute-start | bytes 3145736 | tf_op jit(solution)/shard_map/ppermute | solution.py:32
  99.1 26.7 %collective-permute-start.5 = (bf16[4,128,1024]{2,1,0:T(8,128)(2,1)}, bf16[4,128,1024]{2,1,0:T(8,128)(2,1)}, u32[]{:S(2)}, u32[]{:S(2)}) collective-permute-start(bf16[4,128,1024]{2,1,0:T(8,128)(2,1)} %bitcast.85), channel_id=1, source_target_pairs={{0,2},{2,0},{1,3},{3,1},{4,6},{6,4},{5,7},{7,5},{8,10},{10,8},{9,1... | collective-permute-start | bytes 3145736 | tf_op jit(solution)/shard_map/ppermute | solution.py:32
  100.6 24.7 %collective-permute-start.6 = (bf16[2,640,256]{2,1,0:T(8,128)(2,1)S(1)}, bf16[2,640,256]{2,1,0:T(8,128)(2,1)S(1)}, u32[]{:S(2)}, u32[]{:S(2)}) collective-permute-start(bf16[2,640,256]{2,1,0:T(8,128)(2,1)S(1)} %get-tuple-element.214.refs_0_), channel_id=1, source_target_pairs={{0,1},{1,0},{2,3},{3,2},{4,5},{5,4},{6,7},{7,6},{8,9},{9,8},{10,11... | collective-permute-start | bytes 1966088 | tf_op jit(solution)/shard_map/ppermute | solution.py:32
  103.6 24.8 %collective-permute-start.8 = (bf16[1024,512]{1,0:T(8,128)(2,1)}, bf16[1024,512]{1,0:T(8,128)(2,1)S(1)}, u32[]{:S(2)}, u32[]{:S(2)}) collective-permute-start(bf16[1024,512]{1,0:T(8,128)(2,1)} %gather_out.1.refs_4_), channel_id=1, source_target_pairs={{0,1},{1,0},{2,3},{3,2},{4,5},{5,4},{6,7},{7,6},{8,9},{9,8},{10,11... | collective-permute-start | bytes 3145736 | tf_op jit(solution)/shard_map/ppermute | solution.py:32
  124.8 25.4 %collective-permute-start.11 = (bf16[4,128,1024]{2,1,0:T(8,128)(2,1)}, bf16[4,128,1024]{2,1,0:T(8,128)(2,1)}, u32[]{:S(2)}, u32[]{:S(2)}) collective-permute-start(bf16[4,128,1024]{2,1,0:T(8,128)(2,1)} %collective-permute-done.4.refs_5_), channel_id=1, source_target_pairs={{0,2},{2,0},{1,3},{3,1},{4,6},{6,4},{5,7},{7,5},{8,10},{10,8},{9,1... | collective-permute-start | bytes 3145736 | tf_op jit(solution)/shard_map/ppermute | solution.py:32
  125.3 20.4 %collective-permute-start.9 = (bf16[640,512]{1,0:T(8,128)(2,1)}, bf16[640,512]{1,0:T(8,128)(2,1)S(1)}, u32[]{:S(2)}, u32[]{:S(2)}) collective-permute-start(bf16[640,512]{1,0:T(8,128)(2,1)} %get-tuple-element.231), channel_id=1, source_target_pairs={{0,1},{1,0},{2,3},{3,2},{4,5},{5,4},{6,7},{7,6},{8,9},{9,8},{10,11... | collective-permute-start | bytes 1966088 | tf_op jit(solution)/shard_map/ppermute | solution.py:32
  125.8 19.9 %collective-permute-start.10 = (bf16[640,512]{1,0:T(8,128)(2,1)}, bf16[640,512]{1,0:T(8,128)(2,1)}, u32[]{:S(2)}, u32[]{:S(2)}) collective-permute-start(bf16[640,512]{1,0:T(8,128)(2,1)} %get-tuple-element.232), channel_id=1, source_target_pairs={{0,1},{1,0},{2,3},{3,2},{4,5},{5,4},{6,7},{7,6},{8,9},{9,8},{10,11... | collective-permute-start | bytes 1966088 | tf_op jit(solution)/shard_map/ppermute | solution.py:32
  144.3 48.7 %collective-permute-start.13 = (bf16[4,256,1024]{2,1,0:T(8,128)(2,1)}, bf16[4,256,1024]{2,1,0:T(8,128)(2,1)S(1)}, u32[]{:S(2)}, u32[]{:S(2)}) collective-permute-start(bf16[4,256,1024]{2,1,0:T(8,128)(2,1)} %bitcast.82), channel_id=1, source_target_pairs={{0,4},{4,0},{1,5},{5,1},{2,6},{6,2},{3,7},{7,3},{8,12},{12,8},{9,1... | collective-permute-start | bytes 6291464 | tf_op jit(solution)/shard_map/ppermute | solution.py:32
  180.1 56.9 %collective-permute-start.12 = (bf16[4,256,1024]{2,1,0:T(8,128)(2,1)}, bf16[4,256,1024]{2,1,0:T(8,128)(2,1)}, u32[]{:S(2)}, u32[]{:S(2)}) collective-permute-start(bf16[4,256,1024]{2,1,0:T(8,128)(2,1)} %get-tuple-element.235), channel_id=1, source_target_pairs={{0,4},{4,0},{1,5},{5,1},{2,6},{6,2},{3,7},{7,3},{8,12},{12,8},{9,1... | collective-permute-start | bytes 6291464 | tf_op jit(solution)/shard_map/ppermute | solution.py:32
  241.0 95.8 %reduce-scatter.5.cloned.1.call-start = ((), (), s32[]{:S(2)}) async-start(), calls=%async_computation.7 | async-start | bytes 2621440 | tf_op jit(solution)/shard_map/reduce_scatter | solution.py:81
  241.6 47.8 %collective-permute-start.16 = (bf16[4,256,1024]{2,1,0:T(8,128)(2,1)}, bf16[4,256,1024]{2,1,0:T(8,128)(2,1)S(1)}, u32[]{:S(2)}, u32[]{:S(2)}) collective-permute-start(bf16[4,256,1024]{2,1,0:T(8,128)(2,1)} %get-tuple-element.251), channel_id=1, source_target_pairs={{0,4},{4,0},{1,5},{5,1},{2,6},{6,2},{3,7},{7,3},{8,12},{12,8},{9,1... | collective-permute-start | bytes 6291464 | tf_op jit(solution)/shard_map/ppermute | solution.py:32
  291.8 92.6 %reduce-scatter.9.cloned.1.call-start = ((), (), s32[]{:S(2)}) async-start(), calls=%async_computation.9 | async-start | bytes 1638400 | tf_op jit(solution)/shard_map/reduce_scatter | solution.py:81
  291.8 30.2 %collective-permute-start.19 = (bf16[4,128,768]{2,1,0:T(8,128)(2,1)}, bf16[4,128,768]{2,1,0:T(8,128)(2,1)}, u32[]{:S(2)}, u32[]{:S(2)}) collective-permute-start(bf16[4,128,768]{2,1,0:T(8,128)(2,1)} %get-tuple-element.264), channel_id=1, source_target_pairs={{0,4},{4,0},{1,5},{5,1},{2,6},{6,2},{3,7},{7,3},{8,12},{12,8},{9,1... | collective-permute-start | bytes 2359304 | tf_op jit(solution)/shard_map/ppermute | solution.py:32
  293.4 20.7 %collective-permute-start.20 = (bf16[256,1024]{1,0:T(8,128)(2,1)}, bf16[256,1024]{1,0:T(8,128)(2,1)}, u32[]{:S(2)}, u32[]{:S(2)}) collective-permute-start(bf16[256,1024]{1,0:T(8,128)(2,1)} %reduce-scatter.7.cloned.1.call-done.refs_0_), channel_id=1, source_target_pairs={{0,2},{2,0},{1,3},{3,1},{4,6},{6,4},{5,7},{7,5},{8,10},{10,8},{9,1... | collective-permute-start | bytes 1572872 | tf_op jit(solution)/shard_map/ppermute | solution.py:32
  294.8 27.2 %collective-permute-start.18 = (bf16[4,128,512]{2,1,0:T(8,128)(2,1)}, bf16[4,128,512]{2,1,0:T(8,128)(2,1)S(1)}, u32[]{:S(2)}, u32[]{:S(2)}) collective-permute-start(bf16[4,128,512]{2,1,0:T(8,128)(2,1)} %get-tuple-element.262), channel_id=1, source_target_pairs={{0,4},{4,0},{1,5},{5,1},{2,6},{6,2},{3,7},{7,3},{8,12},{12,8},{9,1... | collective-permute-start | bytes 1572872 | tf_op jit(solution)/shard_map/ppermute | solution.py:32
  324.7 79.1 %reduce-scatter.11.cloned.1.call-start = ((), (), s32[]{:S(2)}) async-start(), calls=%async_computation.10 | async-start | bytes 983040 | tf_op jit(solution)/shard_map/reduce_scatter | solution.py:81
  324.7 26.1 %collective-permute-start.32 = (bf16[4,128,768]{2,1,0:T(8,128)(2,1)}, bf16[4,128,768]{2,1,0:T(8,128)(2,1)}, u32[]{:S(2)}, u32[]{:S(2)}) collective-permute-start(bf16[4,128,768]{2,1,0:T(8,128)(2,1)} %get-tuple-element.292), channel_id=1, source_target_pairs={{0,4},{4,0},{1,5},{5,1},{2,6},{6,2},{3,7},{7,3},{8,12},{12,8},{9,1... | collective-permute-start | bytes 2359304 | tf_op jit(solution)/shard_map/ppermute | solution.py:32
  336.8 20.2 %collective-permute-start.31 = (bf16[256,1024]{1,0:T(8,128)(2,1)}, bf16[256,1024]{1,0:T(8,128)(2,1)}, u32[]{:S(2)}, u32[]{:S(2)}) collective-permute-start(bf16[256,1024]{1,0:T(8,128)(2,1)} %reduce-scatter.5.cloned.1.call-done.refs_4_), channel_id=1, source_target_pairs={{0,2},{2,0},{1,3},{3,1},{4,6},{6,4},{5,7},{7,5},{8,10},{10,8},{9,1... | collective-permute-start | bytes 1572872 | tf_op jit(solution)/shard_map/ppermute | solution.py:32
  350.3 20.3 %collective-permute-start.29 = (bf16[256,1024]{1,0:T(8,128)(2,1)}, bf16[256,1024]{1,0:T(8,128)(2,1)S(1)}, u32[]{:S(2)}, u32[]{:S(2)}) collective-permute-start(bf16[256,1024]{1,0:T(8,128)(2,1)} %reduce-scatter.7.cloned.1.call-done.refs_0_), channel_id=1, source_target_pairs={{0,1},{1,0},{2,3},{3,2},{4,5},{5,4},{6,7},{7,6},{8,9},{9,8},{10,11... | collective-permute-start | bytes 1572872 | tf_op jit(solution)/shard_map/ppermute | solution.py:32
  350.8 19.8 %collective-permute-start.30 = (bf16[256,1024]{1,0:T(8,128)(2,1)}, bf16[256,1024]{1,0:T(8,128)(2,1)S(1)}, u32[]{:S(2)}, u32[]{:S(2)}) collective-permute-start(bf16[256,1024]{1,0:T(8,128)(2,1)} %collective-permute-done.20.refs_1_), channel_id=1, source_target_pairs={{0,1},{1,0},{2,3},{3,2},{4,5},{5,4},{6,7},{7,6},{8,9},{9,8},{10,11... | collective-permute-start | bytes 1572872 | tf_op jit(solution)/shard_map/ppermute | solution.py:32
  357.0 13.7 %collective-permute-start.33 = (bf16[256,1024]{1,0:T(8,128)(2,1)S(1)}, bf16[256,1024]{1,0:T(8,128)(2,1)S(1)}, u32[]{:S(2)}, u32[]{:S(2)}) collective-permute-start(bf16[256,1024]{1,0:T(8,128)(2,1)S(1)} %copy-done.65), channel_id=1, source_target_pairs={{0,1},{1,0},{2,3},{3,2},{4,5},{5,4},{6,7},{7,6},{8,9},{9,8},{10,11... | collective-permute-start | bytes 1572872 | tf_op jit(solution)/shard_map/ppermute | solution.py:32
  359.8 10.9 %collective-permute-start.34 = (bf16[256,1024]{1,0:T(8,128)(2,1)}, bf16[256,1024]{1,0:T(8,128)(2,1)S(1)}, u32[]{:S(2)}, u32[]{:S(2)}) collective-permute-start(bf16[256,1024]{1,0:T(8,128)(2,1)} %collective-permute-done.31.refs_5_), channel_id=1, source_target_pairs={{0,1},{1,0},{2,3},{3,2},{4,5},{5,4},{6,7},{7,6},{8,9},{9,8},{10,11... | collective-permute-start | bytes 1572872 | tf_op jit(solution)/shard_map/ppermute | solution.py:32
  370.1 12.7 %collective-permute-start.27 = (f32[8,1536]{1,0:T(8,128)S(1)}, f32[8,1536]{1,0:T(8,128)S(1)}, u32[]{:S(2)}, u32[]{:S(2)}) collective-permute-start(f32[8,1536]{1,0:T(8,128)S(1)} %add_add_fusion), channel_id=1, source_target_pairs={{0,4},{4,0},{1,5},{5,1},{2,6},{6,2},{3,7},{7,3},{8,12},{12,8},{9,1... | collective-permute-start | bytes 147464 | tf_op jit(solution)/shard_map/ppermute | solution.py:42
  384.3 20.9 %collective-permute-start.39 = (bf16[128,1280]{1,0:T(8,128)(2,1)}, bf16[128,1280]{1,0:T(8,128)(2,1)S(1)}, u32[]{:S(2)}, u32[]{:S(2)}) collective-permute-start(bf16[128,1280]{1,0:T(8,128)(2,1)} %reduce-scatter.9.cloned.1.call-done.refs_0_), channel_id=1, source_target_pairs={{0,2},{2,0},{1,3},{3,1},{4,6},{6,4},{5,7},{7,5},{8,10},{10,8},{9,1... | collective-permute-start | bytes 983048 | tf_op jit(solution)/shard_map/ppermute | solution.py:32
  (102 other events, 553.2 us)
Sparse Core Ops, SparseCore 0:
  35.0 32.5 all-gather.3
  69.7 26.9 all-gather.7
  98.8 45.4 all-gather.5
  241.1 42.7 reduce-scatter.6
  291.9 42.7 reduce-scatter.4
  337.5 33.7 reduce-scatter.8
  374.1 24.2 reduce-scatter.10

commit v7 on v6

--- a/solution.py
+++ b/solution.py
@@ -16,7 +16,16 @@
 GROUPS = 2
 GIVEN = 2
 VMEM_LIMIT = 60
-VMEM_LIMITS = {"attention": 40, "attention_back": 40, "qkv_term": 40, "out_back": 40, "norm_back": 40}
+VMEM_LIMITS = {
+    "attention": 30,
+    "attention_back": 30,
+    "gather_out": 30,
+    "norm_back": 30,
+    "out_back": 40,
+    "pack_terms": 30,
+    "project_next": 40,
+    "qkv_term": 30,
+}
 
 ALL_AXES = ("z", "x", "y", "c")
 
@@ -77,6 +86,12 @@
     return total.reshape(-1, total.shape[-1])
 
 
+def fold_pair(keep_one, got_one, keep_two, got_two):
+    both = [low(wide(keep_one) + wide(got_one)), low(wide(keep_two) + wide(got_two))]
+    total = jnp.concatenate(both, axis=1)
+    return total.reshape(-1, total.shape[-1])
+
+
 def scatter_z(total):
     return lax.psum_scatter(total, "z", scatter_dimension=0, tiled=True)
 
@@ -89,6 +104,13 @@
 
 def with_core(own):
     return own, [swap(one, "c") for one in own]
+
+
+def sum_y_and_core(mine):
+    if lax.axis_size("y") != 2:
+        return with_core(sum_y(mine))
+    across = lax.ppermute(mine, ("y", "c"), [(i, 3 - i) for i in range(4)])
+    return [mine, swap(mine, "y")], [swap(mine, "c"), across]
 
 
 def row_pad(length):
@@ -402,6 +424,8 @@
             for at in range(0, length, LANES):
                 block = wide(joined(part_refs, slice(at, at + LANES)))
                 normed_ref[image, at : at + LANES, :] = low(normalised(block) * gain + bias)
+
+        def one_image(image, carry):
             write_qkv(
                 normed_ref[image],
                 weight,
@@ -412,6 +436,9 @@
                 k_ref,
                 v_ref,
             )
+            return carry
+
+        lax.fori_loop(0, 2, one_image, 0)
 
     part_out = sds((2, length, heads), jnp.bfloat16)
     return call(
@@ -457,8 +484,12 @@
         at = group * heads
         bias_q = vec_ref[BIAS_QV : BIAS_QV + 1, at : at + heads]
         bias_v = vec_ref[BIAS_QV : BIAS_QV + 1, half + at : half + at + heads]
-        for image in range(2):
+
+        def one_image(image, carry):
             write_qkv(normed_ref[image], weight, bias_q, bias_v, image, q_ref, k_ref, v_ref)
+            return carry
+
+        lax.fori_loop(0, 2, one_image, 0)
 
     return call(
         body,
@@ -660,14 +691,18 @@
     _, length, _ = normed.shape
     first_call = running is None
     last_call = chunk == CHUNKS - 1
+    given = GIVEN if last_call else 1
 
     def body(place_ref, normed_ref, own_cot, *refs):
         other_cots, (bias_ref, *refs) = refs[:GIVEN], refs[GIVEN:]
         ins, refs = refs[: 2 * cut], refs[2 * cut :]
         if not first_call:
             before, refs = refs[:4], refs[4:]
-        out_own, out_other, gn_own, gn_other, bsum_ref, keep_ref, send_ref = refs[:7]
-        w_in, w_down, normed_t, grads, sem, out_sem = refs[7:]
+        out_own, *out_other = refs[: 1 + given]
+        gn_own, *gn_other = refs[1 + given : 2 + 2 * given]
+        bsum_ref, *refs = refs[2 + 2 * given :]
+        term_refs, refs = refs[:4], refs[4:]
+        w_in, w_down, cots, into, down, grads, sem, out_sem = refs
         copies = []
         for weight, at, rows, of_shard in (
             (w_in, 0, rows_in, part),
@@ -686,45 +721,63 @@
                     )
                     copy.start()
                     copies.append(copy)
-        for image in range(2):
-            normed_t[:, image * length : (image + 1) * length] = normed_ref[image].T
         for copy in copies:
             copy.wait()
-        into = None
-        down = None
-        column_sum = None
-        for image, cot_refs in enumerate(((own_cot,), other_cots)):
-            preact = dot(normed_ref[image], w_in[...]) + bias_ref[0]
+        cots[0] = own_cot[...]
+        cots[1] = joined(other_cots)
+
+        def one_image(image, carry):
+            first = image == 0
+            normed_rows = normed_ref[image]
+            preact = dot(normed_rows, w_in[...]) + bias_ref[0]
             phi = 0.5 * (1.0 + lax.erf(preact * math.sqrt(0.5)))
             density = jnp.exp(-0.5 * preact * preact) * (1.0 / math.sqrt(2.0 * math.pi))
             hidden = low(preact * phi)
             slope = phi + preact * density
-            cot = joined(cot_refs)
+            cot = cots[image]
             grad = low(dot_tail(cot, w_down[...]) * slope)
-            out_ref, gn_ref = ((out_own, gn_own), (out_other, gn_other))[image]
             to_out = dot(hidden, w_down[...])
             to_normed = dot_tail(grad, w_in[...])
-            if not first_call:
-                to_out = before[image][...] + to_out
-                to_normed = before[2 + image][...] + to_normed
-            out_ref[...] = to_out.astype(out_ref.dtype)
-            gn_ref[...] = to_normed.astype(gn_ref.dtype)
+            for slot, to_refs in enumerate((([out_own], [gn_own]), (out_other, gn_other))):
+
+                @pl.when(image == slot)
+                def _():
+                    for number, (refs_of, value) in enumerate(zip(to_refs, (to_out, to_normed))):
+                        if not first_call:
+                            value = before[2 * number + slot][...] + value
+                        cols = width // len(refs_of)
+                        for at, ref in enumerate(refs_of):
+                            ref[...] = value[:, at * cols : (at + 1) * cols].astype(ref.dtype)
+
             partial = jnp.sum(wide(grad), axis=0, keepdims=True)
-            column_sum = partial if image == 0 else column_sum + partial
-            to_in = dot(normed_t[:, image * length : (image + 1) * length], grad)
-            into = to_in if image == 0 else into + to_in
+            to_in = dot(normed_rows.T, grad)
             to_down = dot(hidden.T, cot)
-            down = to_down if image == 0 else down + to_down
-        bsum_ref[...] = column_sum
-        for z in range(z_size):
-            for x in range(2):
-                dx = x + (1 - 2 * x) * place_ref[1]
-                s = z * 2 + x
-                grads[dx, z, :part, :] = low(into[s * part : (s + 1) * part, :])
-                grads[dx, z, part:, :] = low(down[s * per_shard : (s + 1) * per_shard, :])
+
+            @pl.when(first)
+            def _():
+                bsum_ref[...] = partial
+                into[...] = to_in
+                down[...] = to_down
+
+            @pl.when(jnp.logical_not(first))
+            def _():
+                bsum_ref[...] += partial
+                for slot, (held, value, rows) in enumerate(
+                    ((into, to_in, part), (down, to_down, per_shard))
+                ):
+                    whole_term = low(held[...] + value)
+                    for z in range(z_size):
+                        for x in range(2):
+                            dx = x + (1 - 2 * x) * place_ref[1]
+                            s = z * 2 + x
+                            grads[slot, dx, z] = whole_term[s * rows : (s + 1) * rows, :]
+
+            return carry
+
+        lax.fori_loop(0, 2, one_image, 0)
         copies = [
-            pltpu.make_async_copy(grads.at[slot], ref, out_sem.at[slot])
-            for slot, ref in enumerate((keep_ref, send_ref))
+            pltpu.make_async_copy(grads.at[number // 2, number % 2], ref, out_sem.at[number])
+            for number, ref in enumerate(term_refs)
         ]
         for copy in copies:
             copy.start()
@@ -732,8 +785,11 @@
             copy.wait()
 
     total = sds((length, width), jnp.float32)
-    other = sds((length, width), jnp.bfloat16 if last_call else jnp.float32)
-    piece_out = sds((z_size, part + per_shard, width), jnp.bfloat16)
+    other = sds((length, width // given), jnp.bfloat16 if last_call else jnp.float32)
+    totals = ([total] + [other] * given) * 2
+    if part != per_shard:
+        raise ValueError
+    piece_out = sds((z_size, part, width), jnp.bfloat16)
     carried = () if first_call else tuple(running)
     return call(
         body,
@@ -744,15 +800,17 @@
         + [pl.BlockSpec((1, 1, hidden_width), lambda i, p: (chunk, 0, 0))]
         + [any_spec()] * (2 * cut)
         + [whole((length, width))] * len(carried),
-        [total, other, total, other] + [sds((1, hidden_width), jnp.float32)] + [piece_out] * 2,
-        [whole((length, width))] * 4 + [whole((1, hidden_width))] + [any_spec()] * 2,
+        totals + [sds((1, hidden_width), jnp.float32)] + [piece_out] * 4,
+        [whole(a.shape) for a in totals] + [whole((1, hidden_width))] + [any_spec()] * 4,
         [
             pltpu.VMEM((width, hidden_width), jnp.bfloat16),
             pltpu.VMEM((hidden_width, width), jnp.bfloat16),
-            pltpu.VMEM((width, 2 * length), jnp.bfloat16),
-            pltpu.VMEM((2, z_size, part + per_shard, width), jnp.bfloat16),
+            pltpu.VMEM((2, length, width), jnp.bfloat16),
+            pltpu.VMEM((width, hidden_width), jnp.float32),
+            pltpu.VMEM((hidden_width, width), jnp.float32),
+            pltpu.VMEM((2, 2, z_size, part, width), jnp.bfloat16),
             pltpu.SemaphoreType.DMA((4 * cut * z_size,)),
-            pltpu.SemaphoreType.DMA((2,)),
+            pltpu.SemaphoreType.DMA((4,)),
         ],
         "feed_forward",
     )
@@ -766,16 +824,19 @@
         step = pl.program_id(0)
         values = wide(rows_ref[...])
         if finish:
-            first_ref, second_ref, *refs = refs
+            first_ref, second_refs, refs = refs[0], refs[1 : len(finish)], refs[len(finish) :]
             refs[1][...] = low(
-                values + first_ref[...] + wide(second_ref[...]) + vec_ref[BIAS_DOWN : BIAS_DOWN + 1, :]
+                values
+                + first_ref[...]
+                + wide(joined(second_refs))
+                + vec_ref[BIAS_DOWN : BIAS_DOWN + 1, :]
             )
         sum_ref = refs[0]
         centre = values - jnp.mean(values, axis=-1, keepdims=True)
         spread = jnp.mean(centre * centre, axis=-1, keepdims=True)
         inverse = lax.rsqrt(spread + ln_eps)
         unit = centre * inverse
-        grad = own_ref[...] + jnp.concatenate([wide(ref[...]) for ref in other_refs], axis=1)
+        grad = own_ref[...] + wide(joined(other_refs))
         scaled = grad * vec_ref[gain_row : gain_row + 1, :]
         mean_one = jnp.mean(scaled, axis=-1, keepdims=True)
         mean_two = jnp.mean(scaled * unit, axis=-1, keepdims=True)
@@ -792,20 +853,24 @@
         else:
             refs[2][...] = result
             refs[3][...] = rounded
-        joined = jnp.concatenate(parts, axis=0)
+            for number, ref in enumerate(refs[4:]):
+                at = number * width // GIVEN
+                ref[...] = rounded[:, at : at + width // GIVEN]
+        sums = jnp.concatenate(parts, axis=0)
 
         @pl.when(step == 0)
         def _():
-            sum_ref[...] = joined
+            sum_ref[...] = sums
 
         @pl.when(step > 0)
         def _():
-            sum_ref[...] += joined
+            sum_ref[...] += sums
 
     block = pl.BlockSpec((LANES, width), lambda i, p: (i, 0))
     outs = [sds((8, width), jnp.float32), sds((tokens, width), jnp.bfloat16)]
     if finish:
         outs += [sds((length, width), jnp.float32), sds((length, width), jnp.bfloat16)]
+        outs += [sds((length, width // GIVEN), jnp.bfloat16)] * GIVEN
     other_block = pl.BlockSpec((LANES, others[0].shape[1]), lambda i, p: (i, 0))
     ins = (rows, vectors, grad_own, passed, *others, *finish)
     return call(
@@ -814,22 +879,24 @@
         ins,
         [block, whole(vectors.shape), block, block]
         + [other_block] * len(others)
-        + [block] * len(finish),
+        + ([block] + [other_block] * len(others) if finish else []),
         outs,
-        [whole((8, width))] + [block] * (len(outs) - 1),
+        [whole((8, width))]
+        + [pl.BlockSpec((LANES, a.shape[1]), lambda i, p: (i, 0)) for a in outs[1:]],
         [],
         "norm_back",
         grid=(length // LANES,),
     )
 
 
-def out_back(place, grad_own, grad_other, mine, theirs, weight_mine, weight_theirs):
+def out_back(place, grad_own, grad_others, mine, theirs, weight_mine, weight_theirs):
     width, half = weight_mine.shape
     z_size = lax.axis_size("z")
     part = width // (2 * z_size)
     _, length, heads = mine[0].shape
 
-    def body(place_ref, own_ref, other_ref, own_half, other_half, *refs):
+    def body(place_ref, own_ref, own_half, *refs):
+        other_refs, refs = refs[:GIVEN], refs[GIVEN:]
         mine_refs, theirs_refs, refs = refs[:GROUPS], refs[GROUPS : 2 * GROUPS], refs[2 * GROUPS :]
         wm_ref, wt_ref, *refs = refs
         ga_refs, (keep_ref, send_ref, turned, grads, out_sem) = refs[:GROUPS], refs[GROUPS:]
@@ -840,7 +907,9 @@
                 at_mine, at_theirs = head_rows(core, heads, g)
                 turned[pl.ds(at_mine, heads), lanes] = mine_refs[g][image].T
                 turned[pl.ds(at_theirs, heads), lanes] = theirs_refs[g][1 - image].T
-        term = dot(turned[:, :length], own_half[...]) + dot(turned[:, length:], other_half[...])
+        other = joined(other_refs)
+        other_half = select(core, other[:, :half], other[:, half:])
+        term = dot(turned[:, :length], own_half[...]) + dot(turned[:, length:], other_half)
         for z in range(z_size):
             for x in range(2):
                 dx = x + (1 - 2 * x) * place_ref[1]
@@ -848,8 +917,8 @@
                 grads[dx, z] = low(term[at : at + part, :])
         for slot, ref in enumerate((keep_ref, send_ref)):
             pltpu.make_async_copy(grads.at[slot], ref, out_sem.at[slot]).start()
-        for image, ref in enumerate((own_ref, other_ref)):
-            first, second = ref[:, :half], ref[:, half:]
+        for image, value in enumerate((own_ref[...], other)):
+            first, second = value[:, :half], value[:, half:]
             left = select(core, first, second)
             right = select(core, second, first)
             for g in range(GROUPS):
@@ -866,9 +935,9 @@
     return call(
         body,
         place,
-        (grad_own, grad_other, grad_own, grad_other, *mine, *theirs, weight_mine, weight_theirs),
-        [whole((length, width))] * 2
-        + [half_block] * 2
+        (grad_own, grad_own, *grad_others, *mine, *theirs, weight_mine, weight_theirs),
+        [whole((length, width)), half_block]
+        + [whole((length, width // GIVEN))] * GIVEN
         + [whole((2, length, heads))] * (2 * GROUPS)
         + [whole((width, half))] * 2,
         [sds((2, length, heads), jnp.bfloat16)] * GROUPS + [piece_out] * 2,
@@ -948,7 +1017,8 @@
             copy.start()
         for copy in copies:
             copy.wait()
-        for image in range(2):
+
+        def one_image(image, carry):
             total = None
             for g in range(GROUPS):
                 for slot in range(3):
@@ -957,12 +1027,20 @@
                         weight[g, :, slot * heads : (slot + 1) * heads],
                     )
                     total = add if total is None else total + add
-            if image == 0:
+
+            @pl.when(image == 0)
+            def _():
                 own_ref[...] = total
-            else:
+
+            @pl.when(image == 1)
+            def _():
                 for number, ref in enumerate(other_refs):
                     at = number * width // GIVEN
                     ref[...] = low(total[:, at : at + width // GIVEN])
+
+            return carry
+
+        lax.fori_loop(0, 2, one_image, 0)
 
     return call(
         body,
@@ -1348,7 +1426,7 @@
     rows_own, parts = pad_rows(after(place, near), inputs)
     rows = (rows_own, [swap(one, "c") for one in parts])
     *shards_ff, down_sums = prepare_rest(
-        after(place, rows_own), in_weight, down_weight, cotangent, (2 if by_y else 1, 1)
+        after(place, rows_own), in_weight, down_weight, cotangent, (2 if by_y else 1,) * 2
     )
     cot_own, parts = pad_rows(after(place, (down_sums, rows[1])), cotangent)
     near_ff = [along_z(shards_ff[0])]
@@ -1384,39 +1462,50 @@
         pieces_ff = [[near_ff[0], near_too], [across, swap(across, "y")]]
     else:
         pieces_ff = [[near_ff[0]], [across]]
+    near_ff[1] = after(near_ff[1], across)
+    across_next = swap(near_ff[1], "x")
+    near_first = near_too
+    near_too = (near_too, swap(near_ff[1], "y")) if by_y else None
     middle, normed_mid = project_out(
-        after(place, (across, near_too)), attended, theirs, weight_mine, weight_theirs, rows, vectors
-    )
-    near_ff[1] = after(near_ff[1], normed_mid)
-    pieces_next_ff = by_x(near_ff[1])
-    *running, sums, keep, send = feed_forward(
-        after(place, near_ff[1]), normed_mid, cot, pieces_ff, hidden_bias, 0, None
-    )
+        after(place, (near_ff[1], near_first)), attended, theirs, weight_mine, weight_theirs, rows, vectors
+    )
+    across_next = after(across_next, normed_mid)
+    if by_y:
+        pieces_ff = [
+            [[near_ff[0], near_too[0]], pieces_ff[1]],
+            [[near_ff[1], near_too[1]], [across_next, swap(across_next, "y")]],
+        ]
+    else:
+        pieces_ff = [[[near_ff[0]], [across]], [[near_ff[1]], [across_next]]]
+    *running, sums, keep_in, send_in, keep_down, send_down = feed_forward(
+        after(place, across_next), normed_mid, cot, pieces_ff[0], hidden_bias, 0, None
+    )
+    terms_ff = [(keep_in, swap(send_in, "x"), keep_down, swap(send_down, "x"))]
     hidden_sums = [sums]
-    got = swap(send, "x")
-    *running, sums, keep_next, send_next = feed_forward(
-        place, normed_mid, cot, pieces_next_ff, hidden_bias, 1, running
+    *totals, sums, keep_in, send_in, keep_down, send_down = feed_forward(
+        place, normed_mid, cot, pieces_ff[1], hidden_bias, 1, running
     )
     hidden_sums.append(sums)
-    folded = [fold(*after((keep, got), sums))]
-    got_next = swap(send_next, "x")
+    folded = [fold_pair(*after(terms_ff[0], sums))]
+    terms_ff.append((keep_in, swap(send_in, "x"), keep_down, swap(send_down, "x")))
     scattered = [scatter_z(folded[0])]
-    out_share, out_given, normed_share, normed_given = running
-    sums_mid, output, grad_mid, grad_mid_low = norm_back(
+    out_share, *out_given = totals[: 1 + GIVEN]
+    normed_share, *normed_given = totals[1 + GIVEN :]
+    sums_mid, output, grad_mid, grad_mid_low, *parts = norm_back(
         after(place, folded[0]),
         middle,
         vectors,
         GAIN_TWO,
         normed_share,
-        [swap(normed_given, "c")],
+        [swap(one, "c") for one in normed_given],
         cot_own,
         tokens,
-        (out_share, swap(out_given, "c")),
+        (out_share, *[swap(one, "c") for one in out_given]),
     )
     *grad_attended, keep, send = out_back(
         place,
         grad_mid_low,
-        swap(grad_mid_low, "c"),
+        [swap(one, "c") for one in parts],
         attended,
         theirs,
         weight_mine,
@@ -1426,7 +1515,7 @@
     grad_qkv = [attention_back(place, *qkv[0], probs[0], grad_attended[0])]
     sums_first, keep_first, send_first = qkv_term(place, normed, *grad_qkv[0])
     got_first = swap(send_first, "x")
-    folded.append(fold(*after((keep_next, got_next), sums_first)))
+    folded.append(fold_pair(*after(terms_ff[1], sums_first)))
     scattered.append(scatter_z(folded[1]))
     scattered[0] = after(scattered[0], folded[1])
     own_ff = [sum_y(scattered[0])]
@@ -1477,18 +1566,20 @@
         group,
     )
     scattered[2] = after(scattered[2], rows_early[0])
-    own_mid = sum_y(scattered[2])
+    own_mid = after(sum_y(scattered[2]), terms)
+    pairs.append(with_core(own_mid))
+    pack = sum_over(pack, ("z", "x"))
+    scattered[3] = after(scattered[3], (pack, pairs[-1]))
+    pairs.append(sum_y_and_core(scattered[3]))
     new_early, cols_early, clips_early, _ = update(
-        after(place, (terms, scattered[2])),
+        after(place, scattered[3]),
         grads_early,
         rows_early,
         weights,
         [as_row(state) for state in (in_cols, down_cols)],
-        sum_over(pack, ("z", "x")),
+        pack,
         group,
     )
-    pairs.append(with_core(after(own_mid, clips_early)))
-    pairs.append(with_core(sum_y(after(scattered[3], clips_early))))
     weights = [out_weight, qkv_weight]
     grads_late, rows_late, pack, vector_grads, new_moments = statistics(
         after(place, clips_early),

time: 453 us -> 444 us (0.980)
  waiting for transfers between devices: 109 us -> 96.6 us
  starting transfers between devices: 37.5 us -> 45.6 us
    ppermute x9, waiting for transfers between devices: 24.3 us -> 11.1 us  [shift(): lax.ppermute(value, axis, [(i, (i + step) % size) for i in range(size)])]
    ppermute x35 -> x41, waiting for transfers between devices: 50.5 us -> 44.1 us  [swap(): return lax.ppermute(value, axis, [(0, 1), (1, 0)])]
    reduce_scatter x4, waiting for transfers between devices: 0.01 us -> 6.21 us  [scatter_z(): return lax.psum_scatter(total, 'z', scatter_dimension=0, tiled=True)]
    ppermute x35 -> x41, starting transfers between devices: 22.7 us -> 28.1 us  [swap(): return lax.ppermute(value, axis, [(0, 1), (1, 0)])]
    convert_element_type x5 -> x6, other arithmetic: 9.95 us -> 6.53 us  [low(): return value.astype(jnp.bfloat16)]
    unnamed x156 -> x140, local copies, waits for them, and re-layouts: 39.9 us -> 38.1 us
  transfers between devices with their start and end apart: 56 -> 63, of which waited for: 28 -> 31; matrix products, arithmetic and copies ran while one was open for 2% -> 2% of each run, Pallas kernels for 43% -> 44%
where the time goes in v7:
time: 444 us; the launch traced here: 438 us
  Pallas kernels  204 us (46%)
  waiting for transfers between devices  96.6 us (22%)
  starting transfers between devices  45.6 us (10%)
  local copies, waits for them, and re-layouts  38.1 us (9%)
  blocking collectives  23.7 us (5%)
  between operations  15.3 us (3%)
  other arithmetic  14.8 us (3%)
    pallas_call x25, Pallas kernels, call(): pl.pallas_call(body, out_shape=outs, grid_spec=pltpu.PrefetchScalarGridSp...  204 us
    ppermute x41, waiting for transfers between devices, swap(): return lax.ppermute(value, axis, [(0, 1), (1, 0)])  44.1 us
    unnamed x140, local copies, waits for them, and re-layouts  38.1 us
    ppermute x41, starting transfers between devices, swap(): return lax.ppermute(value, axis, [(0, 1), (1, 0)])  28.1 us
    all_gather x3, waiting for transfers between devices, along_z(): near = lax.all_gather(shard, 'z', axis=0, tiled=True)  24.5 us
    all_gather x1, blocking collectives, along_z(): near = lax.all_gather(shard, 'z', axis=0, tiled=True)  23.7 us
    ppermute x9, starting transfers between devices, shift(): lax.ppermute(value, axis, [(i, (i + step) % size) for i in range(size)])  11.3 us
    ppermute x9, waiting for transfers between devices, shift(): lax.ppermute(value, axis, [(i, (i + step) % size) for i in range(size)])  11.1 us
  transfers between devices with their start and end apart: 63, of which 31 were waited for; matrix products, arithmetic and copies ran while one was open for 2% of the time, Pallas kernels for 44%

profile of v7, /device:TPU:0, one launch (start us, length us, event | category | flops | bytes accessed | tf_op | source)
XLA Modules:
  0.0 438.2 jit_solution(464653671101827288)
XLA Ops:
  7.9 3.2 prepare_qkv.1
  11.1 23.7 %all_gather.12 = bf16[640,768]{1,0:T(8,128)(2,1)S(1)} all-gather(bf16[160,768]{1,0:T(8,128)(2,1)} %get-tuple-element.208), channel_id=1, replica_groups=mesh['z'=4,'x'=2,'y'=2,'c'=2] {'z'}, dimensions={0}, use_global_device_ids=true | all-gather | bytes 1228800 | tf_op jit(solution)/shard_map/all_gather | solution.py:68
  34.9 3.5 pad_rows.2
  38.4 4.3 prepare_rest.1
  44.3 23.2 %all-gather.4.cloned.1.call-done = bf16[512,1280]{1,0:T(8,128)(2,1)} async-done(((bf16[128,1280]{1,0:T(8,128)(2,1)}), bf16[512,1280]{1,0:T(8,128)(2,1)}) %all-gather.4.cloned.1.call-update) | async-done | bytes 1310736 | tf_op jit(solution)/shard_map/all_gather | solution.py:68
  72.2 3.5 pad_rows.3
  76.8 9.4 %project_first.1 = (bf16[2,640,1024]{2,1,0:T(8,128)(2,1)}, bf16[2,640,256]{2,1,0:T(8,128)(2,1)}, bf16[2,640,256]{2,1,0:T(8,128)(2,1)}, bf16[2,640,256]{2,1,0:T(8...) custom-call(s32[4]{0:T(128)} %pad_add_fusion.place_ref, ...), custom_call_target="tpu_custom_call" | custom-call | tf_op jit(solution)/shard_map/project_first/pallas_call | solution.py:151
  89.7 6.9 %attention.2 = (bf16[2,640,256]{2,1,0:T(8,128)(2,1)S(1)}, bf16[2,2,2,640,640]{4,3,2,1,0:T(8,128)(2,1)S(1)}) custom-call(s32[4]{0:T(128)S(1)} %copy-done.45, bf16[2,640,256]{2,1,0:T(8,128)(2,1)S(1)} %copy-done.21, bf16[2,640,256]{2,1,0:T(8,128)(2,1)S(1)} %copy-done.23, bf16[2,640,256]{2,1,0:T(8,128)(2,1)S(1)} %copy-done.25), custom_call_target="tpu_custom_call" | custom-call | tf_op jit(solution)/shard_map/attention/pallas_call | solution.py:151
  107.0 4.3 project_next.1
  111.3 7.5 %attention.3 = (bf16[2,640,256]{2,1,0:T(8,128)(2,1)}, bf16[2,2,2,640,640]{4,3,2,1,0:T(8,128)(2,1)S(1)}) custom-call(s32[4]{0:T(128)S(1)} %copy-done.45, bf16[2,640,256]{2,1,0:T(8,128)(2,1)S(1)} %get-tuple-element.233.q_ref, bf16[2,640,256]{2,1,0:T(8,128)(2,1)S(1)} %get-tuple-element.234.k_ref, bf16[2,640,256]{2,1,0:T(8,128)(2,1)S(1)} %get-tuple-element.235.v_ref), custom_call_target="tpu_custom_call" | custom-call | tf_op jit(solution)/shard_map/attention/pallas_call | solution.py:151
  130.3 9.8 %project_out.1 = (f32[640,1024]{1,0:T(8,128)}, bf16[2,640,1024]{2,1,0:T(8,128)(2,1)}) custom-call(s32[4]{0:T(128)} %pad_add_fusion.place_ref, bf16[2,640,256]{2,1,0:T(8,128)(2,1)} %copy-done.27, bf16[2,640,256]{2,1,0:T(8,128)(2,1)} %get-tuple-element.236.refs_1_.refs_3_, bf16[2,640,256]{2,1,0:T(8,128)(2,1)} %collective-permute-done.7.refs_2_.refs_4_, ...), custom_call_target="tpu_custom_call" | custom-call | tf_op jit(solution)/shard_map/project_out/pallas_call | solution.py:151
  140.0 11.3 %collective-permute-done.5.refs_5_ = bf16[4,128,1024]{2,1,0:T(8,128)(2,1)} collective-permute-done((bf16[4,128,1024]{2,1,0:T(8,128)(2,1)}, bf16[4,128,1024]{2,1,0:T(8,128)(2,1)}, u32[]{:S(2)}, u32[]{:S(2)}) %collective-permute-start.5) | collective-permute-done | bytes 1048608 | tf_op jit(solution)/shard_map/ppermute | solution.py:41
  154.1 32.1 %feed_forward.2 = (f32[640,1024]{1,0:T(8,128)}, f32[640,1024]{1,0:T(8,128)}, f32[640,1024]{1,0:T(8,128)}, f32[640,1024]{1,0:T(8,128)}, f32[1,1024]{1,0:T(1,128)}...) custom-call(s32[4]{0:T(128)} %pad_add_fusion.place_ref, ...), custom_call_target="tpu_custom_call" | custom-call | tf_op jit(solution)/shard_map/feed_forward/pallas_call | solution.py:151
  188.3 9.2 %collective-permute-done.16.refs_6_ = bf16[4,128,1024]{2,1,0:T(8,128)(2,1)} collective-permute-done((bf16[4,128,1024]{2,1,0:T(8,128)(2,1)}, bf16[4,128,1024]{2,1,0:T(8,128)(2,1)}, u32[]{:S(2)}, u32[]{:S(2)}) %collective-permute-start.16) | collective-permute-done | bytes 1048608 | tf_op jit(solution)/shard_map/ppermute | solution.py:41
  197.5 34.9 %feed_forward.3 = (f32[640,1024]{1,0:T(8,128)}, bf16[640,512]{1,0:T(8,128)(2,1)}, bf16[640,512]{1,0:T(8,128)(2,1)}, f32[640,1024]{1,0:T(8,128)}, bf16[640,512]{1...) custom-call(s32[4]{0:T(128)} %pad_add_fusion.place_ref, ...), custom_call_target="tpu_custom_call" | custom-call | tf_op jit(solution)/shard_map/feed_forward/pallas_call | solution.py:151
  248.9 4.4 %norm_back.2 = (f32[8,1024]{1,0:T(8,128)S(1)}, bf16[577,1024]{1,0:T(8,128)(2,1)}, f32[640,1024]{1,0:T(8,128)S(1)}, bf16[640,1024]{1,0:T(8,128)(2,1)S(1)}, bf16[6...) custom-call(s32[4]{0:T(128)S(1)} %copy-done.46, f32[640,1024]{1,0:T(8,128)S(1)} %copy-done.32, ...), custom_call_target="tpu_custom_call" | custom-call | tf_op jit(solution)/shard_map/norm_back/pallas_call | solution.py:151
  257.9 6.9 %out_back.1 = (bf16[2,640,256]{2,1,0:T(8,128)(2,1)S(1)}, bf16[2,640,256]{2,1,0:T(8,128)(2,1)S(1)}, bf16[4,128,512]{2,1,0:T(8,128)(2,1)S(1)}, bf16[4,128,512]{2,1,0:T(8,128)(2,1)S(1)}) custom-call(s32[4]{0:T(128)S(1)} %copy-done.46, bf16[640,1024]{1,0:T(8,128)(2,1)S(1)} %get-tuple-element.275.own_ref.own_half, ...), custom_call_target="tpu_custom_call" | custom-call | tf_op jit(solution)/shard_map/out_back/pallas_call | solution.py:151
  264.8 3.4 copy-done.8
  268.3 10.8 %attention_back.2 = (bf16[2,640,256]{2,1,0:T(8,128)(2,1)S(1)}, bf16[2,640,256]{2,1,0:T(8,128)(2,1)S(1)}, bf16[2,640,256]{2,1,0:T(8,128)(2,1)S(1)}) custom-call(s32[4]{0:T(128)S(1)} %copy-done.46, bf16[2,640,256]{2,1,0:T(8,128)(2,1)S(1)} %copy-done.22, bf16[2,640,256]{2,1,0:T(8,128)(2,1)S(1)} %copy-done.24, bf16[2,640,256]{2,1,0:T(8,128)(2,1)S(1)} %copy-done.26, ...), custom_call_target="tpu_custom_call" | custom-call | tf_op jit(solution)/shard_map/attention_back/pallas_call | solution.py:151
  279.2 3.5 qkv_term.2
  282.7 3.7 collective-permute-done.22
  292.4 3.3 copy-done.6
  300.0 11.0 %attention_back.3 = (bf16[2,640,256]{2,1,0:T(8,128)(2,1)S(1)}, bf16[2,640,256]{2,1,0:T(8,128)(2,1)S(1)}, bf16[2,640,256]{2,1,0:T(8,128)(2,1)S(1)}) custom-call(s32[4]{0:T(128)S(1)} %copy-done.46, bf16[2,640,256]{2,1,0:T(8,128)(2,1)S(1)} %copy-done.16, bf16[2,640,256]{2,1,0:T(8,128)(2,1)S(1)} %copy-done.18, bf16[2,640,256]{2,1,0:T(8,128)(2,1)S(1)} %copy-done.20, ...), custom_call_target="tpu_custom_call" | custom-call | tf_op jit(solution)/shard_map/attention_back/pallas_call | solution.py:151
  311.1 4.3 qkv_term.3
  323.2 11.5 %qkv_back.1 = (f32[640,1024]{1,0:T(8,128)}, bf16[640,512]{1,0:T(8,128)(2,1)}, bf16[640,512]{1,0:T(8,128)(2,1)}) custom-call(s32[4]{0:T(128)} %pad_add_fusion.place_ref, bf16[2,640,256]{2,1,0:T(8,128)(2,1)} %copy-done.9, bf16[2,640,256]{2,1,0:T(8,128)(2,1)} %copy-done.10, bf16[2,640,256]{2,1,0:T(8,128)(2,1)} %copy-done.11, bf16[2,640,256]{2,1,0:T(8,128)(2,1)} %copy-done.12, ...), custom_call_target="tpu_custom_call" | custom-call | tf_op jit(solution)/shard_map/qkv_back/pallas_call | solution.py:151
  341.6 4.3 norm_back.3
  357.6 7.7 %statistics.2 = (f32[128,4096]{1,0:T(8,128)}, f32[512,1024]{1,0:T(8,128)}, f32[1,128]{1,0:T(1,128)}, f32[1,512]{1,0:T(1,128)}, f32[2,5376]{1,0:T(2,128)}) custom-call(s32[4]{0:T(128)} %pad_add_fusion.place_ref, bf16[256,1024]{1,0:T(8,128)(2,1)} %reduce-scatter.7.cloned.1.call-done.refs_0_, bf16[256,1024]{1,0:T(8,128)(2,1)} %copy-done.60, ...), custom_call_target="tpu_custom_call" | custom-call | tf_op jit(solution)/shard_map/statistics/pallas_call | solution.py:151
  391.3 3.3 reduce-scatter.9.cloned.1.call-done.refs_4_
  396.8 7.0 %update.2 = (f32[128,4096]{1,0:T(8,128)}, f32[512,1024]{1,0:T(8,128)}, f32[1,4096]{1,0:T(1,128)}, f32[1,1024]{1,0:T(1,128)}, f32[8,128]{1,0:T(8,128)}) custom-call(s32[4]{0:T(128)} %pad_add_fusion.place_ref, f32[128,4096]{1,0:T(8,128)} %get-tuple-element.175.refs_0_, f32[512,1024]{1,0:T(8,128)} %get-tuple-element.177.refs_1_, ...), custom_call_target="tpu_custom_call" | custom-call | tf_op jit(solution)/shard_map/update/pallas_call | solution.py:151
  406.9 4.9 %statistics.3 = (f32[128,1024]{1,0:T(8,128)}, f32[128,3072]{1,0:T(8,128)}, f32[1,128]{1,0:T(1,128)}, f32[1,128]{1,0:T(1,128)}, f32[2,5376]{1,0:T(2,128)}, /*inde...) custom-call(s32[4]{0:T(128)} %pad_add_fusion.place_ref, ...), custom_call_target="tpu_custom_call" | custom-call | tf_op jit(solution)/shard_map/statistics/pallas_call | solution.py:151
  416.1 3.7 collective-permute-done.53
  426.1 5.0 %update.3 = (f32[128,1024]{1,0:T(8,128)}, f32[128,3072]{1,0:T(8,128)}, f32[1,1024]{1,0:T(1,128)}, f32[1,3072]{1,0:T(1,128)}, f32[1,12]{1,0:T(1,128)}, /*index=5*...) custom-call(s32[4]{0:T(128)} %pad_add_fusion.place_ref, ...), custom_call_target="tpu_custom_call" | custom-call | tf_op jit(solution)/shard_map/update/pallas_call | solution.py:151
  (285 shorter events, 137.4 us)
Async XLA Ops:
  7.2 60.3 %all-gather.4.cloned.1.call-start = ((), (), s32[]{:S(2)}) async-start(), calls=%async_computation.4 | async-start | bytes 1638400 | tf_op jit(solution)/shard_map/all_gather | solution.py:68
  34.8 64.5 %all-gather.8.cloned.1.call-start = ((), (), s32[]{:S(2)}) async-start(), calls=%async_computation.6 | async-start | bytes 1310720 | tf_op jit(solution)/shard_map/all_gather | solution.py:68
  42.7 83.5 %all-gather.6.cloned.1.call-start = ((), (), s32[]{:S(2)}) async-start(), calls=%async_computation.5 | async-start | bytes 1310720 | tf_op jit(solution)/shard_map/all_gather | solution.py:68
  42.8 33.0 %collective-permute-start.2 = (bf16[4,160,768]{2,1,0:T(8,128)(2,1)S(1)}, bf16[4,160,768]{2,1,0:T(8,128)(2,1)S(1)}, u32[]{:S(2)}, u32[]{:S(2)}) collective-permute-start(bf16[4,160,768]{2,1,0:T(8,128)(2,1)S(1)} %bitcast.74), channel_id=1, source_target_pairs={{0,4},{4,0},{1,5},{5,1},{2,6},{6,2},{3,7},{7,3},{8,12},{12,8},{9,1... | collective-permute-start | bytes 2949128 | tf_op jit(solution)/shard_map/ppermute | solution.py:41
  67.5 31.8 %collective-permute-start.3 = (bf16[4,128,1280]{2,1,0:T(8,128)(2,1)}, bf16[4,128,1280]{2,1,0:T(8,128)(2,1)}, u32[]{:S(2)}, u32[]{:S(2)}) collective-permute-start(bf16[4,128,1280]{2,1,0:T(8,128)(2,1)} %bitcast.70), channel_id=1, source_target_pairs={{0,4},{4,0},{1,5},{5,1},{2,6},{6,2},{3,7},{7,3},{8,12},{12,8},{9,1... | collective-permute-start | bytes 3932168 | tf_op jit(solution)/shard_map/ppermute | solution.py:41
  86.2 203.9 %reduce-scatter.7.cloned.1.call-start = ((), (), s32[]{:S(2)}) async-start(), calls=%async_computation.8 | async-start | bytes 2621440 | tf_op jit(solution)/shard_map/reduce_scatter | solution.py:96
  99.4 25.6 %collective-permute-start.4 = (bf16[4,128,1024]{2,1,0:T(8,128)(2,1)}, bf16[4,128,1024]{2,1,0:T(8,128)(2,1)}, u32[]{:S(2)}, u32[]{:S(2)}) collective-permute-start(bf16[4,128,1024]{2,1,0:T(8,128)(2,1)} %bitcast.82), channel_id=1, source_target_pairs={{0,4},{4,0},{1,5},{5,1},{2,6},{6,2},{3,7},{7,3},{8,12},{12,8},{9,1... | collective-permute-start | bytes 3145736 | tf_op jit(solution)/shard_map/ppermute | solution.py:41
  100.1 29.1 %collective-permute-start.6 = (bf16[4,128,1024]{2,1,0:T(8,128)(2,1)}, bf16[4,128,1024]{2,1,0:T(8,128)(2,1)}, u32[]{:S(2)}, u32[]{:S(2)}) collective-permute-start(bf16[4,128,1024]{2,1,0:T(8,128)(2,1)} %bitcast.83), channel_id=1, source_target_pairs={{0,2},{2,0},{1,3},{3,1},{4,6},{6,4},{5,7},{7,5},{8,10},{10,8},{9,1... | collective-permute-start | bytes 3145736 | tf_op jit(solution)/shard_map/ppermute | solution.py:41
  101.5 26.2 %collective-permute-start.7 = (bf16[2,640,256]{2,1,0:T(8,128)(2,1)S(1)}, bf16[2,640,256]{2,1,0:T(8,128)(2,1)}, u32[]{:S(2)}, u32[]{:S(2)}) collective-permute-start(bf16[2,640,256]{2,1,0:T(8,128)(2,1)S(1)} %get-tuple-element.227.refs_0_.refs_2_), channel_id=1, source_target_pairs={{0,1},{1,0},{2,3},{3,2},{4,5},{5,4},{6,7},{7,6},{8,9},{9,8},{10,11... | collective-permute-start | bytes 1966088 | tf_op jit(solution)/shard_map/ppermute | solution.py:41
  126.2 25.1 %collective-permute-start.5 = (bf16[4,128,1024]{2,1,0:T(8,128)(2,1)}, bf16[4,128,1024]{2,1,0:T(8,128)(2,1)}, u32[]{:S(2)}, u32[]{:S(2)}) collective-permute-start(bf16[4,128,1024]{2,1,0:T(8,128)(2,1)} %bitcast.85), channel_id=1, source_target_pairs={{0,4},{4,0},{1,5},{5,1},{2,6},{6,2},{3,7},{7,3},{8,12},{12,8},{9,1... | collective-permute-start | bytes 3145736 | tf_op jit(solution)/shard_map/ppermute | solution.py:41
  127.7 26.4 %collective-permute-start.12 = (bf16[4,128,1024]{2,1,0:T(8,128)(2,1)}, bf16[4,128,1024]{2,1,0:T(8,128)(2,1)}, u32[]{:S(2)}, u32[]{:S(2)}) collective-permute-start(bf16[4,128,1024]{2,1,0:T(8,128)(2,1)} %collective-permute-done.4.refs_5_), channel_id=1, source_target_pairs={{0,2},{2,0},{1,3},{3,1},{4,6},{6,4},{5,7},{7,5},{8,10},{10,8},{9,1... | collective-permute-start | bytes 3145736 | tf_op jit(solution)/shard_map/ppermute | solution.py:41
  129.2 23.6 %collective-permute-start.10 = (bf16[640,512]{1,0:T(8,128)(2,1)}, bf16[640,512]{1,0:T(8,128)(2,1)S(1)}, u32[]{:S(2)}, u32[]{:S(2)}) collective-permute-start(bf16[640,512]{1,0:T(8,128)(2,1)} %get-tuple-element.245), channel_id=1, source_target_pairs={{0,1},{1,0},{2,3},{3,2},{4,5},{5,4},{6,7},{7,6},{8,9},{9,8},{10,11... | collective-permute-start | bytes 1966088 | tf_op jit(solution)/shard_map/ppermute | solution.py:41
  129.2 23.6 %collective-permute-start.11 = (bf16[640,512]{1,0:T(8,128)(2,1)}, bf16[640,512]{1,0:T(8,128)(2,1)}, u32[]{:S(2)}, u32[]{:S(2)}) collective-permute-start(bf16[640,512]{1,0:T(8,128)(2,1)} %get-tuple-element.246), channel_id=1, source_target_pairs={{0,1},{1,0},{2,3},{3,2},{4,5},{5,4},{6,7},{7,6},{8,9},{9,8},{10,11... | collective-permute-start | bytes 1966088 | tf_op jit(solution)/shard_map/ppermute | solution.py:41
  129.7 58.6 %collective-permute-start.15 = (bf16[4,128,1024]{2,1,0:T(8,128)(2,1)}, bf16[4,128,1024]{2,1,0:T(8,128)(2,1)}, u32[]{:S(2)}, u32[]{:S(2)}) collective-permute-start(bf16[4,128,1024]{2,1,0:T(8,128)(2,1)} %bitcast.86), channel_id=1, source_target_pairs={{0,2},{2,0},{1,3},{3,1},{4,6},{6,4},{5,7},{7,5},{8,10},{10,8},{9,1... | collective-permute-start | bytes 3145736 | tf_op jit(solution)/shard_map/ppermute | solution.py:41
  151.3 46.1 %collective-permute-start.16 = (bf16[4,128,1024]{2,1,0:T(8,128)(2,1)}, bf16[4,128,1024]{2,1,0:T(8,128)(2,1)}, u32[]{:S(2)}, u32[]{:S(2)}) collective-permute-start(bf16[4,128,1024]{2,1,0:T(8,128)(2,1)} %collective-permute-done.5.refs_5_), channel_id=1, source_target_pairs={{0,2},{2,0},{1,3},{3,1},{4,6},{6,4},{5,7},{7,5},{8,10},{10,8},{9,1... | collective-permute-start | bytes 3145736 | tf_op jit(solution)/shard_map/ppermute | solution.py:41
  186.2 46.2 %collective-permute-start.13 = (bf16[4,128,1024]{2,1,0:T(8,128)(2,1)}, bf16[4,128,1024]{2,1,0:T(8,128)(2,1)}, u32[]{:S(2)}, u32[]{:S(2)}) collective-permute-start(bf16[4,128,1024]{2,1,0:T(8,128)(2,1)} %get-tuple-element.249), channel_id=1, source_target_pairs={{0,4},{4,0},{1,5},{5,1},{2,6},{6,2},{3,7},{7,3},{8,12},{12,8},{9,1... | collective-permute-start | bytes 3145736 | tf_op jit(solution)/shard_map/ppermute | solution.py:41
  187.2 45.2 %collective-permute-start.14 = (bf16[4,128,1024]{2,1,0:T(8,128)(2,1)}, bf16[4,128,1024]{2,1,0:T(8,128)(2,1)}, u32[]{:S(2)}, u32[]{:S(2)}) collective-permute-start(bf16[4,128,1024]{2,1,0:T(8,128)(2,1)} %get-tuple-element.251), channel_id=1, source_target_pairs={{0,4},{4,0},{1,5},{5,1},{2,6},{6,2},{3,7},{7,3},{8,12},{12,8},{9,1... | collective-permute-start | bytes 3145736 | tf_op jit(solution)/shard_map/ppermute | solution.py:41
  237.1 98.2 %reduce-scatter.5.cloned.1.call-start = ((), (), s32[]{:S(2)}) async-start(), calls=%async_computation.7 | async-start | bytes 2621440 | tf_op jit(solution)/shard_map/reduce_scatter | solution.py:96
  238.2 44.5 %collective-permute-start.21 = (bf16[4,128,1024]{2,1,0:T(8,128)(2,1)}, bf16[4,128,1024]{2,1,0:T(8,128)(2,1)S(1)}, u32[]{:S(2)}, u32[]{:S(2)}) collective-permute-start(bf16[4,128,1024]{2,1,0:T(8,128)(2,1)} %get-tuple-element.271), channel_id=1, source_target_pairs={{0,4},{4,0},{1,5},{5,1},{2,6},{6,2},{3,7},{7,3},{8,12},{12,8},{9,1... | collective-permute-start | bytes 3145736 | tf_op jit(solution)/shard_map/ppermute | solution.py:41
  239.5 46.9 %collective-permute-start.22 = (bf16[4,128,1024]{2,1,0:T(8,128)(2,1)}, bf16[4,128,1024]{2,1,0:T(8,128)(2,1)S(1)}, u32[]{:S(2)}, u32[]{:S(2)}) collective-permute-start(bf16[4,128,1024]{2,1,0:T(8,128)(2,1)} %get-tuple-element.273), channel_id=1, source_target_pairs={{0,4},{4,0},{1,5},{5,1},{2,6},{6,2},{3,7},{7,3},{8,12},{12,8},{9,1... | collective-permute-start | bytes 3145736 | tf_op jit(solution)/shard_map/ppermute | solution.py:41
  288.8 79.4 %reduce-scatter.11.cloned.1.call-start = ((), (), s32[]{:S(2)}) async-start(), calls=%async_computation.10 | async-start | bytes 1638400 | tf_op jit(solution)/shard_map/reduce_scatter | solution.py:96
  288.8 30.4 %collective-permute-start.26 = (bf16[4,128,768]{2,1,0:T(8,128)(2,1)S(1)}, bf16[4,128,768]{2,1,0:T(8,128)(2,1)}, u32[]{:S(2)}, u32[]{:S(2)}) collective-permute-start(bf16[4,128,768]{2,1,0:T(8,128)(2,1)S(1)} %get-tuple-element.290), channel_id=1, source_target_pairs={{0,4},{4,0},{1,5},{5,1},{2,6},{6,2},{3,7},{7,3},{8,12},{12,8},{9,1... | collective-permute-start | bytes 2359304 | tf_op jit(solution)/shard_map/ppermute | solution.py:41
  290.1 21.0 %collective-permute-start.27 = (bf16[256,1024]{1,0:T(8,128)(2,1)}, bf16[256,1024]{1,0:T(8,128)(2,1)S(1)}, u32[]{:S(2)}, u32[]{:S(2)}) collective-permute-start(bf16[256,1024]{1,0:T(8,128)(2,1)} %reduce-scatter.7.cloned.1.call-done.refs_0_), channel_id=1, source_target_pairs={{0,2},{2,0},{1,3},{3,1},{4,6},{6,4},{5,7},{7,5},{8,10},{10,8},{9,1... | collective-permute-start | bytes 1572872 | tf_op jit(solution)/shard_map/ppermute | solution.py:41
  290.9 28.3 %collective-permute-start.25 = (bf16[4,128,512]{2,1,0:T(8,128)(2,1)}, bf16[4,128,512]{2,1,0:T(8,128)(2,1)S(1)}, u32[]{:S(2)}, u32[]{:S(2)}) collective-permute-start(bf16[4,128,512]{2,1,0:T(8,128)(2,1)} %copy-done.51), channel_id=1, source_target_pairs={{0,4},{4,0},{1,5},{5,1},{2,6},{6,2},{3,7},{7,3},{8,12},{12,8},{9,1... | collective-permute-start | bytes 1572872 | tf_op jit(solution)/shard_map/ppermute | solution.py:41
  321.9 72.7 %reduce-scatter.9.cloned.1.call-start = ((), (), s32[]{:S(2)}) async-start(), calls=%async_computation.9 | async-start | bytes 983040 | tf_op jit(solution)/shard_map/reduce_scatter | solution.py:96
  321.9 24.5 %collective-permute-start.30 = (bf16[4,128,768]{2,1,0:T(8,128)(2,1)}, bf16[4,128,768]{2,1,0:T(8,128)(2,1)S(1)}, u32[]{:S(2)}, u32[]{:S(2)}) collective-permute-start(bf16[4,128,768]{2,1,0:T(8,128)(2,1)} %get-tuple-element.315), channel_id=1, source_target_pairs={{0,4},{4,0},{1,5},{5,1},{2,6},{6,2},{3,7},{7,3},{8,12},{12,8},{9,1... | collective-permute-start | bytes 2359304 | tf_op jit(solution)/shard_map/ppermute | solution.py:41
  336.1 18.7 %collective-permute-start.31 = (bf16[256,1024]{1,0:T(8,128)(2,1)}, bf16[256,1024]{1,0:T(8,128)(2,1)}, u32[]{:S(2)}, u32[]{:S(2)}) collective-permute-start(bf16[256,1024]{1,0:T(8,128)(2,1)} %reduce-scatter.7.cloned.1.call-done.refs_0_), channel_id=1, source_target_pairs={{0,1},{1,0},{2,3},{3,2},{4,5},{5,4},{6,7},{7,6},{8,9},{9,8},{10,11... | collective-permute-start | bytes 1572872 | tf_op jit(solution)/shard_map/ppermute | solution.py:41
  337.1 17.8 %collective-permute-start.32 = (bf16[256,1024]{1,0:T(8,128)(2,1)}, bf16[256,1024]{1,0:T(8,128)(2,1)}, u32[]{:S(2)}, u32[]{:S(2)}) collective-permute-start(bf16[256,1024]{1,0:T(8,128)(2,1)} %copy-done.60), channel_id=1, source_target_pairs={{0,1},{1,0},{2,3},{3,2},{4,5},{5,4},{6,7},{7,6},{8,9},{9,8},{10,11... | collective-permute-start | bytes 1572872 | tf_op jit(solution)/shard_map/ppermute | solution.py:41
  352.3 17.4 %collective-permute-start.44 = (f32[8,1536]{1,0:T(8,128)S(1)}, f32[8,1536]{1,0:T(8,128)S(1)}, u32[]{:S(2)}, u32[]{:S(2)}) collective-permute-start(f32[8,1536]{1,0:T(8,128)S(1)} %add.82), channel_id=1, source_target_pairs={{0,24},{8,0},{16,8},{24,16},{1,25},{9,1},{17,9},{25,17},{2,26},{10... | collective-permute-start | bytes 147464 | tf_op jit(solution)/shard_map/ppermute | solution.py:46
  354.9 14.8 %collective-permute-start.43 = (f32[8,1536]{1,0:T(8,128)S(1)}, f32[8,1536]{1,0:T(8,128)S(1)}, u32[]{:S(2)}, u32[]{:S(2)}) collective-permute-start(f32[8,1536]{1,0:T(8,128)S(1)} %add.82), channel_id=1, source_target_pairs={{0,8},{8,16},{16,24},{24,0},{1,9},{9,17},{17,25},{25,1},{2,10},{10... | collective-permute-start | bytes 147464 | tf_op jit(solution)/shard_map/ppermute | solution.py:46
  379.4 15.1 %collective-permute-start.47 = (bf16[128,1280]{1,0:T(8,128)(2,1)}, bf16[128,1280]{1,0:T(8,128)(2,1)S(1)}, u32[]{:S(2)}, u32[]{:S(2)}) collective-permute-start(bf16[128,1280]{1,0:T(8,128)(2,1)} %reduce-scatter.11.cloned.1.call-done.refs_0_), channel_id=1, source_target_pairs={{0,1},{1,0},{2,3},{3,2},{4,5},{5,4},{6,7},{7,6},{8,9},{9,8},{10,11... | collective-permute-start | bytes 983048 | tf_op jit(solution)/shard_map/ppermute | solution.py:41
  379.4 15.1 %collective-permute-start.48 = (bf16[128,1280]{1,0:T(8,128)(2,1)S(1)}, bf16[128,1280]{1,0:T(8,128)(2,1)S(1)}, u32[]{:S(2)}, u32[]{:S(2)}) collective-permute-start(bf16[128,1280]{1,0:T(8,128)(2,1)S(1)} %collective-permute-done.40.refs_1_), channel_id=1, source_target_pairs={{0,1},{1,0},{2,3},{3,2},{4,5},{5,4},{6,7},{7,6},{8,9},{9,8},{10,11... | collective-permute-start | bytes 983048 | tf_op jit(solution)/shard_map/ppermute | solution.py:41
  (101 other events, 562.5 us)
Sparse Core Ops, SparseCore 0:
  34.9 32.5 all-gather.3
  69.7 26.9 all-gather.7
  98.8 27.3 all-gather.5
  237.2 42.8 reduce-scatter.6
  288.9 42.8 reduce-scatter.4
  334.5 33.6 reduce-scatter.10
  371.1 23.3 reduce-scatter.8

commit v8 on v7

--- a/solution.py
+++ b/solution.py
@@ -179,7 +179,7 @@
     return jnp.where(core == 0, first, second)
 
 
-def prepare_qkv(place, weight, out_weight, vectors):
+def prepare_qkv(place, weight, out_weight, vectors, cut):
     part, cols = weight.shape
     half = cols // 6
     heads = half // GROUPS
@@ -192,17 +192,26 @@
     def body(place_ref, weight_ref, out_ref, *refs):
         refs, groups = refs[: len(sizes)], refs[len(sizes) :]
         core = place_ref[2]
+
+        def of_y(rows):
+            if cut == 1:
+                return low(rows)
+            return low(select(place_ref[3], rows[: part // 2], rows[part // 2 :]))
+
         for number, ref in enumerate(groups):
             for slot in range(3):
                 at = 2 * slot * half + number * heads
-                ref[:part, slot * heads : (slot + 1) * heads] = low(
-                    select(
-                        core,
-                        weight_ref[:, at : at + heads],
-                        weight_ref[:, at + half : at + half + heads],
-                    )
+                cols_of = select(
+                    core,
+                    weight_ref[:, at : at + heads],
+                    weight_ref[:, at + half : at + half + heads],
                 )
-        groups[-1][:, width:] = low(select(core, out_ref[:, :out_half], out_ref[:, out_half:]))
+                lanes = slice(slot * heads, (slot + 1) * heads)
+                if number == GROUPS - 1:
+                    ref[:, lanes] = of_y(cols_of)
+                else:
+                    ref[:part, lanes] = low(cols_of)
+        groups[-1][:, width:] = of_y(select(core, out_ref[:, :out_half], out_ref[:, out_half:]))
         at = 0
         for ref, size in zip(refs, sizes):
             done = 0
@@ -217,7 +226,7 @@
             at += size
 
     shapes = [
-        (part + (tiles * TILE if g == 0 else 0), width + (out_half if g == GROUPS - 1 else 0))
+        (part + (tiles * TILE if g == 0 else 0), width) if g < GROUPS - 1 else (part // cut, width + out_half)
         for g in range(GROUPS)
     ]
     return call(
@@ -322,19 +331,25 @@
 GAIN_ONE, BIAS_ONE, BIAS_OUT, GAIN_TWO, BIAS_TWO, BIAS_DOWN, BIAS_QV = range(7)
 
 
-def weight_copies(place_ref, ins, weight, part, sem):
+def row_copies(place_ref, ins, to, part, lanes, sem):
+    cut = len(ins) // 2
+    rows = part // cut
     made = []
-    for dx, ref in enumerate(ins):
+    for number, ref in enumerate(ins):
+        dx, h = number // cut, number % cut
+        y = h + (1 - 2 * h) * place_ref[3] if cut == 2 else 0
         for z in range(ref.shape[0]):
-            row = pl.multiple_of(shard_number(place_ref, z, dx) * part, part)
+            row = pl.multiple_of(shard_number(place_ref, z, dx) * part + y * rows, rows)
             made.append(
                 pltpu.make_async_copy(
-                    ref.at[z, pl.ds(0, part), pl.ds(0, weight.shape[1])],
-                    weight.at[pl.ds(row, part), :],
-                    sem.at[len(made)],
+                    ref.at[z, pl.ds(0, rows), lanes], to.at[pl.ds(row, rows), :], sem.at[len(made)]
                 )
             )
     return made
+
+
+def weight_copies(place_ref, ins, weight, part, sem):
+    return row_copies(place_ref, ins, weight, part, pl.ds(0, weight.shape[1]), sem)
 
 
 def write_qkv(normed, weight, bias_q, bias_v, image, q_ref, k_ref, v_ref):
@@ -467,15 +482,16 @@
 
 
 def project_next(place, normed, vectors, pieces, group):
-    flat = [one for (one,) in pieces]
-    z_size, part, _ = flat[0].shape
+    flat = [one for side in pieces for one in side]
+    z_size = flat[0].shape[0]
     _, length, width = normed.shape
+    part = width // (2 * z_size)
     half = width // 2
     heads = half // GROUPS
     cols = 3 * heads
 
     def body(place_ref, normed_ref, vec_ref, *refs):
-        ins, (q_ref, k_ref, v_ref, weight, sem) = refs[:2], refs[2:]
+        ins, (q_ref, k_ref, v_ref, weight, sem) = refs[: len(flat)], refs[len(flat) :]
         copies = weight_copies(place_ref, ins, weight, part, sem)
         for copy in copies:
             copy.start()
@@ -495,32 +511,25 @@
         body,
         place,
         (normed, vectors, *flat),
-        [whole(normed.shape), whole(vectors.shape)] + [any_spec()] * 2,
+        [whole(normed.shape), whole(vectors.shape)] + [any_spec()] * len(flat),
         [sds((2, length, heads), jnp.bfloat16)] * 3,
         [whole((2, length, heads))] * 3,
-        [pltpu.VMEM((width, cols), jnp.bfloat16), pltpu.SemaphoreType.DMA((2 * z_size,))],
+        [pltpu.VMEM((width, cols), jnp.bfloat16), pltpu.SemaphoreType.DMA((len(flat) * z_size,))],
         "project_next",
     )
 
 
 def gather_out(place, pieces, first):
-    flat = [one for (one,) in pieces]
-    z_size, part, total = flat[0].shape
+    flat = [one for side in pieces for one in side]
+    z_size, rows, total = flat[0].shape
     half = total - first
+    part = rows * len(flat) // 2
 
     def body(place_ref, *refs):
-        ins, out_ref, sem = refs[:2], refs[2], refs[3]
-        copies = []
-        for dx, ref in enumerate(ins):
-            for z in range(z_size):
-                row = pl.multiple_of(shard_number(place_ref, z, dx) * part, part)
-                copy = pltpu.make_async_copy(
-                    ref.at[z, :, pl.ds(first, half)],
-                    out_ref.at[pl.ds(row, part), :],
-                    sem.at[len(copies)],
-                )
-                copy.start()
-                copies.append(copy)
+        ins, (out_ref, sem) = refs[: len(flat)], refs[len(flat) :]
+        copies = row_copies(place_ref, ins, out_ref, part, pl.ds(first, half), sem)
+        for copy in copies:
+            copy.start()
         for copy in copies:
             copy.wait()
 
@@ -529,10 +538,10 @@
         body,
         place,
         tuple(flat),
-        [any_spec()] * 2,
+        [any_spec()] * len(flat),
         [sds(shape, jnp.bfloat16)],
         [whole(shape)],
-        [pltpu.SemaphoreType.DMA((2 * z_size,))],
+        [pltpu.SemaphoreType.DMA((len(flat) * z_size,))],
         "gather_out",
     )[0]
 
@@ -998,11 +1007,12 @@
 
 
 def qkv_back(place, grads, pieces):
-    flat = [one for piece in pieces for (one,) in piece]
+    flat = [one for piece in pieces for side in piece for one in side]
+    counts = [sum(len(side) for side in piece) for piece in pieces]
     z_size, _, cols = flat[0].shape
     heads = cols // 3
     length = grads[0][0].shape[1]
-    part = flat[-1].shape[1]
+    part = flat[-1].shape[1] * counts[-1] // 2
     width = 2 * z_size * part
 
     def body(place_ref, *refs):
@@ -1010,8 +1020,9 @@
         ins, (own_ref, *other_refs, weight, sem) = refs[: len(flat)], refs[len(flat) :]
         copies = []
         for g in range(GROUPS):
+            at = sum(counts[:g])
             copies += weight_copies(
-                place_ref, ins[2 * g : 2 * g + 2], weight.at[g], part, sem.at[g]
+                place_ref, ins[at : at + counts[g]], weight.at[g], part, sem.at[g]
             )
         for copy in copies:
             copy.start()
@@ -1051,7 +1062,7 @@
         [whole((length, width))] + [whole((length, width // GIVEN))] * GIVEN,
         [
             pltpu.VMEM((GROUPS, width, cols), jnp.bfloat16),
-            pltpu.SemaphoreType.DMA((GROUPS, 2 * z_size)),
+            pltpu.SemaphoreType.DMA((GROUPS, max(counts) * z_size)),
         ],
         "qkv_back",
     )
@@ -1419,14 +1430,15 @@
     moments = [as_row(moment) for moment in moments]
     sizes = [param.shape[1] for param in params]
 
-    shard_first, shard_next = prepare_qkv(place, qkv_weight, out_weight, params)
+    cut = 2 if by_y else 1
+    shard_first, shard_next = prepare_qkv(place, qkv_weight, out_weight, params, cut)
     near = along_z(shard_first)
     pieces_first = by_x(near)
     near_next = along_z(after(shard_next, near))
     rows_own, parts = pad_rows(after(place, near), inputs)
     rows = (rows_own, [swap(one, "c") for one in parts])
     *shards_ff, down_sums = prepare_rest(
-        after(place, rows_own), in_weight, down_weight, cotangent, (2 if by_y else 1,) * 2
+        after(place, rows_own), in_weight, down_weight, cotangent, (cut,) * 2
     )
     cot_own, parts = pad_rows(after(place, (down_sums, rows[1])), cotangent)
     near_ff = [along_z(shards_ff[0])]
@@ -1437,8 +1449,9 @@
     near_ff.append(along_z(after(shards_ff[1], normed)))
     cot = (cot_own, [swap(one, "c") for one in after(parts, normed)])
     qkv = [first]
-    pieces_next = by_x(near_next)
-    mixed, prob = attention(place, *first)
+    across_next = after(swap(near_next, "x"), normed)
+    pieces_next = by_y_too([[near_next], [across_next]], by_y)
+    mixed, prob = attention(after(place, across_next), *first)
     attended = [mixed]
     probs = [prob]
     theirs = [swap(mixed, "c")]

time: 444 us -> 437 us (0.984)
  waiting for transfers between devices: 96.6 us -> 69.9 us
  blocking collectives: 23.7 us -> 46.2 us
    all_gather x3 -> x2, waiting for transfers between devices: 24.5 us -> 0.02 us  [along_z(): near = lax.all_gather(shard, 'z', axis=0, tiled=True)]
    all_gather x1 -> x2, blocking collectives: 23.7 us -> 46.2 us  [along_z(): near = lax.all_gather(shard, 'z', axis=0, tiled=True)]
    unnamed x140 -> x134, local copies, waits for them, and re-layouts: 38.1 us -> 33.9 us
    ppermute x41 -> x43, waiting for transfers between devices: 44.1 us -> 41.1 us  [swap(): return lax.ppermute(value, axis, [(0, 1), (1, 0)])]
    ppermute x41 -> x43, starting transfers between devices: 28.1 us -> 29 us  [swap(): return lax.ppermute(value, axis, [(0, 1), (1, 0)])]
  transfers between devices with their start and end apart: 63 -> 64, of which waited for: 31 -> 26; matrix products, arithmetic and copies ran while one was open for 2% -> 2% of each run, Pallas kernels for 44% -> 42%
where the time goes in v8:
time: 437 us; the launch traced here: 432 us
  Pallas kernels  204 us (47%)
  waiting for transfers between devices  69.9 us (16%)
  starting transfers between devices  46.5 us (11%)
  blocking collectives  46.2 us (11%)
  local copies, waits for them, and re-layouts  33.9 us (8%)
  other arithmetic  16 us (4%)
  between operations  15.3 us (4%)
    pallas_call x25, Pallas kernels, call(): pl.pallas_call(body, out_shape=outs, grid_spec=pltpu.PrefetchScalarGridSp...  204 us
    all_gather x2, blocking collectives, along_z(): near = lax.all_gather(shard, 'z', axis=0, tiled=True)  46.2 us
    ppermute x43, waiting for transfers between devices, swap(): return lax.ppermute(value, axis, [(0, 1), (1, 0)])  41.1 us
    unnamed x134, local copies, waits for them, and re-layouts  33.9 us
    ppermute x43, starting transfers between devices, swap(): return lax.ppermute(value, axis, [(0, 1), (1, 0)])  29 us
    ppermute x9, starting transfers between devices, shift(): lax.ppermute(value, axis, [(i, (i + step) % size) for i in range(size)])  11.4 us
    ppermute x9, waiting for transfers between devices, shift(): lax.ppermute(value, axis, [(i, (i + step) % size) for i in range(size)])  11 us
    ppermute x5, waiting for transfers between devices, partner(): return lax.ppermute(value, axis, [(i, i ^ step) for i in range(size)])  10.7 us
  transfers between devices with their start and end apart: 64, of which 26 were waited for; matrix products, arithmetic and copies ran while one was open for 2% of the time, Pallas kernels for 42%

profile of v8, /device:TPU:0, one launch (start us, length us, event | category | flops | bytes accessed | tf_op | source)
XLA Modules:
  0.0 431.6 jit_solution(13848162008182971828)
XLA Ops:
  11.1 23.7 %all_gather.12 = bf16[640,768]{1,0:T(8,128)(2,1)S(1)} all-gather(bf16[160,768]{1,0:T(8,128)(2,1)} %get-tuple-element.212), channel_id=1, replica_groups=mesh['z'=4,'x'=2,'y'=2,'c'=2] {'z'}, dimensions={0}, use_global_device_ids=true | all-gather | bytes 1228800 | tf_op jit(solution)/shard_map/all_gather | solution.py:68
  34.8 3.5 pad_rows.2
  38.3 4.4 %prepare_rest.1 = (bf16[128,1024]{1,0:T(8,128)(2,1)}, bf16[128,1024]{1,0:T(8,128)(2,1)}, f32[1,1024]{1,0:T(1,128)}) custom-call(s32[4]{0:T(128)} %pad_add_fusion.place_ref, f32[128,4096]{1,0:T(8,128)} %refs_4_.2, f32[512,1024]{1,0:T(8,128)} %refs_5_.2, bf16[577,1024]{1,0:T(8,128)(2,1)} %ref.3), custom_call_target="tpu_custom_call" | custom-call | tf_op jit(solution)/shard_map/prepare_rest/pallas_call | solution.py:151
  44.9 22.5 %all_gather.13 = bf16[256,1280]{1,0:T(8,128)(2,1)S(1)} all-gather(bf16[64,1280]{1,0:T(8,128)(2,1)S(1)} %copy-done.65), channel_id=1, replica_groups=mesh['z'=4,'x'=2,'y'=2,'c'=2] {'z'}, dimensions={0}, use_global_device_ids=true | all-gather | bytes 819200 | tf_op jit(solution)/shard_map/all_gather | solution.py:68
  69.3 3.5 pad_rows.3
  73.8 9.4 %project_first.1 = (bf16[2,640,1024]{2,1,0:T(8,128)(2,1)}, bf16[2,640,256]{2,1,0:T(8,128)(2,1)}, bf16[2,640,256]{2,1,0:T(8,128)(2,1)}, bf16[2,640,256]{2,1,0:T(8...) custom-call(s32[4]{0:T(128)} %pad_add_fusion.place_ref, ...), custom_call_target="tpu_custom_call" | custom-call | tf_op jit(solution)/shard_map/project_first/pallas_call | solution.py:151
  87.3 6.9 %attention.2 = (bf16[2,640,256]{2,1,0:T(8,128)(2,1)S(1)}, bf16[2,2,2,640,640]{4,3,2,1,0:T(8,128)(2,1)S(1)}) custom-call(s32[4]{0:T(128)S(1)} %copy-done.42, bf16[2,640,256]{2,1,0:T(8,128)(2,1)S(1)} %copy-done.20, bf16[2,640,256]{2,1,0:T(8,128)(2,1)S(1)} %copy-done.22, bf16[2,640,256]{2,1,0:T(8,128)(2,1)S(1)} %copy-done.24), custom_call_target="tpu_custom_call" | custom-call | tf_op jit(solution)/shard_map/attention/pallas_call | solution.py:151
  103.9 4.5 %project_next.1 = (bf16[2,640,256]{2,1,0:T(8,128)(2,1)S(1)}, bf16[2,640,256]{2,1,0:T(8,128)(2,1)S(1)}, bf16[2,640,256]{2,1,0:T(8,128)(2,1)S(1)}) custom-call(s32[4]{0:T(128)S(1)} %copy-done.42, bf16[2,640,1024]{2,1,0:T(8,128)(2,1)S(1)} %copy-done, f32[8,1024]{1,0:T(8,128)S(1)} %copy-done.38, bf16[4,64,1280]{2,1,0:T(8,128)(2,1)S(1)} %bitcast.73, ...), custom_call_target="tpu_custom_call" | custom-call | tf_op jit(solution)/shard_map/project_next/pallas_call | solution.py:151
  108.4 6.9 %attention.3 = (bf16[2,640,256]{2,1,0:T(8,128)(2,1)S(1)}, bf16[2,2,2,640,640]{4,3,2,1,0:T(8,128)(2,1)S(1)}) custom-call(s32[4]{0:T(128)S(1)} %copy-done.42, bf16[2,640,256]{2,1,0:T(8,128)(2,1)S(1)} %get-tuple-element.241.q_ref, bf16[2,640,256]{2,1,0:T(8,128)(2,1)S(1)} %get-tuple-element.242.k_ref, bf16[2,640,256]{2,1,0:T(8,128)(2,1)S(1)} %get-tuple-element.243.v_ref), custom_call_target="tpu_custom_call" | custom-call | tf_op jit(solution)/shard_map/attention/pallas_call | solution.py:151
  123.6 9.8 %project_out.1 = (f32[640,1024]{1,0:T(8,128)}, bf16[2,640,1024]{2,1,0:T(8,128)(2,1)}) custom-call(s32[4]{0:T(128)} %pad_add_fusion.place_ref, bf16[2,640,256]{2,1,0:T(8,128)(2,1)} %copy-done.26, bf16[2,640,256]{2,1,0:T(8,128)(2,1)} %copy-done.28, bf16[2,640,256]{2,1,0:T(8,128)(2,1)} %collective-permute-done.9.refs_2_.refs_4_, ...), custom_call_target="tpu_custom_call" | custom-call | tf_op jit(solution)/shard_map/project_out/pallas_call | solution.py:151
  133.4 11.2 %collective-permute-done.7.refs_5_ = bf16[4,128,1024]{2,1,0:T(8,128)(2,1)} collective-permute-done((bf16[4,128,1024]{2,1,0:T(8,128)(2,1)}, bf16[4,128,1024]{2,1,0:T(8,128)(2,1)}, u32[]{:S(2)}, u32[]{:S(2)}) %collective-permute-start.7) | collective-permute-done | bytes 1048608 | tf_op jit(solution)/shard_map/ppermute | solution.py:41
  147.4 32.0 %feed_forward.2 = (f32[640,1024]{1,0:T(8,128)}, f32[640,1024]{1,0:T(8,128)}, f32[640,1024]{1,0:T(8,128)}, f32[640,1024]{1,0:T(8,128)}, f32[1,1024]{1,0:T(1,128)}...) custom-call(s32[4]{0:T(128)} %pad_add_fusion.place_ref, ...), custom_call_target="tpu_custom_call" | custom-call | tf_op jit(solution)/shard_map/feed_forward/pallas_call | solution.py:151
  181.6 8.0 %collective-permute-done.18.refs_6_ = bf16[4,128,1024]{2,1,0:T(8,128)(2,1)} collective-permute-done((bf16[4,128,1024]{2,1,0:T(8,128)(2,1)}, bf16[4,128,1024]{2,1,0:T(8,128)(2,1)}, u32[]{:S(2)}, u32[]{:S(2)}) %collective-permute-start.18) | collective-permute-done | bytes 1048608 | tf_op jit(solution)/shard_map/ppermute | solution.py:41
  189.6 34.9 %feed_forward.3 = (f32[640,1024]{1,0:T(8,128)}, bf16[640,512]{1,0:T(8,128)(2,1)}, bf16[640,512]{1,0:T(8,128)(2,1)}, f32[640,1024]{1,0:T(8,128)}, bf16[640,512]{1...) custom-call(s32[4]{0:T(128)} %pad_add_fusion.place_ref, ...), custom_call_target="tpu_custom_call" | custom-call | tf_op jit(solution)/shard_map/feed_forward/pallas_call | solution.py:151
  241.1 4.4 %norm_back.2 = (f32[8,1024]{1,0:T(8,128)S(1)}, bf16[577,1024]{1,0:T(8,128)(2,1)}, f32[640,1024]{1,0:T(8,128)S(1)}, bf16[640,1024]{1,0:T(8,128)(2,1)S(1)}, bf16[6...) custom-call(s32[4]{0:T(128)S(1)} %copy-done.43, f32[640,1024]{1,0:T(8,128)S(1)} %copy-done.33, ...), custom_call_target="tpu_custom_call" | custom-call | tf_op jit(solution)/shard_map/norm_back/pallas_call | solution.py:151
  250.1 6.7 %out_back.1 = (bf16[2,640,256]{2,1,0:T(8,128)(2,1)S(1)}, bf16[2,640,256]{2,1,0:T(8,128)(2,1)S(1)}, bf16[4,128,512]{2,1,0:T(8,128)(2,1)S(1)}, bf16[4,128,512]{2,1,0:T(8,128)(2,1)S(1)}) custom-call(s32[4]{0:T(128)S(1)} %copy-done.43, bf16[640,1024]{1,0:T(8,128)(2,1)S(1)} %get-tuple-element.283.own_ref.own_half, ...), custom_call_target="tpu_custom_call" | custom-call | tf_op jit(solution)/shard_map/out_back/pallas_call | solution.py:151
  260.1 10.8 %attention_back.2 = (bf16[2,640,256]{2,1,0:T(8,128)(2,1)S(1)}, bf16[2,640,256]{2,1,0:T(8,128)(2,1)S(1)}, bf16[2,640,256]{2,1,0:T(8,128)(2,1)S(1)}) custom-call(s32[4]{0:T(128)S(1)} %copy-done.43, bf16[2,640,256]{2,1,0:T(8,128)(2,1)S(1)} %copy-done.21, bf16[2,640,256]{2,1,0:T(8,128)(2,1)S(1)} %copy-done.23, bf16[2,640,256]{2,1,0:T(8,128)(2,1)S(1)} %copy-done.25, ...), custom_call_target="tpu_custom_call" | custom-call | tf_op jit(solution)/shard_map/attention_back/pallas_call | solution.py:151
  271.0 3.5 qkv_term.2
  274.5 4.0 collective-permute-done.24
  290.0 11.0 %attention_back.3 = (bf16[2,640,256]{2,1,0:T(8,128)(2,1)S(1)}, bf16[2,640,256]{2,1,0:T(8,128)(2,1)S(1)}, bf16[2,640,256]{2,1,0:T(8,128)(2,1)S(1)}) custom-call(s32[4]{0:T(128)S(1)} %copy-done.43, bf16[2,640,256]{2,1,0:T(8,128)(2,1)S(1)} %copy-done.15, bf16[2,640,256]{2,1,0:T(8,128)(2,1)S(1)} %copy-done.17, bf16[2,640,256]{2,1,0:T(8,128)(2,1)S(1)} %copy-done.19, ...), custom_call_target="tpu_custom_call" | custom-call | tf_op jit(solution)/shard_map/attention_back/pallas_call | solution.py:151
  301.1 4.3 %qkv_term.3 = (f32[3,256]{1,0:T(4,128)S(1)}, bf16[4,128,768]{2,1,0:T(8,128)(2,1)S(1)}, bf16[4,128,768]{2,1,0:T(8,128)(2,1)}) custom-call(s32[4]{0:T(128)S(1)} %copy-done.43, bf16[2,640,1024]{2,1,0:T(8,128)(2,1)S(1)} %copy-done, bf16[2,640,256]{2,1,0:T(8,128)(2,1)S(1)} %get-tuple-element.303.gq_ref.refs_3_, ...), custom_call_target="tpu_custom_call" | custom-call | tf_op jit(solution)/shard_map/qkv_term/pallas_call | solution.py:151
  305.5 6.1 %collective-permute-done.27 = bf16[4,128,512]{2,1,0:T(8,128)(2,1)S(1)} collective-permute-done((bf16[4,128,512]{2,1,0:T(8,128)(2,1)}, bf16[4,128,512]{2,1,0:T(8,128)(2,1)S(1)}, u32[]{:S(2)}, u32[]{:S(2)}) %collective-permute-start.27) | collective-permute-done | bytes 524320 | tf_op jit(solution)/shard_map/ppermute | solution.py:41
  316.0 11.7 %qkv_back.1 = (f32[640,1024]{1,0:T(8,128)}, bf16[640,512]{1,0:T(8,128)(2,1)}, bf16[640,512]{1,0:T(8,128)(2,1)}) custom-call(s32[4]{0:T(128)} %pad_add_fusion.place_ref, bf16[2,640,256]{2,1,0:T(8,128)(2,1)} %copy-done.8, bf16[2,640,256]{2,1,0:T(8,128)(2,1)} %copy-done.9, bf16[2,640,256]{2,1,0:T(8,128)(2,1)} %copy-done.10, bf16[2,640,256]{2,1,0:T(8,128)(2,1)} %copy-done.11, ...), custom_call_target="tpu_custom_call" | custom-call | tf_op jit(solution)/shard_map/qkv_back/pallas_call | solution.py:151
  334.6 4.3 norm_back.3
  345.2 3.6 collective-permute-start.46
  350.4 7.7 %statistics.2 = (f32[128,4096]{1,0:T(8,128)}, f32[512,1024]{1,0:T(8,128)}, f32[1,128]{1,0:T(1,128)}, f32[1,512]{1,0:T(1,128)}, f32[2,5376]{1,0:T(2,128)}) custom-call(s32[4]{0:T(128)} %pad_add_fusion.place_ref, bf16[256,1024]{1,0:T(8,128)(2,1)} %reduce-scatter.7.cloned.1.call-done.refs_0_, bf16[256,1024]{1,0:T(8,128)(2,1)} %copy-done.56, ...), custom_call_target="tpu_custom_call" | custom-call | tf_op jit(solution)/shard_map/statistics/pallas_call | solution.py:151
  358.2 3.7 reduce-scatter.11.cloned.1.call-done.refs_0_
  385.0 3.3 reduce-scatter.9.cloned.1.call-done.refs_4_
  390.5 7.0 %update.2 = (f32[128,4096]{1,0:T(8,128)}, f32[512,1024]{1,0:T(8,128)}, f32[1,4096]{1,0:T(1,128)}, f32[1,1024]{1,0:T(1,128)}, f32[8,128]{1,0:T(8,128)}) custom-call(s32[4]{0:T(128)} %pad_add_fusion.place_ref, f32[128,4096]{1,0:T(8,128)} %get-tuple-element.179.refs_0_, f32[512,1024]{1,0:T(8,128)} %get-tuple-element.181.refs_1_, ...), custom_call_target="tpu_custom_call" | custom-call | tf_op jit(solution)/shard_map/update/pallas_call | solution.py:151
  400.2 4.9 %statistics.3 = (f32[128,1024]{1,0:T(8,128)}, f32[128,3072]{1,0:T(8,128)}, f32[1,128]{1,0:T(1,128)}, f32[1,128]{1,0:T(1,128)}, f32[2,5376]{1,0:T(2,128)}, /*inde...) custom-call(s32[4]{0:T(128)} %pad_add_fusion.place_ref, ...), custom_call_target="tpu_custom_call" | custom-call | tf_op jit(solution)/shard_map/statistics/pallas_call | solution.py:151
  409.5 3.8 collective-permute-done.55
  419.4 5.0 %update.3 = (f32[128,1024]{1,0:T(8,128)}, f32[128,3072]{1,0:T(8,128)}, f32[1,1024]{1,0:T(1,128)}, f32[1,3072]{1,0:T(1,128)}, f32[1,12]{1,0:T(1,128)}, /*index=5*...) custom-call(s32[4]{0:T(128)} %pad_add_fusion.place_ref, ...), custom_call_target="tpu_custom_call" | custom-call | tf_op jit(solution)/shard_map/update/pallas_call | solution.py:151
  (281 shorter events, 129.2 us)
Async XLA Ops:
  7.2 90.5 %all-gather.5.cloned.1.call-start = ((), (), s32[]{:S(2)}) async-start(), calls=%async_computation.5 | async-start | bytes 1310720 | tf_op jit(solution)/shard_map/all_gather | solution.py:68
  42.7 76.6 %all-gather.3.cloned.1.call-start = ((), (), s32[]{:S(2)}) async-start(), calls=%async_computation.4 | async-start | bytes 1310720 | tf_op jit(solution)/shard_map/all_gather | solution.py:68
  42.8 30.1 %collective-permute-start.2 = (bf16[4,160,768]{2,1,0:T(8,128)(2,1)S(1)}, bf16[4,160,768]{2,1,0:T(8,128)(2,1)S(1)}, u32[]{:S(2)}, u32[]{:S(2)}) collective-permute-start(bf16[4,160,768]{2,1,0:T(8,128)(2,1)S(1)} %bitcast.75), channel_id=1, source_target_pairs={{0,4},{4,0},{1,5},{5,1},{2,6},{6,2},{3,7},{7,3},{8,12},{12,8},{9,1... | collective-permute-start | bytes 2949128 | tf_op jit(solution)/shard_map/ppermute | solution.py:41
  44.3 25.0 %collective-permute-start = (bf16[640,512]{1,0:T(8,128)(2,1)}, bf16[640,512]{1,0:T(8,128)(2,1)S(1)}, u32[]{:S(2)}, u32[]{:S(2)}) collective-permute-start(bf16[640,512]{1,0:T(8,128)(2,1)} %get-tuple-element.218), channel_id=1, source_target_pairs={{0,1},{1,0},{2,3},{3,2},{4,5},{5,4},{6,7},{7,6},{8,9},{9,8},{10,11... | collective-permute-start | bytes 1966088 | tf_op jit(solution)/shard_map/ppermute | solution.py:41
  44.3 25.0 %collective-permute-start.1 = (bf16[640,512]{1,0:T(8,128)(2,1)}, bf16[640,512]{1,0:T(8,128)(2,1)}, u32[]{:S(2)}, u32[]{:S(2)}) collective-permute-start(bf16[640,512]{1,0:T(8,128)(2,1)} %get-tuple-element.219), channel_id=1, source_target_pairs={{0,1},{1,0},{2,3},{3,2},{4,5},{5,4},{6,7},{7,6},{8,9},{9,8},{10,11... | collective-permute-start | bytes 1966088 | tf_op jit(solution)/shard_map/ppermute | solution.py:41
  67.3 15.9 %collective-permute-start.4 = (bf16[4,64,1280]{2,1,0:T(8,128)(2,1)S(1)}, bf16[4,64,1280]{2,1,0:T(8,128)(2,1)}, u32[]{:S(2)}, u32[]{:S(2)}) collective-permute-start(bf16[4,64,1280]{2,1,0:T(8,128)(2,1)S(1)} %bitcast.70), channel_id=1, source_target_pairs={{0,4},{4,0},{1,5},{5,1},{2,6},{6,2},{3,7},{7,3},{8,12},{12,8},{9,1... | collective-permute-start | bytes 1966088 | tf_op jit(solution)/shard_map/ppermute | solution.py:41
  67.8 30.0 %collective-permute-start.3 = (bf16[4,64,1280]{2,1,0:T(8,128)(2,1)S(1)}, bf16[4,64,1280]{2,1,0:T(8,128)(2,1)}, u32[]{:S(2)}, u32[]{:S(2)}) collective-permute-start(bf16[4,64,1280]{2,1,0:T(8,128)(2,1)S(1)} %bitcast.71), channel_id=1, source_target_pairs={{0,2},{2,0},{1,3},{3,1},{4,6},{6,4},{5,7},{7,5},{8,10},{10,8},{9,1... | collective-permute-start | bytes 1966088 | tf_op jit(solution)/shard_map/ppermute | solution.py:41
  83.8 198.9 %reduce-scatter.7.cloned.1.call-start = ((), (), s32[]{:S(2)}) async-start(), calls=%async_computation.7 | async-start | bytes 2621440 | tf_op jit(solution)/shard_map/reduce_scatter | solution.py:96
  97.8 21.5 %collective-permute-start.6 = (bf16[4,128,1024]{2,1,0:T(8,128)(2,1)}, bf16[4,128,1024]{2,1,0:T(8,128)(2,1)}, u32[]{:S(2)}, u32[]{:S(2)}) collective-permute-start(bf16[4,128,1024]{2,1,0:T(8,128)(2,1)} %bitcast.83), channel_id=1, source_target_pairs={{0,4},{4,0},{1,5},{5,1},{2,6},{6,2},{3,7},{7,3},{8,12},{12,8},{9,1... | collective-permute-start | bytes 3145736 | tf_op jit(solution)/shard_map/ppermute | solution.py:41
  99.4 23.1 %collective-permute-start.8 = (bf16[4,128,1024]{2,1,0:T(8,128)(2,1)}, bf16[4,128,1024]{2,1,0:T(8,128)(2,1)}, u32[]{:S(2)}, u32[]{:S(2)}) collective-permute-start(bf16[4,128,1024]{2,1,0:T(8,128)(2,1)} %bitcast.84), channel_id=1, source_target_pairs={{0,2},{2,0},{1,3},{3,1},{4,6},{6,4},{5,7},{7,5},{8,10},{10,8},{9,1... | collective-permute-start | bytes 3145736 | tf_op jit(solution)/shard_map/ppermute | solution.py:41
  101.0 20.0 %collective-permute-start.9 = (bf16[2,640,256]{2,1,0:T(8,128)(2,1)}, bf16[2,640,256]{2,1,0:T(8,128)(2,1)}, u32[]{:S(2)}, u32[]{:S(2)}) collective-permute-start(bf16[2,640,256]{2,1,0:T(8,128)(2,1)} %copy-done.26), channel_id=1, source_target_pairs={{0,1},{1,0},{2,3},{3,2},{4,5},{5,4},{6,7},{7,6},{8,9},{9,8},{10,11... | collective-permute-start | bytes 1966088 | tf_op jit(solution)/shard_map/ppermute | solution.py:41
  119.3 25.2 %collective-permute-start.7 = (bf16[4,128,1024]{2,1,0:T(8,128)(2,1)}, bf16[4,128,1024]{2,1,0:T(8,128)(2,1)}, u32[]{:S(2)}, u32[]{:S(2)}) collective-permute-start(bf16[4,128,1024]{2,1,0:T(8,128)(2,1)} %bitcast.86), channel_id=1, source_target_pairs={{0,4},{4,0},{1,5},{5,1},{2,6},{6,2},{3,7},{7,3},{8,12},{12,8},{9,1... | collective-permute-start | bytes 3145736 | tf_op jit(solution)/shard_map/ppermute | solution.py:41
  121.0 26.4 %collective-permute-start.14 = (bf16[4,128,1024]{2,1,0:T(8,128)(2,1)}, bf16[4,128,1024]{2,1,0:T(8,128)(2,1)}, u32[]{:S(2)}, u32[]{:S(2)}) collective-permute-start(bf16[4,128,1024]{2,1,0:T(8,128)(2,1)} %collective-permute-done.6.refs_5_), channel_id=1, source_target_pairs={{0,2},{2,0},{1,3},{3,1},{4,6},{6,4},{5,7},{7,5},{8,10},{10,8},{9,1... | collective-permute-start | bytes 3145736 | tf_op jit(solution)/shard_map/ppermute | solution.py:41
  122.5 22.4 %collective-permute-start.12 = (bf16[640,512]{1,0:T(8,128)(2,1)}, bf16[640,512]{1,0:T(8,128)(2,1)}, u32[]{:S(2)}, u32[]{:S(2)}) collective-permute-start(bf16[640,512]{1,0:T(8,128)(2,1)} %get-tuple-element.253), channel_id=1, source_target_pairs={{0,1},{1,0},{2,3},{3,2},{4,5},{5,4},{6,7},{7,6},{8,9},{9,8},{10,11... | collective-permute-start | bytes 1966088 | tf_op jit(solution)/shard_map/ppermute | solution.py:41
  122.5 22.4 %collective-permute-start.13 = (bf16[640,512]{1,0:T(8,128)(2,1)}, bf16[640,512]{1,0:T(8,128)(2,1)}, u32[]{:S(2)}, u32[]{:S(2)}) collective-permute-start(bf16[640,512]{1,0:T(8,128)(2,1)} %get-tuple-element.254), channel_id=1, source_target_pairs={{0,1},{1,0},{2,3},{3,2},{4,5},{5,4},{6,7},{7,6},{8,9},{9,8},{10,11... | collective-permute-start | bytes 1966088 | tf_op jit(solution)/shard_map/ppermute | solution.py:41
  123.1 58.5 %collective-permute-start.17 = (bf16[4,128,1024]{2,1,0:T(8,128)(2,1)}, bf16[4,128,1024]{2,1,0:T(8,128)(2,1)}, u32[]{:S(2)}, u32[]{:S(2)}) collective-permute-start(bf16[4,128,1024]{2,1,0:T(8,128)(2,1)} %bitcast.87), channel_id=1, source_target_pairs={{0,2},{2,0},{1,3},{3,1},{4,6},{6,4},{5,7},{7,5},{8,10},{10,8},{9,1... | collective-permute-start | bytes 3145736 | tf_op jit(solution)/shard_map/ppermute | solution.py:41
  144.5 45.1 %collective-permute-start.18 = (bf16[4,128,1024]{2,1,0:T(8,128)(2,1)}, bf16[4,128,1024]{2,1,0:T(8,128)(2,1)}, u32[]{:S(2)}, u32[]{:S(2)}) collective-permute-start(bf16[4,128,1024]{2,1,0:T(8,128)(2,1)} %collective-permute-done.7.refs_5_), channel_id=1, source_target_pairs={{0,2},{2,0},{1,3},{3,1},{4,6},{6,4},{5,7},{7,5},{8,10},{10,8},{9,1... | collective-permute-start | bytes 3145736 | tf_op jit(solution)/shard_map/ppermute | solution.py:41
  179.5 45.0 %collective-permute-start.15 = (bf16[4,128,1024]{2,1,0:T(8,128)(2,1)}, bf16[4,128,1024]{2,1,0:T(8,128)(2,1)}, u32[]{:S(2)}, u32[]{:S(2)}) collective-permute-start(bf16[4,128,1024]{2,1,0:T(8,128)(2,1)} %get-tuple-element.257), channel_id=1, source_target_pairs={{0,4},{4,0},{1,5},{5,1},{2,6},{6,2},{3,7},{7,3},{8,12},{12,8},{9,1... | collective-permute-start | bytes 3145736 | tf_op jit(solution)/shard_map/ppermute | solution.py:41
  179.9 44.7 %collective-permute-start.16 = (bf16[4,128,1024]{2,1,0:T(8,128)(2,1)}, bf16[4,128,1024]{2,1,0:T(8,128)(2,1)}, u32[]{:S(2)}, u32[]{:S(2)}) collective-permute-start(bf16[4,128,1024]{2,1,0:T(8,128)(2,1)} %get-tuple-element.259), channel_id=1, source_target_pairs={{0,4},{4,0},{1,5},{5,1},{2,6},{6,2},{3,7},{7,3},{8,12},{12,8},{9,1... | collective-permute-start | bytes 3145736 | tf_op jit(solution)/shard_map/ppermute | solution.py:41
  229.2 99.0 %reduce-scatter.5.cloned.1.call-start = ((), (), s32[]{:S(2)}) async-start(), calls=%async_computation.6 | async-start | bytes 2621440 | tf_op jit(solution)/shard_map/reduce_scatter | solution.py:96
  230.4 44.2 %collective-permute-start.23 = (bf16[4,128,1024]{2,1,0:T(8,128)(2,1)}, bf16[4,128,1024]{2,1,0:T(8,128)(2,1)S(1)}, u32[]{:S(2)}, u32[]{:S(2)}) collective-permute-start(bf16[4,128,1024]{2,1,0:T(8,128)(2,1)} %get-tuple-element.279), channel_id=1, source_target_pairs={{0,4},{4,0},{1,5},{5,1},{2,6},{6,2},{3,7},{7,3},{8,12},{12,8},{9,1... | collective-permute-start | bytes 3145736 | tf_op jit(solution)/shard_map/ppermute | solution.py:41
  232.0 46.6 %collective-permute-start.24 = (bf16[4,128,1024]{2,1,0:T(8,128)(2,1)}, bf16[4,128,1024]{2,1,0:T(8,128)(2,1)S(1)}, u32[]{:S(2)}, u32[]{:S(2)}) collective-permute-start(bf16[4,128,1024]{2,1,0:T(8,128)(2,1)} %get-tuple-element.281), channel_id=1, source_target_pairs={{0,4},{4,0},{1,5},{5,1},{2,6},{6,2},{3,7},{7,3},{8,12},{12,8},{9,1... | collective-permute-start | bytes 3145736 | tf_op jit(solution)/shard_map/ppermute | solution.py:41
  280.9 80.9 %reduce-scatter.11.cloned.1.call-start = ((), (), s32[]{:S(2)}) async-start(), calls=%async_computation.9 | async-start | bytes 1638400 | tf_op jit(solution)/shard_map/reduce_scatter | solution.py:96
  281.0 30.6 %collective-permute-start.28 = (bf16[4,128,768]{2,1,0:T(8,128)(2,1)}, bf16[4,128,768]{2,1,0:T(8,128)(2,1)}, u32[]{:S(2)}, u32[]{:S(2)}) collective-permute-start(bf16[4,128,768]{2,1,0:T(8,128)(2,1)} %copy-done.48), channel_id=1, source_target_pairs={{0,4},{4,0},{1,5},{5,1},{2,6},{6,2},{3,7},{7,3},{8,12},{12,8},{9,1... | collective-permute-start | bytes 2359304 | tf_op jit(solution)/shard_map/ppermute | solution.py:41
  282.7 18.4 %collective-permute-start.29 = (bf16[256,1024]{1,0:T(8,128)(2,1)}, bf16[256,1024]{1,0:T(8,128)(2,1)S(1)}, u32[]{:S(2)}, u32[]{:S(2)}) collective-permute-start(bf16[256,1024]{1,0:T(8,128)(2,1)} %reduce-scatter.7.cloned.1.call-done.refs_0_), channel_id=1, source_target_pairs={{0,2},{2,0},{1,3},{3,1},{4,6},{6,4},{5,7},{7,5},{8,10},{10,8},{9,1... | collective-permute-start | bytes 1572872 | tf_op jit(solution)/shard_map/ppermute | solution.py:41
  283.1 28.5 %collective-permute-start.27 = (bf16[4,128,512]{2,1,0:T(8,128)(2,1)}, bf16[4,128,512]{2,1,0:T(8,128)(2,1)S(1)}, u32[]{:S(2)}, u32[]{:S(2)}) collective-permute-start(bf16[4,128,512]{2,1,0:T(8,128)(2,1)} %copy-done.49), channel_id=1, source_target_pairs={{0,4},{4,0},{1,5},{5,1},{2,6},{6,2},{3,7},{7,3},{8,12},{12,8},{9,1... | collective-permute-start | bytes 1572872 | tf_op jit(solution)/shard_map/ppermute | solution.py:41
  314.2 74.0 %reduce-scatter.9.cloned.1.call-start = ((), (), s32[]{:S(2)}) async-start(), calls=%async_computation.8 | async-start | bytes 983040 | tf_op jit(solution)/shard_map/reduce_scatter | solution.py:96
  314.3 25.2 %collective-permute-start.32 = (bf16[4,128,768]{2,1,0:T(8,128)(2,1)}, bf16[4,128,768]{2,1,0:T(8,128)(2,1)}, u32[]{:S(2)}, u32[]{:S(2)}) collective-permute-start(bf16[4,128,768]{2,1,0:T(8,128)(2,1)} %get-tuple-element.323), channel_id=1, source_target_pairs={{0,4},{4,0},{1,5},{5,1},{2,6},{6,2},{3,7},{7,3},{8,12},{12,8},{9,1... | collective-permute-start | bytes 2359304 | tf_op jit(solution)/shard_map/ppermute | solution.py:41
  328.7 20.1 %collective-permute-start.33 = (bf16[256,1024]{1,0:T(8,128)(2,1)}, bf16[256,1024]{1,0:T(8,128)(2,1)}, u32[]{:S(2)}, u32[]{:S(2)}) collective-permute-start(bf16[256,1024]{1,0:T(8,128)(2,1)} %reduce-scatter.7.cloned.1.call-done.refs_0_), channel_id=1, source_target_pairs={{0,1},{1,0},{2,3},{3,2},{4,5},{5,4},{6,7},{7,6},{8,9},{9,8},{10,11... | collective-permute-start | bytes 1572872 | tf_op jit(solution)/shard_map/ppermute | solution.py:41
  330.1 18.7 %collective-permute-start.34 = (bf16[256,1024]{1,0:T(8,128)(2,1)}, bf16[256,1024]{1,0:T(8,128)(2,1)}, u32[]{:S(2)}, u32[]{:S(2)}) collective-permute-start(bf16[256,1024]{1,0:T(8,128)(2,1)} %copy-done.56), channel_id=1, source_target_pairs={{0,1},{1,0},{2,3},{3,2},{4,5},{5,4},{6,7},{7,6},{8,9},{9,8},{10,11... | collective-permute-start | bytes 1572872 | tf_op jit(solution)/shard_map/ppermute | solution.py:41
  345.2 18.1 %collective-permute-start.46 = (f32[8,1536]{1,0:T(8,128)S(1)}, f32[8,1536]{1,0:T(8,128)S(1)}, u32[]{:S(2)}, u32[]{:S(2)}) collective-permute-start(f32[8,1536]{1,0:T(8,128)S(1)} %add.82), channel_id=1, source_target_pairs={{0,24},{8,0},{16,8},{24,16},{1,25},{9,1},{17,9},{25,17},{2,26},{10... | collective-permute-start | bytes 147464 | tf_op jit(solution)/shard_map/ppermute | solution.py:46
  373.0 15.2 %collective-permute-start.49 = (bf16[128,1280]{1,0:T(8,128)(2,1)}, bf16[128,1280]{1,0:T(8,128)(2,1)S(1)}, u32[]{:S(2)}, u32[]{:S(2)}) collective-permute-start(bf16[128,1280]{1,0:T(8,128)(2,1)} %reduce-scatter.11.cloned.1.call-done.refs_0_), channel_id=1, source_target_pairs={{0,1},{1,0},{2,3},{3,2},{4,5},{5,4},{6,7},{7,6},{8,9},{9,8},{10,11... | collective-permute-start | bytes 983048 | tf_op jit(solution)/shard_map/ppermute | solution.py:41
  (99 other events, 610.1 us)
Sparse Core Ops, SparseCore 0:
  42.8 33.8 all-gather.4
  83.9 29.2 all-gather.2
  229.3 44.3 reduce-scatter.6
  281.1 44.3 reduce-scatter.4
  328.1 33.6 reduce-scatter.10
  364.6 23.5 reduce-scatter.8

commit v9 on v8

--- a/solution.py
+++ b/solution.py
@@ -1221,7 +1221,7 @@
 SPLIT = {"out": 1, "qkv": 3}
 
 
-def update(place, grads, new_rows, weights, cols_states, pack, group, extra=None, clips=None):
+def update(place, grads, new_rows, weights, cols_states, packs, group, extra=None, clips=None):
     amount = len(weights)
     vectors = 0 if extra is None else len(extra[0])
 
@@ -1234,7 +1234,8 @@
             return taken
 
         grad_refs, row_refs, weight_refs, state_refs = [take(amount) for _ in range(4)]
-        (pack_ref,) = take(1)
+        pack_refs = take(len(packs))
+        pack_ref = sum([ref[...] for ref in pack_refs[1:]], pack_refs[0][...])
         if vectors:
             vector_grads, moment_refs, param_refs = [take(vectors) for _ in range(3)]
             (clips_ref,) = take(1)
@@ -1288,7 +1289,7 @@
                 row = jnp.where(lane == number, value, row)
             clip_ref[...] = row[:, : len(found)]
 
-    ins = [*grads, *new_rows, *weights, *cols_states, pack]
+    ins = [*grads, *new_rows, *weights, *cols_states, *packs]
     outs = [sds(a.shape, jnp.float32) for a in (*weights, *cols_states)]
     outs.append(sds((1, len(MATRICES) + vectors) if vectors else (8, LANES), jnp.float32))
     if vectors:
@@ -1581,7 +1582,8 @@
     scattered[2] = after(scattered[2], rows_early[0])
     own_mid = after(sum_y(scattered[2]), terms)
     pairs.append(with_core(own_mid))
-    pack = sum_over(pack, ("z", "x"))
+    pack = sum_over(pack, ("z",))
+    pack = [pack, swap(pack, "x")]
     scattered[3] = after(scattered[3], (pack, pairs[-1]))
     pairs.append(sum_y_and_core(scattered[3]))
     new_early, cols_early, clips_early, _ = update(
@@ -1605,13 +1607,14 @@
         group,
         (terms, params, moments),
     )
+    pack = sum_over(pack, ("z",))
     new_late, cols_late, clip_factors, new_vectors = update(
         place,
         grads_late,
         rows_late,
         weights,
         [as_row(state) for state in (out_cols, qkv_cols)],
-        sum_over(pack, ("z", "x")),
+        [pack, swap(pack, "x")],
         group,
         (vector_grads, new_moments, params),
         clips_early,

time: 437 us -> 437 us (level)
    ppermute x5 -> x3, waiting for transfers between devices: 10.7 us -> 5.5 us  [partner(): return lax.ppermute(value, axis, [(i, i ^ step) for i in range(size)])]
    ppermute x43 -> x45, waiting for transfers between devices: 41.1 us -> 46.1 us  [swap(): return lax.ppermute(value, axis, [(0, 1), (1, 0)])]
    ppermute x43 -> x45, starting transfers between devices: 29 us -> 32 us  [swap(): return lax.ppermute(value, axis, [(0, 1), (1, 0)])]
    unnamed x134 -> x142, local copies, waits for them, and re-layouts: 33.9 us -> 34.5 us
where the time goes in v9:
time: 437 us; the launch traced here: 432 us
  Pallas kernels  204 us (47%)
  waiting for transfers between devices  70.6 us (16%)
  starting transfers between devices  46.4 us (11%)
  blocking collectives  46.2 us (11%)
  local copies, waits for them, and re-layouts  34.5 us (8%)
  between operations  15.3 us (4%)
  other arithmetic  14.7 us (3%)
    pallas_call x25, Pallas kernels, call(): pl.pallas_call(body, out_shape=outs, grid_spec=pltpu.PrefetchScalarGridSp...  204 us
    all_gather x2, blocking collectives, along_z(): near = lax.all_gather(shard, 'z', axis=0, tiled=True)  46.2 us
    ppermute x45, waiting for transfers between devices, swap(): return lax.ppermute(value, axis, [(0, 1), (1, 0)])  46.1 us
    unnamed x142, local copies, waits for them, and re-layouts  34.5 us
    ppermute x45, starting transfers between devices, swap(): return lax.ppermute(value, axis, [(0, 1), (1, 0)])  32 us
    ppermute x9, starting transfers between devices, shift(): lax.ppermute(value, axis, [(i, (i + step) % size) for i in range(size)])  11.3 us
    ppermute x9, waiting for transfers between devices, shift(): lax.ppermute(value, axis, [(i, (i + step) % size) for i in range(size)])  11.1 us
  transfers between devices with their start and end apart: 64, of which 26 were waited for; matrix products, arithmetic and copies ran while one was open for 2% of the time, Pallas kernels for 42%

profile of v9, /device:TPU:0, one launch (start us, length us, event | category | flops | bytes accessed | tf_op | source)
XLA Modules:
  0.0 431.6 jit_solution(13092929498929782565)
XLA Ops:
  11.1 23.7 %all_gather.12 = bf16[640,768]{1,0:T(8,128)(2,1)S(1)} all-gather(bf16[160,768]{1,0:T(8,128)(2,1)} %get-tuple-element.212), channel_id=1, replica_groups=mesh['z'=4,'x'=2,'y'=2,'c'=2] {'z'}, dimensions={0}, use_global_device_ids=true | all-gather | bytes 1228800 | tf_op jit(solution)/shard_map/all_gather | solution.py:68
  34.8 3.5 pad_rows.2
  38.3 4.4 %prepare_rest.1 = (bf16[128,1024]{1,0:T(8,128)(2,1)}, bf16[128,1024]{1,0:T(8,128)(2,1)}, f32[1,1024]{1,0:T(1,128)}) custom-call(s32[4]{0:T(128)} %pad_add_fusion.place_ref, f32[128,4096]{1,0:T(8,128)} %refs_4_.2, f32[512,1024]{1,0:T(8,128)} %refs_5_.2, bf16[577,1024]{1,0:T(8,128)(2,1)} %ref.3), custom_call_target="tpu_custom_call" | custom-call | tf_op jit(solution)/shard_map/prepare_rest/pallas_call | solution.py:151
  44.9 22.5 %all_gather.13 = bf16[256,1280]{1,0:T(8,128)(2,1)S(1)} all-gather(bf16[64,1280]{1,0:T(8,128)(2,1)S(1)} %copy-done.67), channel_id=1, replica_groups=mesh['z'=4,'x'=2,'y'=2,'c'=2] {'z'}, dimensions={0}, use_global_device_ids=true | all-gather | bytes 819200 | tf_op jit(solution)/shard_map/all_gather | solution.py:68
  69.3 3.5 pad_rows.3
  73.8 9.4 %project_first.1 = (bf16[2,640,1024]{2,1,0:T(8,128)(2,1)}, bf16[2,640,256]{2,1,0:T(8,128)(2,1)}, bf16[2,640,256]{2,1,0:T(8,128)(2,1)}, bf16[2,640,256]{2,1,0:T(8...) custom-call(s32[4]{0:T(128)} %pad_add_fusion.place_ref, ...), custom_call_target="tpu_custom_call" | custom-call | tf_op jit(solution)/shard_map/project_first/pallas_call | solution.py:151
  87.3 6.9 %attention.2 = (bf16[2,640,256]{2,1,0:T(8,128)(2,1)S(1)}, bf16[2,2,2,640,640]{4,3,2,1,0:T(8,128)(2,1)S(1)}) custom-call(s32[4]{0:T(128)S(1)} %copy-done.42, bf16[2,640,256]{2,1,0:T(8,128)(2,1)S(1)} %copy-done.20, bf16[2,640,256]{2,1,0:T(8,128)(2,1)S(1)} %copy-done.22, bf16[2,640,256]{2,1,0:T(8,128)(2,1)S(1)} %copy-done.24), custom_call_target="tpu_custom_call" | custom-call | tf_op jit(solution)/shard_map/attention/pallas_call | solution.py:151
  103.9 4.5 %project_next.1 = (bf16[2,640,256]{2,1,0:T(8,128)(2,1)S(1)}, bf16[2,640,256]{2,1,0:T(8,128)(2,1)S(1)}, bf16[2,640,256]{2,1,0:T(8,128)(2,1)S(1)}) custom-call(s32[4]{0:T(128)S(1)} %copy-done.42, bf16[2,640,1024]{2,1,0:T(8,128)(2,1)S(1)} %copy-done, f32[8,1024]{1,0:T(8,128)S(1)} %copy-done.38, bf16[4,64,1280]{2,1,0:T(8,128)(2,1)S(1)} %bitcast.73, ...), custom_call_target="tpu_custom_call" | custom-call | tf_op jit(solution)/shard_map/project_next/pallas_call | solution.py:151
  108.4 6.9 %attention.3 = (bf16[2,640,256]{2,1,0:T(8,128)(2,1)S(1)}, bf16[2,2,2,640,640]{4,3,2,1,0:T(8,128)(2,1)S(1)}) custom-call(s32[4]{0:T(128)S(1)} %copy-done.42, bf16[2,640,256]{2,1,0:T(8,128)(2,1)S(1)} %get-tuple-element.241.q_ref, bf16[2,640,256]{2,1,0:T(8,128)(2,1)S(1)} %get-tuple-element.242.k_ref, bf16[2,640,256]{2,1,0:T(8,128)(2,1)S(1)} %get-tuple-element.243.v_ref), custom_call_target="tpu_custom_call" | custom-call | tf_op jit(solution)/shard_map/attention/pallas_call | solution.py:151
  123.6 9.8 %project_out.1 = (f32[640,1024]{1,0:T(8,128)}, bf16[2,640,1024]{2,1,0:T(8,128)(2,1)}) custom-call(s32[4]{0:T(128)} %pad_add_fusion.place_ref, bf16[2,640,256]{2,1,0:T(8,128)(2,1)} %copy-done.26, bf16[2,640,256]{2,1,0:T(8,128)(2,1)} %copy-done.28, bf16[2,640,256]{2,1,0:T(8,128)(2,1)} %collective-permute-done.9.refs_2_.refs_4_, ...), custom_call_target="tpu_custom_call" | custom-call | tf_op jit(solution)/shard_map/project_out/pallas_call | solution.py:151
  133.4 11.2 %collective-permute-done.7.refs_5_ = bf16[4,128,1024]{2,1,0:T(8,128)(2,1)} collective-permute-done((bf16[4,128,1024]{2,1,0:T(8,128)(2,1)}, bf16[4,128,1024]{2,1,0:T(8,128)(2,1)}, u32[]{:S(2)}, u32[]{:S(2)}) %collective-permute-start.7) | collective-permute-done | bytes 1048608 | tf_op jit(solution)/shard_map/ppermute | solution.py:41
  147.4 32.0 %feed_forward.2 = (f32[640,1024]{1,0:T(8,128)}, f32[640,1024]{1,0:T(8,128)}, f32[640,1024]{1,0:T(8,128)}, f32[640,1024]{1,0:T(8,128)}, f32[1,1024]{1,0:T(1,128)}...) custom-call(s32[4]{0:T(128)} %pad_add_fusion.place_ref, ...), custom_call_target="tpu_custom_call" | custom-call | tf_op jit(solution)/shard_map/feed_forward/pallas_call | solution.py:151
  181.6 8.0 %collective-permute-done.18.refs_6_ = bf16[4,128,1024]{2,1,0:T(8,128)(2,1)} collective-permute-done((bf16[4,128,1024]{2,1,0:T(8,128)(2,1)}, bf16[4,128,1024]{2,1,0:T(8,128)(2,1)}, u32[]{:S(2)}, u32[]{:S(2)}) %collective-permute-start.18) | collective-permute-done | bytes 1048608 | tf_op jit(solution)/shard_map/ppermute | solution.py:41
  189.6 34.9 %feed_forward.3 = (f32[640,1024]{1,0:T(8,128)}, bf16[640,512]{1,0:T(8,128)(2,1)}, bf16[640,512]{1,0:T(8,128)(2,1)}, f32[640,1024]{1,0:T(8,128)}, bf16[640,512]{1...) custom-call(s32[4]{0:T(128)} %pad_add_fusion.place_ref, ...), custom_call_target="tpu_custom_call" | custom-call | tf_op jit(solution)/shard_map/feed_forward/pallas_call | solution.py:151
  241.1 4.4 %norm_back.2 = (f32[8,1024]{1,0:T(8,128)S(1)}, bf16[577,1024]{1,0:T(8,128)(2,1)}, f32[640,1024]{1,0:T(8,128)S(1)}, bf16[640,1024]{1,0:T(8,128)(2,1)S(1)}, bf16[6...) custom-call(s32[4]{0:T(128)S(1)} %copy-done.43, f32[640,1024]{1,0:T(8,128)S(1)} %copy-done.33, ...), custom_call_target="tpu_custom_call" | custom-call | tf_op jit(solution)/shard_map/norm_back/pallas_call | solution.py:151
  250.1 6.7 %out_back.1 = (bf16[2,640,256]{2,1,0:T(8,128)(2,1)S(1)}, bf16[2,640,256]{2,1,0:T(8,128)(2,1)S(1)}, bf16[4,128,512]{2,1,0:T(8,128)(2,1)S(1)}, bf16[4,128,512]{2,1,0:T(8,128)(2,1)S(1)}) custom-call(s32[4]{0:T(128)S(1)} %copy-done.43, bf16[640,1024]{1,0:T(8,128)(2,1)S(1)} %get-tuple-element.283.own_ref.own_half, ...), custom_call_target="tpu_custom_call" | custom-call | tf_op jit(solution)/shard_map/out_back/pallas_call | solution.py:151
  260.1 10.8 %attention_back.2 = (bf16[2,640,256]{2,1,0:T(8,128)(2,1)S(1)}, bf16[2,640,256]{2,1,0:T(8,128)(2,1)S(1)}, bf16[2,640,256]{2,1,0:T(8,128)(2,1)S(1)}) custom-call(s32[4]{0:T(128)S(1)} %copy-done.43, bf16[2,640,256]{2,1,0:T(8,128)(2,1)S(1)} %copy-done.21, bf16[2,640,256]{2,1,0:T(8,128)(2,1)S(1)} %copy-done.23, bf16[2,640,256]{2,1,0:T(8,128)(2,1)S(1)} %copy-done.25, ...), custom_call_target="tpu_custom_call" | custom-call | tf_op jit(solution)/shard_map/attention_back/pallas_call | solution.py:151
  271.0 3.5 qkv_term.2
  274.5 4.0 collective-permute-done.24
  290.0 11.0 %attention_back.3 = (bf16[2,640,256]{2,1,0:T(8,128)(2,1)S(1)}, bf16[2,640,256]{2,1,0:T(8,128)(2,1)S(1)}, bf16[2,640,256]{2,1,0:T(8,128)(2,1)S(1)}) custom-call(s32[4]{0:T(128)S(1)} %copy-done.43, bf16[2,640,256]{2,1,0:T(8,128)(2,1)S(1)} %copy-done.15, bf16[2,640,256]{2,1,0:T(8,128)(2,1)S(1)} %copy-done.17, bf16[2,640,256]{2,1,0:T(8,128)(2,1)S(1)} %copy-done.19, ...), custom_call_target="tpu_custom_call" | custom-call | tf_op jit(solution)/shard_map/attention_back/pallas_call | solution.py:151
  301.1 4.3 %qkv_term.3 = (f32[3,256]{1,0:T(4,128)S(1)}, bf16[4,128,768]{2,1,0:T(8,128)(2,1)S(1)}, bf16[4,128,768]{2,1,0:T(8,128)(2,1)}) custom-call(s32[4]{0:T(128)S(1)} %copy-done.43, bf16[2,640,1024]{2,1,0:T(8,128)(2,1)S(1)} %copy-done, bf16[2,640,256]{2,1,0:T(8,128)(2,1)S(1)} %get-tuple-element.303.gq_ref.refs_3_, ...), custom_call_target="tpu_custom_call" | custom-call | tf_op jit(solution)/shard_map/qkv_term/pallas_call | solution.py:151
  305.5 6.1 %collective-permute-done.27 = bf16[4,128,512]{2,1,0:T(8,128)(2,1)S(1)} collective-permute-done((bf16[4,128,512]{2,1,0:T(8,128)(2,1)}, bf16[4,128,512]{2,1,0:T(8,128)(2,1)S(1)}, u32[]{:S(2)}, u32[]{:S(2)}) %collective-permute-start.27) | collective-permute-done | bytes 524320 | tf_op jit(solution)/shard_map/ppermute | solution.py:41
  316.0 11.7 %qkv_back.1 = (f32[640,1024]{1,0:T(8,128)}, bf16[640,512]{1,0:T(8,128)(2,1)}, bf16[640,512]{1,0:T(8,128)(2,1)}) custom-call(s32[4]{0:T(128)} %pad_add_fusion.place_ref, bf16[2,640,256]{2,1,0:T(8,128)(2,1)} %copy-done.8, bf16[2,640,256]{2,1,0:T(8,128)(2,1)} %copy-done.9, bf16[2,640,256]{2,1,0:T(8,128)(2,1)} %copy-done.10, bf16[2,640,256]{2,1,0:T(8,128)(2,1)} %copy-done.11, ...), custom_call_target="tpu_custom_call" | custom-call | tf_op jit(solution)/shard_map/qkv_back/pallas_call | solution.py:151
  334.7 4.3 norm_back.3
  345.2 3.5 collective-permute-start.46
  350.4 7.7 %statistics.2 = (f32[128,4096]{1,0:T(8,128)}, f32[512,1024]{1,0:T(8,128)}, f32[1,128]{1,0:T(1,128)}, f32[1,512]{1,0:T(1,128)}, f32[2,5376]{1,0:T(2,128)}) custom-call(s32[4]{0:T(128)} %pad_add_fusion.place_ref, bf16[256,1024]{1,0:T(8,128)(2,1)} %reduce-scatter.7.cloned.1.call-done.refs_0_, bf16[256,1024]{1,0:T(8,128)(2,1)} %copy-done.56, ...), custom_call_target="tpu_custom_call" | custom-call | tf_op jit(solution)/shard_map/statistics/pallas_call | solution.py:151
  358.2 3.7 reduce-scatter.11.cloned.1.call-done.refs_0_
  384.3 3.9 reduce-scatter.9.cloned.1.call-done.refs_4_
  390.5 7.1 %update.2 = (f32[128,4096]{1,0:T(8,128)}, f32[512,1024]{1,0:T(8,128)}, f32[1,4096]{1,0:T(1,128)}, f32[1,1024]{1,0:T(1,128)}, f32[8,128]{1,0:T(8,128)}) custom-call(s32[4]{0:T(128)} %pad_add_fusion.place_ref, f32[128,4096]{1,0:T(8,128)} %get-tuple-element.179.refs_0_, f32[512,1024]{1,0:T(8,128)} %get-tuple-element.181.refs_1_, ...), custom_call_target="tpu_custom_call" | custom-call | tf_op jit(solution)/shard_map/update/pallas_call | solution.py:151
  400.2 4.9 %statistics.3 = (f32[128,1024]{1,0:T(8,128)}, f32[128,3072]{1,0:T(8,128)}, f32[1,128]{1,0:T(1,128)}, f32[1,128]{1,0:T(1,128)}, f32[2,5376]{1,0:T(2,128)}, /*inde...) custom-call(s32[4]{0:T(128)} %pad_add_fusion.place_ref, ...), custom_call_target="tpu_custom_call" | custom-call | tf_op jit(solution)/shard_map/statistics/pallas_call | solution.py:151
  409.6 3.7 collective-permute-done.55
  419.5 5.0 %update.3 = (f32[128,1024]{1,0:T(8,128)}, f32[128,3072]{1,0:T(8,128)}, f32[1,1024]{1,0:T(1,128)}, f32[1,3072]{1,0:T(1,128)}, f32[1,12]{1,0:T(1,128)}, /*index=5*...) custom-call(s32[4]{0:T(128)} %pad_add_fusion.place_ref, ...), custom_call_target="tpu_custom_call" | custom-call | tf_op jit(solution)/shard_map/update/pallas_call | solution.py:151
  (287 shorter events, 128.6 us)
Async XLA Ops:
  7.2 90.5 %all-gather.5.cloned.1.call-start = ((), (), s32[]{:S(2)}) async-start(), calls=%async_computation.5 | async-start | bytes 1310720 | tf_op jit(solution)/shard_map/all_gather | solution.py:68
  42.7 76.6 %all-gather.3.cloned.1.call-start = ((), (), s32[]{:S(2)}) async-start(), calls=%async_computation.4 | async-start | bytes 1310720 | tf_op jit(solution)/shard_map/all_gather | solution.py:68
  42.8 30.1 %collective-permute-start.2 = (bf16[4,160,768]{2,1,0:T(8,128)(2,1)S(1)}, bf16[4,160,768]{2,1,0:T(8,128)(2,1)S(1)}, u32[]{:S(2)}, u32[]{:S(2)}) collective-permute-start(bf16[4,160,768]{2,1,0:T(8,128)(2,1)S(1)} %bitcast.75), channel_id=1, source_target_pairs={{0,4},{4,0},{1,5},{5,1},{2,6},{6,2},{3,7},{7,3},{8,12},{12,8},{9,1... | collective-permute-start | bytes 2949128 | tf_op jit(solution)/shard_map/ppermute | solution.py:41
  44.4 25.0 %collective-permute-start = (bf16[640,512]{1,0:T(8,128)(2,1)}, bf16[640,512]{1,0:T(8,128)(2,1)S(1)}, u32[]{:S(2)}, u32[]{:S(2)}) collective-permute-start(bf16[640,512]{1,0:T(8,128)(2,1)} %get-tuple-element.218), channel_id=1, source_target_pairs={{0,1},{1,0},{2,3},{3,2},{4,5},{5,4},{6,7},{7,6},{8,9},{9,8},{10,11... | collective-permute-start | bytes 1966088 | tf_op jit(solution)/shard_map/ppermute | solution.py:41
  44.4 25.0 %collective-permute-start.1 = (bf16[640,512]{1,0:T(8,128)(2,1)}, bf16[640,512]{1,0:T(8,128)(2,1)}, u32[]{:S(2)}, u32[]{:S(2)}) collective-permute-start(bf16[640,512]{1,0:T(8,128)(2,1)} %get-tuple-element.219), channel_id=1, source_target_pairs={{0,1},{1,0},{2,3},{3,2},{4,5},{5,4},{6,7},{7,6},{8,9},{9,8},{10,11... | collective-permute-start | bytes 1966088 | tf_op jit(solution)/shard_map/ppermute | solution.py:41
  67.3 15.9 %collective-permute-start.4 = (bf16[4,64,1280]{2,1,0:T(8,128)(2,1)S(1)}, bf16[4,64,1280]{2,1,0:T(8,128)(2,1)}, u32[]{:S(2)}, u32[]{:S(2)}) collective-permute-start(bf16[4,64,1280]{2,1,0:T(8,128)(2,1)S(1)} %bitcast.70), channel_id=1, source_target_pairs={{0,4},{4,0},{1,5},{5,1},{2,6},{6,2},{3,7},{7,3},{8,12},{12,8},{9,1... | collective-permute-start | bytes 1966088 | tf_op jit(solution)/shard_map/ppermute | solution.py:41
  67.8 30.0 %collective-permute-start.3 = (bf16[4,64,1280]{2,1,0:T(8,128)(2,1)S(1)}, bf16[4,64,1280]{2,1,0:T(8,128)(2,1)}, u32[]{:S(2)}, u32[]{:S(2)}) collective-permute-start(bf16[4,64,1280]{2,1,0:T(8,128)(2,1)S(1)} %bitcast.71), channel_id=1, source_target_pairs={{0,2},{2,0},{1,3},{3,1},{4,6},{6,4},{5,7},{7,5},{8,10},{10,8},{9,1... | collective-permute-start | bytes 1966088 | tf_op jit(solution)/shard_map/ppermute | solution.py:41
  83.8 198.9 %reduce-scatter.7.cloned.1.call-start = ((), (), s32[]{:S(2)}) async-start(), calls=%async_computation.7 | async-start | bytes 2621440 | tf_op jit(solution)/shard_map/reduce_scatter | solution.py:96
  97.8 21.5 %collective-permute-start.6 = (bf16[4,128,1024]{2,1,0:T(8,128)(2,1)}, bf16[4,128,1024]{2,1,0:T(8,128)(2,1)}, u32[]{:S(2)}, u32[]{:S(2)}) collective-permute-start(bf16[4,128,1024]{2,1,0:T(8,128)(2,1)} %bitcast.83), channel_id=1, source_target_pairs={{0,4},{4,0},{1,5},{5,1},{2,6},{6,2},{3,7},{7,3},{8,12},{12,8},{9,1... | collective-permute-start | bytes 3145736 | tf_op jit(solution)/shard_map/ppermute | solution.py:41
  99.4 23.1 %collective-permute-start.8 = (bf16[4,128,1024]{2,1,0:T(8,128)(2,1)}, bf16[4,128,1024]{2,1,0:T(8,128)(2,1)}, u32[]{:S(2)}, u32[]{:S(2)}) collective-permute-start(bf16[4,128,1024]{2,1,0:T(8,128)(2,1)} %bitcast.84), channel_id=1, source_target_pairs={{0,2},{2,0},{1,3},{3,1},{4,6},{6,4},{5,7},{7,5},{8,10},{10,8},{9,1... | collective-permute-start | bytes 3145736 | tf_op jit(solution)/shard_map/ppermute | solution.py:41
  101.0 20.0 %collective-permute-start.9 = (bf16[2,640,256]{2,1,0:T(8,128)(2,1)}, bf16[2,640,256]{2,1,0:T(8,128)(2,1)}, u32[]{:S(2)}, u32[]{:S(2)}) collective-permute-start(bf16[2,640,256]{2,1,0:T(8,128)(2,1)} %copy-done.26), channel_id=1, source_target_pairs={{0,1},{1,0},{2,3},{3,2},{4,5},{5,4},{6,7},{7,6},{8,9},{9,8},{10,11... | collective-permute-start | bytes 1966088 | tf_op jit(solution)/shard_map/ppermute | solution.py:41
  119.3 25.2 %collective-permute-start.7 = (bf16[4,128,1024]{2,1,0:T(8,128)(2,1)}, bf16[4,128,1024]{2,1,0:T(8,128)(2,1)}, u32[]{:S(2)}, u32[]{:S(2)}) collective-permute-start(bf16[4,128,1024]{2,1,0:T(8,128)(2,1)} %bitcast.86), channel_id=1, source_target_pairs={{0,4},{4,0},{1,5},{5,1},{2,6},{6,2},{3,7},{7,3},{8,12},{12,8},{9,1... | collective-permute-start | bytes 3145736 | tf_op jit(solution)/shard_map/ppermute | solution.py:41
  121.0 26.4 %collective-permute-start.14 = (bf16[4,128,1024]{2,1,0:T(8,128)(2,1)}, bf16[4,128,1024]{2,1,0:T(8,128)(2,1)}, u32[]{:S(2)}, u32[]{:S(2)}) collective-permute-start(bf16[4,128,1024]{2,1,0:T(8,128)(2,1)} %collective-permute-done.6.refs_5_), channel_id=1, source_target_pairs={{0,2},{2,0},{1,3},{3,1},{4,6},{6,4},{5,7},{7,5},{8,10},{10,8},{9,1... | collective-permute-start | bytes 3145736 | tf_op jit(solution)/shard_map/ppermute | solution.py:41
  122.5 22.4 %collective-permute-start.12 = (bf16[640,512]{1,0:T(8,128)(2,1)}, bf16[640,512]{1,0:T(8,128)(2,1)}, u32[]{:S(2)}, u32[]{:S(2)}) collective-permute-start(bf16[640,512]{1,0:T(8,128)(2,1)} %get-tuple-element.253), channel_id=1, source_target_pairs={{0,1},{1,0},{2,3},{3,2},{4,5},{5,4},{6,7},{7,6},{8,9},{9,8},{10,11... | collective-permute-start | bytes 1966088 | tf_op jit(solution)/shard_map/ppermute | solution.py:41
  122.5 22.4 %collective-permute-start.13 = (bf16[640,512]{1,0:T(8,128)(2,1)}, bf16[640,512]{1,0:T(8,128)(2,1)}, u32[]{:S(2)}, u32[]{:S(2)}) collective-permute-start(bf16[640,512]{1,0:T(8,128)(2,1)} %get-tuple-element.254), channel_id=1, source_target_pairs={{0,1},{1,0},{2,3},{3,2},{4,5},{5,4},{6,7},{7,6},{8,9},{9,8},{10,11... | collective-permute-start | bytes 1966088 | tf_op jit(solution)/shard_map/ppermute | solution.py:41
  123.0 58.5 %collective-permute-start.17 = (bf16[4,128,1024]{2,1,0:T(8,128)(2,1)}, bf16[4,128,1024]{2,1,0:T(8,128)(2,1)}, u32[]{:S(2)}, u32[]{:S(2)}) collective-permute-start(bf16[4,128,1024]{2,1,0:T(8,128)(2,1)} %bitcast.87), channel_id=1, source_target_pairs={{0,2},{2,0},{1,3},{3,1},{4,6},{6,4},{5,7},{7,5},{8,10},{10,8},{9,1... | collective-permute-start | bytes 3145736 | tf_op jit(solution)/shard_map/ppermute | solution.py:41
  144.5 45.1 %collective-permute-start.18 = (bf16[4,128,1024]{2,1,0:T(8,128)(2,1)}, bf16[4,128,1024]{2,1,0:T(8,128)(2,1)}, u32[]{:S(2)}, u32[]{:S(2)}) collective-permute-start(bf16[4,128,1024]{2,1,0:T(8,128)(2,1)} %collective-permute-done.7.refs_5_), channel_id=1, source_target_pairs={{0,2},{2,0},{1,3},{3,1},{4,6},{6,4},{5,7},{7,5},{8,10},{10,8},{9,1... | collective-permute-start | bytes 3145736 | tf_op jit(solution)/shard_map/ppermute | solution.py:41
  179.5 45.0 %collective-permute-start.15 = (bf16[4,128,1024]{2,1,0:T(8,128)(2,1)}, bf16[4,128,1024]{2,1,0:T(8,128)(2,1)}, u32[]{:S(2)}, u32[]{:S(2)}) collective-permute-start(bf16[4,128,1024]{2,1,0:T(8,128)(2,1)} %get-tuple-element.257), channel_id=1, source_target_pairs={{0,4},{4,0},{1,5},{5,1},{2,6},{6,2},{3,7},{7,3},{8,12},{12,8},{9,1... | collective-permute-start | bytes 3145736 | tf_op jit(solution)/shard_map/ppermute | solution.py:41
  179.9 44.6 %collective-permute-start.16 = (bf16[4,128,1024]{2,1,0:T(8,128)(2,1)}, bf16[4,128,1024]{2,1,0:T(8,128)(2,1)}, u32[]{:S(2)}, u32[]{:S(2)}) collective-permute-start(bf16[4,128,1024]{2,1,0:T(8,128)(2,1)} %get-tuple-element.259), channel_id=1, source_target_pairs={{0,4},{4,0},{1,5},{5,1},{2,6},{6,2},{3,7},{7,3},{8,12},{12,8},{9,1... | collective-permute-start | bytes 3145736 | tf_op jit(solution)/shard_map/ppermute | solution.py:41
  229.2 99.1 %reduce-scatter.5.cloned.1.call-start = ((), (), s32[]{:S(2)}) async-start(), calls=%async_computation.6 | async-start | bytes 2621440 | tf_op jit(solution)/shard_map/reduce_scatter | solution.py:96
  230.4 44.2 %collective-permute-start.23 = (bf16[4,128,1024]{2,1,0:T(8,128)(2,1)}, bf16[4,128,1024]{2,1,0:T(8,128)(2,1)S(1)}, u32[]{:S(2)}, u32[]{:S(2)}) collective-permute-start(bf16[4,128,1024]{2,1,0:T(8,128)(2,1)} %get-tuple-element.279), channel_id=1, source_target_pairs={{0,4},{4,0},{1,5},{5,1},{2,6},{6,2},{3,7},{7,3},{8,12},{12,8},{9,1... | collective-permute-start | bytes 3145736 | tf_op jit(solution)/shard_map/ppermute | solution.py:41
  232.0 46.6 %collective-permute-start.24 = (bf16[4,128,1024]{2,1,0:T(8,128)(2,1)}, bf16[4,128,1024]{2,1,0:T(8,128)(2,1)S(1)}, u32[]{:S(2)}, u32[]{:S(2)}) collective-permute-start(bf16[4,128,1024]{2,1,0:T(8,128)(2,1)} %get-tuple-element.281), channel_id=1, source_target_pairs={{0,4},{4,0},{1,5},{5,1},{2,6},{6,2},{3,7},{7,3},{8,12},{12,8},{9,1... | collective-permute-start | bytes 3145736 | tf_op jit(solution)/shard_map/ppermute | solution.py:41
  280.9 80.9 %reduce-scatter.11.cloned.1.call-start = ((), (), s32[]{:S(2)}) async-start(), calls=%async_computation.9 | async-start | bytes 1638400 | tf_op jit(solution)/shard_map/reduce_scatter | solution.py:96
  281.0 30.6 %collective-permute-start.28 = (bf16[4,128,768]{2,1,0:T(8,128)(2,1)}, bf16[4,128,768]{2,1,0:T(8,128)(2,1)}, u32[]{:S(2)}, u32[]{:S(2)}) collective-permute-start(bf16[4,128,768]{2,1,0:T(8,128)(2,1)} %copy-done.48), channel_id=1, source_target_pairs={{0,4},{4,0},{1,5},{5,1},{2,6},{6,2},{3,7},{7,3},{8,12},{12,8},{9,1... | collective-permute-start | bytes 2359304 | tf_op jit(solution)/shard_map/ppermute | solution.py:41
  282.7 18.5 %collective-permute-start.29 = (bf16[256,1024]{1,0:T(8,128)(2,1)}, bf16[256,1024]{1,0:T(8,128)(2,1)S(1)}, u32[]{:S(2)}, u32[]{:S(2)}) collective-permute-start(bf16[256,1024]{1,0:T(8,128)(2,1)} %reduce-scatter.7.cloned.1.call-done.refs_0_), channel_id=1, source_target_pairs={{0,2},{2,0},{1,3},{3,1},{4,6},{6,4},{5,7},{7,5},{8,10},{10,8},{9,1... | collective-permute-start | bytes 1572872 | tf_op jit(solution)/shard_map/ppermute | solution.py:41
  283.1 28.5 %collective-permute-start.27 = (bf16[4,128,512]{2,1,0:T(8,128)(2,1)}, bf16[4,128,512]{2,1,0:T(8,128)(2,1)S(1)}, u32[]{:S(2)}, u32[]{:S(2)}) collective-permute-start(bf16[4,128,512]{2,1,0:T(8,128)(2,1)} %copy-done.49), channel_id=1, source_target_pairs={{0,4},{4,0},{1,5},{5,1},{2,6},{6,2},{3,7},{7,3},{8,12},{12,8},{9,1... | collective-permute-start | bytes 1572872 | tf_op jit(solution)/shard_map/ppermute | solution.py:41
  314.2 74.0 %reduce-scatter.9.cloned.1.call-start = ((), (), s32[]{:S(2)}) async-start(), calls=%async_computation.8 | async-start | bytes 983040 | tf_op jit(solution)/shard_map/reduce_scatter | solution.py:96
  314.3 25.2 %collective-permute-start.32 = (bf16[4,128,768]{2,1,0:T(8,128)(2,1)}, bf16[4,128,768]{2,1,0:T(8,128)(2,1)}, u32[]{:S(2)}, u32[]{:S(2)}) collective-permute-start(bf16[4,128,768]{2,1,0:T(8,128)(2,1)} %get-tuple-element.323), channel_id=1, source_target_pairs={{0,4},{4,0},{1,5},{5,1},{2,6},{6,2},{3,7},{7,3},{8,12},{12,8},{9,1... | collective-permute-start | bytes 2359304 | tf_op jit(solution)/shard_map/ppermute | solution.py:41
  328.7 20.1 %collective-permute-start.33 = (bf16[256,1024]{1,0:T(8,128)(2,1)}, bf16[256,1024]{1,0:T(8,128)(2,1)}, u32[]{:S(2)}, u32[]{:S(2)}) collective-permute-start(bf16[256,1024]{1,0:T(8,128)(2,1)} %reduce-scatter.7.cloned.1.call-done.refs_0_), channel_id=1, source_target_pairs={{0,1},{1,0},{2,3},{3,2},{4,5},{5,4},{6,7},{7,6},{8,9},{9,8},{10,11... | collective-permute-start | bytes 1572872 | tf_op jit(solution)/shard_map/ppermute | solution.py:41
  330.1 18.7 %collective-permute-start.34 = (bf16[256,1024]{1,0:T(8,128)(2,1)}, bf16[256,1024]{1,0:T(8,128)(2,1)}, u32[]{:S(2)}, u32[]{:S(2)}) collective-permute-start(bf16[256,1024]{1,0:T(8,128)(2,1)} %copy-done.56), channel_id=1, source_target_pairs={{0,1},{1,0},{2,3},{3,2},{4,5},{5,4},{6,7},{7,6},{8,9},{9,8},{10,11... | collective-permute-start | bytes 1572872 | tf_op jit(solution)/shard_map/ppermute | solution.py:41
  345.2 18.1 %collective-permute-start.46 = (f32[8,1536]{1,0:T(8,128)S(1)}, f32[8,1536]{1,0:T(8,128)S(1)}, u32[]{:S(2)}, u32[]{:S(2)}) collective-permute-start(f32[8,1536]{1,0:T(8,128)S(1)} %add.75), channel_id=1, source_target_pairs={{0,24},{8,0},{16,8},{24,16},{1,25},{9,1},{17,9},{25,17},{2,26},{10... | collective-permute-start | bytes 147464 | tf_op jit(solution)/shard_map/ppermute | solution.py:46
  373.0 15.2 %collective-permute-start.49 = (bf16[128,1280]{1,0:T(8,128)(2,1)}, bf16[128,1280]{1,0:T(8,128)(2,1)S(1)}, u32[]{:S(2)}, u32[]{:S(2)}) collective-permute-start(bf16[128,1280]{1,0:T(8,128)(2,1)} %reduce-scatter.11.cloned.1.call-done.refs_0_), channel_id=1, source_target_pairs={{0,1},{1,0},{2,3},{3,2},{4,5},{5,4},{6,7},{7,6},{8,9},{9,8},{10,11... | collective-permute-start | bytes 983048 | tf_op jit(solution)/shard_map/ppermute | solution.py:41
  (103 other events, 631.7 us)
Sparse Core Ops, SparseCore 0:
  42.9 33.8 all-gather.4
  83.9 29.2 all-gather.2
  229.3 44.2 reduce-scatter.6
  281.1 44.3 reduce-scatter.4
  328.1 33.6 reduce-scatter.10
  364.6 23.6 reduce-scatter.8
